TPU v7x, 128 devices: a whole 4x4x4 slice. The times are simulated.
128 devices in a mesh: section: 8 (over z, core), tensor: 16 (over x, y).
Axes of the slice: x: 4, y: 4, z: 4, core: 2. Of those that a mesh axis runs over, the one named last changes fastest.
Arguments:
- dy_top: bfloat16 [2, 64, 8192], replicated, may hold values from -6 to 6
- loss_mask: int32 [2, 64], replicated, may hold values 0 or 1
- counts: int32 [2], replicated, may hold values from 8 to 64, as said below
- layer_in: bfloat16 [8, 2, 64, 8192], P('section'), may hold values from -60 to 60
- conv_in: bfloat16 [8, 2, 64, 10240], P('section', None, None, 'tensor'), may hold values from -6 to 6
- norm_gain: float32 [8, 8192], P('section'), may hold values from 0.3 to 3
- conv_weight: float32 [8, 4, 10240], P('section', None, 'tensor'), may hold values from -2.5 to 2.5
- in_proj: bfloat16 [8, 8192, 10240], P('section', None, 'tensor'), may hold values from -1 to 1
- out_proj: bfloat16 [8, 10240, 8192], P('section', 'tensor'), may hold values from -0.0625 to 0.0625
Outputs:
- section_grads: bfloat16 [8, 2, 64, 8192], P('section')
- gain_grads: float32 [8, 8192], P('section')
- conv_grads: float32 [8, 4, 10240], P('section', None, 'tensor')
Inputs may be any that keep to these rules, and one draw needn't show every extreme that they name: `counts`: one micro-batch holds all 64 positions; the other holds 8 to 32 tokens.
All inputs are finite; a program needn't handle non-finite values.
Results may differ from a plain program's by a relative error of at most 0.033.
Values may be sent and summed in bfloat16 or wider, within the bound.
A program may use at most 128 MiB of HBM per device.

v0:
```python
import jax
import jax.numpy as jnp
from jax import lax
from jax.sharding import PartitionSpec as P

EPSILON = 1e-05


def sent_to_all(x, axis):
    copies = jnp.broadcast_to(x, (lax.axis_size(axis), *x.shape))
    return lax.all_to_all(copies, axis, split_axis=0, concat_axis=0, tiled=True)


def laid_out(parts, dim):
    lengths = list(parts.shape[1:])
    lengths[dim] *= parts.shape[0]
    return jnp.moveaxis(parts, 0, dim).reshape(lengths)


def gathered_copies(x, axis, dim):
    parts = sent_to_all(x, axis)
    return laid_out(parts, dim)


def split_up(x, dim, devices):
    lengths = x.shape
    parts = x.reshape(*lengths[:dim], devices, lengths[dim] // devices, *lengths[dim + 1 :])
    return jnp.moveaxis(parts, dim, 0)


def summed_on_arrival(x, axis, dim):
    parts = split_up(x, dim, lax.axis_size(axis))
    arrived = lax.all_to_all(parts, axis, split_axis=0, concat_axis=0, tiled=True)
    return arrived.astype(jnp.float32).sum(axis=0)


def passed_along(x, axis, by):
    devices = lax.axis_size(axis)
    pairs = [(i, i + by) for i in range(devices) if 0 <= i + by < devices]
    return lax.ppermute(x, axis, pairs)


def of_everyone(x, axis):
    return sent_to_all(x, axis).astype(jnp.float32).sum(axis=0)


def conv_block(weights, ext_vals, tail_rows, d_act):
    kernel_width = weights.shape[0]
    length = d_act.shape[0]
    pre_act = jnp.zeros_like(d_act)
    for lag_idx in range(kernel_width):
        pre_act = (
            pre_act
            + weights[lag_idx]
            * ext_vals[kernel_width - 1 - lag_idx : kernel_width - 1 - lag_idx + length]
        )
    gate_sig = jax.nn.sigmoid(pre_act)
    d_pre = d_act * gate_sig * (1.0 + pre_act * (1.0 - gate_sig))
    padded_back = jnp.concatenate([d_pre, tail_rows], axis=0)
    d_vals = jnp.zeros_like(d_pre)
    for lag_idx in range(kernel_width):
        d_vals = d_vals + weights[lag_idx] * padded_back[lag_idx : lag_idx + length]
    lag_grads = jnp.stack(
        [
            jnp.sum(
                d_pre * ext_vals[kernel_width - 1 - lag_idx : kernel_width - 1 - lag_idx + length],
                axis=0,
            )
            for lag_idx in range(kernel_width)
        ]
    )
    return (d_vals.astype(jnp.bfloat16), lag_grads, d_pre[: kernel_width - 1])


def norm_backward(d_norm, saved_now, upstream, gain_vec):
    values = saved_now.astype(jnp.float32)
    inv_rms = lax.rsqrt(jnp.mean(values * values, axis=-1, keepdims=True) + EPSILON)
    normed = values * inv_rms
    d_hat = d_norm * gain_vec
    d_in = inv_rms * (d_hat - normed * jnp.mean(d_hat * normed, axis=-1, keepdims=True))
    return (upstream.astype(jnp.float32) + d_in, jnp.sum(d_norm * normed, axis=0))


def local(dy_top, loss_mask, counts, layer_in, conv_in, norm_gain, conv_weight, in_proj, out_proj):
    sections = lax.axis_size("section")
    tensors = lax.axis_size("tensor")
    section_idx = lax.axis_index("section")
    tensor_idx = lax.axis_index("tensor")
    batches = dy_top.shape[0]
    seq_len = dy_top.shape[1]
    model_width = dy_top.shape[2]
    saved_rows = layer_in[0]
    gain_vec = norm_gain[0]
    weights = conv_weight[0]
    kernel_width = weights.shape[0]
    local_channels = weights.shape[1]
    w_in = in_proj[0]
    w_out = out_proj[0]
    conv_padded = jnp.pad(conv_in[0], ((0, 0), (kernel_width - 1, 0), (0, 0)))
    positions = jnp.arange(seq_len, dtype=jnp.int32)
    keep_mask = (loss_mask == 1) & (positions[None, :] < counts[:, None])
    top_grads = jnp.where(keep_mask[:, :, None], dy_top, jnp.zeros_like(dy_top))
    is_last = section_idx == sections - 1
    contract = (((1,), (1,)), ((), ()))
    block_slot = jnp.arange(batches, dtype=jnp.int32)
    block_half = jnp.zeros((batches,), jnp.int32)
    block_join = jnp.zeros((batches,), jnp.bool_)
    halves_count = seq_len // seq_len
    total_steps = sections + batches - 1

    def pick_block(step_idx):
        block_raw = step_idx - (sections - 1 - section_idx)
        active = (block_raw >= 0) & (block_raw < batches)
        block_now = jnp.clip(block_raw, 0, batches - 1)
        return (block_slot[block_now], block_half[block_now], block_join[block_now], active)

    def middle(d_act, batch_slot, row_start, join_now, tail_carry):
        ext_vals = lax.dynamic_slice(
            conv_padded, (batch_slot, row_start, 0), (1, seq_len + kernel_width - 1, local_channels)
        )[0].astype(jnp.float32)
        tail_rows = jnp.where(join_now, tail_carry, 0.0)
        return conv_block(weights, ext_vals, tail_rows, d_act)

    def rows_of(array, batch_slot, first_row, row_count):
        return lax.dynamic_slice(array, (batch_slot, first_row, 0), (1, row_count, array.shape[2]))[
            0
        ]

    tail_init = jnp.zeros((kernel_width - 1, local_channels), jnp.float32)
    local_rows = seq_len // tensors

    def step_rows(step_idx, loop_state):
        incoming, results, gain_acc, conv_acc, tail_carry = loop_state
        batch_slot, half_now, join_now, active = pick_block(step_idx)
        row_start = half_now * seq_len
        own_start = tensor_idx * local_rows
        upstream = jnp.where(
            is_last, rows_of(top_grads, batch_slot, own_start, local_rows), incoming
        )
        d_act = lax.dot_general(
            gathered_copies(upstream, "tensor", 0),
            w_out,
            contract,
            preferred_element_type=jnp.float32,
        )
        d_vals, conv_part, new_tail = middle(d_act, batch_slot, row_start, join_now, tail_carry)
        d_norm = summed_on_arrival(
            lax.dot_general(d_vals, w_in, contract, preferred_element_type=jnp.float32).astype(
                jnp.bfloat16
            ),
            "tensor",
            0,
        )
        saved_now = rows_of(saved_rows, batch_slot, own_start, local_rows)
        grad_in, gain_part = norm_backward(d_norm, saved_now, upstream, gain_vec)
        grad_out = grad_in.astype(jnp.bfloat16)
        previous = lax.dynamic_slice(
            results, (batch_slot, half_now, 0, 0), (1, 1, local_rows, model_width)
        )
        updated = jnp.where(active, grad_out[None, None], previous)
        results = lax.dynamic_update_slice(results, updated, (batch_slot, half_now, 0, 0))
        gain_acc = gain_acc + jnp.where(active, gain_part, 0.0)
        conv_acc = conv_acc + jnp.where(active, conv_part, 0.0)
        tail_carry = jnp.where(active, new_tail, tail_carry)
        incoming = passed_along(grad_out, "section", -1)
        return (incoming, results, gain_acc, conv_acc, tail_carry)

    initial = (
        jnp.zeros((local_rows, model_width), jnp.bfloat16),
        jnp.zeros((batches, halves_count, local_rows, model_width), jnp.bfloat16),
        jnp.zeros(gain_vec.shape, jnp.float32),
        jnp.zeros(weights.shape, jnp.float32),
        tail_init,
    )
    last_state = lax.fori_loop(0, total_steps, step_rows, initial)
    gathered = gathered_copies(last_state[1], "tensor", 2)
    results = gathered.reshape(batches, seq_len, model_width)
    conv_acc = last_state[3]
    gain_total = of_everyone(last_state[2].astype(jnp.bfloat16), "tensor").astype(jnp.float32)
    return (results[None], gain_total[None], conv_acc[None])


def solution(mesh):
    placed = (
        P(),
        P(),
        P(),
        P("section", None, None, None),
        P("section", None, None, "tensor"),
        P("section", None),
        P("section", None, "tensor"),
        P("section", None, "tensor"),
        P("section", "tensor", None),
    )
    return jax.shard_map(
        local,
        mesh=mesh,
        in_specs=placed,
        out_specs=(
            P("section", None, None, None),
            P("section", None),
            P("section", None, "tensor"),
        ),
        check_vma=False,
    )
```

profile of v0, /device:TPU:32, one launch (start us, length us, event | category | flops | bytes accessed | tf_op | source)
XLA Modules:
  0.0 669.9 jit_solution(1525086684898112083)
XLA Ops:
  4.7 610.2 %while.26 = (s32[]{:T(128)}, bf16[4,8192]{1,0:T(4,128)(2,1)S(1)}, bf16[2,1,4,8192]{3,2,1,0:T(4,128)(2,1)S(1)}, f32[8192]{0:T(1024)S(1)}, f32[4,640]{1,0:T(4,128)...) while((s32[]{:T(128)}, bf16[4,8192]{1,0:T(4,128)(2,1)S(1)}, ...), condition=%wide.region_9.10_spmd.clone, body=%wide.region_0.9_spmd.clone.sunk | while | flops 1345747328 | bytes 80511800 | solution.py:175
  9.9 7.0 %all-to-all-start = ((bf16[16,4,8192]{2,1,0:T(4,128)(2,1)}), bf16[16,4,8192]{2,1,0:T(4,128)(2,1)S(1)}, u32[]{:S(2)}, u32[]{:S(2)}) async-start(bf16[16,4,8192]{2,1,0:T(4,128)(2,1)} %broadcast_in_dim.104), calls=%async_computation | async-start | bytes 2097152 | tf_op jit(solution)/shard_map/while/body/eval_jaxpr/all_to_all | solution.py:11
  17.0 17.6 %all-to-all-done = bf16[16,4,8192]{2,1,0:T(4,128)(2,1)S(1)} async-done(((bf16[16,4,8192]{2,1,0:T(4,128)(2,1)}), bf16[16,4,8192]{2,1,0:T(4,128)(2,1)S(1)}, u32[]{:S(2)}, u32[]{:S(2)}) %all-to-all-start) | async-done | bytes 1048608 | tf_op jit(solution)/shard_map/while/body/eval_jaxpr/all_to_all | solution.py:11
  34.9 7.6 %multiply_reduce_fusion.5 = (f32[640]{0:T(1024)S(1)}, f32[640]{0:T(1024)S(1)}, f32[640]{0:T(1024)S(1)}, f32[640]{0:T(1024)S(1)}, f32[64,640]{1,0:T(8,128)S(1)}) fusion(f32[1,67,640]{2,1,0:T(8,128)S(1)} %dynamic-slice_convert_fusion.2, f32[640]{0:T(1024)S(1)} %get-tuple-element.601, f32[640]{0:T(1024)S(1)} %get-tuple-element.602, ...), kind=kOutput, calls=%fused_computation.26.clone.1 | convolution fusion | flops 672028160 | bytes 12374016 | tf_op jit(solution)/shard_map/while/body/eval_jaxpr/dot_general | solution.py:140
  47.0 3.7 all-to-all-start.1
  51.9 14.0 %all-to-all-done.1 = bf16[16,4,8192]{2,1,0:T(4,128)(2,1)S(1)} async-done(((bf16[16,4,8192]{2,1,0:T(4,128)(2,1)}), bf16[16,4,8192]{2,1,0:T(4,128)(2,1)S(1)}, u32[]{:S(2)}, u32[]{:S(2)}) %all-to-all-start.1) | async-done | bytes 1048608 | tf_op jit(solution)/shard_map/while/body/eval_jaxpr/all_to_all | solution.py:33
  77.6 3.7 all-to-all-start
  81.4 16.7 %all-to-all-done = bf16[16,4,8192]{2,1,0:T(4,128)(2,1)S(1)} async-done(((bf16[16,4,8192]{2,1,0:T(4,128)(2,1)}), bf16[16,4,8192]{2,1,0:T(4,128)(2,1)S(1)}, u32[]{:S(2)}, u32[]{:S(2)}) %all-to-all-start) | async-done | bytes 1048608 | tf_op jit(solution)/shard_map/while/body/eval_jaxpr/all_to_all | solution.py:11
  98.3 7.6 %multiply_reduce_fusion.5 = (f32[640]{0:T(1024)S(1)}, f32[640]{0:T(1024)S(1)}, f32[640]{0:T(1024)S(1)}, f32[640]{0:T(1024)S(1)}, f32[64,640]{1,0:T(8,128)S(1)}) fusion(f32[1,67,640]{2,1,0:T(8,128)S(1)} %dynamic-slice_convert_fusion.2, f32[640]{0:T(1024)S(1)} %get-tuple-element.601, f32[640]{0:T(1024)S(1)} %get-tuple-element.602, ...), kind=kOutput, calls=%fused_computation.26.clone.1 | convolution fusion | flops 672028160 | bytes 12374016 | tf_op jit(solution)/shard_map/while/body/eval_jaxpr/dot_general | solution.py:140
  110.5 4.8 all-to-all-start.1
  116.5 18.3 %all-to-all-done.1 = bf16[16,4,8192]{2,1,0:T(4,128)(2,1)S(1)} async-done(((bf16[16,4,8192]{2,1,0:T(4,128)(2,1)}), bf16[16,4,8192]{2,1,0:T(4,128)(2,1)S(1)}, u32[]{:S(2)}, u32[]{:S(2)}) %all-to-all-start.1) | async-done | bytes 1048608 | tf_op jit(solution)/shard_map/while/body/eval_jaxpr/all_to_all | solution.py:33
  146.5 3.7 all-to-all-start
  150.3 16.2 %all-to-all-done = bf16[16,4,8192]{2,1,0:T(4,128)(2,1)S(1)} async-done(((bf16[16,4,8192]{2,1,0:T(4,128)(2,1)}), bf16[16,4,8192]{2,1,0:T(4,128)(2,1)S(1)}, u32[]{:S(2)}, u32[]{:S(2)}) %all-to-all-start) | async-done | bytes 1048608 | tf_op jit(solution)/shard_map/while/body/eval_jaxpr/all_to_all | solution.py:11
  166.8 7.6 %multiply_reduce_fusion.5 = (f32[640]{0:T(1024)S(1)}, f32[640]{0:T(1024)S(1)}, f32[640]{0:T(1024)S(1)}, f32[640]{0:T(1024)S(1)}, f32[64,640]{1,0:T(8,128)S(1)}) fusion(f32[1,67,640]{2,1,0:T(8,128)S(1)} %dynamic-slice_convert_fusion.2, f32[640]{0:T(1024)S(1)} %get-tuple-element.601, f32[640]{0:T(1024)S(1)} %get-tuple-element.602, ...), kind=kOutput, calls=%fused_computation.26.clone.1 | convolution fusion | flops 672028160 | bytes 12374016 | tf_op jit(solution)/shard_map/while/body/eval_jaxpr/dot_general | solution.py:140
  178.9 5.2 all-to-all-start.1
  185.4 18.4 %all-to-all-done.1 = bf16[16,4,8192]{2,1,0:T(4,128)(2,1)S(1)} async-done(((bf16[16,4,8192]{2,1,0:T(4,128)(2,1)}), bf16[16,4,8192]{2,1,0:T(4,128)(2,1)S(1)}, u32[]{:S(2)}, u32[]{:S(2)}) %all-to-all-start.1) | async-done | bytes 1048608 | tf_op jit(solution)/shard_map/while/body/eval_jaxpr/all_to_all | solution.py:33
  215.4 3.7 all-to-all-start
  219.2 16.6 %all-to-all-done = bf16[16,4,8192]{2,1,0:T(4,128)(2,1)S(1)} async-done(((bf16[16,4,8192]{2,1,0:T(4,128)(2,1)}), bf16[16,4,8192]{2,1,0:T(4,128)(2,1)S(1)}, u32[]{:S(2)}, u32[]{:S(2)}) %all-to-all-start) | async-done | bytes 1048608 | tf_op jit(solution)/shard_map/while/body/eval_jaxpr/all_to_all | solution.py:11
  236.1 7.6 %multiply_reduce_fusion.5 = (f32[640]{0:T(1024)S(1)}, f32[640]{0:T(1024)S(1)}, f32[640]{0:T(1024)S(1)}, f32[640]{0:T(1024)S(1)}, f32[64,640]{1,0:T(8,128)S(1)}) fusion(f32[1,67,640]{2,1,0:T(8,128)S(1)} %dynamic-slice_convert_fusion.2, f32[640]{0:T(1024)S(1)} %get-tuple-element.601, f32[640]{0:T(1024)S(1)} %get-tuple-element.602, ...), kind=kOutput, calls=%fused_computation.26.clone.1 | convolution fusion | flops 672028160 | bytes 12374016 | tf_op jit(solution)/shard_map/while/body/eval_jaxpr/dot_general | solution.py:140
  248.2 4.4 all-to-all-start.1
  253.8 18.1 %all-to-all-done.1 = bf16[16,4,8192]{2,1,0:T(4,128)(2,1)S(1)} async-done(((bf16[16,4,8192]{2,1,0:T(4,128)(2,1)}), bf16[16,4,8192]{2,1,0:T(4,128)(2,1)S(1)}, u32[]{:S(2)}, u32[]{:S(2)}) %all-to-all-start.1) | async-done | bytes 1048608 | tf_op jit(solution)/shard_map/while/body/eval_jaxpr/all_to_all | solution.py:33
  283.6 3.7 all-to-all-start
  287.4 16.9 %all-to-all-done = bf16[16,4,8192]{2,1,0:T(4,128)(2,1)S(1)} async-done(((bf16[16,4,8192]{2,1,0:T(4,128)(2,1)}), bf16[16,4,8192]{2,1,0:T(4,128)(2,1)S(1)}, u32[]{:S(2)}, u32[]{:S(2)}) %all-to-all-start) | async-done | bytes 1048608 | tf_op jit(solution)/shard_map/while/body/eval_jaxpr/all_to_all | solution.py:11
  304.5 7.6 %multiply_reduce_fusion.5 = (f32[640]{0:T(1024)S(1)}, f32[640]{0:T(1024)S(1)}, f32[640]{0:T(1024)S(1)}, f32[640]{0:T(1024)S(1)}, f32[64,640]{1,0:T(8,128)S(1)}) fusion(f32[1,67,640]{2,1,0:T(8,128)S(1)} %dynamic-slice_convert_fusion.2, f32[640]{0:T(1024)S(1)} %get-tuple-element.601, f32[640]{0:T(1024)S(1)} %get-tuple-element.602, ...), kind=kOutput, calls=%fused_computation.26.clone.1 | convolution fusion | flops 672028160 | bytes 12374016 | tf_op jit(solution)/shard_map/while/body/eval_jaxpr/dot_general | solution.py:140
  316.7 4.8 all-to-all-start.1
  322.6 18.5 %all-to-all-done.1 = bf16[16,4,8192]{2,1,0:T(4,128)(2,1)S(1)} async-done(((bf16[16,4,8192]{2,1,0:T(4,128)(2,1)}), bf16[16,4,8192]{2,1,0:T(4,128)(2,1)S(1)}, u32[]{:S(2)}, u32[]{:S(2)}) %all-to-all-start.1) | async-done | bytes 1048608 | tf_op jit(solution)/shard_map/while/body/eval_jaxpr/all_to_all | solution.py:33
  352.9 3.7 all-to-all-start
  356.6 18.9 %all-to-all-done = bf16[16,4,8192]{2,1,0:T(4,128)(2,1)S(1)} async-done(((bf16[16,4,8192]{2,1,0:T(4,128)(2,1)}), bf16[16,4,8192]{2,1,0:T(4,128)(2,1)S(1)}, u32[]{:S(2)}, u32[]{:S(2)}) %all-to-all-start) | async-done | bytes 1048608 | tf_op jit(solution)/shard_map/while/body/eval_jaxpr/all_to_all | solution.py:11
  375.7 7.6 %multiply_reduce_fusion.5 = (f32[640]{0:T(1024)S(1)}, f32[640]{0:T(1024)S(1)}, f32[640]{0:T(1024)S(1)}, f32[640]{0:T(1024)S(1)}, f32[64,640]{1,0:T(8,128)S(1)}) fusion(f32[1,67,640]{2,1,0:T(8,128)S(1)} %dynamic-slice_convert_fusion.2, f32[640]{0:T(1024)S(1)} %get-tuple-element.601, f32[640]{0:T(1024)S(1)} %get-tuple-element.602, ...), kind=kOutput, calls=%fused_computation.26.clone.1 | convolution fusion | flops 672028160 | bytes 12374016 | tf_op jit(solution)/shard_map/while/body/eval_jaxpr/dot_general | solution.py:140
  387.9 3.7 all-to-all-start.1
  392.7 17.3 %all-to-all-done.1 = bf16[16,4,8192]{2,1,0:T(4,128)(2,1)S(1)} async-done(((bf16[16,4,8192]{2,1,0:T(4,128)(2,1)}), bf16[16,4,8192]{2,1,0:T(4,128)(2,1)S(1)}, u32[]{:S(2)}, u32[]{:S(2)}) %all-to-all-start.1) | async-done | bytes 1048608 | tf_op jit(solution)/shard_map/while/body/eval_jaxpr/all_to_all | solution.py:33
  421.7 3.7 all-to-all-start
  425.4 19.1 %all-to-all-done = bf16[16,4,8192]{2,1,0:T(4,128)(2,1)S(1)} async-done(((bf16[16,4,8192]{2,1,0:T(4,128)(2,1)}), bf16[16,4,8192]{2,1,0:T(4,128)(2,1)S(1)}, u32[]{:S(2)}, u32[]{:S(2)}) %all-to-all-start) | async-done | bytes 1048608 | tf_op jit(solution)/shard_map/while/body/eval_jaxpr/all_to_all | solution.py:11
  444.8 7.6 %multiply_reduce_fusion.5 = (f32[640]{0:T(1024)S(1)}, f32[640]{0:T(1024)S(1)}, f32[640]{0:T(1024)S(1)}, f32[640]{0:T(1024)S(1)}, f32[64,640]{1,0:T(8,128)S(1)}) fusion(f32[1,67,640]{2,1,0:T(8,128)S(1)} %dynamic-slice_convert_fusion.2, f32[640]{0:T(1024)S(1)} %get-tuple-element.601, f32[640]{0:T(1024)S(1)} %get-tuple-element.602, ...), kind=kOutput, calls=%fused_computation.26.clone.1 | convolution fusion | flops 672028160 | bytes 12374016 | tf_op jit(solution)/shard_map/while/body/eval_jaxpr/dot_general | solution.py:140
  457.0 3.7 all-to-all-start.1
  461.8 16.3 %all-to-all-done.1 = bf16[16,4,8192]{2,1,0:T(4,128)(2,1)S(1)} async-done(((bf16[16,4,8192]{2,1,0:T(4,128)(2,1)}), bf16[16,4,8192]{2,1,0:T(4,128)(2,1)S(1)}, u32[]{:S(2)}, u32[]{:S(2)}) %all-to-all-start.1) | async-done | bytes 1048608 | tf_op jit(solution)/shard_map/while/body/eval_jaxpr/all_to_all | solution.py:33
  489.9 3.7 all-to-all-start
  493.6 17.5 %all-to-all-done = bf16[16,4,8192]{2,1,0:T(4,128)(2,1)S(1)} async-done(((bf16[16,4,8192]{2,1,0:T(4,128)(2,1)}), bf16[16,4,8192]{2,1,0:T(4,128)(2,1)S(1)}, u32[]{:S(2)}, u32[]{:S(2)}) %all-to-all-start) | async-done | bytes 1048608 | tf_op jit(solution)/shard_map/while/body/eval_jaxpr/all_to_all | solution.py:11
  511.4 7.6 %multiply_reduce_fusion.5 = (f32[640]{0:T(1024)S(1)}, f32[640]{0:T(1024)S(1)}, f32[640]{0:T(1024)S(1)}, f32[640]{0:T(1024)S(1)}, f32[64,640]{1,0:T(8,128)S(1)}) fusion(f32[1,67,640]{2,1,0:T(8,128)S(1)} %dynamic-slice_convert_fusion.2, f32[640]{0:T(1024)S(1)} %get-tuple-element.601, f32[640]{0:T(1024)S(1)} %get-tuple-element.602, ...), kind=kOutput, calls=%fused_computation.26.clone.1 | convolution fusion | flops 672028160 | bytes 12374016 | tf_op jit(solution)/shard_map/while/body/eval_jaxpr/dot_general | solution.py:140
  523.5 3.7 all-to-all-start.1
  528.4 14.0 %all-to-all-done.1 = bf16[16,4,8192]{2,1,0:T(4,128)(2,1)S(1)} async-done(((bf16[16,4,8192]{2,1,0:T(4,128)(2,1)}), bf16[16,4,8192]{2,1,0:T(4,128)(2,1)S(1)}, u32[]{:S(2)}, u32[]{:S(2)}) %all-to-all-start.1) | async-done | bytes 1048608 | tf_op jit(solution)/shard_map/while/body/eval_jaxpr/all_to_all | solution.py:33
  554.0 3.7 all-to-all-start
  557.8 18.3 %all-to-all-done = bf16[16,4,8192]{2,1,0:T(4,128)(2,1)S(1)} async-done(((bf16[16,4,8192]{2,1,0:T(4,128)(2,1)}), bf16[16,4,8192]{2,1,0:T(4,128)(2,1)S(1)}, u32[]{:S(2)}, u32[]{:S(2)}) %all-to-all-start) | async-done | bytes 1048608 | tf_op jit(solution)/shard_map/while/body/eval_jaxpr/all_to_all | solution.py:11
  576.3 7.6 %multiply_reduce_fusion.5 = (f32[640]{0:T(1024)S(1)}, f32[640]{0:T(1024)S(1)}, f32[640]{0:T(1024)S(1)}, f32[640]{0:T(1024)S(1)}, f32[64,640]{1,0:T(8,128)S(1)}) fusion(f32[1,67,640]{2,1,0:T(8,128)S(1)} %dynamic-slice_convert_fusion.2, f32[640]{0:T(1024)S(1)} %get-tuple-element.601, f32[640]{0:T(1024)S(1)} %get-tuple-element.602, ...), kind=kOutput, calls=%fused_computation.26.clone.1 | convolution fusion | flops 672028160 | bytes 12374016 | tf_op jit(solution)/shard_map/while/body/eval_jaxpr/dot_general | solution.py:140
  593.3 15.0 %all-to-all-done.1 = bf16[16,4,8192]{2,1,0:T(4,128)(2,1)S(1)} async-done(((bf16[16,4,8192]{2,1,0:T(4,128)(2,1)}), bf16[16,4,8192]{2,1,0:T(4,128)(2,1)S(1)}, u32[]{:S(2)}, u32[]{:S(2)}) %all-to-all-start.1) | async-done | bytes 1048608 | tf_op jit(solution)/shard_map/while/body/eval_jaxpr/all_to_all | solution.py:33
  618.3 12.1 %all_to_all.37 = bf16[16,2,4096]{2,1,0:T(2,128)(2,1)S(1)} all-to-all(bf16[16,2,4096]{2,1,0:T(2,128)(2,1)S(1)} %reshape.65), channel_id=1, replica_groups=mesh['section'=8,'tensor'=16] {'tensor'}, dimensions={0} | all-to-all | bytes 524288 | tf_op jit(solution)/shard_map/all_to_all | solution.py:11
  632.7 3.9 all-to-all-start.2
  637.8 27.3 %all-to-all-done.2 = bf16[16,2,1,4,8192]{4,3,1,2,0:T(4,128)(2,1)S(1)} async-done(((bf16[16,2,1,4,8192]{4,3,1,2,0:T(4,128)(2,1)}), bf16[16,2,1,4,8192]{4,3,1,2,0:T(4,128)(2,1)S(1)}, u32[]{:S(2)}, u32[]{:S(2)}) %all-to-all-start.2) | async-done | bytes 2097184 | tf_op jit(solution)/shard_map/all_to_all | solution.py:11
  (243 shorter events, 159.7 us)
Async XLA Ops:
  1.4 3.2 copy-start.4
  1.4 3.3 copy-start.1
  1.4 3.3 copy-start.2
  9.9 24.7 %all-to-all-start = ((bf16[16,4,8192]{2,1,0:T(4,128)(2,1)}), bf16[16,4,8192]{2,1,0:T(4,128)(2,1)S(1)}, u32[]{:S(2)}, u32[]{:S(2)}) async-start(bf16[16,4,8192]{2,1,0:T(4,128)(2,1)} %broadcast_in_dim.104), calls=%async_computation | async-start | bytes 2097152 | tf_op jit(solution)/shard_map/while/body/eval_jaxpr/all_to_all | solution.py:11
  34.9 7.6 %copy-start = (bf16[8192,640]{1,0:T(8,128)(2,1)S(1)}, bf16[8192,640]{1,0:T(8,128)(2,1)}, u32[]{:S(2)}) copy-start(bf16[8192,640]{1,0:T(8,128)(2,1)} %get-tuple-element.666) | copy-start | bytes 31457284 | tf_op jit(solution)/shard_map/while
  47.0 18.9 %all-to-all-start.1 = ((bf16[16,4,8192]{2,1,0:T(4,128)(2,1)}), bf16[16,4,8192]{2,1,0:T(4,128)(2,1)S(1)}, u32[]{:S(2)}, u32[]{:S(2)}) async-start(bf16[16,4,8192]{2,1,0:T(4,128)(2,1)} %reshape.70), calls=%async_computation.1 | async-start | bytes 2097152 | tf_op jit(solution)/shard_map/while/body/eval_jaxpr/all_to_all | solution.py:33
  68.7 3.8 collective-permute-start
  77.6 20.4 %all-to-all-start = ((bf16[16,4,8192]{2,1,0:T(4,128)(2,1)}), bf16[16,4,8192]{2,1,0:T(4,128)(2,1)S(1)}, u32[]{:S(2)}, u32[]{:S(2)}) async-start(bf16[16,4,8192]{2,1,0:T(4,128)(2,1)} %broadcast_in_dim.104), calls=%async_computation | async-start | bytes 2097152 | tf_op jit(solution)/shard_map/while/body/eval_jaxpr/all_to_all | solution.py:11
  98.3 7.6 %copy-start = (bf16[8192,640]{1,0:T(8,128)(2,1)S(1)}, bf16[8192,640]{1,0:T(8,128)(2,1)}, u32[]{:S(2)}) copy-start(bf16[8192,640]{1,0:T(8,128)(2,1)} %get-tuple-element.666) | copy-start | bytes 31457284 | tf_op jit(solution)/shard_map/while
  110.5 24.3 %all-to-all-start.1 = ((bf16[16,4,8192]{2,1,0:T(4,128)(2,1)}), bf16[16,4,8192]{2,1,0:T(4,128)(2,1)S(1)}, u32[]{:S(2)}, u32[]{:S(2)}) async-start(bf16[16,4,8192]{2,1,0:T(4,128)(2,1)} %reshape.70), calls=%async_computation.1 | async-start | bytes 2097152 | tf_op jit(solution)/shard_map/while/body/eval_jaxpr/all_to_all | solution.py:33
  137.6 3.8 collective-permute-start
  146.5 20.0 %all-to-all-start = ((bf16[16,4,8192]{2,1,0:T(4,128)(2,1)}), bf16[16,4,8192]{2,1,0:T(4,128)(2,1)S(1)}, u32[]{:S(2)}, u32[]{:S(2)}) async-start(bf16[16,4,8192]{2,1,0:T(4,128)(2,1)} %broadcast_in_dim.104), calls=%async_computation | async-start | bytes 2097152 | tf_op jit(solution)/shard_map/while/body/eval_jaxpr/all_to_all | solution.py:11
  166.8 7.6 %copy-start = (bf16[8192,640]{1,0:T(8,128)(2,1)S(1)}, bf16[8192,640]{1,0:T(8,128)(2,1)}, u32[]{:S(2)}) copy-start(bf16[8192,640]{1,0:T(8,128)(2,1)} %get-tuple-element.666) | copy-start | bytes 31457284 | tf_op jit(solution)/shard_map/while
  178.9 24.8 %all-to-all-start.1 = ((bf16[16,4,8192]{2,1,0:T(4,128)(2,1)}), bf16[16,4,8192]{2,1,0:T(4,128)(2,1)S(1)}, u32[]{:S(2)}, u32[]{:S(2)}) async-start(bf16[16,4,8192]{2,1,0:T(4,128)(2,1)} %reshape.70), calls=%async_computation.1 | async-start | bytes 2097152 | tf_op jit(solution)/shard_map/while/body/eval_jaxpr/all_to_all | solution.py:33
  206.5 3.8 collective-permute-start
  215.4 20.4 %all-to-all-start = ((bf16[16,4,8192]{2,1,0:T(4,128)(2,1)}), bf16[16,4,8192]{2,1,0:T(4,128)(2,1)S(1)}, u32[]{:S(2)}, u32[]{:S(2)}) async-start(bf16[16,4,8192]{2,1,0:T(4,128)(2,1)} %broadcast_in_dim.104), calls=%async_computation | async-start | bytes 2097152 | tf_op jit(solution)/shard_map/while/body/eval_jaxpr/all_to_all | solution.py:11
  236.1 7.6 %copy-start = (bf16[8192,640]{1,0:T(8,128)(2,1)S(1)}, bf16[8192,640]{1,0:T(8,128)(2,1)}, u32[]{:S(2)}) copy-start(bf16[8192,640]{1,0:T(8,128)(2,1)} %get-tuple-element.666) | copy-start | bytes 31457284 | tf_op jit(solution)/shard_map/while
  248.2 23.7 %all-to-all-start.1 = ((bf16[16,4,8192]{2,1,0:T(4,128)(2,1)}), bf16[16,4,8192]{2,1,0:T(4,128)(2,1)S(1)}, u32[]{:S(2)}, u32[]{:S(2)}) async-start(bf16[16,4,8192]{2,1,0:T(4,128)(2,1)} %reshape.70), calls=%async_computation.1 | async-start | bytes 2097152 | tf_op jit(solution)/shard_map/while/body/eval_jaxpr/all_to_all | solution.py:33
  274.7 3.8 collective-permute-start
  283.6 20.6 %all-to-all-start = ((bf16[16,4,8192]{2,1,0:T(4,128)(2,1)}), bf16[16,4,8192]{2,1,0:T(4,128)(2,1)S(1)}, u32[]{:S(2)}, u32[]{:S(2)}) async-start(bf16[16,4,8192]{2,1,0:T(4,128)(2,1)} %broadcast_in_dim.104), calls=%async_computation | async-start | bytes 2097152 | tf_op jit(solution)/shard_map/while/body/eval_jaxpr/all_to_all | solution.py:11
  304.5 7.6 %copy-start = (bf16[8192,640]{1,0:T(8,128)(2,1)S(1)}, bf16[8192,640]{1,0:T(8,128)(2,1)}, u32[]{:S(2)}) copy-start(bf16[8192,640]{1,0:T(8,128)(2,1)} %get-tuple-element.666) | copy-start | bytes 31457284 | tf_op jit(solution)/shard_map/while
  316.7 24.5 %all-to-all-start.1 = ((bf16[16,4,8192]{2,1,0:T(4,128)(2,1)}), bf16[16,4,8192]{2,1,0:T(4,128)(2,1)S(1)}, u32[]{:S(2)}, u32[]{:S(2)}) async-start(bf16[16,4,8192]{2,1,0:T(4,128)(2,1)} %reshape.70), calls=%async_computation.1 | async-start | bytes 2097152 | tf_op jit(solution)/shard_map/while/body/eval_jaxpr/all_to_all | solution.py:33
  343.9 3.8 collective-permute-start
  352.9 22.6 %all-to-all-start = ((bf16[16,4,8192]{2,1,0:T(4,128)(2,1)}), bf16[16,4,8192]{2,1,0:T(4,128)(2,1)S(1)}, u32[]{:S(2)}, u32[]{:S(2)}) async-start(bf16[16,4,8192]{2,1,0:T(4,128)(2,1)} %broadcast_in_dim.104), calls=%async_computation | async-start | bytes 2097152 | tf_op jit(solution)/shard_map/while/body/eval_jaxpr/all_to_all | solution.py:11
  375.7 7.6 %copy-start = (bf16[8192,640]{1,0:T(8,128)(2,1)S(1)}, bf16[8192,640]{1,0:T(8,128)(2,1)}, u32[]{:S(2)}) copy-start(bf16[8192,640]{1,0:T(8,128)(2,1)} %get-tuple-element.666) | copy-start | bytes 31457284 | tf_op jit(solution)/shard_map/while
  387.9 22.1 %all-to-all-start.1 = ((bf16[16,4,8192]{2,1,0:T(4,128)(2,1)}), bf16[16,4,8192]{2,1,0:T(4,128)(2,1)S(1)}, u32[]{:S(2)}, u32[]{:S(2)}) async-start(bf16[16,4,8192]{2,1,0:T(4,128)(2,1)} %reshape.70), calls=%async_computation.1 | async-start | bytes 2097152 | tf_op jit(solution)/shard_map/while/body/eval_jaxpr/all_to_all | solution.py:33
  412.8 3.8 collective-permute-start
  421.7 22.9 %all-to-all-start = ((bf16[16,4,8192]{2,1,0:T(4,128)(2,1)}), bf16[16,4,8192]{2,1,0:T(4,128)(2,1)S(1)}, u32[]{:S(2)}, u32[]{:S(2)}) async-start(bf16[16,4,8192]{2,1,0:T(4,128)(2,1)} %broadcast_in_dim.104), calls=%async_computation | async-start | bytes 2097152 | tf_op jit(solution)/shard_map/while/body/eval_jaxpr/all_to_all | solution.py:11
  444.8 7.6 %copy-start = (bf16[8192,640]{1,0:T(8,128)(2,1)S(1)}, bf16[8192,640]{1,0:T(8,128)(2,1)}, u32[]{:S(2)}) copy-start(bf16[8192,640]{1,0:T(8,128)(2,1)} %get-tuple-element.666) | copy-start | bytes 31457284 | tf_op jit(solution)/shard_map/while
  457.0 21.2 %all-to-all-start.1 = ((bf16[16,4,8192]{2,1,0:T(4,128)(2,1)}), bf16[16,4,8192]{2,1,0:T(4,128)(2,1)S(1)}, u32[]{:S(2)}, u32[]{:S(2)}) async-start(bf16[16,4,8192]{2,1,0:T(4,128)(2,1)} %reshape.70), calls=%async_computation.1 | async-start | bytes 2097152 | tf_op jit(solution)/shard_map/while/body/eval_jaxpr/all_to_all | solution.py:33
  480.9 3.8 collective-permute-start
  489.9 21.2 %all-to-all-start = ((bf16[16,4,8192]{2,1,0:T(4,128)(2,1)}), bf16[16,4,8192]{2,1,0:T(4,128)(2,1)S(1)}, u32[]{:S(2)}, u32[]{:S(2)}) async-start(bf16[16,4,8192]{2,1,0:T(4,128)(2,1)} %broadcast_in_dim.104), calls=%async_computation | async-start | bytes 2097152 | tf_op jit(solution)/shard_map/while/body/eval_jaxpr/all_to_all | solution.py:11
  511.4 7.6 %copy-start = (bf16[8192,640]{1,0:T(8,128)(2,1)S(1)}, bf16[8192,640]{1,0:T(8,128)(2,1)}, u32[]{:S(2)}) copy-start(bf16[8192,640]{1,0:T(8,128)(2,1)} %get-tuple-element.666) | copy-start | bytes 31457284 | tf_op jit(solution)/shard_map/while
  523.5 18.8 %all-to-all-start.1 = ((bf16[16,4,8192]{2,1,0:T(4,128)(2,1)}), bf16[16,4,8192]{2,1,0:T(4,128)(2,1)S(1)}, u32[]{:S(2)}, u32[]{:S(2)}) async-start(bf16[16,4,8192]{2,1,0:T(4,128)(2,1)} %reshape.70), calls=%async_computation.1 | async-start | bytes 2097152 | tf_op jit(solution)/shard_map/while/body/eval_jaxpr/all_to_all | solution.py:33
  545.1 3.8 collective-permute-start
  554.0 22.0 %all-to-all-start = ((bf16[16,4,8192]{2,1,0:T(4,128)(2,1)}), bf16[16,4,8192]{2,1,0:T(4,128)(2,1)S(1)}, u32[]{:S(2)}, u32[]{:S(2)}) async-start(bf16[16,4,8192]{2,1,0:T(4,128)(2,1)} %broadcast_in_dim.104), calls=%async_computation | async-start | bytes 2097152 | tf_op jit(solution)/shard_map/while/body/eval_jaxpr/all_to_all | solution.py:11
  576.3 7.6 %copy-start = (bf16[8192,640]{1,0:T(8,128)(2,1)S(1)}, bf16[8192,640]{1,0:T(8,128)(2,1)}, u32[]{:S(2)}) copy-start(bf16[8192,640]{1,0:T(8,128)(2,1)} %get-tuple-element.666) | copy-start | bytes 31457284 | tf_op jit(solution)/shard_map/while
  588.5 19.9 %all-to-all-start.1 = ((bf16[16,4,8192]{2,1,0:T(4,128)(2,1)}), bf16[16,4,8192]{2,1,0:T(4,128)(2,1)S(1)}, u32[]{:S(2)}, u32[]{:S(2)}) async-start(bf16[16,4,8192]{2,1,0:T(4,128)(2,1)} %reshape.70), calls=%async_computation.1 | async-start | bytes 2097152 | tf_op jit(solution)/shard_map/while/body/eval_jaxpr/all_to_all | solution.py:33
  611.2 3.8 collective-permute-start
  615.0 17.7 %copy-start.3 = (f32[4,640]{1,0:T(4,128)}, f32[4,640]{1,0:T(4,128)S(1)}, u32[]{:S(2)}) copy-start(f32[4,640]{1,0:T(4,128)S(1)} %get-tuple-element.382) | copy-start | bytes 30724
  632.7 32.5 %all-to-all-start.2 = ((bf16[16,2,1,4,8192]{4,3,1,2,0:T(4,128)(2,1)}), bf16[16,2,1,4,8192]{4,3,1,2,0:T(4,128)(2,1)S(1)}, u32[]{:S(2)}, u32[]{:S(2)}) async-start(bf16[16,2,1,4,8192]{4,3,1,2,0:T(4,128)(2,1)} %broadcast_in_dim.93), calls=%async_computation.2 | async-start | bytes 4194304 | tf_op jit(solution)/shard_map/all_to_all | solution.py:11
where the time goes:
time: 673 us; the launch traced here: 670 us
  waiting for transfers between devices  352 us (52%)
  matrix products  97.9 us (15%)
  starting transfers between devices  95 us (14%)
  other arithmetic  51.3 us (8%)
  local copies, waits for them, and re-layouts  40.9 us (6%)
  loops' own time  19.9 us (3%)
  blocking collectives  12.1 us (2%)
    all_to_all x10, waiting for transfers between devices, sent_to_all(): return lax.all_to_all(copies, axis, split_axis=0, concat_axis=0, tiled=True)  185 us
    all_to_all x9, waiting for transfers between devices, summed_on_arrival(): lax.all_to_all(parts, axis, split_axis=0, concat_axis=0, tiled=True)  150 us
    dot_general x9, matrix products, step_rows(): lax.dot_general(gathered_copies(upstream, 'tensor', 0), w_out, contract,...  68.1 us
    all_to_all x10, starting transfers between devices, sent_to_all(): return lax.all_to_all(copies, axis, split_axis=0, concat_axis=0, tiled=True)  40.2 us
    all_to_all x9, starting transfers between devices, summed_on_arrival(): lax.all_to_all(parts, axis, split_axis=0, concat_axis=0, tiled=True)  37.5 us
    dot_general x9, matrix products, step_rows(): lax.dot_general(d_vals, w_in, contract, preferred_element_type=jnp.float32)  29.8 us
    another operation x1, loops' own time, local(): last_state = lax.fori_loop(0, total_steps, step_rows, initial)  19.9 us
    ppermute x9, starting transfers between devices, passed_along(): return lax.ppermute(x, axis, pairs)  17.3 us
  transfers between devices with their start and end apart: 28, of which 28 were waited for; matrix products, arithmetic and copies ran while one was open for 2% of the time, Pallas kernels for 0%

commit v1 on v0

v1 whole, which is shorter than its diff:
```python
import jax
import jax.numpy as jnp
from jax import lax
from jax.sharding import PartitionSpec as P

EPSILON = 1e-05
CHUNKS_PER_BATCH = 2


def sent_to_all(x, axis):
    copies = jnp.broadcast_to(x, (lax.axis_size(axis), *x.shape))
    return lax.all_to_all(copies, axis, split_axis=0, concat_axis=0, tiled=True)


def summed_on_arrival(x, axis):
    devices = lax.axis_size(axis)
    parts = x.reshape(devices, x.shape[0] // devices, x.shape[1])
    arrived = lax.all_to_all(parts, axis, split_axis=0, concat_axis=0, tiled=True)
    return arrived.astype(jnp.float32).sum(axis=0)


def of_everyone(x, axis):
    return sent_to_all(x, axis).astype(jnp.float32).sum(axis=0)


def conv_block(weights, ext_vals, tail_rows, d_act):
    kernel_width = weights.shape[0]
    length = d_act.shape[0]
    pre_act = jnp.zeros_like(d_act)
    for lag_idx in range(kernel_width):
        start = kernel_width - 1 - lag_idx
        pre_act = pre_act + weights[lag_idx] * ext_vals[start : start + length]
    gate_sig = jax.nn.sigmoid(pre_act)
    d_pre = d_act * gate_sig * (1.0 + pre_act * (1.0 - gate_sig))
    padded_back = jnp.concatenate([d_pre, tail_rows], axis=0)
    d_vals = jnp.zeros_like(d_pre)
    for lag_idx in range(kernel_width):
        d_vals = d_vals + weights[lag_idx] * padded_back[lag_idx : lag_idx + length]
    lag_grads = jnp.stack(
        [
            jnp.sum(
                d_pre * ext_vals[kernel_width - 1 - lag_idx : kernel_width - 1 - lag_idx + length],
                axis=0,
            )
            for lag_idx in range(kernel_width)
        ]
    )
    return (d_vals.astype(jnp.bfloat16), lag_grads, d_pre[: kernel_width - 1])


def norm_backward(d_norm, saved_now, upstream, gain_vec):
    values = saved_now.astype(jnp.float32)
    inv_rms = lax.rsqrt(jnp.mean(values * values, axis=-1, keepdims=True) + EPSILON)
    normed = values * inv_rms
    d_hat = d_norm * gain_vec
    d_in = inv_rms * (d_hat - normed * jnp.mean(d_hat * normed, axis=-1, keepdims=True))
    return (upstream.astype(jnp.float32) + d_in, jnp.sum(d_norm * normed, axis=0))


def local(dy_top, loss_mask, counts, layer_in, conv_in, norm_gain, conv_weight, in_proj, out_proj):
    sections = lax.axis_size("section")
    tensors = lax.axis_size("tensor")
    section_idx = lax.axis_index("section")
    tensor_idx = lax.axis_index("tensor")
    batches, seq_len, model_width = dy_top.shape
    saved_rows = layer_in[0]
    gain_vec = norm_gain[0]
    weights = conv_weight[0]
    kernel_width = weights.shape[0]
    local_channels = weights.shape[1]
    w_in = in_proj[0]
    w_out = out_proj[0]
    conv_padded = jnp.pad(conv_in[0], ((0, 0), (kernel_width - 1, 0), (0, 0)))
    positions = jnp.arange(seq_len, dtype=jnp.int32)
    keep_mask = (loss_mask == 1) & (positions[None, :] < counts[:, None])
    top_grads = jnp.where(keep_mask[:, :, None], dy_top, jnp.zeros_like(dy_top))
    is_last = section_idx == sections - 1
    contract = (((1,), (1,)), ((), ()))

    halves = CHUNKS_PER_BATCH
    chunk_len = seq_len // halves
    local_rows = chunk_len // tensors
    order = [(b, h) for b in range(batches) for h in reversed(range(halves))]
    block_slot = jnp.array([b for b, _ in order], jnp.int32)
    block_half = jnp.array([h for _, h in order], jnp.int32)
    block_join = jnp.array([h < halves - 1 for _, h in order], jnp.bool_)
    n_chunks = len(order)
    total_steps = sections + n_chunks - 1

    def pick_block(step_idx):
        block_raw = step_idx - (sections - 1 - section_idx)
        active = (block_raw >= 0) & (block_raw < n_chunks)
        block_now = jnp.clip(block_raw, 0, n_chunks - 1)
        return (block_slot[block_now], block_half[block_now], block_join[block_now], active)

    def rows_of(array, batch_slot, first_row, row_count):
        return lax.dynamic_slice(array, (batch_slot, first_row, 0), (1, row_count, array.shape[2]))[0]

    tail_init = jnp.zeros((kernel_width - 1, local_channels), jnp.float32)

    def step_rows(step_idx, loop_state):
        incoming, results, gain_acc, conv_acc, tail_carry = loop_state
        batch_slot, half_now, join_now, active = pick_block(step_idx)
        row_start = half_now * chunk_len
        own_start = row_start + tensor_idx * local_rows
        upstream = jnp.where(is_last, rows_of(top_grads, batch_slot, own_start, local_rows), incoming)
        gathered = sent_to_all(incoming, "tensor").reshape(chunk_len, model_width)
        full_chunk = jnp.where(is_last, rows_of(top_grads, batch_slot, row_start, chunk_len), gathered)
        d_act = lax.dot_general(full_chunk, w_out, contract, preferred_element_type=jnp.float32)
        d_act = lax.optimization_barrier(d_act)
        ext_vals = lax.dynamic_slice(
            conv_padded, (batch_slot, row_start, 0), (1, chunk_len + kernel_width - 1, local_channels)
        )[0].astype(jnp.float32)
        tail_rows = jnp.where(join_now, tail_carry, 0.0)
        d_vals, conv_part, new_tail = conv_block(weights, ext_vals, tail_rows, d_act)
        partial = lax.dot_general(d_vals, w_in, contract, preferred_element_type=jnp.float32)
        d_norm = summed_on_arrival(partial.astype(jnp.bfloat16), "tensor")
        saved_now = rows_of(saved_rows, batch_slot, own_start, local_rows)
        grad_in, gain_part = norm_backward(d_norm, saved_now, upstream, gain_vec)
        grad_out = grad_in.astype(jnp.bfloat16)
        previous = lax.dynamic_slice(results, (batch_slot, half_now, 0, 0), (1, 1, local_rows, model_width))
        updated = jnp.where(active, grad_out[None, None], previous)
        results = lax.dynamic_update_slice(results, updated, (batch_slot, half_now, 0, 0))
        gain_acc = gain_acc + jnp.where(active, gain_part, 0.0)
        conv_acc = conv_acc + jnp.where(active, conv_part, 0.0)
        tail_carry = jnp.where(active, new_tail, tail_carry)
        incoming = lax.ppermute(grad_out, "section", [(i, i - 1) for i in range(1, sections)])
        return (incoming, results, gain_acc, conv_acc, tail_carry)

    initial = (
        jnp.zeros((local_rows, model_width), jnp.bfloat16),
        jnp.zeros((batches, halves, local_rows, model_width), jnp.bfloat16),
        jnp.zeros(gain_vec.shape, jnp.float32),
        jnp.zeros(weights.shape, jnp.float32),
        tail_init,
    )
    last_state = lax.fori_loop(0, total_steps, step_rows, initial)
    gathered = sent_to_all(last_state[1], "tensor")
    results = jnp.transpose(gathered, (1, 2, 0, 3, 4)).reshape(batches, seq_len, model_width)
    conv_acc = last_state[3]
    gain_total = of_everyone(last_state[2].astype(jnp.bfloat16), "tensor")
    return (results[None], gain_total[None], conv_acc[None])


def solution(mesh):
    placed = (
        P(),
        P(),
        P(),
        P("section", None, None, None),
        P("section", None, None, "tensor"),
        P("section", None),
        P("section", None, "tensor"),
        P("section", None, "tensor"),
        P("section", "tensor", None),
    )
    return jax.shard_map(
        local,
        mesh=mesh,
        in_specs=placed,
        out_specs=(
            P("section", None, None, None),
            P("section", None),
            P("section", None, "tensor"),
        ),
        check_vma=False,
    )
```

time: 673 us -> 626 us (0.930)
  waiting for transfers between devices: 352 us -> 218 us
  loops' own time: 19.9 us -> 47.4 us
  local copies, waits for them, and re-layouts: 40.9 us -> 59.8 us
  matrix products: 97.9 us -> 116 us
  starting transfers between devices: 95 us -> 110 us
    all_to_all x10 -> x12, waiting for transfers between devices: 185 us -> 107 us  [sent_to_all(): return lax.all_to_all(copies, axis, split_axis=0, concat_axis=0, tiled=True)]
    all_to_all x9 -> x11, waiting for transfers between devices: 150 us -> 94.1 us  [summed_on_arrival(): lax.all_to_all(parts, axis, split_axis=0, concat_axis=0, tiled=True)]
    another operation x1, loops' own time: 19.9 us -> 47.4 us  [local(): last_state = lax.fori_loop(0, total_steps, step_rows, initial)]
    dynamic_slice x0 -> x22, local copies, waits for them, and re-layouts: none -> 13.7 us  [the longest x11 7.17 us: pick_block(): block_join[block_now]]
    dot_general x9 -> x11, matrix products: 68.1 us -> 80.6 us  [step_rows(): lax.dot_general(full_chunk, w_out, contract, preferred_element_type=jnp.f...]
    all_to_all x10 -> x12, starting transfers between devices: 40.2 us -> 46.7 us  [sent_to_all(): return lax.all_to_all(copies, axis, split_axis=0, concat_axis=0, tiled=True)]
    dot_general x9 -> x11, matrix products: 29.8 us -> 35.1 us  [step_rows(): lax.dot_general(d_vals, w_in, contract, preferred_element_type=jnp.float32)]
    all_to_all x9 -> x11, starting transfers between devices: 37.5 us -> 42.7 us  [summed_on_arrival(): lax.all_to_all(parts, axis, split_axis=0, concat_axis=0, tiled=True)]
  transfers between devices with their start and end apart: 28 -> 34, of which waited for: 28 -> 34; matrix products, arithmetic and copies ran while one was open for 2% -> 6% of each run, Pallas kernels for 0% -> 0%
where the time goes in v1:
time: 626 us; the launch traced here: 622 us
  waiting for transfers between devices  218 us (35%)
  matrix products  116 us (19%)
  starting transfers between devices  110 us (18%)
  local copies, waits for them, and re-layouts  59.8 us (10%)
  other arithmetic  57.3 us (9%)
  loops' own time  47.4 us (8%)
  blocking collectives  11.8 us (2%)
    all_to_all x12, waiting for transfers between devices, sent_to_all(): return lax.all_to_all(copies, axis, split_axis=0, concat_axis=0, tiled=True)  107 us
    all_to_all x11, waiting for transfers between devices, summed_on_arrival(): lax.all_to_all(parts, axis, split_axis=0, concat_axis=0, tiled=True)  94.1 us
    dot_general x11, matrix products, step_rows(): lax.dot_general(full_chunk, w_out, contract, preferred_element_type=jnp.f...  80.6 us
    another operation x1, loops' own time, local(): last_state = lax.fori_loop(0, total_steps, step_rows, initial)  47.4 us
    all_to_all x12, starting transfers between devices, sent_to_all(): return lax.all_to_all(copies, axis, split_axis=0, concat_axis=0, tiled=True)  46.7 us
    all_to_all x11, starting transfers between devices, summed_on_arrival(): lax.all_to_all(parts, axis, split_axis=0, concat_axis=0, tiled=True)  42.7 us
    dot_general x11, matrix products, step_rows(): lax.dot_general(d_vals, w_in, contract, preferred_element_type=jnp.float32)  35.1 us
    ppermute x11, starting transfers between devices, step_rows(): lax.ppermute(grad_out, 'section', [(i, i - 1) for i in range(1, sections)])  21.1 us
  transfers between devices with their start and end apart: 34, of which 34 were waited for; matrix products, arithmetic and copies ran while one was open for 6% of the time, Pallas kernels for 0%

profile of v1, /device:TPU:32, one launch (start us, length us, event | category | flops | bytes accessed | tf_op | source)
XLA Modules:
  0.0 621.7 jit_solution(8293684404287939256)
XLA Ops:
  4.4 562.0 %while.25 = (s32[]{:T(128)}, bf16[2,8192]{1,0:T(2,128)(2,1)S(1)}, bf16[2,2,2,8192]{3,2,1,0:T(2,128)(2,1)S(1)}, f32[8192]{0:T(1024)S(1)}, f32[4,640]{1,0:T(4,128)...) while((s32[]{:T(128)}, bf16[2,8192]{1,0:T(2,128)(2,1)S(1)}, ...), condition=%wide.region_9.10_spmd.clone.clone, body=%wide.region_0.9_spmd.sunk.clone.clone.sunk | while | flops 673218560 | bytes 73902632 | solution.py:137
  5.7 7.0 %all-to-all-start = ((bf16[16,2,8192]{2,1,0:T(2,128)(2,1)}), bf16[16,2,8192]{2,1,0:T(2,128)(2,1)S(1)}, u32[]{:S(2)}, u32[]{:S(2)}) async-start(bf16[16,2,8192]{2,1,0:T(2,128)(2,1)} %broadcast_in_dim.124), calls=%async_computation | async-start | bytes 1048576 | tf_op jit(solution)/shard_map/while/body/eval_jaxpr/all_to_all | solution.py:12
  17.1 7.0 %all-to-all-done = bf16[16,2,8192]{2,1,0:T(2,128)(2,1)S(1)} async-done(((bf16[16,2,8192]{2,1,0:T(2,128)(2,1)}), bf16[16,2,8192]{2,1,0:T(2,128)(2,1)S(1)}, u32[]{:S(2)}, u32[]{:S(2)}) %all-to-all-start) | async-done | bytes 524320 | tf_op jit(solution)/shard_map/while/body/eval_jaxpr/all_to_all | solution.py:12
  24.4 7.3 %fusion.45 = f32[32,640]{1,0:T(8,128)S(1)} fusion(bf16[640,8192]{1,0:T(8,128)(2,1)} %get-tuple-element.790, bf16[32,8192]{1,0:T(8,128)(2,1)S(1)} %reshape.72, bf16[2,64,8192]{2,1,0:T(8,128)(2,1)S(1)} %get-tuple-element.787, s32[]{:T(128)S(6)} %select_n.315, s32[]{:T(128)S(6)} %select_n.318, pred[]{:T(512)} %get-tuple-element.784), kind=kOutput, calls=%fused_computation.3.clone.1 | convolution fusion | flops 335806464 | bytes 11616265 | tf_op jit(solution)/shard_map/while/body/eval_jaxpr/dot_general | solution.py:109
  36.9 3.7 all-to-all-start.1
  43.4 7.4 %all-to-all-done.1 = bf16[16,2,8192]{2,1,0:T(2,128)(2,1)S(1)} async-done(((bf16[16,2,8192]{2,1,0:T(2,128)(2,1)}), bf16[16,2,8192]{2,1,0:T(2,128)(2,1)S(1)}, u32[]{:S(2)}, u32[]{:S(2)}) %all-to-all-start.1) | async-done | bytes 524320 | tf_op jit(solution)/shard_map/while/body/eval_jaxpr/all_to_all | solution.py:18
  66.3 7.1 %all-to-all-done = bf16[16,2,8192]{2,1,0:T(2,128)(2,1)S(1)} async-done(((bf16[16,2,8192]{2,1,0:T(2,128)(2,1)}), bf16[16,2,8192]{2,1,0:T(2,128)(2,1)S(1)}, u32[]{:S(2)}, u32[]{:S(2)}) %all-to-all-start) | async-done | bytes 524320 | tf_op jit(solution)/shard_map/while/body/eval_jaxpr/all_to_all | solution.py:12
  73.7 7.3 %fusion.45 = f32[32,640]{1,0:T(8,128)S(1)} fusion(bf16[640,8192]{1,0:T(8,128)(2,1)} %get-tuple-element.790, bf16[32,8192]{1,0:T(8,128)(2,1)S(1)} %reshape.72, bf16[2,64,8192]{2,1,0:T(8,128)(2,1)S(1)} %get-tuple-element.787, s32[]{:T(128)S(6)} %select_n.315, s32[]{:T(128)S(6)} %select_n.318, pred[]{:T(512)} %get-tuple-element.784), kind=kOutput, calls=%fused_computation.3.clone.1 | convolution fusion | flops 335806464 | bytes 11616265 | tf_op jit(solution)/shard_map/while/body/eval_jaxpr/dot_general | solution.py:109
  86.1 4.0 all-to-all-start.1
  93.0 9.9 %all-to-all-done.1 = bf16[16,2,8192]{2,1,0:T(2,128)(2,1)S(1)} async-done(((bf16[16,2,8192]{2,1,0:T(2,128)(2,1)}), bf16[16,2,8192]{2,1,0:T(2,128)(2,1)S(1)}, u32[]{:S(2)}, u32[]{:S(2)}) %all-to-all-start.1) | async-done | bytes 524320 | tf_op jit(solution)/shard_map/while/body/eval_jaxpr/all_to_all | solution.py:18
  118.4 7.0 %all-to-all-done = bf16[16,2,8192]{2,1,0:T(2,128)(2,1)S(1)} async-done(((bf16[16,2,8192]{2,1,0:T(2,128)(2,1)}), bf16[16,2,8192]{2,1,0:T(2,128)(2,1)S(1)}, u32[]{:S(2)}, u32[]{:S(2)}) %all-to-all-start) | async-done | bytes 524320 | tf_op jit(solution)/shard_map/while/body/eval_jaxpr/all_to_all | solution.py:12
  125.6 7.3 %fusion.45 = f32[32,640]{1,0:T(8,128)S(1)} fusion(bf16[640,8192]{1,0:T(8,128)(2,1)} %get-tuple-element.790, bf16[32,8192]{1,0:T(8,128)(2,1)S(1)} %reshape.72, bf16[2,64,8192]{2,1,0:T(8,128)(2,1)S(1)} %get-tuple-element.787, s32[]{:T(128)S(6)} %select_n.315, s32[]{:T(128)S(6)} %select_n.318, pred[]{:T(512)} %get-tuple-element.784), kind=kOutput, calls=%fused_computation.3.clone.1 | convolution fusion | flops 335806464 | bytes 11616265 | tf_op jit(solution)/shard_map/while/body/eval_jaxpr/dot_general | solution.py:109
  138.1 4.1 all-to-all-start.1
  145.0 9.9 %all-to-all-done.1 = bf16[16,2,8192]{2,1,0:T(2,128)(2,1)S(1)} async-done(((bf16[16,2,8192]{2,1,0:T(2,128)(2,1)}), bf16[16,2,8192]{2,1,0:T(2,128)(2,1)S(1)}, u32[]{:S(2)}, u32[]{:S(2)}) %all-to-all-start.1) | async-done | bytes 524320 | tf_op jit(solution)/shard_map/while/body/eval_jaxpr/all_to_all | solution.py:18
  170.4 7.0 %all-to-all-done = bf16[16,2,8192]{2,1,0:T(2,128)(2,1)S(1)} async-done(((bf16[16,2,8192]{2,1,0:T(2,128)(2,1)}), bf16[16,2,8192]{2,1,0:T(2,128)(2,1)S(1)}, u32[]{:S(2)}, u32[]{:S(2)}) %all-to-all-start) | async-done | bytes 524320 | tf_op jit(solution)/shard_map/while/body/eval_jaxpr/all_to_all | solution.py:12
  177.7 7.3 %fusion.45 = f32[32,640]{1,0:T(8,128)S(1)} fusion(bf16[640,8192]{1,0:T(8,128)(2,1)} %get-tuple-element.790, bf16[32,8192]{1,0:T(8,128)(2,1)S(1)} %reshape.72, bf16[2,64,8192]{2,1,0:T(8,128)(2,1)S(1)} %get-tuple-element.787, s32[]{:T(128)S(6)} %select_n.315, s32[]{:T(128)S(6)} %select_n.318, pred[]{:T(512)} %get-tuple-element.784), kind=kOutput, calls=%fused_computation.3.clone.1 | convolution fusion | flops 335806464 | bytes 11616265 | tf_op jit(solution)/shard_map/while/body/eval_jaxpr/dot_general | solution.py:109
  190.1 4.0 all-to-all-start.1
  197.0 10.0 %all-to-all-done.1 = bf16[16,2,8192]{2,1,0:T(2,128)(2,1)S(1)} async-done(((bf16[16,2,8192]{2,1,0:T(2,128)(2,1)}), bf16[16,2,8192]{2,1,0:T(2,128)(2,1)S(1)}, u32[]{:S(2)}, u32[]{:S(2)}) %all-to-all-start.1) | async-done | bytes 524320 | tf_op jit(solution)/shard_map/while/body/eval_jaxpr/all_to_all | solution.py:18
  222.5 6.8 %all-to-all-done = bf16[16,2,8192]{2,1,0:T(2,128)(2,1)S(1)} async-done(((bf16[16,2,8192]{2,1,0:T(2,128)(2,1)}), bf16[16,2,8192]{2,1,0:T(2,128)(2,1)S(1)}, u32[]{:S(2)}, u32[]{:S(2)}) %all-to-all-start) | async-done | bytes 524320 | tf_op jit(solution)/shard_map/while/body/eval_jaxpr/all_to_all | solution.py:12
  229.5 7.3 %fusion.45 = f32[32,640]{1,0:T(8,128)S(1)} fusion(bf16[640,8192]{1,0:T(8,128)(2,1)} %get-tuple-element.790, bf16[32,8192]{1,0:T(8,128)(2,1)S(1)} %reshape.72, bf16[2,64,8192]{2,1,0:T(8,128)(2,1)S(1)} %get-tuple-element.787, s32[]{:T(128)S(6)} %select_n.315, s32[]{:T(128)S(6)} %select_n.318, pred[]{:T(512)} %get-tuple-element.784), kind=kOutput, calls=%fused_computation.3.clone.1 | convolution fusion | flops 335806464 | bytes 11616265 | tf_op jit(solution)/shard_map/while/body/eval_jaxpr/dot_general | solution.py:109
  241.9 4.7 all-to-all-start.1
  249.5 9.5 %all-to-all-done.1 = bf16[16,2,8192]{2,1,0:T(2,128)(2,1)S(1)} async-done(((bf16[16,2,8192]{2,1,0:T(2,128)(2,1)}), bf16[16,2,8192]{2,1,0:T(2,128)(2,1)S(1)}, u32[]{:S(2)}, u32[]{:S(2)}) %all-to-all-start.1) | async-done | bytes 524320 | tf_op jit(solution)/shard_map/while/body/eval_jaxpr/all_to_all | solution.py:18
  274.5 8.3 %all-to-all-done = bf16[16,2,8192]{2,1,0:T(2,128)(2,1)S(1)} async-done(((bf16[16,2,8192]{2,1,0:T(2,128)(2,1)}), bf16[16,2,8192]{2,1,0:T(2,128)(2,1)S(1)}, u32[]{:S(2)}, u32[]{:S(2)}) %all-to-all-start) | async-done | bytes 524320 | tf_op jit(solution)/shard_map/while/body/eval_jaxpr/all_to_all | solution.py:12
  283.1 7.3 %fusion.45 = f32[32,640]{1,0:T(8,128)S(1)} fusion(bf16[640,8192]{1,0:T(8,128)(2,1)} %get-tuple-element.790, bf16[32,8192]{1,0:T(8,128)(2,1)S(1)} %reshape.72, bf16[2,64,8192]{2,1,0:T(8,128)(2,1)S(1)} %get-tuple-element.787, s32[]{:T(128)S(6)} %select_n.315, s32[]{:T(128)S(6)} %select_n.318, pred[]{:T(512)} %get-tuple-element.784), kind=kOutput, calls=%fused_computation.3.clone.1 | convolution fusion | flops 335806464 | bytes 11616265 | tf_op jit(solution)/shard_map/while/body/eval_jaxpr/dot_general | solution.py:109
  295.5 3.7 all-to-all-start.1
  302.1 9.0 %all-to-all-done.1 = bf16[16,2,8192]{2,1,0:T(2,128)(2,1)S(1)} async-done(((bf16[16,2,8192]{2,1,0:T(2,128)(2,1)}), bf16[16,2,8192]{2,1,0:T(2,128)(2,1)S(1)}, u32[]{:S(2)}, u32[]{:S(2)}) %all-to-all-start.1) | async-done | bytes 524320 | tf_op jit(solution)/shard_map/while/body/eval_jaxpr/all_to_all | solution.py:18
  326.6 8.0 %all-to-all-done = bf16[16,2,8192]{2,1,0:T(2,128)(2,1)S(1)} async-done(((bf16[16,2,8192]{2,1,0:T(2,128)(2,1)}), bf16[16,2,8192]{2,1,0:T(2,128)(2,1)S(1)}, u32[]{:S(2)}, u32[]{:S(2)}) %all-to-all-start) | async-done | bytes 524320 | tf_op jit(solution)/shard_map/while/body/eval_jaxpr/all_to_all | solution.py:12
  334.8 7.3 %fusion.45 = f32[32,640]{1,0:T(8,128)S(1)} fusion(bf16[640,8192]{1,0:T(8,128)(2,1)} %get-tuple-element.790, bf16[32,8192]{1,0:T(8,128)(2,1)S(1)} %reshape.72, bf16[2,64,8192]{2,1,0:T(8,128)(2,1)S(1)} %get-tuple-element.787, s32[]{:T(128)S(6)} %select_n.315, s32[]{:T(128)S(6)} %select_n.318, pred[]{:T(512)} %get-tuple-element.784), kind=kOutput, calls=%fused_computation.3.clone.1 | convolution fusion | flops 335806464 | bytes 11616265 | tf_op jit(solution)/shard_map/while/body/eval_jaxpr/dot_general | solution.py:109
  347.3 3.7 all-to-all-start.1
  353.9 8.2 %all-to-all-done.1 = bf16[16,2,8192]{2,1,0:T(2,128)(2,1)S(1)} async-done(((bf16[16,2,8192]{2,1,0:T(2,128)(2,1)}), bf16[16,2,8192]{2,1,0:T(2,128)(2,1)S(1)}, u32[]{:S(2)}, u32[]{:S(2)}) %all-to-all-start.1) | async-done | bytes 524320 | tf_op jit(solution)/shard_map/while/body/eval_jaxpr/all_to_all | solution.py:18
  377.6 7.2 %all-to-all-done = bf16[16,2,8192]{2,1,0:T(2,128)(2,1)S(1)} async-done(((bf16[16,2,8192]{2,1,0:T(2,128)(2,1)}), bf16[16,2,8192]{2,1,0:T(2,128)(2,1)S(1)}, u32[]{:S(2)}, u32[]{:S(2)}) %all-to-all-start) | async-done | bytes 524320 | tf_op jit(solution)/shard_map/while/body/eval_jaxpr/all_to_all | solution.py:12
  385.0 7.3 %fusion.45 = f32[32,640]{1,0:T(8,128)S(1)} fusion(bf16[640,8192]{1,0:T(8,128)(2,1)} %get-tuple-element.790, bf16[32,8192]{1,0:T(8,128)(2,1)S(1)} %reshape.72, bf16[2,64,8192]{2,1,0:T(8,128)(2,1)S(1)} %get-tuple-element.787, s32[]{:T(128)S(6)} %select_n.315, s32[]{:T(128)S(6)} %select_n.318, pred[]{:T(512)} %get-tuple-element.784), kind=kOutput, calls=%fused_computation.3.clone.1 | convolution fusion | flops 335806464 | bytes 11616265 | tf_op jit(solution)/shard_map/while/body/eval_jaxpr/dot_general | solution.py:109
  397.5 3.7 all-to-all-start.1
  404.1 7.5 %all-to-all-done.1 = bf16[16,2,8192]{2,1,0:T(2,128)(2,1)S(1)} async-done(((bf16[16,2,8192]{2,1,0:T(2,128)(2,1)}), bf16[16,2,8192]{2,1,0:T(2,128)(2,1)S(1)}, u32[]{:S(2)}, u32[]{:S(2)}) %all-to-all-start.1) | async-done | bytes 524320 | tf_op jit(solution)/shard_map/while/body/eval_jaxpr/all_to_all | solution.py:18
  427.1 7.2 %all-to-all-done = bf16[16,2,8192]{2,1,0:T(2,128)(2,1)S(1)} async-done(((bf16[16,2,8192]{2,1,0:T(2,128)(2,1)}), bf16[16,2,8192]{2,1,0:T(2,128)(2,1)S(1)}, u32[]{:S(2)}, u32[]{:S(2)}) %all-to-all-start) | async-done | bytes 524320 | tf_op jit(solution)/shard_map/while/body/eval_jaxpr/all_to_all | solution.py:12
  434.6 7.3 %fusion.45 = f32[32,640]{1,0:T(8,128)S(1)} fusion(bf16[640,8192]{1,0:T(8,128)(2,1)} %get-tuple-element.790, bf16[32,8192]{1,0:T(8,128)(2,1)S(1)} %reshape.72, bf16[2,64,8192]{2,1,0:T(8,128)(2,1)S(1)} %get-tuple-element.787, s32[]{:T(128)S(6)} %select_n.315, s32[]{:T(128)S(6)} %select_n.318, pred[]{:T(512)} %get-tuple-element.784), kind=kOutput, calls=%fused_computation.3.clone.1 | convolution fusion | flops 335806464 | bytes 11616265 | tf_op jit(solution)/shard_map/while/body/eval_jaxpr/dot_general | solution.py:109
  447.0 3.7 all-to-all-start.1
  453.6 7.5 %all-to-all-done.1 = bf16[16,2,8192]{2,1,0:T(2,128)(2,1)S(1)} async-done(((bf16[16,2,8192]{2,1,0:T(2,128)(2,1)}), bf16[16,2,8192]{2,1,0:T(2,128)(2,1)S(1)}, u32[]{:S(2)}, u32[]{:S(2)}) %all-to-all-start.1) | async-done | bytes 524320 | tf_op jit(solution)/shard_map/while/body/eval_jaxpr/all_to_all | solution.py:18
  476.6 7.2 %all-to-all-done = bf16[16,2,8192]{2,1,0:T(2,128)(2,1)S(1)} async-done(((bf16[16,2,8192]{2,1,0:T(2,128)(2,1)}), bf16[16,2,8192]{2,1,0:T(2,128)(2,1)S(1)}, u32[]{:S(2)}, u32[]{:S(2)}) %all-to-all-start) | async-done | bytes 524320 | tf_op jit(solution)/shard_map/while/body/eval_jaxpr/all_to_all | solution.py:12
  484.1 7.3 %fusion.45 = f32[32,640]{1,0:T(8,128)S(1)} fusion(bf16[640,8192]{1,0:T(8,128)(2,1)} %get-tuple-element.790, bf16[32,8192]{1,0:T(8,128)(2,1)S(1)} %reshape.72, bf16[2,64,8192]{2,1,0:T(8,128)(2,1)S(1)} %get-tuple-element.787, s32[]{:T(128)S(6)} %select_n.315, s32[]{:T(128)S(6)} %select_n.318, pred[]{:T(512)} %get-tuple-element.784), kind=kOutput, calls=%fused_computation.3.clone.1 | convolution fusion | flops 335806464 | bytes 11616265 | tf_op jit(solution)/shard_map/while/body/eval_jaxpr/dot_general | solution.py:109
  496.5 3.7 all-to-all-start.1
  503.1 7.5 %all-to-all-done.1 = bf16[16,2,8192]{2,1,0:T(2,128)(2,1)S(1)} async-done(((bf16[16,2,8192]{2,1,0:T(2,128)(2,1)}), bf16[16,2,8192]{2,1,0:T(2,128)(2,1)S(1)}, u32[]{:S(2)}, u32[]{:S(2)}) %all-to-all-start.1) | async-done | bytes 524320 | tf_op jit(solution)/shard_map/while/body/eval_jaxpr/all_to_all | solution.py:18
  526.2 7.2 %all-to-all-done = bf16[16,2,8192]{2,1,0:T(2,128)(2,1)S(1)} async-done(((bf16[16,2,8192]{2,1,0:T(2,128)(2,1)}), bf16[16,2,8192]{2,1,0:T(2,128)(2,1)S(1)}, u32[]{:S(2)}, u32[]{:S(2)}) %all-to-all-start) | async-done | bytes 524320 | tf_op jit(solution)/shard_map/while/body/eval_jaxpr/all_to_all | solution.py:12
  533.6 7.3 %fusion.45 = f32[32,640]{1,0:T(8,128)S(1)} fusion(bf16[640,8192]{1,0:T(8,128)(2,1)} %get-tuple-element.790, bf16[32,8192]{1,0:T(8,128)(2,1)S(1)} %reshape.72, bf16[2,64,8192]{2,1,0:T(8,128)(2,1)S(1)} %get-tuple-element.787, s32[]{:T(128)S(6)} %select_n.315, s32[]{:T(128)S(6)} %select_n.318, pred[]{:T(512)} %get-tuple-element.784), kind=kOutput, calls=%fused_computation.3.clone.1 | convolution fusion | flops 335806464 | bytes 11616265 | tf_op jit(solution)/shard_map/while/body/eval_jaxpr/dot_general | solution.py:109
  552.6 7.5 %all-to-all-done.1 = bf16[16,2,8192]{2,1,0:T(2,128)(2,1)S(1)} async-done(((bf16[16,2,8192]{2,1,0:T(2,128)(2,1)}), bf16[16,2,8192]{2,1,0:T(2,128)(2,1)S(1)}, u32[]{:S(2)}, u32[]{:S(2)}) %all-to-all-start.1) | async-done | bytes 524320 | tf_op jit(solution)/shard_map/while/body/eval_jaxpr/all_to_all | solution.py:18
  569.7 11.8 %all_to_all.41 = bf16[16,2,4096]{2,1,0:T(2,128)(2,1)S(1)} all-to-all(bf16[16,2,4096]{2,1,0:T(2,128)(2,1)S(1)} %reshape.68), channel_id=1, replica_groups=mesh['section'=8,'tensor'=16] {'tensor'}, dimensions={0} | all-to-all | bytes 524288 | tf_op jit(solution)/shard_map/all_to_all | solution.py:12
  584.9 3.9 all-to-all-start.2
  590.0 27.1 %all-to-all-done.2 = bf16[16,2,2,2,8192]{4,3,2,1,0:T(2,128)(2,1)S(1)} async-done(((bf16[16,2,2,2,8192]{4,3,2,1,0:T(2,128)(2,1)}), bf16[16,2,2,2,8192]{4,3,2,1,0:T(2,128)(2,1)S(1)}, u32[]{:S(2)}, u32[]{:S(2)}) %all-to-all-start.2) | async-done | bytes 2097184 | tf_op jit(solution)/shard_map/all_to_all | solution.py:12
  (382 shorter events, 229.9 us)
Async XLA Ops:
  4.4 12.7 %copy-start.2 = (bf16[2,67,640]{2,1,0:T(8,128)(2,1)}, bf16[2,67,640]{2,1,0:T(8,128)(2,1)S(1)}, u32[]{:S(2)}) copy-start(bf16[2,67,640]{2,1,0:T(8,128)(2,1)S(1)} %get-tuple-element.791) | copy-start | bytes 514564 | tf_op jit(solution)/shard_map/while
  5.7 18.5 %all-to-all-start = ((bf16[16,2,8192]{2,1,0:T(2,128)(2,1)}), bf16[16,2,8192]{2,1,0:T(2,128)(2,1)S(1)}, u32[]{:S(2)}, u32[]{:S(2)}) async-start(bf16[16,2,8192]{2,1,0:T(2,128)(2,1)} %broadcast_in_dim.124), calls=%async_computation | async-start | bytes 1048576 | tf_op jit(solution)/shard_map/while/body/eval_jaxpr/all_to_all | solution.py:12
  36.9 20.3 %copy-start.3 = (bf16[2,67,640]{2,1,0:T(8,128)(2,1)S(1)}, bf16[2,67,640]{2,1,0:T(8,128)(2,1)}, u32[]{:S(2)}) copy-start(bf16[2,67,640]{2,1,0:T(8,128)(2,1)} %copy-done.2) | copy-start | bytes 514564 | tf_op jit(solution)/shard_map/while
  36.9 14.0 %all-to-all-start.1 = ((bf16[16,2,8192]{2,1,0:T(2,128)(2,1)}), bf16[16,2,8192]{2,1,0:T(2,128)(2,1)S(1)}, u32[]{:S(2)}, u32[]{:S(2)}) async-start(bf16[16,2,8192]{2,1,0:T(2,128)(2,1)} %reshape.73), calls=%async_computation.1 | async-start | bytes 1048576 | tf_op jit(solution)/shard_map/while/body/eval_jaxpr/all_to_all | solution.py:18
  53.6 3.5 collective-permute-start
  58.3 15.1 %all-to-all-start = ((bf16[16,2,8192]{2,1,0:T(2,128)(2,1)}), bf16[16,2,8192]{2,1,0:T(2,128)(2,1)S(1)}, u32[]{:S(2)}, u32[]{:S(2)}) async-start(bf16[16,2,8192]{2,1,0:T(2,128)(2,1)} %broadcast_in_dim.124), calls=%async_computation | async-start | bytes 1048576 | tf_op jit(solution)/shard_map/while/body/eval_jaxpr/all_to_all | solution.py:12
  86.1 23.0 %copy-start.3 = (bf16[2,67,640]{2,1,0:T(8,128)(2,1)S(1)}, bf16[2,67,640]{2,1,0:T(8,128)(2,1)}, u32[]{:S(2)}) copy-start(bf16[2,67,640]{2,1,0:T(8,128)(2,1)} %copy-done.2) | copy-start | bytes 514564 | tf_op jit(solution)/shard_map/while
  86.1 16.7 %all-to-all-start.1 = ((bf16[16,2,8192]{2,1,0:T(2,128)(2,1)}), bf16[16,2,8192]{2,1,0:T(2,128)(2,1)S(1)}, u32[]{:S(2)}, u32[]{:S(2)}) async-start(bf16[16,2,8192]{2,1,0:T(2,128)(2,1)} %reshape.73), calls=%async_computation.1 | async-start | bytes 1048576 | tf_op jit(solution)/shard_map/while/body/eval_jaxpr/all_to_all | solution.py:18
  105.6 3.5 collective-permute-start
  109.1 9.2 %copy-start.2 = (bf16[2,67,640]{2,1,0:T(8,128)(2,1)}, bf16[2,67,640]{2,1,0:T(8,128)(2,1)S(1)}, u32[]{:S(2)}) copy-start(bf16[2,67,640]{2,1,0:T(8,128)(2,1)S(1)} %get-tuple-element.791) | copy-start | bytes 514564 | tf_op jit(solution)/shard_map/while
  110.4 15.0 %all-to-all-start = ((bf16[16,2,8192]{2,1,0:T(2,128)(2,1)}), bf16[16,2,8192]{2,1,0:T(2,128)(2,1)S(1)}, u32[]{:S(2)}, u32[]{:S(2)}) async-start(bf16[16,2,8192]{2,1,0:T(2,128)(2,1)} %broadcast_in_dim.124), calls=%async_computation | async-start | bytes 1048576 | tf_op jit(solution)/shard_map/while/body/eval_jaxpr/all_to_all | solution.py:12
  138.1 23.1 %copy-start.3 = (bf16[2,67,640]{2,1,0:T(8,128)(2,1)S(1)}, bf16[2,67,640]{2,1,0:T(8,128)(2,1)}, u32[]{:S(2)}) copy-start(bf16[2,67,640]{2,1,0:T(8,128)(2,1)} %copy-done.2) | copy-start | bytes 514564 | tf_op jit(solution)/shard_map/while
  138.1 16.9 %all-to-all-start.1 = ((bf16[16,2,8192]{2,1,0:T(2,128)(2,1)}), bf16[16,2,8192]{2,1,0:T(2,128)(2,1)S(1)}, u32[]{:S(2)}, u32[]{:S(2)}) async-start(bf16[16,2,8192]{2,1,0:T(2,128)(2,1)} %reshape.73), calls=%async_computation.1 | async-start | bytes 1048576 | tf_op jit(solution)/shard_map/while/body/eval_jaxpr/all_to_all | solution.py:18
  157.7 3.5 collective-permute-start
  162.4 15.1 %all-to-all-start = ((bf16[16,2,8192]{2,1,0:T(2,128)(2,1)}), bf16[16,2,8192]{2,1,0:T(2,128)(2,1)S(1)}, u32[]{:S(2)}, u32[]{:S(2)}) async-start(bf16[16,2,8192]{2,1,0:T(2,128)(2,1)} %broadcast_in_dim.124), calls=%async_computation | async-start | bytes 1048576 | tf_op jit(solution)/shard_map/while/body/eval_jaxpr/all_to_all | solution.py:12
  190.1 23.1 %copy-start.3 = (bf16[2,67,640]{2,1,0:T(8,128)(2,1)S(1)}, bf16[2,67,640]{2,1,0:T(8,128)(2,1)}, u32[]{:S(2)}) copy-start(bf16[2,67,640]{2,1,0:T(8,128)(2,1)} %copy-done.2) | copy-start | bytes 514564 | tf_op jit(solution)/shard_map/while
  190.1 16.8 %all-to-all-start.1 = ((bf16[16,2,8192]{2,1,0:T(2,128)(2,1)}), bf16[16,2,8192]{2,1,0:T(2,128)(2,1)S(1)}, u32[]{:S(2)}, u32[]{:S(2)}) async-start(bf16[16,2,8192]{2,1,0:T(2,128)(2,1)} %reshape.73), calls=%async_computation.1 | async-start | bytes 1048576 | tf_op jit(solution)/shard_map/while/body/eval_jaxpr/all_to_all | solution.py:18
  209.7 3.5 collective-permute-start
  214.4 14.8 %all-to-all-start = ((bf16[16,2,8192]{2,1,0:T(2,128)(2,1)}), bf16[16,2,8192]{2,1,0:T(2,128)(2,1)S(1)}, u32[]{:S(2)}, u32[]{:S(2)}) async-start(bf16[16,2,8192]{2,1,0:T(2,128)(2,1)} %broadcast_in_dim.124), calls=%async_computation | async-start | bytes 1048576 | tf_op jit(solution)/shard_map/while/body/eval_jaxpr/all_to_all | solution.py:12
  241.9 23.3 %copy-start.3 = (bf16[2,67,640]{2,1,0:T(8,128)(2,1)S(1)}, bf16[2,67,640]{2,1,0:T(8,128)(2,1)}, u32[]{:S(2)}) copy-start(bf16[2,67,640]{2,1,0:T(8,128)(2,1)} %copy-done.2) | copy-start | bytes 514564 | tf_op jit(solution)/shard_map/while
  241.9 17.1 %all-to-all-start.1 = ((bf16[16,2,8192]{2,1,0:T(2,128)(2,1)}), bf16[16,2,8192]{2,1,0:T(2,128)(2,1)S(1)}, u32[]{:S(2)}, u32[]{:S(2)}) async-start(bf16[16,2,8192]{2,1,0:T(2,128)(2,1)} %reshape.73), calls=%async_computation.1 | async-start | bytes 1048576 | tf_op jit(solution)/shard_map/while/body/eval_jaxpr/all_to_all | solution.py:18
  261.8 3.5 collective-permute-start
  266.5 16.4 %all-to-all-start = ((bf16[16,2,8192]{2,1,0:T(2,128)(2,1)}), bf16[16,2,8192]{2,1,0:T(2,128)(2,1)S(1)}, u32[]{:S(2)}, u32[]{:S(2)}) async-start(bf16[16,2,8192]{2,1,0:T(2,128)(2,1)} %broadcast_in_dim.124), calls=%async_computation | async-start | bytes 1048576 | tf_op jit(solution)/shard_map/while/body/eval_jaxpr/all_to_all | solution.py:12
  295.5 21.9 %copy-start.3 = (bf16[2,67,640]{2,1,0:T(8,128)(2,1)S(1)}, bf16[2,67,640]{2,1,0:T(8,128)(2,1)}, u32[]{:S(2)}) copy-start(bf16[2,67,640]{2,1,0:T(8,128)(2,1)} %copy-done.2) | copy-start | bytes 514564 | tf_op jit(solution)/shard_map/while
  295.5 15.6 %all-to-all-start.1 = ((bf16[16,2,8192]{2,1,0:T(2,128)(2,1)}), bf16[16,2,8192]{2,1,0:T(2,128)(2,1)S(1)}, u32[]{:S(2)}, u32[]{:S(2)}) async-start(bf16[16,2,8192]{2,1,0:T(2,128)(2,1)} %reshape.73), calls=%async_computation.1 | async-start | bytes 1048576 | tf_op jit(solution)/shard_map/while/body/eval_jaxpr/all_to_all | solution.py:18
  313.9 3.5 collective-permute-start
  318.6 16.0 %all-to-all-start = ((bf16[16,2,8192]{2,1,0:T(2,128)(2,1)}), bf16[16,2,8192]{2,1,0:T(2,128)(2,1)S(1)}, u32[]{:S(2)}, u32[]{:S(2)}) async-start(bf16[16,2,8192]{2,1,0:T(2,128)(2,1)} %broadcast_in_dim.124), calls=%async_computation | async-start | bytes 1048576 | tf_op jit(solution)/shard_map/while/body/eval_jaxpr/all_to_all | solution.py:12
  347.3 21.1 %copy-start.3 = (bf16[2,67,640]{2,1,0:T(8,128)(2,1)S(1)}, bf16[2,67,640]{2,1,0:T(8,128)(2,1)}, u32[]{:S(2)}) copy-start(bf16[2,67,640]{2,1,0:T(8,128)(2,1)} %copy-done.2) | copy-start | bytes 514564 | tf_op jit(solution)/shard_map/while
  347.3 14.8 %all-to-all-start.1 = ((bf16[16,2,8192]{2,1,0:T(2,128)(2,1)}), bf16[16,2,8192]{2,1,0:T(2,128)(2,1)S(1)}, u32[]{:S(2)}, u32[]{:S(2)}) async-start(bf16[16,2,8192]{2,1,0:T(2,128)(2,1)} %reshape.73), calls=%async_computation.1 | async-start | bytes 1048576 | tf_op jit(solution)/shard_map/while/body/eval_jaxpr/all_to_all | solution.py:18
  364.9 3.5 collective-permute-start
  369.6 15.2 %all-to-all-start = ((bf16[16,2,8192]{2,1,0:T(2,128)(2,1)}), bf16[16,2,8192]{2,1,0:T(2,128)(2,1)S(1)}, u32[]{:S(2)}, u32[]{:S(2)}) async-start(bf16[16,2,8192]{2,1,0:T(2,128)(2,1)} %broadcast_in_dim.124), calls=%async_computation | async-start | bytes 1048576 | tf_op jit(solution)/shard_map/while/body/eval_jaxpr/all_to_all | solution.py:12
  397.5 20.4 %copy-start.3 = (bf16[2,67,640]{2,1,0:T(8,128)(2,1)S(1)}, bf16[2,67,640]{2,1,0:T(8,128)(2,1)}, u32[]{:S(2)}) copy-start(bf16[2,67,640]{2,1,0:T(8,128)(2,1)} %copy-done.2) | copy-start | bytes 514564 | tf_op jit(solution)/shard_map/while
  397.5 14.1 %all-to-all-start.1 = ((bf16[16,2,8192]{2,1,0:T(2,128)(2,1)}), bf16[16,2,8192]{2,1,0:T(2,128)(2,1)S(1)}, u32[]{:S(2)}, u32[]{:S(2)}) async-start(bf16[16,2,8192]{2,1,0:T(2,128)(2,1)} %reshape.73), calls=%async_computation.1 | async-start | bytes 1048576 | tf_op jit(solution)/shard_map/while/body/eval_jaxpr/all_to_all | solution.py:18
  414.4 3.5 collective-permute-start
  419.1 15.2 %all-to-all-start = ((bf16[16,2,8192]{2,1,0:T(2,128)(2,1)}), bf16[16,2,8192]{2,1,0:T(2,128)(2,1)S(1)}, u32[]{:S(2)}, u32[]{:S(2)}) async-start(bf16[16,2,8192]{2,1,0:T(2,128)(2,1)} %broadcast_in_dim.124), calls=%async_computation | async-start | bytes 1048576 | tf_op jit(solution)/shard_map/while/body/eval_jaxpr/all_to_all | solution.py:12
  447.0 20.4 %copy-start.3 = (bf16[2,67,640]{2,1,0:T(8,128)(2,1)S(1)}, bf16[2,67,640]{2,1,0:T(8,128)(2,1)}, u32[]{:S(2)}) copy-start(bf16[2,67,640]{2,1,0:T(8,128)(2,1)} %copy-done.2) | copy-start | bytes 514564 | tf_op jit(solution)/shard_map/while
  447.0 14.1 %all-to-all-start.1 = ((bf16[16,2,8192]{2,1,0:T(2,128)(2,1)}), bf16[16,2,8192]{2,1,0:T(2,128)(2,1)S(1)}, u32[]{:S(2)}, u32[]{:S(2)}) async-start(bf16[16,2,8192]{2,1,0:T(2,128)(2,1)} %reshape.73), calls=%async_computation.1 | async-start | bytes 1048576 | tf_op jit(solution)/shard_map/while/body/eval_jaxpr/all_to_all | solution.py:18
  463.9 3.5 collective-permute-start
  468.6 15.2 %all-to-all-start = ((bf16[16,2,8192]{2,1,0:T(2,128)(2,1)}), bf16[16,2,8192]{2,1,0:T(2,128)(2,1)S(1)}, u32[]{:S(2)}, u32[]{:S(2)}) async-start(bf16[16,2,8192]{2,1,0:T(2,128)(2,1)} %broadcast_in_dim.124), calls=%async_computation | async-start | bytes 1048576 | tf_op jit(solution)/shard_map/while/body/eval_jaxpr/all_to_all | solution.py:12
  496.5 20.4 %copy-start.3 = (bf16[2,67,640]{2,1,0:T(8,128)(2,1)S(1)}, bf16[2,67,640]{2,1,0:T(8,128)(2,1)}, u32[]{:S(2)}) copy-start(bf16[2,67,640]{2,1,0:T(8,128)(2,1)} %copy-done.2) | copy-start | bytes 514564 | tf_op jit(solution)/shard_map/while
  496.5 14.1 %all-to-all-start.1 = ((bf16[16,2,8192]{2,1,0:T(2,128)(2,1)}), bf16[16,2,8192]{2,1,0:T(2,128)(2,1)S(1)}, u32[]{:S(2)}, u32[]{:S(2)}) async-start(bf16[16,2,8192]{2,1,0:T(2,128)(2,1)} %reshape.73), calls=%async_computation.1 | async-start | bytes 1048576 | tf_op jit(solution)/shard_map/while/body/eval_jaxpr/all_to_all | solution.py:18
  513.4 3.5 collective-permute-start
  518.1 15.2 %all-to-all-start = ((bf16[16,2,8192]{2,1,0:T(2,128)(2,1)}), bf16[16,2,8192]{2,1,0:T(2,128)(2,1)S(1)}, u32[]{:S(2)}, u32[]{:S(2)}) async-start(bf16[16,2,8192]{2,1,0:T(2,128)(2,1)} %broadcast_in_dim.124), calls=%async_computation | async-start | bytes 1048576 | tf_op jit(solution)/shard_map/while/body/eval_jaxpr/all_to_all | solution.py:12
  546.1 20.4 %copy-start.3 = (bf16[2,67,640]{2,1,0:T(8,128)(2,1)S(1)}, bf16[2,67,640]{2,1,0:T(8,128)(2,1)}, u32[]{:S(2)}) copy-start(bf16[2,67,640]{2,1,0:T(8,128)(2,1)} %copy-done.2) | copy-start | bytes 514564 | tf_op jit(solution)/shard_map/while
  546.1 14.1 %all-to-all-start.1 = ((bf16[16,2,8192]{2,1,0:T(2,128)(2,1)}), bf16[16,2,8192]{2,1,0:T(2,128)(2,1)S(1)}, u32[]{:S(2)}, u32[]{:S(2)}) async-start(bf16[16,2,8192]{2,1,0:T(2,128)(2,1)} %reshape.73), calls=%async_computation.1 | async-start | bytes 1048576 | tf_op jit(solution)/shard_map/while/body/eval_jaxpr/all_to_all | solution.py:18
  562.9 3.5 collective-permute-start
  566.5 18.4 %copy-start.5 = (f32[4,640]{1,0:T(4,128)}, f32[4,640]{1,0:T(4,128)S(1)}, u32[]{:S(2)}) copy-start(f32[4,640]{1,0:T(4,128)S(1)} %get-tuple-element.431) | copy-start | bytes 30724
  584.9 32.2 %all-to-all-start.2 = ((bf16[16,2,2,2,8192]{4,3,2,1,0:T(2,128)(2,1)}), bf16[16,2,2,2,8192]{4,3,2,1,0:T(2,128)(2,1)S(1)}, u32[]{:S(2)}, u32[]{:S(2)}) async-start(bf16[16,2,2,2,8192]{4,3,2,1,0:T(2,128)(2,1)} %broadcast_in_dim.102), calls=%async_computation.2 | async-start | bytes 4194304 | tf_op jit(solution)/shard_map/all_to_all | solution.py:12
  (25 other events, 182.1 us)

commit v2 on v1

--- a/solution.py
+++ b/solution.py
@@ -1,9 +1,14 @@
+import functools
+
 import jax
 import jax.numpy as jnp
 from jax import lax
+from jax.experimental import pallas as pl
+from jax.experimental.pallas import tpu as pltpu
 from jax.sharding import PartitionSpec as P
 
 EPSILON = 1e-05
+MESH = pl.DeviceIdType.MESH
 CHUNKS_PER_BATCH = 2
 
 
@@ -12,15 +17,133 @@
     return lax.all_to_all(copies, axis, split_axis=0, concat_axis=0, tiled=True)
 
 
-def summed_on_arrival(x, axis):
-    devices = lax.axis_size(axis)
-    parts = x.reshape(devices, x.shape[0] // devices, x.shape[1])
-    arrived = lax.all_to_all(parts, axis, split_axis=0, concat_axis=0, tiled=True)
-    return arrived.astype(jnp.float32).sum(axis=0)
-
-
-def of_everyone(x, axis):
-    return sent_to_all(x, axis).astype(jnp.float32).sum(axis=0)
+def scatter_sum_kernel(n, width, x_ref, s_ref, out_ref, sum_ref, recv, srecv, send_sem, recv_sem, ssend_sem, srecv_sem):
+    me = lax.axis_index("tensor")
+    sec = lax.axis_index("section")
+    barrier = pltpu.get_barrier_semaphore()
+    for k in range(1, n):
+        pl.semaphore_signal(barrier, inc=1, device_id=(sec, lax.rem(me + k, n)), device_id_type=MESH)
+    pl.semaphore_wait(barrier, n - 1)
+    copies = []
+    for k in range(1, n):
+        peer = lax.rem(me + k, n)
+        cols = pl.ds(pl.multiple_of(peer * width, 128), width)
+        block = pltpu.make_async_remote_copy(
+            src_ref=x_ref.at[:, cols],
+            dst_ref=recv.at[me],
+            send_sem=send_sem.at[k],
+            recv_sem=recv_sem.at[k],
+            device_id=(sec, peer),
+            device_id_type=MESH,
+        )
+        block.start()
+        stat = pltpu.make_async_remote_copy(
+            src_ref=s_ref,
+            dst_ref=srecv.at[me],
+            send_sem=ssend_sem.at[k],
+            recv_sem=srecv_sem.at[k],
+            device_id=(sec, peer),
+            device_id_type=MESH,
+        )
+        stat.start()
+        copies.append((block, stat))
+    for block, stat in copies:
+        block.wait()
+        stat.wait()
+    mine = pl.ds(pl.multiple_of(me * width, 128), width)
+    total = x_ref[:, mine].astype(jnp.float32)
+    stat_total = s_ref[...]
+    for k in range(1, n):
+        src = lax.rem(me + n - k, n)
+        total = total + recv[src].astype(jnp.float32)
+        stat_total = stat_total + srecv[src]
+    out_ref[...] = total
+    sum_ref[...] = stat_total
+
+
+def scatter_sum(x, stats, n, width):
+    rows = x.shape[0]
+    return pl.pallas_call(
+        functools.partial(scatter_sum_kernel, n, width),
+        out_shape=(
+            jax.ShapeDtypeStruct((rows, width), jnp.float32),
+            jax.ShapeDtypeStruct(stats.shape, jnp.float32),
+        ),
+        in_specs=[pl.BlockSpec(memory_space=pltpu.VMEM)] * 2,
+        out_specs=(pl.BlockSpec(memory_space=pltpu.VMEM), pl.BlockSpec(memory_space=pltpu.VMEM)),
+        scratch_shapes=[
+            pltpu.VMEM((n, rows, width), x.dtype),
+            pltpu.VMEM((n, *stats.shape), jnp.float32),
+            pltpu.SemaphoreType.DMA((n,)),
+            pltpu.SemaphoreType.DMA((n,)),
+            pltpu.SemaphoreType.DMA((n,)),
+            pltpu.SemaphoreType.DMA((n,)),
+        ],
+        compiler_params=pltpu.CompilerParams(collective_id=0, has_side_effects=True),
+    )(x, stats)
+
+
+def handed_down_kernel(n, n_sec, width, g_ref, out_ref, recv, send_sem, recv_sem):
+    me = lax.axis_index("tensor")
+    sec = lax.axis_index("section")
+    barrier = pltpu.get_barrier_semaphore()
+    mine = pl.ds(pl.multiple_of(me * width, 128), width)
+
+    @pl.when(sec < n_sec - 1)
+    def _():
+        for t in range(n):
+            pl.semaphore_signal(barrier, inc=1, device_id=(sec + 1, t), device_id_type=MESH)
+
+    @pl.when(sec > 0)
+    def _():
+        pl.semaphore_wait(barrier, n)
+        copies = []
+        for t in range(n):
+            copy = pltpu.make_async_remote_copy(
+                src_ref=g_ref,
+                dst_ref=recv.at[:, mine],
+                send_sem=send_sem.at[t],
+                recv_sem=recv_sem.at[me],
+                device_id=(sec - 1, t),
+                device_id_type=MESH,
+            )
+            copy.start()
+            copies.append(copy)
+        for copy in copies:
+            copy.wait_send()
+
+    @pl.when(sec < n_sec - 1)
+    def _():
+        for src in range(n):
+            pltpu.make_async_remote_copy(
+                src_ref=g_ref,
+                dst_ref=recv.at[:, pl.ds(src * width, width)],
+                send_sem=send_sem.at[src],
+                recv_sem=recv_sem.at[src],
+                device_id=(sec + 1, src),
+                device_id_type=MESH,
+            ).wait_recv()
+        out_ref[...] = recv[...]
+
+    @pl.when(sec == n_sec - 1)
+    def _():
+        out_ref[...] = jnp.zeros_like(out_ref)
+
+
+def handed_down(g_block, n, n_sec, width):
+    rows = g_block.shape[0]
+    return pl.pallas_call(
+        functools.partial(handed_down_kernel, n, n_sec, width),
+        out_shape=jax.ShapeDtypeStruct((rows, n * width), g_block.dtype),
+        in_specs=[pl.BlockSpec(memory_space=pltpu.VMEM)],
+        out_specs=pl.BlockSpec(memory_space=pltpu.VMEM),
+        scratch_shapes=[
+            pltpu.VMEM((rows, n * width), g_block.dtype),
+            pltpu.SemaphoreType.DMA((n,)),
+            pltpu.SemaphoreType.DMA((n,)),
+        ],
+        compiler_params=pltpu.CompilerParams(collective_id=1, has_side_effects=True),
+    )(g_block)
 
 
 def conv_block(weights, ext_vals, tail_rows, d_act):
@@ -48,22 +171,13 @@
     return (d_vals.astype(jnp.bfloat16), lag_grads, d_pre[: kernel_width - 1])
 
 
-def norm_backward(d_norm, saved_now, upstream, gain_vec):
-    values = saved_now.astype(jnp.float32)
-    inv_rms = lax.rsqrt(jnp.mean(values * values, axis=-1, keepdims=True) + EPSILON)
-    normed = values * inv_rms
-    d_hat = d_norm * gain_vec
-    d_in = inv_rms * (d_hat - normed * jnp.mean(d_hat * normed, axis=-1, keepdims=True))
-    return (upstream.astype(jnp.float32) + d_in, jnp.sum(d_norm * normed, axis=0))
-
-
 def local(dy_top, loss_mask, counts, layer_in, conv_in, norm_gain, conv_weight, in_proj, out_proj):
     sections = lax.axis_size("section")
     tensors = lax.axis_size("tensor")
     section_idx = lax.axis_index("section")
     tensor_idx = lax.axis_index("tensor")
     batches, seq_len, model_width = dy_top.shape
-    saved_rows = layer_in[0]
+    width = model_width // tensors
     gain_vec = norm_gain[0]
     weights = conv_weight[0]
     kernel_width = weights.shape[0]
@@ -77,9 +191,13 @@
     is_last = section_idx == sections - 1
     contract = (((1,), (1,)), ((), ()))
 
+    values = layer_in[0].astype(jnp.float32)
+    inv_rms_all = lax.rsqrt(jnp.mean(values * values, axis=-1, keepdims=True) + EPSILON)
+    normed_all = values * inv_rms_all
+    gain_own = lax.dynamic_slice(gain_vec, (tensor_idx * width,), (width,))
+
     halves = CHUNKS_PER_BATCH
     chunk_len = seq_len // halves
-    local_rows = chunk_len // tensors
     order = [(b, h) for b in range(batches) for h in reversed(range(halves))]
     block_slot = jnp.array([b for b, _ in order], jnp.int32)
     block_half = jnp.array([h for _, h in order], jnp.int32)
@@ -102,10 +220,7 @@
         incoming, results, gain_acc, conv_acc, tail_carry = loop_state
         batch_slot, half_now, join_now, active = pick_block(step_idx)
         row_start = half_now * chunk_len
-        own_start = row_start + tensor_idx * local_rows
-        upstream = jnp.where(is_last, rows_of(top_grads, batch_slot, own_start, local_rows), incoming)
-        gathered = sent_to_all(incoming, "tensor").reshape(chunk_len, model_width)
-        full_chunk = jnp.where(is_last, rows_of(top_grads, batch_slot, row_start, chunk_len), gathered)
+        full_chunk = jnp.where(is_last, rows_of(top_grads, batch_slot, row_start, chunk_len), incoming)
         d_act = lax.dot_general(full_chunk, w_out, contract, preferred_element_type=jnp.float32)
         d_act = lax.optimization_barrier(d_act)
         ext_vals = lax.dynamic_slice(
@@ -113,32 +228,39 @@
         )[0].astype(jnp.float32)
         tail_rows = jnp.where(join_now, tail_carry, 0.0)
         d_vals, conv_part, new_tail = conv_block(weights, ext_vals, tail_rows, d_act)
-        partial = lax.dot_general(d_vals, w_in, contract, preferred_element_type=jnp.float32)
-        d_norm = summed_on_arrival(partial.astype(jnp.bfloat16), "tensor")
-        saved_now = rows_of(saved_rows, batch_slot, own_start, local_rows)
-        grad_in, gain_part = norm_backward(d_norm, saved_now, upstream, gain_vec)
-        grad_out = grad_in.astype(jnp.bfloat16)
-        previous = lax.dynamic_slice(results, (batch_slot, half_now, 0, 0), (1, 1, local_rows, model_width))
+        partial = lax.dot_general(d_vals, w_in, contract, preferred_element_type=jnp.float32).astype(jnp.bfloat16)
+        normed = rows_of(normed_all, batch_slot, row_start, chunk_len)
+        inv_rms = rows_of(inv_rms_all, batch_slot, row_start, chunk_len)
+        row_part = jnp.sum(partial.astype(jnp.float32) * gain_vec * normed, axis=-1)
+        stats = jnp.zeros((8, 128), jnp.float32).at[0, :chunk_len].set(row_part)
+        d_norm, stats_total = scatter_sum(partial, stats, tensors, width)
+        row_mean = stats_total[0, :chunk_len][:, None] / model_width
+        normed_own = lax.dynamic_slice(normed, (0, tensor_idx * width), (chunk_len, width))
+        upstream_own = lax.dynamic_slice(full_chunk, (0, tensor_idx * width), (chunk_len, width))
+        d_in = inv_rms * (d_norm * gain_own - normed_own * row_mean)
+        grad_out = (upstream_own.astype(jnp.float32) + d_in).astype(jnp.bfloat16)
+        gain_part = jnp.sum(d_norm * normed_own, axis=0)
+        previous = lax.dynamic_slice(results, (batch_slot, half_now, 0, 0), (1, 1, chunk_len, width))
         updated = jnp.where(active, grad_out[None, None], previous)
         results = lax.dynamic_update_slice(results, updated, (batch_slot, half_now, 0, 0))
         gain_acc = gain_acc + jnp.where(active, gain_part, 0.0)
         conv_acc = conv_acc + jnp.where(active, conv_part, 0.0)
         tail_carry = jnp.where(active, new_tail, tail_carry)
-        incoming = lax.ppermute(grad_out, "section", [(i, i - 1) for i in range(1, sections)])
+        incoming = handed_down(grad_out, tensors, sections, width)
         return (incoming, results, gain_acc, conv_acc, tail_carry)
 
     initial = (
-        jnp.zeros((local_rows, model_width), jnp.bfloat16),
-        jnp.zeros((batches, halves, local_rows, model_width), jnp.bfloat16),
-        jnp.zeros(gain_vec.shape, jnp.float32),
+        jnp.zeros((chunk_len, model_width), jnp.bfloat16),
+        jnp.zeros((batches, halves, chunk_len, width), jnp.bfloat16),
+        jnp.zeros((width,), jnp.float32),
         jnp.zeros(weights.shape, jnp.float32),
         tail_init,
     )
     last_state = lax.fori_loop(0, total_steps, step_rows, initial)
     gathered = sent_to_all(last_state[1], "tensor")
-    results = jnp.transpose(gathered, (1, 2, 0, 3, 4)).reshape(batches, seq_len, model_width)
+    results = jnp.transpose(gathered, (1, 2, 3, 0, 4)).reshape(batches, seq_len, model_width)
     conv_acc = last_state[3]
-    gain_total = of_everyone(last_state[2].astype(jnp.bfloat16), "tensor")
+    gain_total = sent_to_all(last_state[2], "tensor").reshape(model_width)
     return (results[None], gain_total[None], conv_acc[None])
 
 

time: 626 us -> 639 us (1.021)
  Pallas kernels: 0 us -> 294 us
  waiting for transfers between devices: 218 us -> 26.8 us
  starting transfers between devices: 110 us -> 3.72 us
  matrix products: 116 us -> 139 us
  local copies, waits for them, and re-layouts: 59.8 us -> 44.5 us
    pallas_call x0 -> x22, Pallas kernels: none -> 294 us  [the longest x11 158 us: scatter_sum(): pl.pallas_call(functools.partial(scatter_sum_kernel, n, width), out_shape...]
    all_to_all x11 -> x0, waiting for transfers between devices: 94.1 us -> none  [summed_on_arrival(): lax.all_to_all(parts, axis, split_axis=0, concat_axis=0, tiled=True)]
    all_to_all x12 -> x1, waiting for transfers between devices: 107 us -> 26.8 us  [sent_to_all(): return lax.all_to_all(copies, axis, split_axis=0, concat_axis=0, tiled=True)]
    all_to_all x12 -> x1, starting transfers between devices: 46.7 us -> 3.72 us  [sent_to_all(): return lax.all_to_all(copies, axis, split_axis=0, concat_axis=0, tiled=True)]
    all_to_all x11 -> x0, starting transfers between devices: 42.7 us -> none  [summed_on_arrival(): lax.all_to_all(parts, axis, split_axis=0, concat_axis=0, tiled=True)]
    dot_general x11, matrix products: 35.1 us -> 58.8 us  [step_rows(): lax.dot_general(d_vals, w_in, contract, preferred_element_type=jnp.float32)]
    ppermute x11 -> x0, starting transfers between devices: 21.1 us -> none  [step_rows(): lax.ppermute(grad_out, 'section', [(i, i - 1) for i in range(1, sections)])]
    reduce_sum x34 -> x12, other arithmetic: 31.3 us -> 13.4 us  [the longest x11 11.3 us: step_rows(): gain_part = jnp.sum(d_norm * normed_own, axis=0)]
  transfers between devices with their start and end apart: 34 -> 1, of which waited for: 34 -> 1; matrix products, arithmetic and copies ran while one was open for 6% -> 0% of each run, Pallas kernels for 0% -> 0%
where the time goes in v2:
time: 639 us; the launch traced here: 630 us
  Pallas kernels  294 us (46%)
  matrix products  139 us (22%)
  other arithmetic  55.3 us (9%)
  loops' own time  51.5 us (8%)
  local copies, waits for them, and re-layouts  44.5 us (7%)
  waiting for transfers between devices  26.8 us (4%)
  blocking collectives  14.3 us (2%)
    pallas_call x11, Pallas kernels, scatter_sum(): pl.pallas_call(functools.partial(scatter_sum_kernel, n, width), out_shape...  158 us
    pallas_call x11, Pallas kernels, handed_down(): pl.pallas_call(functools.partial(handed_down_kernel, n, n_sec, width), ou...  137 us
    dot_general x11, matrix products, step_rows(): lax.dot_general(full_chunk, w_out, contract, preferred_element_type=jnp.f...  80.5 us
    dot_general x11, matrix products, step_rows(): lax.dot_general(d_vals, w_in, contract, preferred_element_type=jnp.float32)  58.8 us
    another operation x1, loops' own time, local(): last_state = lax.fori_loop(0, total_steps, step_rows, initial)  51.5 us
    all_to_all x1, waiting for transfers between devices, sent_to_all(): return lax.all_to_all(copies, axis, split_axis=0, concat_axis=0, tiled=True)  26.8 us
    dynamic_update_slice x11, other arithmetic, step_rows(): lax.dynamic_update_slice(results, updated, (batch_slot, half_now, 0, 0))  17.7 us
    all_to_all x1, blocking collectives, sent_to_all(): return lax.all_to_all(copies, axis, split_axis=0, concat_axis=0, tiled=True)  14.3 us
  transfers between devices with their start and end apart: 1, of which 1 were waited for; matrix products, arithmetic and copies ran while one was open for 0% of the time, Pallas kernels for 0%

profile of v2, /device:TPU:32, one launch (start us, length us, event | category | flops | bytes accessed | tf_op | source)
XLA Modules:
  0.0 630.5 jit_solution(2167182672286996712)
XLA Ops:
  9.7 567.1 %while.27 = (s32[]{:T(128)}, bf16[32,8192]{1,0:T(8,128)(2,1)S(1)}, bf16[2,2,32,512]{3,2,1,0:T(8,128)(2,1)S(1)}, f32[512]{0:T(512)S(1)}, f32[4,640]{1,0:T(4,128)S...) while((s32[]{:T(128)}, bf16[32,8192]{1,0:T(8,128)(2,1)S(1)}, ...), condition=%wide.region_8.9_spmd.clone.clone, body=%wide.region_1.8_spmd.sunk.clone.clone.sunk | while | flops 673563648 | bytes 67957888 | solution.py:259
  17.0 7.3 %fusion.42 = f32[32,640]{1,0:T(8,128)S(1)} fusion(bf16[32,8192]{1,0:T(8,128)(2,1)S(1)} %bitcast_select_fusion.3, bf16[640,8192]{1,0:T(8,128)(2,1)} %get-tuple-element.1059), kind=kOutput, calls=%fused_computation.61.clone.1 | convolution fusion | flops 335544320 | bytes 11091968 | tf_op jit(solution)/shard_map/while/body/eval_jaxpr/dot_general | solution.py:224
  25.2 5.3 fusion.43
  31.1 16.0 %eval_jaxpr.18 = (f32[32,512]{1,0:T(8,128)}, f32[8,128]{1,0:T(8,128)}) custom-call(bf16[32,8192]{1,0:T(8,128)(2,1)} %get-tuple-element.974.x_ref, f32[8,128]{1,0:T(8,128)} %scatter.9.s_ref), custom_call_target="tpu_custom_call" | custom-call | tf_op jit(solution)/shard_map/while/body/eval_jaxpr/pallas_call | solution.py:66
  50.4 13.6 %eval_jaxpr.19 = bf16[32,8192]{1,0:T(8,128)(2,1)S(1)} custom-call(bf16[32,512]{1,0:T(8,128)(2,1)} %get-tuple-element.978.g_ref), custom_call_target="tpu_custom_call" | custom-call | tf_op jit(solution)/shard_map/while/body/eval_jaxpr/pallas_call | solution.py:135
  71.3 7.3 %fusion.42 = f32[32,640]{1,0:T(8,128)S(1)} fusion(bf16[32,8192]{1,0:T(8,128)(2,1)S(1)} %bitcast_select_fusion.3, bf16[640,8192]{1,0:T(8,128)(2,1)} %get-tuple-element.1059), kind=kOutput, calls=%fused_computation.61.clone.1 | convolution fusion | flops 335544320 | bytes 11091968 | tf_op jit(solution)/shard_map/while/body/eval_jaxpr/dot_general | solution.py:224
  79.5 5.4 fusion.43
  85.5 15.3 %eval_jaxpr.18 = (f32[32,512]{1,0:T(8,128)}, f32[8,128]{1,0:T(8,128)}) custom-call(bf16[32,8192]{1,0:T(8,128)(2,1)} %get-tuple-element.974.x_ref, f32[8,128]{1,0:T(8,128)} %scatter.9.s_ref), custom_call_target="tpu_custom_call" | custom-call | tf_op jit(solution)/shard_map/while/body/eval_jaxpr/pallas_call | solution.py:66
  104.1 12.7 %eval_jaxpr.19 = bf16[32,8192]{1,0:T(8,128)(2,1)S(1)} custom-call(bf16[32,512]{1,0:T(8,128)(2,1)} %get-tuple-element.978.g_ref), custom_call_target="tpu_custom_call" | custom-call | tf_op jit(solution)/shard_map/while/body/eval_jaxpr/pallas_call | solution.py:135
  124.1 7.3 %fusion.42 = f32[32,640]{1,0:T(8,128)S(1)} fusion(bf16[32,8192]{1,0:T(8,128)(2,1)S(1)} %bitcast_select_fusion.3, bf16[640,8192]{1,0:T(8,128)(2,1)} %get-tuple-element.1059), kind=kOutput, calls=%fused_computation.61.clone.1 | convolution fusion | flops 335544320 | bytes 11091968 | tf_op jit(solution)/shard_map/while/body/eval_jaxpr/dot_general | solution.py:224
  132.3 5.3 fusion.43
  138.3 14.5 %eval_jaxpr.18 = (f32[32,512]{1,0:T(8,128)}, f32[8,128]{1,0:T(8,128)}) custom-call(bf16[32,8192]{1,0:T(8,128)(2,1)} %get-tuple-element.974.x_ref, f32[8,128]{1,0:T(8,128)} %scatter.9.s_ref), custom_call_target="tpu_custom_call" | custom-call | tf_op jit(solution)/shard_map/while/body/eval_jaxpr/pallas_call | solution.py:66
  156.0 12.4 %eval_jaxpr.19 = bf16[32,8192]{1,0:T(8,128)(2,1)S(1)} custom-call(bf16[32,512]{1,0:T(8,128)(2,1)} %get-tuple-element.978.g_ref), custom_call_target="tpu_custom_call" | custom-call | tf_op jit(solution)/shard_map/while/body/eval_jaxpr/pallas_call | solution.py:135
  175.8 7.3 %fusion.42 = f32[32,640]{1,0:T(8,128)S(1)} fusion(bf16[32,8192]{1,0:T(8,128)(2,1)S(1)} %bitcast_select_fusion.3, bf16[640,8192]{1,0:T(8,128)(2,1)} %get-tuple-element.1059), kind=kOutput, calls=%fused_computation.61.clone.1 | convolution fusion | flops 335544320 | bytes 11091968 | tf_op jit(solution)/shard_map/while/body/eval_jaxpr/dot_general | solution.py:224
  184.0 5.3 fusion.43
  189.9 14.0 %eval_jaxpr.18 = (f32[32,512]{1,0:T(8,128)}, f32[8,128]{1,0:T(8,128)}) custom-call(bf16[32,8192]{1,0:T(8,128)(2,1)} %get-tuple-element.974.x_ref, f32[8,128]{1,0:T(8,128)} %scatter.9.s_ref), custom_call_target="tpu_custom_call" | custom-call | tf_op jit(solution)/shard_map/while/body/eval_jaxpr/pallas_call | solution.py:66
  207.2 11.7 %eval_jaxpr.19 = bf16[32,8192]{1,0:T(8,128)(2,1)S(1)} custom-call(bf16[32,512]{1,0:T(8,128)(2,1)} %get-tuple-element.978.g_ref), custom_call_target="tpu_custom_call" | custom-call | tf_op jit(solution)/shard_map/while/body/eval_jaxpr/pallas_call | solution.py:135
  226.2 7.3 %fusion.42 = f32[32,640]{1,0:T(8,128)S(1)} fusion(bf16[32,8192]{1,0:T(8,128)(2,1)S(1)} %bitcast_select_fusion.3, bf16[640,8192]{1,0:T(8,128)(2,1)} %get-tuple-element.1059), kind=kOutput, calls=%fused_computation.61.clone.1 | convolution fusion | flops 335544320 | bytes 11091968 | tf_op jit(solution)/shard_map/while/body/eval_jaxpr/dot_general | solution.py:224
  234.4 5.4 fusion.43
  240.4 14.2 %eval_jaxpr.18 = (f32[32,512]{1,0:T(8,128)}, f32[8,128]{1,0:T(8,128)}) custom-call(bf16[32,8192]{1,0:T(8,128)(2,1)} %get-tuple-element.974.x_ref, f32[8,128]{1,0:T(8,128)} %scatter.9.s_ref), custom_call_target="tpu_custom_call" | custom-call | tf_op jit(solution)/shard_map/while/body/eval_jaxpr/pallas_call | solution.py:66
  257.9 12.8 %eval_jaxpr.19 = bf16[32,8192]{1,0:T(8,128)(2,1)S(1)} custom-call(bf16[32,512]{1,0:T(8,128)(2,1)} %get-tuple-element.978.g_ref), custom_call_target="tpu_custom_call" | custom-call | tf_op jit(solution)/shard_map/while/body/eval_jaxpr/pallas_call | solution.py:135
  278.0 7.3 %fusion.42 = f32[32,640]{1,0:T(8,128)S(1)} fusion(bf16[32,8192]{1,0:T(8,128)(2,1)S(1)} %bitcast_select_fusion.3, bf16[640,8192]{1,0:T(8,128)(2,1)} %get-tuple-element.1059), kind=kOutput, calls=%fused_computation.61.clone.1 | convolution fusion | flops 335544320 | bytes 11091968 | tf_op jit(solution)/shard_map/while/body/eval_jaxpr/dot_general | solution.py:224
  286.2 5.3 fusion.43
  292.2 14.7 %eval_jaxpr.18 = (f32[32,512]{1,0:T(8,128)}, f32[8,128]{1,0:T(8,128)}) custom-call(bf16[32,8192]{1,0:T(8,128)(2,1)} %get-tuple-element.974.x_ref, f32[8,128]{1,0:T(8,128)} %scatter.9.s_ref), custom_call_target="tpu_custom_call" | custom-call | tf_op jit(solution)/shard_map/while/body/eval_jaxpr/pallas_call | solution.py:66
  310.2 12.6 %eval_jaxpr.19 = bf16[32,8192]{1,0:T(8,128)(2,1)S(1)} custom-call(bf16[32,512]{1,0:T(8,128)(2,1)} %get-tuple-element.978.g_ref), custom_call_target="tpu_custom_call" | custom-call | tf_op jit(solution)/shard_map/while/body/eval_jaxpr/pallas_call | solution.py:135
  330.1 7.3 %fusion.42 = f32[32,640]{1,0:T(8,128)S(1)} fusion(bf16[32,8192]{1,0:T(8,128)(2,1)S(1)} %bitcast_select_fusion.3, bf16[640,8192]{1,0:T(8,128)(2,1)} %get-tuple-element.1059), kind=kOutput, calls=%fused_computation.61.clone.1 | convolution fusion | flops 335544320 | bytes 11091968 | tf_op jit(solution)/shard_map/while/body/eval_jaxpr/dot_general | solution.py:224
  338.3 5.3 fusion.43
  344.3 13.4 %eval_jaxpr.18 = (f32[32,512]{1,0:T(8,128)}, f32[8,128]{1,0:T(8,128)}) custom-call(bf16[32,8192]{1,0:T(8,128)(2,1)} %get-tuple-element.974.x_ref, f32[8,128]{1,0:T(8,128)} %scatter.9.s_ref), custom_call_target="tpu_custom_call" | custom-call | tf_op jit(solution)/shard_map/while/body/eval_jaxpr/pallas_call | solution.py:66
  361.0 11.8 %eval_jaxpr.19 = bf16[32,8192]{1,0:T(8,128)(2,1)S(1)} custom-call(bf16[32,512]{1,0:T(8,128)(2,1)} %get-tuple-element.978.g_ref), custom_call_target="tpu_custom_call" | custom-call | tf_op jit(solution)/shard_map/while/body/eval_jaxpr/pallas_call | solution.py:135
  380.2 7.3 %fusion.42 = f32[32,640]{1,0:T(8,128)S(1)} fusion(bf16[32,8192]{1,0:T(8,128)(2,1)S(1)} %bitcast_select_fusion.3, bf16[640,8192]{1,0:T(8,128)(2,1)} %get-tuple-element.1059), kind=kOutput, calls=%fused_computation.61.clone.1 | convolution fusion | flops 335544320 | bytes 11091968 | tf_op jit(solution)/shard_map/while/body/eval_jaxpr/dot_general | solution.py:224
  388.4 5.3 fusion.43
  394.3 13.9 %eval_jaxpr.18 = (f32[32,512]{1,0:T(8,128)}, f32[8,128]{1,0:T(8,128)}) custom-call(bf16[32,8192]{1,0:T(8,128)(2,1)} %get-tuple-element.974.x_ref, f32[8,128]{1,0:T(8,128)} %scatter.9.s_ref), custom_call_target="tpu_custom_call" | custom-call | tf_op jit(solution)/shard_map/while/body/eval_jaxpr/pallas_call | solution.py:66
  411.6 12.2 %eval_jaxpr.19 = bf16[32,8192]{1,0:T(8,128)(2,1)S(1)} custom-call(bf16[32,512]{1,0:T(8,128)(2,1)} %get-tuple-element.978.g_ref), custom_call_target="tpu_custom_call" | custom-call | tf_op jit(solution)/shard_map/while/body/eval_jaxpr/pallas_call | solution.py:135
  431.1 7.3 %fusion.42 = f32[32,640]{1,0:T(8,128)S(1)} fusion(bf16[32,8192]{1,0:T(8,128)(2,1)S(1)} %bitcast_select_fusion.3, bf16[640,8192]{1,0:T(8,128)(2,1)} %get-tuple-element.1059), kind=kOutput, calls=%fused_computation.61.clone.1 | convolution fusion | flops 335544320 | bytes 11091968 | tf_op jit(solution)/shard_map/while/body/eval_jaxpr/dot_general | solution.py:224
  439.3 5.4 fusion.43
  445.3 14.3 %eval_jaxpr.18 = (f32[32,512]{1,0:T(8,128)}, f32[8,128]{1,0:T(8,128)}) custom-call(bf16[32,8192]{1,0:T(8,128)(2,1)} %get-tuple-element.974.x_ref, f32[8,128]{1,0:T(8,128)} %scatter.9.s_ref), custom_call_target="tpu_custom_call" | custom-call | tf_op jit(solution)/shard_map/while/body/eval_jaxpr/pallas_call | solution.py:66
  462.9 12.3 %eval_jaxpr.19 = bf16[32,8192]{1,0:T(8,128)(2,1)S(1)} custom-call(bf16[32,512]{1,0:T(8,128)(2,1)} %get-tuple-element.978.g_ref), custom_call_target="tpu_custom_call" | custom-call | tf_op jit(solution)/shard_map/while/body/eval_jaxpr/pallas_call | solution.py:135
  482.5 7.3 %fusion.42 = f32[32,640]{1,0:T(8,128)S(1)} fusion(bf16[32,8192]{1,0:T(8,128)(2,1)S(1)} %bitcast_select_fusion.3, bf16[640,8192]{1,0:T(8,128)(2,1)} %get-tuple-element.1059), kind=kOutput, calls=%fused_computation.61.clone.1 | convolution fusion | flops 335544320 | bytes 11091968 | tf_op jit(solution)/shard_map/while/body/eval_jaxpr/dot_general | solution.py:224
  490.7 5.4 fusion.43
  496.7 13.8 %eval_jaxpr.18 = (f32[32,512]{1,0:T(8,128)}, f32[8,128]{1,0:T(8,128)}) custom-call(bf16[32,8192]{1,0:T(8,128)(2,1)} %get-tuple-element.974.x_ref, f32[8,128]{1,0:T(8,128)} %scatter.9.s_ref), custom_call_target="tpu_custom_call" | custom-call | tf_op jit(solution)/shard_map/while/body/eval_jaxpr/pallas_call | solution.py:66
  513.8 12.2 %eval_jaxpr.19 = bf16[32,8192]{1,0:T(8,128)(2,1)S(1)} custom-call(bf16[32,512]{1,0:T(8,128)(2,1)} %get-tuple-element.978.g_ref), custom_call_target="tpu_custom_call" | custom-call | tf_op jit(solution)/shard_map/while/body/eval_jaxpr/pallas_call | solution.py:135
  533.3 7.3 %fusion.42 = f32[32,640]{1,0:T(8,128)S(1)} fusion(bf16[32,8192]{1,0:T(8,128)(2,1)S(1)} %bitcast_select_fusion.3, bf16[640,8192]{1,0:T(8,128)(2,1)} %get-tuple-element.1059), kind=kOutput, calls=%fused_computation.61.clone.1 | convolution fusion | flops 335544320 | bytes 11091968 | tf_op jit(solution)/shard_map/while/body/eval_jaxpr/dot_general | solution.py:224
  541.5 5.3 fusion.43
  547.4 13.8 %eval_jaxpr.18 = (f32[32,512]{1,0:T(8,128)}, f32[8,128]{1,0:T(8,128)}) custom-call(bf16[32,8192]{1,0:T(8,128)(2,1)} %get-tuple-element.974.x_ref, f32[8,128]{1,0:T(8,128)} %scatter.9.s_ref), custom_call_target="tpu_custom_call" | custom-call | tf_op jit(solution)/shard_map/while/body/eval_jaxpr/pallas_call | solution.py:66
  564.6 12.1 %eval_jaxpr.19 = bf16[32,8192]{1,0:T(8,128)(2,1)S(1)} custom-call(bf16[32,512]{1,0:T(8,128)(2,1)} %get-tuple-element.978.g_ref), custom_call_target="tpu_custom_call" | custom-call | tf_op jit(solution)/shard_map/while/body/eval_jaxpr/pallas_call | solution.py:135
  576.8 14.3 %all_to_all.11 = f32[16,1,512]{2,1,0:T(1,128)S(1)} all-to-all(f32[16,1,512]{2,1,0:T(1,128)S(1)} %broadcast_in_dim.97), channel_id=1, replica_groups=mesh['section'=8,'tensor'=16] {'tensor'}, dimensions={0} | all-to-all | bytes 65536 | tf_op jit(solution)/shard_map/all_to_all | solution.py:17
  596.4 26.8 %all-to-all-done = bf16[16,2,2,32,512]{4,3,2,1,0:T(8,128)(2,1)S(1)} async-done(((bf16[16,2,2,32,512]{4,3,2,1,0:T(8,128)(2,1)}), bf16[16,2,2,32,512]{4,3,2,1,0:T(8,128)(2,1)S(1)}, u32[]{:S(2)}, u32[]{:S(2)}) %all-to-all-start) | async-done | bytes 2097184 | tf_op jit(solution)/shard_map/all_to_all | solution.py:17
  625.7 4.2 broadcast_in_dim_reshape.6
  (264 shorter events, 99.3 us)
Async XLA Ops:
  0.7 7.0 %copy-start.5 = (s32[2,64]{1,0:T(2,128)S(1)}, s32[2,64]{1,0:T(2,128)}, u32[]{:S(2)}) copy-start(s32[2,64]{1,0:T(2,128)} %param.17) | copy-start | bytes 1540
  0.7 6.9 %copy-start.6 = (s32[2]{0:T(128)S(1)}, s32[2]{0:T(128)}, u32[]{:S(2)}) copy-start(s32[2]{0:T(128)} %param.18) | copy-start | bytes 28
  0.7 7.0 %copy-start.4 = (bf16[1,2,64,640]{3,2,1,0:T(8,128)(2,1)S(1)}, bf16[1,2,64,640]{3,2,1,0:T(8,128)(2,1)}, u32[]{:S(2)}) copy-start(bf16[1,2,64,640]{3,2,1,0:T(8,128)(2,1)} %param.20) | copy-start | bytes 491524
  3.6 6.1 copy-start.1
  3.6 6.1 copy-start.2
  3.6 6.1 copy-start.7
  3.6 6.1 copy-start.8
  16.9 8.2 %copy-start = (bf16[8192,640]{1,0:T(8,128)(2,1)S(1)}, bf16[8192,640]{1,0:T(8,128)(2,1)}, u32[]{:S(2)}) copy-start(bf16[8192,640]{1,0:T(8,128)(2,1)} %get-tuple-element.1061) | copy-start | bytes 31457284 | tf_op jit(solution)/shard_map/while
  71.3 8.2 %copy-start = (bf16[8192,640]{1,0:T(8,128)(2,1)S(1)}, bf16[8192,640]{1,0:T(8,128)(2,1)}, u32[]{:S(2)}) copy-start(bf16[8192,640]{1,0:T(8,128)(2,1)} %get-tuple-element.1061) | copy-start | bytes 31457284 | tf_op jit(solution)/shard_map/while
  124.1 8.2 %copy-start = (bf16[8192,640]{1,0:T(8,128)(2,1)S(1)}, bf16[8192,640]{1,0:T(8,128)(2,1)}, u32[]{:S(2)}) copy-start(bf16[8192,640]{1,0:T(8,128)(2,1)} %get-tuple-element.1061) | copy-start | bytes 31457284 | tf_op jit(solution)/shard_map/while
  175.8 8.2 %copy-start = (bf16[8192,640]{1,0:T(8,128)(2,1)S(1)}, bf16[8192,640]{1,0:T(8,128)(2,1)}, u32[]{:S(2)}) copy-start(bf16[8192,640]{1,0:T(8,128)(2,1)} %get-tuple-element.1061) | copy-start | bytes 31457284 | tf_op jit(solution)/shard_map/while
  226.2 8.2 %copy-start = (bf16[8192,640]{1,0:T(8,128)(2,1)S(1)}, bf16[8192,640]{1,0:T(8,128)(2,1)}, u32[]{:S(2)}) copy-start(bf16[8192,640]{1,0:T(8,128)(2,1)} %get-tuple-element.1061) | copy-start | bytes 31457284 | tf_op jit(solution)/shard_map/while
  278.0 8.2 %copy-start = (bf16[8192,640]{1,0:T(8,128)(2,1)S(1)}, bf16[8192,640]{1,0:T(8,128)(2,1)}, u32[]{:S(2)}) copy-start(bf16[8192,640]{1,0:T(8,128)(2,1)} %get-tuple-element.1061) | copy-start | bytes 31457284 | tf_op jit(solution)/shard_map/while
  330.1 8.2 %copy-start = (bf16[8192,640]{1,0:T(8,128)(2,1)S(1)}, bf16[8192,640]{1,0:T(8,128)(2,1)}, u32[]{:S(2)}) copy-start(bf16[8192,640]{1,0:T(8,128)(2,1)} %get-tuple-element.1061) | copy-start | bytes 31457284 | tf_op jit(solution)/shard_map/while
  380.1 8.2 %copy-start = (bf16[8192,640]{1,0:T(8,128)(2,1)S(1)}, bf16[8192,640]{1,0:T(8,128)(2,1)}, u32[]{:S(2)}) copy-start(bf16[8192,640]{1,0:T(8,128)(2,1)} %get-tuple-element.1061) | copy-start | bytes 31457284 | tf_op jit(solution)/shard_map/while
  431.1 8.2 %copy-start = (bf16[8192,640]{1,0:T(8,128)(2,1)S(1)}, bf16[8192,640]{1,0:T(8,128)(2,1)}, u32[]{:S(2)}) copy-start(bf16[8192,640]{1,0:T(8,128)(2,1)} %get-tuple-element.1061) | copy-start | bytes 31457284 | tf_op jit(solution)/shard_map/while
  482.5 8.2 %copy-start = (bf16[8192,640]{1,0:T(8,128)(2,1)S(1)}, bf16[8192,640]{1,0:T(8,128)(2,1)}, u32[]{:S(2)}) copy-start(bf16[8192,640]{1,0:T(8,128)(2,1)} %get-tuple-element.1061) | copy-start | bytes 31457284 | tf_op jit(solution)/shard_map/while
  533.3 8.2 %copy-start = (bf16[8192,640]{1,0:T(8,128)(2,1)S(1)}, bf16[8192,640]{1,0:T(8,128)(2,1)}, u32[]{:S(2)}) copy-start(bf16[8192,640]{1,0:T(8,128)(2,1)} %get-tuple-element.1061) | copy-start | bytes 31457284 | tf_op jit(solution)/shard_map/while
  576.7 48.9 %copy-start.3 = (f32[4,640]{1,0:T(4,128)}, f32[4,640]{1,0:T(4,128)S(1)}, u32[]{:S(2)}) copy-start(f32[4,640]{1,0:T(4,128)S(1)} %get-tuple-element.595) | copy-start | bytes 30724
  592.6 30.5 %all-to-all-start = ((bf16[16,2,2,32,512]{4,3,2,1,0:T(8,128)(2,1)}), bf16[16,2,2,32,512]{4,3,2,1,0:T(8,128)(2,1)S(1)}, u32[]{:S(2)}, u32[]{:S(2)}) async-start(bf16[16,2,2,32,512]{4,3,2,1,0:T(8,128)(2,1)} %broadcast_in_dim.96), calls=%async_computation | async-start | bytes 4194304 | tf_op jit(solution)/shard_map/all_to_all | solution.py:17

commit v3 on v2

--- a/solution.py
+++ b/solution.py
@@ -17,7 +17,7 @@
     return lax.all_to_all(copies, axis, split_axis=0, concat_axis=0, tiled=True)
 
 
-def scatter_sum_kernel(n, width, x_ref, s_ref, out_ref, sum_ref, recv, srecv, send_sem, recv_sem, ssend_sem, srecv_sem):
+def scatter_sum_kernel(n, width, x_ref, out_ref, recv, send_sem, recv_sem):
     me = lax.axis_index("tensor")
     sec = lax.axis_index("section")
     barrier = pltpu.get_barrier_semaphore()
@@ -37,50 +37,31 @@
             device_id_type=MESH,
         )
         block.start()
-        stat = pltpu.make_async_remote_copy(
-            src_ref=s_ref,
-            dst_ref=srecv.at[me],
-            send_sem=ssend_sem.at[k],
-            recv_sem=srecv_sem.at[k],
-            device_id=(sec, peer),
-            device_id_type=MESH,
-        )
-        stat.start()
-        copies.append((block, stat))
-    for block, stat in copies:
+        copies.append(block)
+    for block in copies:
         block.wait()
-        stat.wait()
     mine = pl.ds(pl.multiple_of(me * width, 128), width)
     total = x_ref[:, mine].astype(jnp.float32)
-    stat_total = s_ref[...]
     for k in range(1, n):
         src = lax.rem(me + n - k, n)
         total = total + recv[src].astype(jnp.float32)
-        stat_total = stat_total + srecv[src]
     out_ref[...] = total
-    sum_ref[...] = stat_total
-
-
-def scatter_sum(x, stats, n, width):
+
+
+def scatter_sum(x, n, width):
     rows = x.shape[0]
     return pl.pallas_call(
         functools.partial(scatter_sum_kernel, n, width),
-        out_shape=(
-            jax.ShapeDtypeStruct((rows, width), jnp.float32),
-            jax.ShapeDtypeStruct(stats.shape, jnp.float32),
-        ),
-        in_specs=[pl.BlockSpec(memory_space=pltpu.VMEM)] * 2,
-        out_specs=(pl.BlockSpec(memory_space=pltpu.VMEM), pl.BlockSpec(memory_space=pltpu.VMEM)),
+        out_shape=jax.ShapeDtypeStruct((rows, width), jnp.float32),
+        in_specs=[pl.BlockSpec(memory_space=pltpu.VMEM)],
+        out_specs=pl.BlockSpec(memory_space=pltpu.VMEM),
         scratch_shapes=[
             pltpu.VMEM((n, rows, width), x.dtype),
-            pltpu.VMEM((n, *stats.shape), jnp.float32),
-            pltpu.SemaphoreType.DMA((n,)),
-            pltpu.SemaphoreType.DMA((n,)),
             pltpu.SemaphoreType.DMA((n,)),
             pltpu.SemaphoreType.DMA((n,)),
         ],
         compiler_params=pltpu.CompilerParams(collective_id=0, has_side_effects=True),
-    )(x, stats)
+    )(x)
 
 
 def handed_down_kernel(n, n_sec, width, g_ref, out_ref, recv, send_sem, recv_sem):
@@ -183,7 +164,7 @@
     kernel_width = weights.shape[0]
     local_channels = weights.shape[1]
     w_in = in_proj[0]
-    w_out = out_proj[0]
+    w_out_t = jnp.transpose(out_proj[0])
     conv_padded = jnp.pad(conv_in[0], ((0, 0), (kernel_width - 1, 0), (0, 0)))
     positions = jnp.arange(seq_len, dtype=jnp.int32)
     keep_mask = (loss_mask == 1) & (positions[None, :] < counts[:, None])
@@ -196,6 +177,7 @@
     normed_all = values * inv_rms_all
     gain_own = lax.dynamic_slice(gain_vec, (tensor_idx * width,), (width,))
 
+    stat_rows_n = 16
     halves = CHUNKS_PER_BATCH
     chunk_len = seq_len // halves
     order = [(b, h) for b in range(batches) for h in reversed(range(halves))]
@@ -221,7 +203,7 @@
         batch_slot, half_now, join_now, active = pick_block(step_idx)
         row_start = half_now * chunk_len
         full_chunk = jnp.where(is_last, rows_of(top_grads, batch_slot, row_start, chunk_len), incoming)
-        d_act = lax.dot_general(full_chunk, w_out, contract, preferred_element_type=jnp.float32)
+        d_act = jnp.dot(full_chunk, w_out_t, preferred_element_type=jnp.float32)
         d_act = lax.optimization_barrier(d_act)
         ext_vals = lax.dynamic_slice(
             conv_padded, (batch_slot, row_start, 0), (1, chunk_len + kernel_width - 1, local_channels)
@@ -232,9 +214,14 @@
         normed = rows_of(normed_all, batch_slot, row_start, chunk_len)
         inv_rms = rows_of(inv_rms_all, batch_slot, row_start, chunk_len)
         row_part = jnp.sum(partial.astype(jnp.float32) * gain_vec * normed, axis=-1)
-        stats = jnp.zeros((8, 128), jnp.float32).at[0, :chunk_len].set(row_part)
-        d_norm, stats_total = scatter_sum(partial, stats, tensors, width)
-        row_mean = stats_total[0, :chunk_len][:, None] / model_width
+        part_hi = row_part.astype(jnp.bfloat16)
+        part_lo = (row_part - part_hi.astype(jnp.float32)).astype(jnp.bfloat16)
+        stat_rows = jnp.zeros((stat_rows_n, width), jnp.bfloat16)
+        stat_rows = stat_rows.at[0, :chunk_len].set(part_hi).at[1, :chunk_len].set(part_lo)
+        sent = jnp.concatenate([partial, jnp.tile(stat_rows, (1, tensors))], axis=0)
+        summed = scatter_sum(sent, tensors, width)
+        d_norm = summed[:chunk_len]
+        row_mean = (summed[chunk_len, :chunk_len] + summed[chunk_len + 1, :chunk_len])[:, None] / model_width
         normed_own = lax.dynamic_slice(normed, (0, tensor_idx * width), (chunk_len, width))
         upstream_own = lax.dynamic_slice(full_chunk, (0, tensor_idx * width), (chunk_len, width))
         d_in = inv_rms * (d_norm * gain_own - normed_own * row_mean)

time: 639 us -> 721 us (1.13)
  the two profiles are of different devices: /device:TPU:32 before, /device:TPU:64 now
where the time goes in v3:
time: 721 us; the launch traced here: 716 us
  Pallas kernels  335 us (46%)
  matrix products  114 us (16%)
  local copies, waits for them, and re-layouts  92.4 us (13%)
  other arithmetic  73.2 us (10%)
  loops' own time  52.1 us (7%)
  waiting for transfers between devices  30.7 us (4%)
  blocking collectives  14.3 us (2%)
    pallas_call x11, Pallas kernels, scatter_sum(): pl.pallas_call(functools.partial(scatter_sum_kernel, n, width), out_shape...  197 us
    pallas_call x11, Pallas kernels, handed_down(): pl.pallas_call(functools.partial(handed_down_kernel, n, n_sec, width), ou...  138 us
    dot_general x11, matrix products, step_rows(): d_act = jnp.dot(full_chunk, w_out_t, preferred_element_type=jnp.float32)  64.1 us
    another operation x1, loops' own time, local(): last_state = lax.fori_loop(0, total_steps, step_rows, initial)  52.1 us
    dot_general x11, matrix products, step_rows(): lax.dot_general(d_vals, w_in, contract, preferred_element_type=jnp.float32)  50 us
    all_to_all x1, waiting for transfers between devices, sent_to_all(): return lax.all_to_all(copies, axis, split_axis=0, concat_axis=0, tiled=True)  30.7 us
    dynamic_update_slice x11, other arithmetic, step_rows(): lax.dynamic_update_slice(results, updated, (batch_slot, half_now, 0, 0))  18.1 us
    unnamed x14, local copies, waits for them, and re-layouts  15.1 us
  transfers between devices with their start and end apart: 1, of which 1 were waited for; matrix products, arithmetic and copies ran while one was open for 0% of the time, Pallas kernels for 0%

profile of v3, /device:TPU:64, one launch (start us, length us, event | category | flops | bytes accessed | tf_op | source)
XLA Modules:
  0.0 716.4 jit_solution(17888395012493510440)
XLA Ops:
  8.2 14.5 %copy.19 = bf16[1,640,8192]{1,2,0:T(8,128)(2,1)} copy(bf16[1,640,8192]{2,1,0:T(8,128)(2,1)} %param.26) | data formatting | bytes 20971520 | tf_op args[8]
  24.8 634.0 %while.28 = (s32[]{:T(128)}, bf16[32,8192]{1,0:T(8,128)(2,1)S(1)}, bf16[2,2,32,512]{3,2,1,0:T(8,128)(2,1)S(1)}, f32[512]{0:T(512)S(1)}, f32[4,640]{1,0:T(4,128)S...) while((s32[]{:T(128)}, bf16[32,8192]{1,0:T(8,128)(2,1)S(1)}, ...), condition=%wide.region_8.9_spmd.clone.clone, body=%wide.region_1.8_spmd.sunk.clone.clone.sunk | while | flops 675136704 | bytes 59860344 | solution.py:246
  34.5 5.8 fusion.44
  41.5 4.5 fusion.45
  48.5 17.8 %eval_jaxpr.18 = f32[48,512]{1,0:T(8,128)} custom-call(bf16[48,8192]{1,0:T(8,128)(2,1)} %pad_maximum_fusion.3.x_ref), custom_call_target="tpu_custom_call" | custom-call | tf_op jit(solution)/shard_map/while/body/eval_jaxpr/pallas_call | solution.py:53
  69.7 13.6 %eval_jaxpr.19 = bf16[32,8192]{1,0:T(8,128)(2,1)S(1)} custom-call(bf16[32,512]{1,0:T(8,128)(2,1)} %get-tuple-element.993.g_ref), custom_call_target="tpu_custom_call" | custom-call | tf_op jit(solution)/shard_map/while/body/eval_jaxpr/pallas_call | solution.py:116
  93.1 5.8 fusion.44
  100.0 4.5 fusion.45
  107.0 17.6 %eval_jaxpr.18 = f32[48,512]{1,0:T(8,128)} custom-call(bf16[48,8192]{1,0:T(8,128)(2,1)} %pad_maximum_fusion.3.x_ref), custom_call_target="tpu_custom_call" | custom-call | tf_op jit(solution)/shard_map/while/body/eval_jaxpr/pallas_call | solution.py:53
  128.0 15.2 %eval_jaxpr.19 = bf16[32,8192]{1,0:T(8,128)(2,1)S(1)} custom-call(bf16[32,512]{1,0:T(8,128)(2,1)} %get-tuple-element.993.g_ref), custom_call_target="tpu_custom_call" | custom-call | tf_op jit(solution)/shard_map/while/body/eval_jaxpr/pallas_call | solution.py:116
  153.0 5.8 fusion.44
  159.9 4.5 fusion.45
  166.9 17.7 %eval_jaxpr.18 = f32[48,512]{1,0:T(8,128)} custom-call(bf16[48,8192]{1,0:T(8,128)(2,1)} %pad_maximum_fusion.3.x_ref), custom_call_target="tpu_custom_call" | custom-call | tf_op jit(solution)/shard_map/while/body/eval_jaxpr/pallas_call | solution.py:53
  188.0 12.6 %eval_jaxpr.19 = bf16[32,8192]{1,0:T(8,128)(2,1)S(1)} custom-call(bf16[32,512]{1,0:T(8,128)(2,1)} %get-tuple-element.993.g_ref), custom_call_target="tpu_custom_call" | custom-call | tf_op jit(solution)/shard_map/while/body/eval_jaxpr/pallas_call | solution.py:116
  210.4 5.8 fusion.44
  217.3 4.5 fusion.45
  224.3 16.6 %eval_jaxpr.18 = f32[48,512]{1,0:T(8,128)} custom-call(bf16[48,8192]{1,0:T(8,128)(2,1)} %pad_maximum_fusion.3.x_ref), custom_call_target="tpu_custom_call" | custom-call | tf_op jit(solution)/shard_map/while/body/eval_jaxpr/pallas_call | solution.py:53
  244.3 12.2 %eval_jaxpr.19 = bf16[32,8192]{1,0:T(8,128)(2,1)S(1)} custom-call(bf16[32,512]{1,0:T(8,128)(2,1)} %get-tuple-element.993.g_ref), custom_call_target="tpu_custom_call" | custom-call | tf_op jit(solution)/shard_map/while/body/eval_jaxpr/pallas_call | solution.py:116
  266.3 5.8 fusion.44
  273.2 4.5 fusion.45
  280.2 16.7 %eval_jaxpr.18 = f32[48,512]{1,0:T(8,128)} custom-call(bf16[48,8192]{1,0:T(8,128)(2,1)} %pad_maximum_fusion.3.x_ref), custom_call_target="tpu_custom_call" | custom-call | tf_op jit(solution)/shard_map/while/body/eval_jaxpr/pallas_call | solution.py:53
  300.4 11.8 %eval_jaxpr.19 = bf16[32,8192]{1,0:T(8,128)(2,1)S(1)} custom-call(bf16[32,512]{1,0:T(8,128)(2,1)} %get-tuple-element.993.g_ref), custom_call_target="tpu_custom_call" | custom-call | tf_op jit(solution)/shard_map/while/body/eval_jaxpr/pallas_call | solution.py:116
  322.0 5.8 fusion.44
  328.9 4.5 fusion.45
  335.9 17.4 %eval_jaxpr.18 = f32[48,512]{1,0:T(8,128)} custom-call(bf16[48,8192]{1,0:T(8,128)(2,1)} %pad_maximum_fusion.3.x_ref), custom_call_target="tpu_custom_call" | custom-call | tf_op jit(solution)/shard_map/while/body/eval_jaxpr/pallas_call | solution.py:53
  356.7 11.5 %eval_jaxpr.19 = bf16[32,8192]{1,0:T(8,128)(2,1)S(1)} custom-call(bf16[32,512]{1,0:T(8,128)(2,1)} %get-tuple-element.993.g_ref), custom_call_target="tpu_custom_call" | custom-call | tf_op jit(solution)/shard_map/while/body/eval_jaxpr/pallas_call | solution.py:116
  378.0 5.8 fusion.44
  384.9 4.5 fusion.45
  391.9 17.6 %eval_jaxpr.18 = f32[48,512]{1,0:T(8,128)} custom-call(bf16[48,8192]{1,0:T(8,128)(2,1)} %pad_maximum_fusion.3.x_ref), custom_call_target="tpu_custom_call" | custom-call | tf_op jit(solution)/shard_map/while/body/eval_jaxpr/pallas_call | solution.py:53
  413.0 12.6 %eval_jaxpr.19 = bf16[32,8192]{1,0:T(8,128)(2,1)S(1)} custom-call(bf16[32,512]{1,0:T(8,128)(2,1)} %get-tuple-element.993.g_ref), custom_call_target="tpu_custom_call" | custom-call | tf_op jit(solution)/shard_map/while/body/eval_jaxpr/pallas_call | solution.py:116
  435.4 5.8 fusion.44
  442.3 4.5 fusion.45
  449.3 18.9 %eval_jaxpr.18 = f32[48,512]{1,0:T(8,128)} custom-call(bf16[48,8192]{1,0:T(8,128)(2,1)} %pad_maximum_fusion.3.x_ref), custom_call_target="tpu_custom_call" | custom-call | tf_op jit(solution)/shard_map/while/body/eval_jaxpr/pallas_call | solution.py:53
  471.7 12.3 %eval_jaxpr.19 = bf16[32,8192]{1,0:T(8,128)(2,1)S(1)} custom-call(bf16[32,512]{1,0:T(8,128)(2,1)} %get-tuple-element.993.g_ref), custom_call_target="tpu_custom_call" | custom-call | tf_op jit(solution)/shard_map/while/body/eval_jaxpr/pallas_call | solution.py:116
  493.8 5.8 fusion.44
  500.7 4.5 fusion.45
  507.7 19.0 %eval_jaxpr.18 = f32[48,512]{1,0:T(8,128)} custom-call(bf16[48,8192]{1,0:T(8,128)(2,1)} %pad_maximum_fusion.3.x_ref), custom_call_target="tpu_custom_call" | custom-call | tf_op jit(solution)/shard_map/while/body/eval_jaxpr/pallas_call | solution.py:53
  530.2 12.5 %eval_jaxpr.19 = bf16[32,8192]{1,0:T(8,128)(2,1)S(1)} custom-call(bf16[32,512]{1,0:T(8,128)(2,1)} %get-tuple-element.993.g_ref), custom_call_target="tpu_custom_call" | custom-call | tf_op jit(solution)/shard_map/while/body/eval_jaxpr/pallas_call | solution.py:116
  552.4 5.8 fusion.44
  559.4 4.5 fusion.45
  566.4 18.8 %eval_jaxpr.18 = f32[48,512]{1,0:T(8,128)} custom-call(bf16[48,8192]{1,0:T(8,128)(2,1)} %pad_maximum_fusion.3.x_ref), custom_call_target="tpu_custom_call" | custom-call | tf_op jit(solution)/shard_map/while/body/eval_jaxpr/pallas_call | solution.py:53
  588.6 11.9 %eval_jaxpr.19 = bf16[32,8192]{1,0:T(8,128)(2,1)S(1)} custom-call(bf16[32,512]{1,0:T(8,128)(2,1)} %get-tuple-element.993.g_ref), custom_call_target="tpu_custom_call" | custom-call | tf_op jit(solution)/shard_map/while/body/eval_jaxpr/pallas_call | solution.py:116
  610.3 5.8 fusion.44
  617.3 4.5 fusion.45
  624.3 18.6 %eval_jaxpr.18 = f32[48,512]{1,0:T(8,128)} custom-call(bf16[48,8192]{1,0:T(8,128)(2,1)} %pad_maximum_fusion.3.x_ref), custom_call_target="tpu_custom_call" | custom-call | tf_op jit(solution)/shard_map/while/body/eval_jaxpr/pallas_call | solution.py:53
  646.4 12.4 %eval_jaxpr.19 = bf16[32,8192]{1,0:T(8,128)(2,1)S(1)} custom-call(bf16[32,512]{1,0:T(8,128)(2,1)} %get-tuple-element.993.g_ref), custom_call_target="tpu_custom_call" | custom-call | tf_op jit(solution)/shard_map/while/body/eval_jaxpr/pallas_call | solution.py:116
  658.8 14.3 %all_to_all.11 = f32[16,1,512]{2,1,0:T(1,128)S(1)} all-to-all(f32[16,1,512]{2,1,0:T(1,128)S(1)} %broadcast_in_dim.100), channel_id=1, replica_groups=mesh['section'=8,'tensor'=16] {'tensor'}, dimensions={0} | all-to-all | bytes 65536 | tf_op jit(solution)/shard_map/all_to_all | solution.py:17
  678.4 30.7 %all-to-all-done = bf16[16,2,2,32,512]{4,3,2,1,0:T(8,128)(2,1)S(1)} async-done(((bf16[16,2,2,32,512]{4,3,2,1,0:T(8,128)(2,1)}), bf16[16,2,2,32,512]{4,3,2,1,0:T(8,128)(2,1)S(1)}, u32[]{:S(2)}, u32[]{:S(2)}) %all-to-all-start) | async-done | bytes 2097184 | tf_op jit(solution)/shard_map/all_to_all | solution.py:17
  (382 shorter events, 154.8 us)
Async XLA Ops:
  8.2 14.5 %copy-start.4 = (s32[2,64]{1,0:T(2,128)S(1)}, s32[2,64]{1,0:T(2,128)}, u32[]{:S(2)}) copy-start(s32[2,64]{1,0:T(2,128)} %param.19) | copy-start | bytes 1540
  8.2 14.5 %copy-start.5 = (s32[2]{0:T(128)S(1)}, s32[2]{0:T(128)}, u32[]{:S(2)}) copy-start(s32[2]{0:T(128)} %param.20) | copy-start | bytes 28
  8.2 14.6 %copy-start.3 = (bf16[1,2,64,640]{3,2,1,0:T(8,128)(2,1)S(1)}, bf16[1,2,64,640]{3,2,1,0:T(8,128)(2,1)}, u32[]{:S(2)}) copy-start(bf16[1,2,64,640]{3,2,1,0:T(8,128)(2,1)} %param.22) | copy-start | bytes 491524
  22.7 2.0 copy-start
  22.7 2.0 copy-start.1
  34.4 6.9 slice-start
  34.5 6.7 slice-start.1
  34.5 6.9 slice-start.2
  92.9 6.9 slice-start
  93.0 6.7 slice-start.1
  93.0 6.9 slice-start.2
  152.8 6.9 slice-start
  152.9 6.7 slice-start.1
  153.0 6.9 slice-start.2
  210.2 6.9 slice-start
  210.4 6.7 slice-start.1
  210.4 6.9 slice-start.2
  266.1 6.9 slice-start
  266.3 6.7 slice-start.1
  266.3 6.9 slice-start.2
  321.8 6.9 slice-start
  322.0 6.7 slice-start.1
  322.0 6.9 slice-start.2
  377.8 6.9 slice-start
  378.0 6.7 slice-start.1
  378.0 6.9 slice-start.2
  435.2 6.9 slice-start
  435.4 6.7 slice-start.1
  435.4 6.9 slice-start.2
  493.6 6.9 slice-start
  493.8 6.7 slice-start.1
  493.8 6.9 slice-start.2
  552.3 6.9 slice-start
  552.4 6.7 slice-start.1
  552.4 6.9 slice-start.2
  610.2 6.9 slice-start
  610.3 6.7 slice-start.1
  610.3 6.9 slice-start.2
  658.8 52.9 %copy-start.2 = (f32[4,640]{1,0:T(4,128)}, f32[4,640]{1,0:T(4,128)S(1)}, u32[]{:S(2)}) copy-start(f32[4,640]{1,0:T(4,128)S(1)} %get-tuple-element.620) | copy-start | bytes 30724
  674.7 34.4 %all-to-all-start = ((bf16[16,2,2,32,512]{4,3,2,1,0:T(8,128)(2,1)}), bf16[16,2,2,32,512]{4,3,2,1,0:T(8,128)(2,1)S(1)}, u32[]{:S(2)}, u32[]{:S(2)}) async-start(bf16[16,2,2,32,512]{4,3,2,1,0:T(8,128)(2,1)} %broadcast_in_dim.99), calls=%async_computation | async-start | bytes 4194304 | tf_op jit(solution)/shard_map/all_to_all | solution.py:17

commit v4 on v2

--- a/solution.py
+++ b/solution.py
@@ -198,18 +198,15 @@
 
     halves = CHUNKS_PER_BATCH
     chunk_len = seq_len // halves
-    order = [(b, h) for b in range(batches) for h in reversed(range(halves))]
-    block_slot = jnp.array([b for b, _ in order], jnp.int32)
-    block_half = jnp.array([h for _, h in order], jnp.int32)
-    block_join = jnp.array([h < halves - 1 for _, h in order], jnp.bool_)
-    n_chunks = len(order)
+    n_chunks = batches * halves
     total_steps = sections + n_chunks - 1
 
     def pick_block(step_idx):
         block_raw = step_idx - (sections - 1 - section_idx)
         active = (block_raw >= 0) & (block_raw < n_chunks)
         block_now = jnp.clip(block_raw, 0, n_chunks - 1)
-        return (block_slot[block_now], block_half[block_now], block_join[block_now], active)
+        within = lax.rem(block_now, halves)
+        return (block_now // halves, halves - 1 - within, within > 0, active)
 
     def rows_of(array, batch_slot, first_row, row_count):
         return lax.dynamic_slice(array, (batch_slot, first_row, 0), (1, row_count, array.shape[2]))[0]

time: 639 us -> 555 us (0.87)
  loops' own time: 51.5 us -> 1.74 us
  local copies, waits for them, and re-layouts: 44.5 us -> 17.8 us
  other arithmetic: 55.3 us -> 48.2 us
    another operation x1, loops' own time: 51.5 us -> 1.74 us  [local(): last_state = lax.fori_loop(0, total_steps, step_rows, initial)]
    dynamic_slice x33 -> x0, local copies, waits for them, and re-layouts: 26.7 us -> none  [the longest x11 13.7 us: pick_block(): block_slot[block_now]]
    select_n x11, other arithmetic: 7.27 us -> 0.17 us  [step_rows(): tail_carry = jnp.where(active, new_tail, tail_carry)]
where the time goes in v4:
time: 555 us; the launch traced here: 546 us
  Pallas kernels  296 us (53%)
  matrix products  139 us (25%)
  other arithmetic  48.2 us (9%)
  waiting for transfers between devices  25.5 us (5%)
  local copies, waits for them, and re-layouts  17.8 us (3%)
  blocking collectives  12.9 us (2%)
    pallas_call x11, Pallas kernels, scatter_sum(): pl.pallas_call(functools.partial(scatter_sum_kernel, n, width), out_shape...  155 us
    pallas_call x11, Pallas kernels, handed_down(): pl.pallas_call(functools.partial(handed_down_kernel, n, n_sec, width), ou...  140 us
    dot_general x11, matrix products, step_rows(): lax.dot_general(full_chunk, w_out, contract, preferred_element_type=jnp.f...  80.5 us
    dot_general x11, matrix products, step_rows(): lax.dot_general(d_vals, w_in, contract, preferred_element_type=jnp.float32)  58.8 us
    all_to_all x1, waiting for transfers between devices, sent_to_all(): return lax.all_to_all(copies, axis, split_axis=0, concat_axis=0, tiled=True)  25.5 us
    dynamic_update_slice x11, other arithmetic, step_rows(): lax.dynamic_update_slice(results, updated, (batch_slot, half_now, 0, 0))  17.7 us
    all_to_all x1, blocking collectives, sent_to_all(): return lax.all_to_all(copies, axis, split_axis=0, concat_axis=0, tiled=True)  12.9 us
    reduce_sum x11, other arithmetic, step_rows(): gain_part = jnp.sum(d_norm * normed_own, axis=0)  11.3 us
  transfers between devices with their start and end apart: 1, of which 1 were waited for; matrix products, arithmetic and copies ran while one was open for 0% of the time, Pallas kernels for 0%

profile of v4, /device:TPU:32, one launch (start us, length us, event | category | flops | bytes accessed | tf_op | source)
XLA Modules:
  0.0 545.7 jit_solution(16837895054474213557)
XLA Ops:
  9.6 485.1 %while.26 = (s32[]{:T(128)}, bf16[32,8192]{1,0:T(8,128)(2,1)S(1)}, bf16[2,2,32,512]{3,2,1,0:T(8,128)(2,1)S(1)}, f32[512]{0:T(512)S(1)}, f32[4,640]{1,0:T(4,128)S...) while((s32[]{:T(128)}, bf16[32,8192]{1,0:T(8,128)(2,1)S(1)}, ...), condition=%wide.region_8.9_spmd.clone, body=%wide.region_1.8_spmd.clone.sunk | while | flops 673563648 | bytes 67957952 | solution.py:256
  9.9 7.3 %fusion.42 = f32[32,640]{1,0:T(8,128)S(1)} fusion(bf16[32,8192]{1,0:T(8,128)(2,1)S(1)} %bitcast_select_fusion.3, bf16[640,8192]{1,0:T(8,128)(2,1)} %get-tuple-element.924), kind=kOutput, calls=%fused_computation.61.clone.1 | convolution fusion | flops 335544320 | bytes 11091968 | tf_op jit(solution)/shard_map/while/body/eval_jaxpr/dot_general | solution.py:221
  17.5 5.3 fusion.43
  23.4 16.0 %eval_jaxpr.18 = (f32[32,512]{1,0:T(8,128)}, f32[8,128]{1,0:T(8,128)}) custom-call(bf16[32,8192]{1,0:T(8,128)(2,1)} %get-tuple-element.843.x_ref, f32[8,128]{1,0:T(8,128)} %scatter.7.s_ref), custom_call_target="tpu_custom_call" | custom-call | tf_op jit(solution)/shard_map/while/body/eval_jaxpr/pallas_call | solution.py:66
  42.7 13.6 %eval_jaxpr.19 = bf16[32,8192]{1,0:T(8,128)(2,1)S(1)} custom-call(bf16[32,512]{1,0:T(8,128)(2,1)} %get-tuple-element.847.g_ref), custom_call_target="tpu_custom_call" | custom-call | tf_op jit(solution)/shard_map/while/body/eval_jaxpr/pallas_call | solution.py:135
  56.7 7.3 %fusion.42 = f32[32,640]{1,0:T(8,128)S(1)} fusion(bf16[32,8192]{1,0:T(8,128)(2,1)S(1)} %bitcast_select_fusion.3, bf16[640,8192]{1,0:T(8,128)(2,1)} %get-tuple-element.924), kind=kOutput, calls=%fused_computation.61.clone.1 | convolution fusion | flops 335544320 | bytes 11091968 | tf_op jit(solution)/shard_map/while/body/eval_jaxpr/dot_general | solution.py:221
  64.3 5.3 fusion.43
  70.2 15.3 %eval_jaxpr.18 = (f32[32,512]{1,0:T(8,128)}, f32[8,128]{1,0:T(8,128)}) custom-call(bf16[32,8192]{1,0:T(8,128)(2,1)} %get-tuple-element.843.x_ref, f32[8,128]{1,0:T(8,128)} %scatter.7.s_ref), custom_call_target="tpu_custom_call" | custom-call | tf_op jit(solution)/shard_map/while/body/eval_jaxpr/pallas_call | solution.py:66
  88.9 12.7 %eval_jaxpr.19 = bf16[32,8192]{1,0:T(8,128)(2,1)S(1)} custom-call(bf16[32,512]{1,0:T(8,128)(2,1)} %get-tuple-element.847.g_ref), custom_call_target="tpu_custom_call" | custom-call | tf_op jit(solution)/shard_map/while/body/eval_jaxpr/pallas_call | solution.py:135
  101.9 7.3 %fusion.42 = f32[32,640]{1,0:T(8,128)S(1)} fusion(bf16[32,8192]{1,0:T(8,128)(2,1)S(1)} %bitcast_select_fusion.3, bf16[640,8192]{1,0:T(8,128)(2,1)} %get-tuple-element.924), kind=kOutput, calls=%fused_computation.61.clone.1 | convolution fusion | flops 335544320 | bytes 11091968 | tf_op jit(solution)/shard_map/while/body/eval_jaxpr/dot_general | solution.py:221
  109.5 5.3 fusion.43
  115.4 14.5 %eval_jaxpr.18 = (f32[32,512]{1,0:T(8,128)}, f32[8,128]{1,0:T(8,128)}) custom-call(bf16[32,8192]{1,0:T(8,128)(2,1)} %get-tuple-element.843.x_ref, f32[8,128]{1,0:T(8,128)} %scatter.7.s_ref), custom_call_target="tpu_custom_call" | custom-call | tf_op jit(solution)/shard_map/while/body/eval_jaxpr/pallas_call | solution.py:66
  133.2 12.4 %eval_jaxpr.19 = bf16[32,8192]{1,0:T(8,128)(2,1)S(1)} custom-call(bf16[32,512]{1,0:T(8,128)(2,1)} %get-tuple-element.847.g_ref), custom_call_target="tpu_custom_call" | custom-call | tf_op jit(solution)/shard_map/while/body/eval_jaxpr/pallas_call | solution.py:135
  146.0 7.3 %fusion.42 = f32[32,640]{1,0:T(8,128)S(1)} fusion(bf16[32,8192]{1,0:T(8,128)(2,1)S(1)} %bitcast_select_fusion.3, bf16[640,8192]{1,0:T(8,128)(2,1)} %get-tuple-element.924), kind=kOutput, calls=%fused_computation.61.clone.1 | convolution fusion | flops 335544320 | bytes 11091968 | tf_op jit(solution)/shard_map/while/body/eval_jaxpr/dot_general | solution.py:221
  153.5 5.3 fusion.43
  159.5 14.0 %eval_jaxpr.18 = (f32[32,512]{1,0:T(8,128)}, f32[8,128]{1,0:T(8,128)}) custom-call(bf16[32,8192]{1,0:T(8,128)(2,1)} %get-tuple-element.843.x_ref, f32[8,128]{1,0:T(8,128)} %scatter.7.s_ref), custom_call_target="tpu_custom_call" | custom-call | tf_op jit(solution)/shard_map/while/body/eval_jaxpr/pallas_call | solution.py:66
  176.8 11.7 %eval_jaxpr.19 = bf16[32,8192]{1,0:T(8,128)(2,1)S(1)} custom-call(bf16[32,512]{1,0:T(8,128)(2,1)} %get-tuple-element.847.g_ref), custom_call_target="tpu_custom_call" | custom-call | tf_op jit(solution)/shard_map/while/body/eval_jaxpr/pallas_call | solution.py:135
  188.9 7.3 %fusion.42 = f32[32,640]{1,0:T(8,128)S(1)} fusion(bf16[32,8192]{1,0:T(8,128)(2,1)S(1)} %bitcast_select_fusion.3, bf16[640,8192]{1,0:T(8,128)(2,1)} %get-tuple-element.924), kind=kOutput, calls=%fused_computation.61.clone.1 | convolution fusion | flops 335544320 | bytes 11091968 | tf_op jit(solution)/shard_map/while/body/eval_jaxpr/dot_general | solution.py:221
  196.4 5.3 fusion.43
  202.4 14.0 %eval_jaxpr.18 = (f32[32,512]{1,0:T(8,128)}, f32[8,128]{1,0:T(8,128)}) custom-call(bf16[32,8192]{1,0:T(8,128)(2,1)} %get-tuple-element.843.x_ref, f32[8,128]{1,0:T(8,128)} %scatter.7.s_ref), custom_call_target="tpu_custom_call" | custom-call | tf_op jit(solution)/shard_map/while/body/eval_jaxpr/pallas_call | solution.py:66
  219.7 13.0 %eval_jaxpr.19 = bf16[32,8192]{1,0:T(8,128)(2,1)S(1)} custom-call(bf16[32,512]{1,0:T(8,128)(2,1)} %get-tuple-element.847.g_ref), custom_call_target="tpu_custom_call" | custom-call | tf_op jit(solution)/shard_map/while/body/eval_jaxpr/pallas_call | solution.py:135
  233.1 7.3 %fusion.42 = f32[32,640]{1,0:T(8,128)S(1)} fusion(bf16[32,8192]{1,0:T(8,128)(2,1)S(1)} %bitcast_select_fusion.3, bf16[640,8192]{1,0:T(8,128)(2,1)} %get-tuple-element.924), kind=kOutput, calls=%fused_computation.61.clone.1 | convolution fusion | flops 335544320 | bytes 11091968 | tf_op jit(solution)/shard_map/while/body/eval_jaxpr/dot_general | solution.py:221
  240.7 5.3 fusion.43
  246.7 15.5 %eval_jaxpr.18 = (f32[32,512]{1,0:T(8,128)}, f32[8,128]{1,0:T(8,128)}) custom-call(bf16[32,8192]{1,0:T(8,128)(2,1)} %get-tuple-element.843.x_ref, f32[8,128]{1,0:T(8,128)} %scatter.7.s_ref), custom_call_target="tpu_custom_call" | custom-call | tf_op jit(solution)/shard_map/while/body/eval_jaxpr/pallas_call | solution.py:66
  265.5 12.4 %eval_jaxpr.19 = bf16[32,8192]{1,0:T(8,128)(2,1)S(1)} custom-call(bf16[32,512]{1,0:T(8,128)(2,1)} %get-tuple-element.847.g_ref), custom_call_target="tpu_custom_call" | custom-call | tf_op jit(solution)/shard_map/while/body/eval_jaxpr/pallas_call | solution.py:135
  278.2 7.3 %fusion.42 = f32[32,640]{1,0:T(8,128)S(1)} fusion(bf16[32,8192]{1,0:T(8,128)(2,1)S(1)} %bitcast_select_fusion.3, bf16[640,8192]{1,0:T(8,128)(2,1)} %get-tuple-element.924), kind=kOutput, calls=%fused_computation.61.clone.1 | convolution fusion | flops 335544320 | bytes 11091968 | tf_op jit(solution)/shard_map/while/body/eval_jaxpr/dot_general | solution.py:221
  285.8 5.3 fusion.43
  291.7 13.3 %eval_jaxpr.18 = (f32[32,512]{1,0:T(8,128)}, f32[8,128]{1,0:T(8,128)}) custom-call(bf16[32,8192]{1,0:T(8,128)(2,1)} %get-tuple-element.843.x_ref, f32[8,128]{1,0:T(8,128)} %scatter.7.s_ref), custom_call_target="tpu_custom_call" | custom-call | tf_op jit(solution)/shard_map/while/body/eval_jaxpr/pallas_call | solution.py:66
  308.4 12.4 %eval_jaxpr.19 = bf16[32,8192]{1,0:T(8,128)(2,1)S(1)} custom-call(bf16[32,512]{1,0:T(8,128)(2,1)} %get-tuple-element.847.g_ref), custom_call_target="tpu_custom_call" | custom-call | tf_op jit(solution)/shard_map/while/body/eval_jaxpr/pallas_call | solution.py:135
  321.2 7.3 %fusion.42 = f32[32,640]{1,0:T(8,128)S(1)} fusion(bf16[32,8192]{1,0:T(8,128)(2,1)S(1)} %bitcast_select_fusion.3, bf16[640,8192]{1,0:T(8,128)(2,1)} %get-tuple-element.924), kind=kOutput, calls=%fused_computation.61.clone.1 | convolution fusion | flops 335544320 | bytes 11091968 | tf_op jit(solution)/shard_map/while/body/eval_jaxpr/dot_general | solution.py:221
  328.8 5.3 fusion.43
  334.7 13.3 %eval_jaxpr.18 = (f32[32,512]{1,0:T(8,128)}, f32[8,128]{1,0:T(8,128)}) custom-call(bf16[32,8192]{1,0:T(8,128)(2,1)} %get-tuple-element.843.x_ref, f32[8,128]{1,0:T(8,128)} %scatter.7.s_ref), custom_call_target="tpu_custom_call" | custom-call | tf_op jit(solution)/shard_map/while/body/eval_jaxpr/pallas_call | solution.py:66
  351.3 12.6 %eval_jaxpr.19 = bf16[32,8192]{1,0:T(8,128)(2,1)S(1)} custom-call(bf16[32,512]{1,0:T(8,128)(2,1)} %get-tuple-element.847.g_ref), custom_call_target="tpu_custom_call" | custom-call | tf_op jit(solution)/shard_map/while/body/eval_jaxpr/pallas_call | solution.py:135
  364.3 7.3 %fusion.42 = f32[32,640]{1,0:T(8,128)S(1)} fusion(bf16[32,8192]{1,0:T(8,128)(2,1)S(1)} %bitcast_select_fusion.3, bf16[640,8192]{1,0:T(8,128)(2,1)} %get-tuple-element.924), kind=kOutput, calls=%fused_computation.61.clone.1 | convolution fusion | flops 335544320 | bytes 11091968 | tf_op jit(solution)/shard_map/while/body/eval_jaxpr/dot_general | solution.py:221
  371.9 5.3 fusion.43
  377.8 13.5 %eval_jaxpr.18 = (f32[32,512]{1,0:T(8,128)}, f32[8,128]{1,0:T(8,128)}) custom-call(bf16[32,8192]{1,0:T(8,128)(2,1)} %get-tuple-element.843.x_ref, f32[8,128]{1,0:T(8,128)} %scatter.7.s_ref), custom_call_target="tpu_custom_call" | custom-call | tf_op jit(solution)/shard_map/while/body/eval_jaxpr/pallas_call | solution.py:66
  394.6 13.1 %eval_jaxpr.19 = bf16[32,8192]{1,0:T(8,128)(2,1)S(1)} custom-call(bf16[32,512]{1,0:T(8,128)(2,1)} %get-tuple-element.847.g_ref), custom_call_target="tpu_custom_call" | custom-call | tf_op jit(solution)/shard_map/while/body/eval_jaxpr/pallas_call | solution.py:135
  408.1 7.3 %fusion.42 = f32[32,640]{1,0:T(8,128)S(1)} fusion(bf16[32,8192]{1,0:T(8,128)(2,1)S(1)} %bitcast_select_fusion.3, bf16[640,8192]{1,0:T(8,128)(2,1)} %get-tuple-element.924), kind=kOutput, calls=%fused_computation.61.clone.1 | convolution fusion | flops 335544320 | bytes 11091968 | tf_op jit(solution)/shard_map/while/body/eval_jaxpr/dot_general | solution.py:221
  415.7 5.3 fusion.43
  421.6 13.1 %eval_jaxpr.18 = (f32[32,512]{1,0:T(8,128)}, f32[8,128]{1,0:T(8,128)}) custom-call(bf16[32,8192]{1,0:T(8,128)(2,1)} %get-tuple-element.843.x_ref, f32[8,128]{1,0:T(8,128)} %scatter.7.s_ref), custom_call_target="tpu_custom_call" | custom-call | tf_op jit(solution)/shard_map/while/body/eval_jaxpr/pallas_call | solution.py:66
  438.1 13.0 %eval_jaxpr.19 = bf16[32,8192]{1,0:T(8,128)(2,1)S(1)} custom-call(bf16[32,512]{1,0:T(8,128)(2,1)} %get-tuple-element.847.g_ref), custom_call_target="tpu_custom_call" | custom-call | tf_op jit(solution)/shard_map/while/body/eval_jaxpr/pallas_call | solution.py:135
  451.5 7.3 %fusion.42 = f32[32,640]{1,0:T(8,128)S(1)} fusion(bf16[32,8192]{1,0:T(8,128)(2,1)S(1)} %bitcast_select_fusion.3, bf16[640,8192]{1,0:T(8,128)(2,1)} %get-tuple-element.924), kind=kOutput, calls=%fused_computation.61.clone.1 | convolution fusion | flops 335544320 | bytes 11091968 | tf_op jit(solution)/shard_map/while/body/eval_jaxpr/dot_general | solution.py:221
  459.0 5.3 fusion.43
  465.0 13.0 %eval_jaxpr.18 = (f32[32,512]{1,0:T(8,128)}, f32[8,128]{1,0:T(8,128)}) custom-call(bf16[32,8192]{1,0:T(8,128)(2,1)} %get-tuple-element.843.x_ref, f32[8,128]{1,0:T(8,128)} %scatter.7.s_ref), custom_call_target="tpu_custom_call" | custom-call | tf_op jit(solution)/shard_map/while/body/eval_jaxpr/pallas_call | solution.py:66
  481.4 13.3 %eval_jaxpr.19 = bf16[32,8192]{1,0:T(8,128)(2,1)S(1)} custom-call(bf16[32,512]{1,0:T(8,128)(2,1)} %get-tuple-element.847.g_ref), custom_call_target="tpu_custom_call" | custom-call | tf_op jit(solution)/shard_map/while/body/eval_jaxpr/pallas_call | solution.py:135
  494.7 12.9 %all_to_all.11 = f32[16,1,512]{2,1,0:T(1,128)S(1)} all-to-all(f32[16,1,512]{2,1,0:T(1,128)S(1)} %broadcast_in_dim.97), channel_id=1, replica_groups=mesh['section'=8,'tensor'=16] {'tensor'}, dimensions={0} | all-to-all | bytes 65536 | tf_op jit(solution)/shard_map/all_to_all | solution.py:17
  512.9 25.5 %all-to-all-done = bf16[16,2,2,32,512]{4,3,2,1,0:T(8,128)(2,1)S(1)} async-done(((bf16[16,2,2,32,512]{4,3,2,1,0:T(8,128)(2,1)}), bf16[16,2,2,32,512]{4,3,2,1,0:T(8,128)(2,1)S(1)}, u32[]{:S(2)}, u32[]{:S(2)}) %all-to-all-start) | async-done | bytes 2097184 | tf_op jit(solution)/shard_map/all_to_all | solution.py:17
  540.9 4.2 broadcast_in_dim_reshape.6
  (227 shorter events, 65.5 us)
Async XLA Ops:
  0.7 6.9 %copy-start.5 = (s32[2,64]{1,0:T(2,128)S(1)}, s32[2,64]{1,0:T(2,128)}, u32[]{:S(2)}) copy-start(s32[2,64]{1,0:T(2,128)} %param.14) | copy-start | bytes 1540
  0.7 6.9 %copy-start.6 = (s32[2]{0:T(128)S(1)}, s32[2]{0:T(128)}, u32[]{:S(2)}) copy-start(s32[2]{0:T(128)} %param.15) | copy-start | bytes 28
  0.7 7.0 %copy-start.4 = (bf16[1,2,64,640]{3,2,1,0:T(8,128)(2,1)S(1)}, bf16[1,2,64,640]{3,2,1,0:T(8,128)(2,1)}, u32[]{:S(2)}) copy-start(bf16[1,2,64,640]{3,2,1,0:T(8,128)(2,1)} %param.17) | copy-start | bytes 491524
  3.6 6.0 %copy-start.1 = (f32[1,8192]{1,0:T(1,128)S(1)}, f32[1,8192]{1,0:T(1,128)}, u32[]{:S(2)}) copy-start(f32[1,8192]{1,0:T(1,128)} %param.18) | copy-start | bytes 98308
  3.6 6.0 %copy-start.2 = (f32[1,4,640]{2,1,0:T(4,128)S(1)}, f32[1,4,640]{2,1,0:T(4,128)}, u32[]{:S(2)}) copy-start(f32[1,4,640]{2,1,0:T(4,128)} %param.19) | copy-start | bytes 30724
  9.9 7.6 %copy-start = (bf16[8192,640]{1,0:T(8,128)(2,1)S(1)}, bf16[8192,640]{1,0:T(8,128)(2,1)}, u32[]{:S(2)}) copy-start(bf16[8192,640]{1,0:T(8,128)(2,1)} %get-tuple-element.926) | copy-start | bytes 31457284 | tf_op jit(solution)/shard_map/while
  56.7 7.6 %copy-start = (bf16[8192,640]{1,0:T(8,128)(2,1)S(1)}, bf16[8192,640]{1,0:T(8,128)(2,1)}, u32[]{:S(2)}) copy-start(bf16[8192,640]{1,0:T(8,128)(2,1)} %get-tuple-element.926) | copy-start | bytes 31457284 | tf_op jit(solution)/shard_map/while
  101.9 7.6 %copy-start = (bf16[8192,640]{1,0:T(8,128)(2,1)S(1)}, bf16[8192,640]{1,0:T(8,128)(2,1)}, u32[]{:S(2)}) copy-start(bf16[8192,640]{1,0:T(8,128)(2,1)} %get-tuple-element.926) | copy-start | bytes 31457284 | tf_op jit(solution)/shard_map/while
  146.0 7.6 %copy-start = (bf16[8192,640]{1,0:T(8,128)(2,1)S(1)}, bf16[8192,640]{1,0:T(8,128)(2,1)}, u32[]{:S(2)}) copy-start(bf16[8192,640]{1,0:T(8,128)(2,1)} %get-tuple-element.926) | copy-start | bytes 31457284 | tf_op jit(solution)/shard_map/while
  188.9 7.6 %copy-start = (bf16[8192,640]{1,0:T(8,128)(2,1)S(1)}, bf16[8192,640]{1,0:T(8,128)(2,1)}, u32[]{:S(2)}) copy-start(bf16[8192,640]{1,0:T(8,128)(2,1)} %get-tuple-element.926) | copy-start | bytes 31457284 | tf_op jit(solution)/shard_map/while
  233.1 7.6 %copy-start = (bf16[8192,640]{1,0:T(8,128)(2,1)S(1)}, bf16[8192,640]{1,0:T(8,128)(2,1)}, u32[]{:S(2)}) copy-start(bf16[8192,640]{1,0:T(8,128)(2,1)} %get-tuple-element.926) | copy-start | bytes 31457284 | tf_op jit(solution)/shard_map/while
  278.2 7.6 %copy-start = (bf16[8192,640]{1,0:T(8,128)(2,1)S(1)}, bf16[8192,640]{1,0:T(8,128)(2,1)}, u32[]{:S(2)}) copy-start(bf16[8192,640]{1,0:T(8,128)(2,1)} %get-tuple-element.926) | copy-start | bytes 31457284 | tf_op jit(solution)/shard_map/while
  321.2 7.6 %copy-start = (bf16[8192,640]{1,0:T(8,128)(2,1)S(1)}, bf16[8192,640]{1,0:T(8,128)(2,1)}, u32[]{:S(2)}) copy-start(bf16[8192,640]{1,0:T(8,128)(2,1)} %get-tuple-element.926) | copy-start | bytes 31457284 | tf_op jit(solution)/shard_map/while
  364.3 7.6 %copy-start = (bf16[8192,640]{1,0:T(8,128)(2,1)S(1)}, bf16[8192,640]{1,0:T(8,128)(2,1)}, u32[]{:S(2)}) copy-start(bf16[8192,640]{1,0:T(8,128)(2,1)} %get-tuple-element.926) | copy-start | bytes 31457284 | tf_op jit(solution)/shard_map/while
  408.1 7.6 %copy-start = (bf16[8192,640]{1,0:T(8,128)(2,1)S(1)}, bf16[8192,640]{1,0:T(8,128)(2,1)}, u32[]{:S(2)}) copy-start(bf16[8192,640]{1,0:T(8,128)(2,1)} %get-tuple-element.926) | copy-start | bytes 31457284 | tf_op jit(solution)/shard_map/while
  451.5 7.6 %copy-start = (bf16[8192,640]{1,0:T(8,128)(2,1)S(1)}, bf16[8192,640]{1,0:T(8,128)(2,1)}, u32[]{:S(2)}) copy-start(bf16[8192,640]{1,0:T(8,128)(2,1)} %get-tuple-element.926) | copy-start | bytes 31457284 | tf_op jit(solution)/shard_map/while
  494.6 46.2 %copy-start.3 = (f32[4,640]{1,0:T(4,128)}, f32[4,640]{1,0:T(4,128)S(1)}, u32[]{:S(2)}) copy-start(f32[4,640]{1,0:T(4,128)S(1)} %get-tuple-element.532) | copy-start | bytes 30724
  509.1 29.2 %all-to-all-start = ((bf16[16,2,2,32,512]{4,3,2,1,0:T(8,128)(2,1)}), bf16[16,2,2,32,512]{4,3,2,1,0:T(8,128)(2,1)S(1)}, u32[]{:S(2)}, u32[]{:S(2)}) async-start(bf16[16,2,2,32,512]{4,3,2,1,0:T(8,128)(2,1)} %broadcast_in_dim.96), calls=%async_computation | async-start | bytes 4194304 | tf_op jit(solution)/shard_map/all_to_all | solution.py:17

commit v5 on v4

--- a/solution.py
+++ b/solution.py
@@ -146,6 +146,44 @@
     )(g_block)
 
 
+def matmul_nt_kernel(x_ref, w_ref, out_ref):
+    product = lax.dot_general(
+        x_ref[...], w_ref[...], (((1,), (1,)), ((), ())), preferred_element_type=jnp.float32
+    )
+
+    @pl.when(pl.program_id(1) == 0)
+    def _():
+        out_ref[...] = product.astype(out_ref.dtype)
+
+    @pl.when(pl.program_id(1) > 0)
+    def _():
+        out_ref[...] += product.astype(out_ref.dtype)
+
+
+def matmul_nt(x, w, block_n, block_k, out_dtype):
+    rows, depth = x.shape
+    cols = w.shape[0]
+    grid = (cols // block_n, depth // block_k)
+    return pl.pallas_call(
+        matmul_nt_kernel,
+        out_shape=jax.ShapeDtypeStruct((rows, cols), out_dtype),
+        grid=grid,
+        in_specs=[
+            pl.BlockSpec((rows, block_k), lambda n, k: (0, k)),
+            pl.BlockSpec((block_n, block_k), lambda n, k: (n, k)),
+        ],
+        out_specs=pl.BlockSpec((rows, block_n), lambda n, k: (0, n)),
+        compiler_params=pltpu.CompilerParams(
+            dimension_semantics=("arbitrary", "arbitrary"), vmem_limit_bytes=48 * 1024 * 1024
+        ),
+        cost_estimate=pl.CostEstimate(
+            flops=2 * rows * cols * depth,
+            bytes_accessed=2 * (rows * depth + cols * depth) + rows * cols * jnp.dtype(out_dtype).itemsize,
+            transcendentals=0,
+        ),
+    )(x, w)
+
+
 def conv_block(weights, ext_vals, tail_rows, d_act):
     kernel_width = weights.shape[0]
     length = d_act.shape[0]
@@ -218,8 +256,7 @@
         batch_slot, half_now, join_now, active = pick_block(step_idx)
         row_start = half_now * chunk_len
         full_chunk = jnp.where(is_last, rows_of(top_grads, batch_slot, row_start, chunk_len), incoming)
-        d_act = lax.dot_general(full_chunk, w_out, contract, preferred_element_type=jnp.float32)
-        d_act = lax.optimization_barrier(d_act)
+        d_act = matmul_nt(full_chunk, w_out, w_out.shape[0], 2048, jnp.float32)
         ext_vals = lax.dynamic_slice(
             conv_padded, (batch_slot, row_start, 0), (1, chunk_len + kernel_width - 1, local_channels)
         )[0].astype(jnp.float32)

time: 555 us -> 551 us (level)
  matrix products: 139 us -> 58.7 us
  Pallas kernels: 296 us -> 369 us
    dot_general x11 -> x0, matrix products: 80.5 us -> none  [step_rows(): lax.dot_general(full_chunk, w_out, contract, preferred_element_type=jnp.f...]
    pallas_call x0 -> x11, Pallas kernels: none -> 73.1 us  [matmul_nt(): pl.pallas_call(matmul_nt_kernel, out_shape=jax.ShapeDtypeStruct((rows, co...]
where the time goes in v5:
time: 551 us; the launch traced here: 542 us
  Pallas kernels  369 us (67%)
  matrix products  58.7 us (11%)
  other arithmetic  48.1 us (9%)
  waiting for transfers between devices  26.1 us (5%)
  local copies, waits for them, and re-layouts  20.6 us (4%)
  blocking collectives  13.4 us (2%)
    pallas_call x11, Pallas kernels, scatter_sum(): pl.pallas_call(functools.partial(scatter_sum_kernel, n, width), out_shape...  156 us
    pallas_call x11, Pallas kernels, handed_down(): pl.pallas_call(functools.partial(handed_down_kernel, n, n_sec, width), ou...  141 us
    pallas_call x11, Pallas kernels, matmul_nt(): pl.pallas_call(matmul_nt_kernel, out_shape=jax.ShapeDtypeStruct((rows, co...  73.1 us
    dot_general x11, matrix products, step_rows(): lax.dot_general(d_vals, w_in, contract, preferred_element_type=jnp.float32)  58.7 us
    all_to_all x1, waiting for transfers between devices, sent_to_all(): return lax.all_to_all(copies, axis, split_axis=0, concat_axis=0, tiled=True)  26.1 us
    dynamic_update_slice x11, other arithmetic, step_rows(): lax.dynamic_update_slice(results, updated, (batch_slot, half_now, 0, 0))  17.7 us
    all_to_all x1, blocking collectives, sent_to_all(): return lax.all_to_all(copies, axis, split_axis=0, concat_axis=0, tiled=True)  13.4 us
    reduce_sum x11, other arithmetic, step_rows(): gain_part = jnp.sum(d_norm * normed_own, axis=0)  11.3 us
  transfers between devices with their start and end apart: 1, of which 1 were waited for; matrix products, arithmetic and copies ran while one was open for 0% of the time, Pallas kernels for 0%

profile of v5, /device:TPU:32, one launch (start us, length us, event | category | flops | bytes accessed | tf_op | source)
XLA Modules:
  0.0 542.3 jit_solution(3405106077552874671)
XLA Ops:
  9.6 480.5 %while.26 = (s32[]{:T(128)}, bf16[32,8192]{1,0:T(8,128)(2,1)S(1)}, bf16[2,2,32,512]{3,2,1,0:T(8,128)(2,1)S(1)}, f32[512]{0:T(512)S(1)}, f32[4,640]{1,0:T(4,128)S...) while((s32[]{:T(128)}, bf16[32,8192]{1,0:T(8,128)(2,1)S(1)}, ...), condition=%wide.region_8.9_spmd.clone, body=%wide.region_1.8_spmd.clone.sunk | while | flops 673563648 | bytes 67957952 | solution.py:293
  9.9 6.6 %eval_jaxpr.27 = f32[32,640]{1,0:T(8,128)S(1)} custom-call(bf16[32,8192]{1,0:T(8,128)(2,1)S(1)} %bitcast_select_fusion.3.x_ref, bf16[640,8192]{1,0:T(8,128)(2,1)} %get-tuple-element.922.w_ref), custom_call_target="tpu_custom_call" | custom-call | flops 335544320 | bytes 11091968 | tf_op jit(solution)/shard_map/while/body/eval_jaxpr/pallas_call | solution.py:167
  17.1 5.3 fusion.34
  23.0 16.0 %eval_jaxpr.28 = (f32[32,512]{1,0:T(8,128)}, f32[8,128]{1,0:T(8,128)}) custom-call(bf16[32,8192]{1,0:T(8,128)(2,1)} %get-tuple-element.841.x_ref, f32[8,128]{1,0:T(8,128)} %scatter.7.s_ref), custom_call_target="tpu_custom_call" | custom-call | tf_op jit(solution)/shard_map/while/body/eval_jaxpr/pallas_call | solution.py:66
  42.3 13.6 %eval_jaxpr.29 = bf16[32,8192]{1,0:T(8,128)(2,1)S(1)} custom-call(bf16[32,512]{1,0:T(8,128)(2,1)} %get-tuple-element.845.g_ref), custom_call_target="tpu_custom_call" | custom-call | tf_op jit(solution)/shard_map/while/body/eval_jaxpr/pallas_call | solution.py:135
  56.3 6.6 %eval_jaxpr.27 = f32[32,640]{1,0:T(8,128)S(1)} custom-call(bf16[32,8192]{1,0:T(8,128)(2,1)S(1)} %bitcast_select_fusion.3.x_ref, bf16[640,8192]{1,0:T(8,128)(2,1)} %get-tuple-element.922.w_ref), custom_call_target="tpu_custom_call" | custom-call | flops 335544320 | bytes 11091968 | tf_op jit(solution)/shard_map/while/body/eval_jaxpr/pallas_call | solution.py:167
  63.4 5.3 fusion.34
  69.3 15.3 %eval_jaxpr.28 = (f32[32,512]{1,0:T(8,128)}, f32[8,128]{1,0:T(8,128)}) custom-call(bf16[32,8192]{1,0:T(8,128)(2,1)} %get-tuple-element.841.x_ref, f32[8,128]{1,0:T(8,128)} %scatter.7.s_ref), custom_call_target="tpu_custom_call" | custom-call | tf_op jit(solution)/shard_map/while/body/eval_jaxpr/pallas_call | solution.py:66
  88.0 12.7 %eval_jaxpr.29 = bf16[32,8192]{1,0:T(8,128)(2,1)S(1)} custom-call(bf16[32,512]{1,0:T(8,128)(2,1)} %get-tuple-element.845.g_ref), custom_call_target="tpu_custom_call" | custom-call | tf_op jit(solution)/shard_map/while/body/eval_jaxpr/pallas_call | solution.py:135
  101.0 6.6 %eval_jaxpr.27 = f32[32,640]{1,0:T(8,128)S(1)} custom-call(bf16[32,8192]{1,0:T(8,128)(2,1)S(1)} %bitcast_select_fusion.3.x_ref, bf16[640,8192]{1,0:T(8,128)(2,1)} %get-tuple-element.922.w_ref), custom_call_target="tpu_custom_call" | custom-call | flops 335544320 | bytes 11091968 | tf_op jit(solution)/shard_map/while/body/eval_jaxpr/pallas_call | solution.py:167
  108.1 5.3 fusion.34
  114.1 14.5 %eval_jaxpr.28 = (f32[32,512]{1,0:T(8,128)}, f32[8,128]{1,0:T(8,128)}) custom-call(bf16[32,8192]{1,0:T(8,128)(2,1)} %get-tuple-element.841.x_ref, f32[8,128]{1,0:T(8,128)} %scatter.7.s_ref), custom_call_target="tpu_custom_call" | custom-call | tf_op jit(solution)/shard_map/while/body/eval_jaxpr/pallas_call | solution.py:66
  131.9 12.4 %eval_jaxpr.29 = bf16[32,8192]{1,0:T(8,128)(2,1)S(1)} custom-call(bf16[32,512]{1,0:T(8,128)(2,1)} %get-tuple-element.845.g_ref), custom_call_target="tpu_custom_call" | custom-call | tf_op jit(solution)/shard_map/while/body/eval_jaxpr/pallas_call | solution.py:135
  144.6 6.6 %eval_jaxpr.27 = f32[32,640]{1,0:T(8,128)S(1)} custom-call(bf16[32,8192]{1,0:T(8,128)(2,1)S(1)} %bitcast_select_fusion.3.x_ref, bf16[640,8192]{1,0:T(8,128)(2,1)} %get-tuple-element.922.w_ref), custom_call_target="tpu_custom_call" | custom-call | flops 335544320 | bytes 11091968 | tf_op jit(solution)/shard_map/while/body/eval_jaxpr/pallas_call | solution.py:167
  151.8 5.3 fusion.34
  157.7 13.9 %eval_jaxpr.28 = (f32[32,512]{1,0:T(8,128)}, f32[8,128]{1,0:T(8,128)}) custom-call(bf16[32,8192]{1,0:T(8,128)(2,1)} %get-tuple-element.841.x_ref, f32[8,128]{1,0:T(8,128)} %scatter.7.s_ref), custom_call_target="tpu_custom_call" | custom-call | tf_op jit(solution)/shard_map/while/body/eval_jaxpr/pallas_call | solution.py:66
  175.0 11.8 %eval_jaxpr.29 = bf16[32,8192]{1,0:T(8,128)(2,1)S(1)} custom-call(bf16[32,512]{1,0:T(8,128)(2,1)} %get-tuple-element.845.g_ref), custom_call_target="tpu_custom_call" | custom-call | tf_op jit(solution)/shard_map/while/body/eval_jaxpr/pallas_call | solution.py:135
  187.1 6.6 %eval_jaxpr.27 = f32[32,640]{1,0:T(8,128)S(1)} custom-call(bf16[32,8192]{1,0:T(8,128)(2,1)S(1)} %bitcast_select_fusion.3.x_ref, bf16[640,8192]{1,0:T(8,128)(2,1)} %get-tuple-element.922.w_ref), custom_call_target="tpu_custom_call" | custom-call | flops 335544320 | bytes 11091968 | tf_op jit(solution)/shard_map/while/body/eval_jaxpr/pallas_call | solution.py:167
  194.2 5.3 fusion.34
  200.2 14.0 %eval_jaxpr.28 = (f32[32,512]{1,0:T(8,128)}, f32[8,128]{1,0:T(8,128)}) custom-call(bf16[32,8192]{1,0:T(8,128)(2,1)} %get-tuple-element.841.x_ref, f32[8,128]{1,0:T(8,128)} %scatter.7.s_ref), custom_call_target="tpu_custom_call" | custom-call | tf_op jit(solution)/shard_map/while/body/eval_jaxpr/pallas_call | solution.py:66
  217.5 13.3 %eval_jaxpr.29 = bf16[32,8192]{1,0:T(8,128)(2,1)S(1)} custom-call(bf16[32,512]{1,0:T(8,128)(2,1)} %get-tuple-element.845.g_ref), custom_call_target="tpu_custom_call" | custom-call | tf_op jit(solution)/shard_map/while/body/eval_jaxpr/pallas_call | solution.py:135
  231.2 6.6 %eval_jaxpr.27 = f32[32,640]{1,0:T(8,128)S(1)} custom-call(bf16[32,8192]{1,0:T(8,128)(2,1)S(1)} %bitcast_select_fusion.3.x_ref, bf16[640,8192]{1,0:T(8,128)(2,1)} %get-tuple-element.922.w_ref), custom_call_target="tpu_custom_call" | custom-call | flops 335544320 | bytes 11091968 | tf_op jit(solution)/shard_map/while/body/eval_jaxpr/pallas_call | solution.py:167
  238.3 5.3 fusion.34
  244.3 15.0 %eval_jaxpr.28 = (f32[32,512]{1,0:T(8,128)}, f32[8,128]{1,0:T(8,128)}) custom-call(bf16[32,8192]{1,0:T(8,128)(2,1)} %get-tuple-element.841.x_ref, f32[8,128]{1,0:T(8,128)} %scatter.7.s_ref), custom_call_target="tpu_custom_call" | custom-call | tf_op jit(solution)/shard_map/while/body/eval_jaxpr/pallas_call | solution.py:66
  262.6 12.4 %eval_jaxpr.29 = bf16[32,8192]{1,0:T(8,128)(2,1)S(1)} custom-call(bf16[32,512]{1,0:T(8,128)(2,1)} %get-tuple-element.845.g_ref), custom_call_target="tpu_custom_call" | custom-call | tf_op jit(solution)/shard_map/while/body/eval_jaxpr/pallas_call | solution.py:135
  275.4 6.6 %eval_jaxpr.27 = f32[32,640]{1,0:T(8,128)S(1)} custom-call(bf16[32,8192]{1,0:T(8,128)(2,1)S(1)} %bitcast_select_fusion.3.x_ref, bf16[640,8192]{1,0:T(8,128)(2,1)} %get-tuple-element.922.w_ref), custom_call_target="tpu_custom_call" | custom-call | flops 335544320 | bytes 11091968 | tf_op jit(solution)/shard_map/while/body/eval_jaxpr/pallas_call | solution.py:167
  282.5 5.3 fusion.34
  288.5 13.4 %eval_jaxpr.28 = (f32[32,512]{1,0:T(8,128)}, f32[8,128]{1,0:T(8,128)}) custom-call(bf16[32,8192]{1,0:T(8,128)(2,1)} %get-tuple-element.841.x_ref, f32[8,128]{1,0:T(8,128)} %scatter.7.s_ref), custom_call_target="tpu_custom_call" | custom-call | tf_op jit(solution)/shard_map/while/body/eval_jaxpr/pallas_call | solution.py:66
  305.2 12.1 %eval_jaxpr.29 = bf16[32,8192]{1,0:T(8,128)(2,1)S(1)} custom-call(bf16[32,512]{1,0:T(8,128)(2,1)} %get-tuple-element.845.g_ref), custom_call_target="tpu_custom_call" | custom-call | tf_op jit(solution)/shard_map/while/body/eval_jaxpr/pallas_call | solution.py:135
  317.7 6.6 %eval_jaxpr.27 = f32[32,640]{1,0:T(8,128)S(1)} custom-call(bf16[32,8192]{1,0:T(8,128)(2,1)S(1)} %bitcast_select_fusion.3.x_ref, bf16[640,8192]{1,0:T(8,128)(2,1)} %get-tuple-element.922.w_ref), custom_call_target="tpu_custom_call" | custom-call | flops 335544320 | bytes 11091968 | tf_op jit(solution)/shard_map/while/body/eval_jaxpr/pallas_call | solution.py:167
  324.8 5.3 fusion.34
  330.7 13.6 %eval_jaxpr.28 = (f32[32,512]{1,0:T(8,128)}, f32[8,128]{1,0:T(8,128)}) custom-call(bf16[32,8192]{1,0:T(8,128)(2,1)} %get-tuple-element.841.x_ref, f32[8,128]{1,0:T(8,128)} %scatter.7.s_ref), custom_call_target="tpu_custom_call" | custom-call | tf_op jit(solution)/shard_map/while/body/eval_jaxpr/pallas_call | solution.py:66
  347.6 12.7 %eval_jaxpr.29 = bf16[32,8192]{1,0:T(8,128)(2,1)S(1)} custom-call(bf16[32,512]{1,0:T(8,128)(2,1)} %get-tuple-element.845.g_ref), custom_call_target="tpu_custom_call" | custom-call | tf_op jit(solution)/shard_map/while/body/eval_jaxpr/pallas_call | solution.py:135
  360.7 6.6 %eval_jaxpr.27 = f32[32,640]{1,0:T(8,128)S(1)} custom-call(bf16[32,8192]{1,0:T(8,128)(2,1)S(1)} %bitcast_select_fusion.3.x_ref, bf16[640,8192]{1,0:T(8,128)(2,1)} %get-tuple-element.922.w_ref), custom_call_target="tpu_custom_call" | custom-call | flops 335544320 | bytes 11091968 | tf_op jit(solution)/shard_map/while/body/eval_jaxpr/pallas_call | solution.py:167
  367.8 5.3 fusion.34
  373.7 13.5 %eval_jaxpr.28 = (f32[32,512]{1,0:T(8,128)}, f32[8,128]{1,0:T(8,128)}) custom-call(bf16[32,8192]{1,0:T(8,128)(2,1)} %get-tuple-element.841.x_ref, f32[8,128]{1,0:T(8,128)} %scatter.7.s_ref), custom_call_target="tpu_custom_call" | custom-call | tf_op jit(solution)/shard_map/while/body/eval_jaxpr/pallas_call | solution.py:66
  390.6 13.3 %eval_jaxpr.29 = bf16[32,8192]{1,0:T(8,128)(2,1)S(1)} custom-call(bf16[32,512]{1,0:T(8,128)(2,1)} %get-tuple-element.845.g_ref), custom_call_target="tpu_custom_call" | custom-call | tf_op jit(solution)/shard_map/while/body/eval_jaxpr/pallas_call | solution.py:135
  404.2 6.6 %eval_jaxpr.27 = f32[32,640]{1,0:T(8,128)S(1)} custom-call(bf16[32,8192]{1,0:T(8,128)(2,1)S(1)} %bitcast_select_fusion.3.x_ref, bf16[640,8192]{1,0:T(8,128)(2,1)} %get-tuple-element.922.w_ref), custom_call_target="tpu_custom_call" | custom-call | flops 335544320 | bytes 11091968 | tf_op jit(solution)/shard_map/while/body/eval_jaxpr/pallas_call | solution.py:167
  411.3 5.3 fusion.34
  417.3 13.0 %eval_jaxpr.28 = (f32[32,512]{1,0:T(8,128)}, f32[8,128]{1,0:T(8,128)}) custom-call(bf16[32,8192]{1,0:T(8,128)(2,1)} %get-tuple-element.841.x_ref, f32[8,128]{1,0:T(8,128)} %scatter.7.s_ref), custom_call_target="tpu_custom_call" | custom-call | tf_op jit(solution)/shard_map/while/body/eval_jaxpr/pallas_call | solution.py:66
  433.7 13.3 %eval_jaxpr.29 = bf16[32,8192]{1,0:T(8,128)(2,1)S(1)} custom-call(bf16[32,512]{1,0:T(8,128)(2,1)} %get-tuple-element.845.g_ref), custom_call_target="tpu_custom_call" | custom-call | tf_op jit(solution)/shard_map/while/body/eval_jaxpr/pallas_call | solution.py:135
  447.4 6.6 %eval_jaxpr.27 = f32[32,640]{1,0:T(8,128)S(1)} custom-call(bf16[32,8192]{1,0:T(8,128)(2,1)S(1)} %bitcast_select_fusion.3.x_ref, bf16[640,8192]{1,0:T(8,128)(2,1)} %get-tuple-element.922.w_ref), custom_call_target="tpu_custom_call" | custom-call | flops 335544320 | bytes 11091968 | tf_op jit(solution)/shard_map/while/body/eval_jaxpr/pallas_call | solution.py:167
  454.5 5.3 fusion.34
  460.4 13.3 %eval_jaxpr.28 = (f32[32,512]{1,0:T(8,128)}, f32[8,128]{1,0:T(8,128)}) custom-call(bf16[32,8192]{1,0:T(8,128)(2,1)} %get-tuple-element.841.x_ref, f32[8,128]{1,0:T(8,128)} %scatter.7.s_ref), custom_call_target="tpu_custom_call" | custom-call | tf_op jit(solution)/shard_map/while/body/eval_jaxpr/pallas_call | solution.py:66
  477.1 13.0 %eval_jaxpr.29 = bf16[32,8192]{1,0:T(8,128)(2,1)S(1)} custom-call(bf16[32,512]{1,0:T(8,128)(2,1)} %get-tuple-element.845.g_ref), custom_call_target="tpu_custom_call" | custom-call | tf_op jit(solution)/shard_map/while/body/eval_jaxpr/pallas_call | solution.py:135
  490.2 13.4 %all_to_all.11 = f32[16,1,512]{2,1,0:T(1,128)S(1)} all-to-all(f32[16,1,512]{2,1,0:T(1,128)S(1)} %broadcast_in_dim.97), channel_id=1, replica_groups=mesh['section'=8,'tensor'=16] {'tensor'}, dimensions={0} | all-to-all | bytes 65536 | tf_op jit(solution)/shard_map/all_to_all | solution.py:17
  508.9 26.1 %all-to-all-done = bf16[16,2,2,32,512]{4,3,2,1,0:T(8,128)(2,1)S(1)} async-done(((bf16[16,2,2,32,512]{4,3,2,1,0:T(8,128)(2,1)}), bf16[16,2,2,32,512]{4,3,2,1,0:T(8,128)(2,1)S(1)}, u32[]{:S(2)}, u32[]{:S(2)}) %all-to-all-start) | async-done | bytes 2097184 | tf_op jit(solution)/shard_map/all_to_all | solution.py:17
  537.5 4.2 broadcast_in_dim_reshape.6
  (227 shorter events, 68.2 us)
Async XLA Ops:
  0.7 6.9 %copy-start.5 = (s32[2,64]{1,0:T(2,128)S(1)}, s32[2,64]{1,0:T(2,128)}, u32[]{:S(2)}) copy-start(s32[2,64]{1,0:T(2,128)} %param.14) | copy-start | bytes 1540
  0.7 6.9 %copy-start.6 = (s32[2]{0:T(128)S(1)}, s32[2]{0:T(128)}, u32[]{:S(2)}) copy-start(s32[2]{0:T(128)} %param.15) | copy-start | bytes 28
  0.7 7.0 %copy-start.4 = (bf16[1,2,64,640]{3,2,1,0:T(8,128)(2,1)S(1)}, bf16[1,2,64,640]{3,2,1,0:T(8,128)(2,1)}, u32[]{:S(2)}) copy-start(bf16[1,2,64,640]{3,2,1,0:T(8,128)(2,1)} %param.17) | copy-start | bytes 491524
  3.6 6.0 %copy-start.1 = (f32[1,8192]{1,0:T(1,128)S(1)}, f32[1,8192]{1,0:T(1,128)}, u32[]{:S(2)}) copy-start(f32[1,8192]{1,0:T(1,128)} %param.18) | copy-start | bytes 98308
  3.6 6.0 %copy-start.2 = (f32[1,4,640]{2,1,0:T(4,128)S(1)}, f32[1,4,640]{2,1,0:T(4,128)}, u32[]{:S(2)}) copy-start(f32[1,4,640]{2,1,0:T(4,128)} %param.19) | copy-start | bytes 30724
  9.9 7.1 %copy-start = (bf16[8192,640]{1,0:T(8,128)(2,1)S(1)}, bf16[8192,640]{1,0:T(8,128)(2,1)}, u32[]{:S(2)}) copy-start(bf16[8192,640]{1,0:T(8,128)(2,1)} %get-tuple-element.924) | copy-start | bytes 31457284 | tf_op jit(solution)/shard_map/while
  56.3 7.1 %copy-start = (bf16[8192,640]{1,0:T(8,128)(2,1)S(1)}, bf16[8192,640]{1,0:T(8,128)(2,1)}, u32[]{:S(2)}) copy-start(bf16[8192,640]{1,0:T(8,128)(2,1)} %get-tuple-element.924) | copy-start | bytes 31457284 | tf_op jit(solution)/shard_map/while
  101.0 7.1 %copy-start = (bf16[8192,640]{1,0:T(8,128)(2,1)S(1)}, bf16[8192,640]{1,0:T(8,128)(2,1)}, u32[]{:S(2)}) copy-start(bf16[8192,640]{1,0:T(8,128)(2,1)} %get-tuple-element.924) | copy-start | bytes 31457284 | tf_op jit(solution)/shard_map/while
  144.6 7.1 %copy-start = (bf16[8192,640]{1,0:T(8,128)(2,1)S(1)}, bf16[8192,640]{1,0:T(8,128)(2,1)}, u32[]{:S(2)}) copy-start(bf16[8192,640]{1,0:T(8,128)(2,1)} %get-tuple-element.924) | copy-start | bytes 31457284 | tf_op jit(solution)/shard_map/while
  187.1 7.1 %copy-start = (bf16[8192,640]{1,0:T(8,128)(2,1)S(1)}, bf16[8192,640]{1,0:T(8,128)(2,1)}, u32[]{:S(2)}) copy-start(bf16[8192,640]{1,0:T(8,128)(2,1)} %get-tuple-element.924) | copy-start | bytes 31457284 | tf_op jit(solution)/shard_map/while
  231.2 7.1 %copy-start = (bf16[8192,640]{1,0:T(8,128)(2,1)S(1)}, bf16[8192,640]{1,0:T(8,128)(2,1)}, u32[]{:S(2)}) copy-start(bf16[8192,640]{1,0:T(8,128)(2,1)} %get-tuple-element.924) | copy-start | bytes 31457284 | tf_op jit(solution)/shard_map/while
  275.4 7.1 %copy-start = (bf16[8192,640]{1,0:T(8,128)(2,1)S(1)}, bf16[8192,640]{1,0:T(8,128)(2,1)}, u32[]{:S(2)}) copy-start(bf16[8192,640]{1,0:T(8,128)(2,1)} %get-tuple-element.924) | copy-start | bytes 31457284 | tf_op jit(solution)/shard_map/while
  317.7 7.1 %copy-start = (bf16[8192,640]{1,0:T(8,128)(2,1)S(1)}, bf16[8192,640]{1,0:T(8,128)(2,1)}, u32[]{:S(2)}) copy-start(bf16[8192,640]{1,0:T(8,128)(2,1)} %get-tuple-element.924) | copy-start | bytes 31457284 | tf_op jit(solution)/shard_map/while
  360.6 7.1 %copy-start = (bf16[8192,640]{1,0:T(8,128)(2,1)S(1)}, bf16[8192,640]{1,0:T(8,128)(2,1)}, u32[]{:S(2)}) copy-start(bf16[8192,640]{1,0:T(8,128)(2,1)} %get-tuple-element.924) | copy-start | bytes 31457284 | tf_op jit(solution)/shard_map/while
  404.2 7.1 %copy-start = (bf16[8192,640]{1,0:T(8,128)(2,1)S(1)}, bf16[8192,640]{1,0:T(8,128)(2,1)}, u32[]{:S(2)}) copy-start(bf16[8192,640]{1,0:T(8,128)(2,1)} %get-tuple-element.924) | copy-start | bytes 31457284 | tf_op jit(solution)/shard_map/while
  447.3 7.1 %copy-start = (bf16[8192,640]{1,0:T(8,128)(2,1)S(1)}, bf16[8192,640]{1,0:T(8,128)(2,1)}, u32[]{:S(2)}) copy-start(bf16[8192,640]{1,0:T(8,128)(2,1)} %get-tuple-element.924) | copy-start | bytes 31457284 | tf_op jit(solution)/shard_map/while
  490.1 47.4 %copy-start.3 = (f32[4,640]{1,0:T(4,128)}, f32[4,640]{1,0:T(4,128)S(1)}, u32[]{:S(2)}) copy-start(f32[4,640]{1,0:T(4,128)S(1)} %get-tuple-element.530) | copy-start | bytes 30724
  505.2 29.8 %all-to-all-start = ((bf16[16,2,2,32,512]{4,3,2,1,0:T(8,128)(2,1)}), bf16[16,2,2,32,512]{4,3,2,1,0:T(8,128)(2,1)S(1)}, u32[]{:S(2)}, u32[]{:S(2)}) async-start(bf16[16,2,2,32,512]{4,3,2,1,0:T(8,128)(2,1)} %broadcast_in_dim.96), calls=%async_computation | async-start | bytes 4194304 | tf_op jit(solution)/shard_map/all_to_all | solution.py:17

commit v6 on v4

--- a/solution.py
+++ b/solution.py
@@ -17,13 +17,68 @@
     return lax.all_to_all(copies, axis, split_axis=0, concat_axis=0, tiled=True)
 
 
-def scatter_sum_kernel(n, width, x_ref, s_ref, out_ref, sum_ref, recv, srecv, send_sem, recv_sem, ssend_sem, srecv_sem):
+def matmul_nt_kernel(x_ref, w_ref, out_ref):
+    product = lax.dot_general(
+        x_ref[...], w_ref[...], (((1,), (1,)), ((), ())), preferred_element_type=jnp.float32
+    )
+
+    @pl.when(pl.program_id(1) == 0)
+    def _():
+        out_ref[...] = product.astype(out_ref.dtype)
+
+    @pl.when(pl.program_id(1) > 0)
+    def _():
+        out_ref[...] += product.astype(out_ref.dtype)
+
+
+def matmul_nt(x, w, block_n, block_k, out_dtype):
+    rows, depth = x.shape
+    cols = w.shape[0]
+    grid = (cols // block_n, depth // block_k)
+    return pl.pallas_call(
+        matmul_nt_kernel,
+        out_shape=jax.ShapeDtypeStruct((rows, cols), out_dtype),
+        grid=grid,
+        in_specs=[
+            pl.BlockSpec((rows, block_k), lambda n, k: (0, k)),
+            pl.BlockSpec((block_n, block_k), lambda n, k: (n, k)),
+        ],
+        out_specs=pl.BlockSpec((rows, block_n), lambda n, k: (0, n)),
+        compiler_params=pltpu.CompilerParams(
+            dimension_semantics=("arbitrary", "arbitrary"), vmem_limit_bytes=48 * 1024 * 1024
+        ),
+        cost_estimate=pl.CostEstimate(
+            flops=2 * rows * cols * depth,
+            bytes_accessed=2 * (rows * depth + cols * depth) + rows * cols * jnp.dtype(out_dtype).itemsize,
+            transcendentals=0,
+        ),
+    )(x, w)
+
+
+def layer_exchange_kernel(
+    n, n_sec, width, x_ref, s_ref, normed_ref, inv_ref, gain_ref, up_ref,
+    g_ref, next_ref, gain_out_ref,
+    recv, srecv, gbuf, down, send_sem, recv_sem, ssend_sem, srecv_sem, dsend_sem, drecv_sem,
+):
     me = lax.axis_index("tensor")
     sec = lax.axis_index("section")
     barrier = pltpu.get_barrier_semaphore()
     for k in range(1, n):
         pl.semaphore_signal(barrier, inc=1, device_id=(sec, lax.rem(me + k, n)), device_id_type=MESH)
-    pl.semaphore_wait(barrier, n - 1)
+
+    @pl.when(sec < n_sec - 1)
+    def _():
+        for t in range(n):
+            pl.semaphore_signal(barrier, inc=1, device_id=(sec + 1, t), device_id_type=MESH)
+
+    @pl.when(sec > 0)
+    def _():
+        pl.semaphore_wait(barrier, 2 * n - 1)
+
+    @pl.when(sec == 0)
+    def _():
+        pl.semaphore_wait(barrier, n - 1)
+
     copies = []
     for k in range(1, n):
         peer = lax.rem(me + k, n)
@@ -57,93 +112,76 @@
         src = lax.rem(me + n - k, n)
         total = total + recv[src].astype(jnp.float32)
         stat_total = stat_total + srecv[src]
-    out_ref[...] = total
-    sum_ref[...] = stat_total
-
-
-def scatter_sum(x, stats, n, width):
-    rows = x.shape[0]
-    return pl.pallas_call(
-        functools.partial(scatter_sum_kernel, n, width),
-        out_shape=(
-            jax.ShapeDtypeStruct((rows, width), jnp.float32),
-            jax.ShapeDtypeStruct(stats.shape, jnp.float32),
-        ),
-        in_specs=[pl.BlockSpec(memory_space=pltpu.VMEM)] * 2,
-        out_specs=(pl.BlockSpec(memory_space=pltpu.VMEM), pl.BlockSpec(memory_space=pltpu.VMEM)),
-        scratch_shapes=[
-            pltpu.VMEM((n, rows, width), x.dtype),
-            pltpu.VMEM((n, *stats.shape), jnp.float32),
-            pltpu.SemaphoreType.DMA((n,)),
-            pltpu.SemaphoreType.DMA((n,)),
-            pltpu.SemaphoreType.DMA((n,)),
-            pltpu.SemaphoreType.DMA((n,)),
-        ],
-        compiler_params=pltpu.CompilerParams(collective_id=0, has_side_effects=True),
-    )(x, stats)
-
-
-def handed_down_kernel(n, n_sec, width, g_ref, out_ref, recv, send_sem, recv_sem):
-    me = lax.axis_index("tensor")
-    sec = lax.axis_index("section")
-    barrier = pltpu.get_barrier_semaphore()
-    mine = pl.ds(pl.multiple_of(me * width, 128), width)
-
-    @pl.when(sec < n_sec - 1)
-    def _():
-        for t in range(n):
-            pl.semaphore_signal(barrier, inc=1, device_id=(sec + 1, t), device_id_type=MESH)
+    rows = total.shape[0]
+    row_mean = stat_total[:, 0:1] * (1.0 / (n * width))
+    normed = normed_ref[...]
+    d_in = inv_ref[...] * (total * gain_ref[...] - normed * row_mean)
+    result = (up_ref[...].astype(jnp.float32) + d_in).astype(g_ref.dtype)
+    gbuf[...] = result
+    g_ref[...] = result
+    gain_out_ref[...] = jnp.sum(total * normed, axis=0, keepdims=True)
 
     @pl.when(sec > 0)
     def _():
-        pl.semaphore_wait(barrier, n)
-        copies = []
+        sends = []
         for t in range(n):
             copy = pltpu.make_async_remote_copy(
-                src_ref=g_ref,
-                dst_ref=recv.at[:, mine],
-                send_sem=send_sem.at[t],
-                recv_sem=recv_sem.at[me],
+                src_ref=gbuf,
+                dst_ref=down.at[:, mine],
+                send_sem=dsend_sem.at[t],
+                recv_sem=drecv_sem.at[me],
                 device_id=(sec - 1, t),
                 device_id_type=MESH,
             )
             copy.start()
-            copies.append(copy)
-        for copy in copies:
+            sends.append(copy)
+        for copy in sends:
             copy.wait_send()
 
     @pl.when(sec < n_sec - 1)
     def _():
         for src in range(n):
             pltpu.make_async_remote_copy(
-                src_ref=g_ref,
-                dst_ref=recv.at[:, pl.ds(src * width, width)],
-                send_sem=send_sem.at[src],
-                recv_sem=recv_sem.at[src],
+                src_ref=gbuf,
+                dst_ref=down.at[:, pl.ds(src * width, width)],
+                send_sem=dsend_sem.at[src],
+                recv_sem=drecv_sem.at[src],
                 device_id=(sec + 1, src),
                 device_id_type=MESH,
             ).wait_recv()
-        out_ref[...] = recv[...]
+        next_ref[...] = down[...]
 
     @pl.when(sec == n_sec - 1)
     def _():
-        out_ref[...] = jnp.zeros_like(out_ref)
-
-
-def handed_down(g_block, n, n_sec, width):
-    rows = g_block.shape[0]
+        next_ref[...] = jnp.zeros_like(next_ref)
+
+
+def layer_exchange(partial, stats, normed, inv_rms, gain_own, upstream, n, n_sec, width):
+    rows = partial.shape[0]
+    vmem = pl.BlockSpec(memory_space=pltpu.VMEM)
     return pl.pallas_call(
-        functools.partial(handed_down_kernel, n, n_sec, width),
-        out_shape=jax.ShapeDtypeStruct((rows, n * width), g_block.dtype),
-        in_specs=[pl.BlockSpec(memory_space=pltpu.VMEM)],
-        out_specs=pl.BlockSpec(memory_space=pltpu.VMEM),
+        functools.partial(layer_exchange_kernel, n, n_sec, width),
+        out_shape=(
+            jax.ShapeDtypeStruct((rows, width), jnp.bfloat16),
+            jax.ShapeDtypeStruct((rows, n * width), jnp.bfloat16),
+            jax.ShapeDtypeStruct((1, width), jnp.float32),
+        ),
+        in_specs=[vmem] * 6,
+        out_specs=(vmem, vmem, vmem),
         scratch_shapes=[
-            pltpu.VMEM((rows, n * width), g_block.dtype),
+            pltpu.VMEM((n, rows, width), partial.dtype),
+            pltpu.VMEM((n, *stats.shape), jnp.float32),
+            pltpu.VMEM((rows, width), jnp.bfloat16),
+            pltpu.VMEM((rows, n * width), jnp.bfloat16),
+            pltpu.SemaphoreType.DMA((n,)),
+            pltpu.SemaphoreType.DMA((n,)),
+            pltpu.SemaphoreType.DMA((n,)),
+            pltpu.SemaphoreType.DMA((n,)),
             pltpu.SemaphoreType.DMA((n,)),
             pltpu.SemaphoreType.DMA((n,)),
         ],
-        compiler_params=pltpu.CompilerParams(collective_id=1, has_side_effects=True),
-    )(g_block)
+        compiler_params=pltpu.CompilerParams(collective_id=2, has_side_effects=True),
+    )(partial, stats, normed, inv_rms, gain_own, upstream)
 
 
 def conv_block(weights, ext_vals, tail_rows, d_act):
@@ -218,8 +256,7 @@
         batch_slot, half_now, join_now, active = pick_block(step_idx)
         row_start = half_now * chunk_len
         full_chunk = jnp.where(is_last, rows_of(top_grads, batch_slot, row_start, chunk_len), incoming)
-        d_act = lax.dot_general(full_chunk, w_out, contract, preferred_element_type=jnp.float32)
-        d_act = lax.optimization_barrier(d_act)
+        d_act = matmul_nt(full_chunk, w_out, w_out.shape[0], 2048, jnp.float32)
         ext_vals = lax.dynamic_slice(
             conv_padded, (batch_slot, row_start, 0), (1, chunk_len + kernel_width - 1, local_channels)
         )[0].astype(jnp.float32)
@@ -229,21 +266,20 @@
         normed = rows_of(normed_all, batch_slot, row_start, chunk_len)
         inv_rms = rows_of(inv_rms_all, batch_slot, row_start, chunk_len)
         row_part = jnp.sum(partial.astype(jnp.float32) * gain_vec * normed, axis=-1)
-        stats = jnp.zeros((8, 128), jnp.float32).at[0, :chunk_len].set(row_part)
-        d_norm, stats_total = scatter_sum(partial, stats, tensors, width)
-        row_mean = stats_total[0, :chunk_len][:, None] / model_width
+        stats = jnp.zeros((chunk_len, 128), jnp.float32).at[:, 0].set(row_part)
         normed_own = lax.dynamic_slice(normed, (0, tensor_idx * width), (chunk_len, width))
         upstream_own = lax.dynamic_slice(full_chunk, (0, tensor_idx * width), (chunk_len, width))
-        d_in = inv_rms * (d_norm * gain_own - normed_own * row_mean)
-        grad_out = (upstream_own.astype(jnp.float32) + d_in).astype(jnp.bfloat16)
-        gain_part = jnp.sum(d_norm * normed_own, axis=0)
+        grad_out, incoming_next, gain_part = layer_exchange(
+            partial, stats, normed_own, inv_rms, gain_own[None, :], upstream_own, tensors, sections, width
+        )
+        gain_part = gain_part[0]
         previous = lax.dynamic_slice(results, (batch_slot, half_now, 0, 0), (1, 1, chunk_len, width))
         updated = jnp.where(active, grad_out[None, None], previous)
         results = lax.dynamic_update_slice(results, updated, (batch_slot, half_now, 0, 0))
         gain_acc = gain_acc + jnp.where(active, gain_part, 0.0)
         conv_acc = conv_acc + jnp.where(active, conv_part, 0.0)
         tail_carry = jnp.where(active, new_tail, tail_carry)
-        incoming = handed_down(grad_out, tensors, sections, width)
+        incoming = incoming_next
         return (incoming, results, gain_acc, conv_acc, tail_carry)
 
     initial = (

time: 555 us -> 589 us (1.061)
  Pallas kernels: 296 us -> 358 us
  matrix products: 139 us -> 91.6 us
  local copies, waits for them, and re-layouts: 17.8 us -> 50.7 us
  other arithmetic: 48.2 us -> 35.7 us
    dot_general x11 -> x0, matrix products: 80.5 us -> none  [step_rows(): lax.dot_general(full_chunk, w_out, contract, preferred_element_type=jnp.f...]
    pallas_call x22, Pallas kernels: 296 us -> 358 us  [the longest x11 288 us: layer_exchange(): pl.pallas_call(functools.partial(layer_exchange_kernel, n, n_sec, width),...]
    dot_general x11, matrix products: 58.8 us -> 91.6 us  [step_rows(): lax.dot_general(d_vals, w_in, contract, preferred_element_type=jnp.float32)]
    dynamic_slice x0 -> x22, local copies, waits for them, and re-layouts: none -> 24.5 us  [the longest x11 17.7 us: step_rows(): lax.dynamic_slice(normed, (0, tensor_idx * width), (chunk_len, width))]
    another operation x0 -> x22, other arithmetic: none -> 14.2 us
    reduce_sum x11 -> x0, other arithmetic: 11.3 us -> none  [step_rows(): gain_part = jnp.sum(d_norm * normed_own, axis=0)]
    dynamic_update_slice x11, other arithmetic: 17.7 us -> 8.54 us  [step_rows(): lax.dynamic_update_slice(results, updated, (batch_slot, half_now, 0, 0))]
    squeeze x0 -> x22, local copies, waits for them, and re-layouts: none -> 8.32 us  [rows_of(): lax.dynamic_slice(array, (batch_slot, first_row, 0), (1, row_count, array...]
where the time goes in v6:
time: 589 us; the launch traced here: 583 us
  Pallas kernels  358 us (61%)
  matrix products  91.6 us (16%)
  local copies, waits for them, and re-layouts  50.7 us (9%)
  other arithmetic  35.7 us (6%)
  waiting for transfers between devices  27 us (5%)
  blocking collectives  14.2 us (2%)
    pallas_call x11, Pallas kernels, layer_exchange(): pl.pallas_call(functools.partial(layer_exchange_kernel, n, n_sec, width),...  288 us
    dot_general x11, matrix products, step_rows(): lax.dot_general(d_vals, w_in, contract, preferred_element_type=jnp.float32)  91.6 us
    pallas_call x11, Pallas kernels, matmul_nt(): pl.pallas_call(matmul_nt_kernel, out_shape=jax.ShapeDtypeStruct((rows, co...  69.8 us
    all_to_all x1, waiting for transfers between devices, sent_to_all(): return lax.all_to_all(copies, axis, split_axis=0, concat_axis=0, tiled=True)  27 us
    dynamic_slice x11, local copies, waits for them, and re-layouts, step_rows(): lax.dynamic_slice(normed, (0, tensor_idx * width), (chunk_len, width))  17.7 us
    another operation x22, other arithmetic  14.2 us
    all_to_all x1, blocking collectives, sent_to_all(): return lax.all_to_all(copies, axis, split_axis=0, concat_axis=0, tiled=True)  14.2 us
  transfers between devices with their start and end apart: 1, of which 1 were waited for; matrix products, arithmetic and copies ran while one was open for 0% of the time, Pallas kernels for 0%

profile of v6, /device:TPU:32, one launch (start us, length us, event | category | flops | bytes accessed | tf_op | source)
XLA Modules:
  0.0 583.4 jit_solution(15679827897140188871)
XLA Ops:
  1.4 2.3 fusion.20
  3.7 4.0 convert_multiply_fusion
  8.1 521.4 %while.26 = (s32[]{:T(128)}, bf16[32,8192]{1,0:T(8,128)(2,1)S(1)}, bf16[2,2,32,512]{3,2,1,0:T(8,128)(2,1)S(1)}, f32[512]{0:T(512)S(1)}, f32[4,640]{1,0:T(4,128)S...) while((s32[]{:T(128)}, bf16[32,8192]{1,0:T(8,128)(2,1)S(1)}, ...), condition=%wide.region_8.9_spmd.clone, body=%wide.region_1.8_spmd.clone.sunk | while | flops 673416704 | bytes 25928336 | solution.py:292
  8.3 6.3 %eval_jaxpr.18 = f32[32,640]{1,0:T(8,128)S(1)} custom-call(bf16[32,8192]{1,0:T(8,128)(2,1)S(1)} %bitcast_select_fusion.3.x_ref, bf16[640,8192]{1,0:T(8,128)(2,1)} %get-tuple-element.921.w_ref), custom_call_target="tpu_custom_call" | custom-call | flops 335544320 | bytes 11091968 | tf_op jit(solution)/shard_map/while/body/eval_jaxpr/pallas_call | solution.py:38
  15.0 8.3 %fusion.29 = (f32[32]{0:T(128)S(1)}, bf16[32,8192]{1,0:T(8,128)(2,1)}) fusion(f32[2,64,8192]{2,1,0:T(8,128)} %get-tuple-element.925, s32[]{:T(128)S(6)} %select_n.293, s32[]{:T(128)S(6)} %select_n.294, f32[8192]{0:T(1024)S(1)} %bitcast.88, bf16[8192,640]{1,0:T(8,128)(2,1)} %get-tuple-element.923, f32[32,640]{1,0:T(8,128)S(1)} %get-tuple-element.841, ...), kind=kOutput, calls=%fused_computation.2.clone.1 | convolution fusion | flops 337080288 | bytes 12191368 | tf_op jit(solution)/shard_map/while/body/eval_jaxpr/dot_general | solution.py:265
  25.9 1.6 dynamic-slice_bitcast_fusion.2.normed_ref
  28.3 28.2 %eval_jaxpr.19 = (bf16[32,512]{1,0:T(8,128)(2,1)}, bf16[32,8192]{1,0:T(8,128)(2,1)S(1)}, f32[1,512]{1,0:T(1,128)}) custom-call(bf16[32,8192]{1,0:T(8,128)(2,1)} %get-tuple-element.843.x_ref, f32[32,128]{1,0:T(8,128)} %scatter.7.s_ref, f32[32,512]{1,0:T(8,128)} %dynamic-slice_bitcast_fusion.2.normed_ref, f32[32,1]{1,0:T(8,128)} %copy.25.inv_ref, ...), custom_call_target="tpu_custom_call" | custom-call | tf_op jit(solution)/shard_map/while/body/eval_jaxpr/pallas_call | solution.py:162
  57.5 6.3 %eval_jaxpr.18 = f32[32,640]{1,0:T(8,128)S(1)} custom-call(bf16[32,8192]{1,0:T(8,128)(2,1)S(1)} %bitcast_select_fusion.3.x_ref, bf16[640,8192]{1,0:T(8,128)(2,1)} %get-tuple-element.921.w_ref), custom_call_target="tpu_custom_call" | custom-call | flops 335544320 | bytes 11091968 | tf_op jit(solution)/shard_map/while/body/eval_jaxpr/pallas_call | solution.py:38
  64.1 8.3 %fusion.29 = (f32[32]{0:T(128)S(1)}, bf16[32,8192]{1,0:T(8,128)(2,1)}) fusion(f32[2,64,8192]{2,1,0:T(8,128)} %get-tuple-element.925, s32[]{:T(128)S(6)} %select_n.293, s32[]{:T(128)S(6)} %select_n.294, f32[8192]{0:T(1024)S(1)} %bitcast.88, bf16[8192,640]{1,0:T(8,128)(2,1)} %get-tuple-element.923, f32[32,640]{1,0:T(8,128)S(1)} %get-tuple-element.841, ...), kind=kOutput, calls=%fused_computation.2.clone.1 | convolution fusion | flops 337080288 | bytes 12191368 | tf_op jit(solution)/shard_map/while/body/eval_jaxpr/dot_general | solution.py:265
  75.1 1.6 dynamic-slice_bitcast_fusion.2.normed_ref
  77.4 29.0 %eval_jaxpr.19 = (bf16[32,512]{1,0:T(8,128)(2,1)}, bf16[32,8192]{1,0:T(8,128)(2,1)S(1)}, f32[1,512]{1,0:T(1,128)}) custom-call(bf16[32,8192]{1,0:T(8,128)(2,1)} %get-tuple-element.843.x_ref, f32[32,128]{1,0:T(8,128)} %scatter.7.s_ref, f32[32,512]{1,0:T(8,128)} %dynamic-slice_bitcast_fusion.2.normed_ref, f32[32,1]{1,0:T(8,128)} %copy.25.inv_ref, ...), custom_call_target="tpu_custom_call" | custom-call | tf_op jit(solution)/shard_map/while/body/eval_jaxpr/pallas_call | solution.py:162
  107.4 6.3 %eval_jaxpr.18 = f32[32,640]{1,0:T(8,128)S(1)} custom-call(bf16[32,8192]{1,0:T(8,128)(2,1)S(1)} %bitcast_select_fusion.3.x_ref, bf16[640,8192]{1,0:T(8,128)(2,1)} %get-tuple-element.921.w_ref), custom_call_target="tpu_custom_call" | custom-call | flops 335544320 | bytes 11091968 | tf_op jit(solution)/shard_map/while/body/eval_jaxpr/pallas_call | solution.py:38
  114.1 8.3 %fusion.29 = (f32[32]{0:T(128)S(1)}, bf16[32,8192]{1,0:T(8,128)(2,1)}) fusion(f32[2,64,8192]{2,1,0:T(8,128)} %get-tuple-element.925, s32[]{:T(128)S(6)} %select_n.293, s32[]{:T(128)S(6)} %select_n.294, f32[8192]{0:T(1024)S(1)} %bitcast.88, bf16[8192,640]{1,0:T(8,128)(2,1)} %get-tuple-element.923, f32[32,640]{1,0:T(8,128)S(1)} %get-tuple-element.841, ...), kind=kOutput, calls=%fused_computation.2.clone.1 | convolution fusion | flops 337080288 | bytes 12191368 | tf_op jit(solution)/shard_map/while/body/eval_jaxpr/dot_general | solution.py:265
  125.1 1.6 dynamic-slice_bitcast_fusion.2.normed_ref
  127.4 28.1 %eval_jaxpr.19 = (bf16[32,512]{1,0:T(8,128)(2,1)}, bf16[32,8192]{1,0:T(8,128)(2,1)S(1)}, f32[1,512]{1,0:T(1,128)}) custom-call(bf16[32,8192]{1,0:T(8,128)(2,1)} %get-tuple-element.843.x_ref, f32[32,128]{1,0:T(8,128)} %scatter.7.s_ref, f32[32,512]{1,0:T(8,128)} %dynamic-slice_bitcast_fusion.2.normed_ref, f32[32,1]{1,0:T(8,128)} %copy.25.inv_ref, ...), custom_call_target="tpu_custom_call" | custom-call | tf_op jit(solution)/shard_map/while/body/eval_jaxpr/pallas_call | solution.py:162
  156.5 6.4 %eval_jaxpr.18 = f32[32,640]{1,0:T(8,128)S(1)} custom-call(bf16[32,8192]{1,0:T(8,128)(2,1)S(1)} %bitcast_select_fusion.3.x_ref, bf16[640,8192]{1,0:T(8,128)(2,1)} %get-tuple-element.921.w_ref), custom_call_target="tpu_custom_call" | custom-call | flops 335544320 | bytes 11091968 | tf_op jit(solution)/shard_map/while/body/eval_jaxpr/pallas_call | solution.py:38
  163.2 8.3 %fusion.29 = (f32[32]{0:T(128)S(1)}, bf16[32,8192]{1,0:T(8,128)(2,1)}) fusion(f32[2,64,8192]{2,1,0:T(8,128)} %get-tuple-element.925, s32[]{:T(128)S(6)} %select_n.293, s32[]{:T(128)S(6)} %select_n.294, f32[8192]{0:T(1024)S(1)} %bitcast.88, bf16[8192,640]{1,0:T(8,128)(2,1)} %get-tuple-element.923, f32[32,640]{1,0:T(8,128)S(1)} %get-tuple-element.841, ...), kind=kOutput, calls=%fused_computation.2.clone.1 | convolution fusion | flops 337080288 | bytes 12191368 | tf_op jit(solution)/shard_map/while/body/eval_jaxpr/dot_general | solution.py:265
  176.5 23.1 %eval_jaxpr.19 = (bf16[32,512]{1,0:T(8,128)(2,1)}, bf16[32,8192]{1,0:T(8,128)(2,1)S(1)}, f32[1,512]{1,0:T(1,128)}) custom-call(bf16[32,8192]{1,0:T(8,128)(2,1)} %get-tuple-element.843.x_ref, f32[32,128]{1,0:T(8,128)} %scatter.7.s_ref, f32[32,512]{1,0:T(8,128)} %dynamic-slice_bitcast_fusion.2.normed_ref, f32[32,1]{1,0:T(8,128)} %copy.25.inv_ref, ...), custom_call_target="tpu_custom_call" | custom-call | tf_op jit(solution)/shard_map/while/body/eval_jaxpr/pallas_call | solution.py:162
  200.6 6.3 %eval_jaxpr.18 = f32[32,640]{1,0:T(8,128)S(1)} custom-call(bf16[32,8192]{1,0:T(8,128)(2,1)S(1)} %bitcast_select_fusion.3.x_ref, bf16[640,8192]{1,0:T(8,128)(2,1)} %get-tuple-element.921.w_ref), custom_call_target="tpu_custom_call" | custom-call | flops 335544320 | bytes 11091968 | tf_op jit(solution)/shard_map/while/body/eval_jaxpr/pallas_call | solution.py:38
  207.2 8.3 %fusion.29 = (f32[32]{0:T(128)S(1)}, bf16[32,8192]{1,0:T(8,128)(2,1)}) fusion(f32[2,64,8192]{2,1,0:T(8,128)} %get-tuple-element.925, s32[]{:T(128)S(6)} %select_n.293, s32[]{:T(128)S(6)} %select_n.294, f32[8192]{0:T(1024)S(1)} %bitcast.88, bf16[8192,640]{1,0:T(8,128)(2,1)} %get-tuple-element.923, f32[32,640]{1,0:T(8,128)S(1)} %get-tuple-element.841, ...), kind=kOutput, calls=%fused_computation.2.clone.1 | convolution fusion | flops 337080288 | bytes 12191368 | tf_op jit(solution)/shard_map/while/body/eval_jaxpr/dot_general | solution.py:265
  220.6 25.4 %eval_jaxpr.19 = (bf16[32,512]{1,0:T(8,128)(2,1)}, bf16[32,8192]{1,0:T(8,128)(2,1)S(1)}, f32[1,512]{1,0:T(1,128)}) custom-call(bf16[32,8192]{1,0:T(8,128)(2,1)} %get-tuple-element.843.x_ref, f32[32,128]{1,0:T(8,128)} %scatter.7.s_ref, f32[32,512]{1,0:T(8,128)} %dynamic-slice_bitcast_fusion.2.normed_ref, f32[32,1]{1,0:T(8,128)} %copy.25.inv_ref, ...), custom_call_target="tpu_custom_call" | custom-call | tf_op jit(solution)/shard_map/while/body/eval_jaxpr/pallas_call | solution.py:162
  247.0 6.3 %eval_jaxpr.18 = f32[32,640]{1,0:T(8,128)S(1)} custom-call(bf16[32,8192]{1,0:T(8,128)(2,1)S(1)} %bitcast_select_fusion.3.x_ref, bf16[640,8192]{1,0:T(8,128)(2,1)} %get-tuple-element.921.w_ref), custom_call_target="tpu_custom_call" | custom-call | flops 335544320 | bytes 11091968 | tf_op jit(solution)/shard_map/while/body/eval_jaxpr/pallas_call | solution.py:38
  253.7 8.3 %fusion.29 = (f32[32]{0:T(128)S(1)}, bf16[32,8192]{1,0:T(8,128)(2,1)}) fusion(f32[2,64,8192]{2,1,0:T(8,128)} %get-tuple-element.925, s32[]{:T(128)S(6)} %select_n.293, s32[]{:T(128)S(6)} %select_n.294, f32[8192]{0:T(1024)S(1)} %bitcast.88, bf16[8192,640]{1,0:T(8,128)(2,1)} %get-tuple-element.923, f32[32,640]{1,0:T(8,128)S(1)} %get-tuple-element.841, ...), kind=kOutput, calls=%fused_computation.2.clone.1 | convolution fusion | flops 337080288 | bytes 12191368 | tf_op jit(solution)/shard_map/while/body/eval_jaxpr/dot_general | solution.py:265
  267.0 27.5 %eval_jaxpr.19 = (bf16[32,512]{1,0:T(8,128)(2,1)}, bf16[32,8192]{1,0:T(8,128)(2,1)S(1)}, f32[1,512]{1,0:T(1,128)}) custom-call(bf16[32,8192]{1,0:T(8,128)(2,1)} %get-tuple-element.843.x_ref, f32[32,128]{1,0:T(8,128)} %scatter.7.s_ref, f32[32,512]{1,0:T(8,128)} %dynamic-slice_bitcast_fusion.2.normed_ref, f32[32,1]{1,0:T(8,128)} %copy.25.inv_ref, ...), custom_call_target="tpu_custom_call" | custom-call | tf_op jit(solution)/shard_map/while/body/eval_jaxpr/pallas_call | solution.py:162
  296.0 6.3 %eval_jaxpr.18 = f32[32,640]{1,0:T(8,128)S(1)} custom-call(bf16[32,8192]{1,0:T(8,128)(2,1)S(1)} %bitcast_select_fusion.3.x_ref, bf16[640,8192]{1,0:T(8,128)(2,1)} %get-tuple-element.921.w_ref), custom_call_target="tpu_custom_call" | custom-call | flops 335544320 | bytes 11091968 | tf_op jit(solution)/shard_map/while/body/eval_jaxpr/pallas_call | solution.py:38
  302.7 8.3 %fusion.29 = (f32[32]{0:T(128)S(1)}, bf16[32,8192]{1,0:T(8,128)(2,1)}) fusion(f32[2,64,8192]{2,1,0:T(8,128)} %get-tuple-element.925, s32[]{:T(128)S(6)} %select_n.293, s32[]{:T(128)S(6)} %select_n.294, f32[8192]{0:T(1024)S(1)} %bitcast.88, bf16[8192,640]{1,0:T(8,128)(2,1)} %get-tuple-element.923, f32[32,640]{1,0:T(8,128)S(1)} %get-tuple-element.841, ...), kind=kOutput, calls=%fused_computation.2.clone.1 | convolution fusion | flops 337080288 | bytes 12191368 | tf_op jit(solution)/shard_map/while/body/eval_jaxpr/dot_general | solution.py:265
  313.6 1.6 dynamic-slice_bitcast_fusion.2.normed_ref
  316.0 25.4 %eval_jaxpr.19 = (bf16[32,512]{1,0:T(8,128)(2,1)}, bf16[32,8192]{1,0:T(8,128)(2,1)S(1)}, f32[1,512]{1,0:T(1,128)}) custom-call(bf16[32,8192]{1,0:T(8,128)(2,1)} %get-tuple-element.843.x_ref, f32[32,128]{1,0:T(8,128)} %scatter.7.s_ref, f32[32,512]{1,0:T(8,128)} %dynamic-slice_bitcast_fusion.2.normed_ref, f32[32,1]{1,0:T(8,128)} %copy.25.inv_ref, ...), custom_call_target="tpu_custom_call" | custom-call | tf_op jit(solution)/shard_map/while/body/eval_jaxpr/pallas_call | solution.py:162
  343.0 6.3 %eval_jaxpr.18 = f32[32,640]{1,0:T(8,128)S(1)} custom-call(bf16[32,8192]{1,0:T(8,128)(2,1)S(1)} %bitcast_select_fusion.3.x_ref, bf16[640,8192]{1,0:T(8,128)(2,1)} %get-tuple-element.921.w_ref), custom_call_target="tpu_custom_call" | custom-call | flops 335544320 | bytes 11091968 | tf_op jit(solution)/shard_map/while/body/eval_jaxpr/pallas_call | solution.py:38
  349.7 8.3 %fusion.29 = (f32[32]{0:T(128)S(1)}, bf16[32,8192]{1,0:T(8,128)(2,1)}) fusion(f32[2,64,8192]{2,1,0:T(8,128)} %get-tuple-element.925, s32[]{:T(128)S(6)} %select_n.293, s32[]{:T(128)S(6)} %select_n.294, f32[8192]{0:T(1024)S(1)} %bitcast.88, bf16[8192,640]{1,0:T(8,128)(2,1)} %get-tuple-element.923, f32[32,640]{1,0:T(8,128)S(1)} %get-tuple-element.841, ...), kind=kOutput, calls=%fused_computation.2.clone.1 | convolution fusion | flops 337080288 | bytes 12191368 | tf_op jit(solution)/shard_map/while/body/eval_jaxpr/dot_general | solution.py:265
  363.0 25.2 %eval_jaxpr.19 = (bf16[32,512]{1,0:T(8,128)(2,1)}, bf16[32,8192]{1,0:T(8,128)(2,1)S(1)}, f32[1,512]{1,0:T(1,128)}) custom-call(bf16[32,8192]{1,0:T(8,128)(2,1)} %get-tuple-element.843.x_ref, f32[32,128]{1,0:T(8,128)} %scatter.7.s_ref, f32[32,512]{1,0:T(8,128)} %dynamic-slice_bitcast_fusion.2.normed_ref, f32[32,1]{1,0:T(8,128)} %copy.25.inv_ref, ...), custom_call_target="tpu_custom_call" | custom-call | tf_op jit(solution)/shard_map/while/body/eval_jaxpr/pallas_call | solution.py:162
  389.8 6.3 %eval_jaxpr.18 = f32[32,640]{1,0:T(8,128)S(1)} custom-call(bf16[32,8192]{1,0:T(8,128)(2,1)S(1)} %bitcast_select_fusion.3.x_ref, bf16[640,8192]{1,0:T(8,128)(2,1)} %get-tuple-element.921.w_ref), custom_call_target="tpu_custom_call" | custom-call | flops 335544320 | bytes 11091968 | tf_op jit(solution)/shard_map/while/body/eval_jaxpr/pallas_call | solution.py:38
  396.5 8.3 %fusion.29 = (f32[32]{0:T(128)S(1)}, bf16[32,8192]{1,0:T(8,128)(2,1)}) fusion(f32[2,64,8192]{2,1,0:T(8,128)} %get-tuple-element.925, s32[]{:T(128)S(6)} %select_n.293, s32[]{:T(128)S(6)} %select_n.294, f32[8192]{0:T(1024)S(1)} %bitcast.88, bf16[8192,640]{1,0:T(8,128)(2,1)} %get-tuple-element.923, f32[32,640]{1,0:T(8,128)S(1)} %get-tuple-element.841, ...), kind=kOutput, calls=%fused_computation.2.clone.1 | convolution fusion | flops 337080288 | bytes 12191368 | tf_op jit(solution)/shard_map/while/body/eval_jaxpr/dot_general | solution.py:265
  407.4 1.6 dynamic-slice_bitcast_fusion.2.normed_ref
  409.8 25.1 %eval_jaxpr.19 = (bf16[32,512]{1,0:T(8,128)(2,1)}, bf16[32,8192]{1,0:T(8,128)(2,1)S(1)}, f32[1,512]{1,0:T(1,128)}) custom-call(bf16[32,8192]{1,0:T(8,128)(2,1)} %get-tuple-element.843.x_ref, f32[32,128]{1,0:T(8,128)} %scatter.7.s_ref, f32[32,512]{1,0:T(8,128)} %dynamic-slice_bitcast_fusion.2.normed_ref, f32[32,1]{1,0:T(8,128)} %copy.25.inv_ref, ...), custom_call_target="tpu_custom_call" | custom-call | tf_op jit(solution)/shard_map/while/body/eval_jaxpr/pallas_call | solution.py:162
  436.6 6.3 %eval_jaxpr.18 = f32[32,640]{1,0:T(8,128)S(1)} custom-call(bf16[32,8192]{1,0:T(8,128)(2,1)S(1)} %bitcast_select_fusion.3.x_ref, bf16[640,8192]{1,0:T(8,128)(2,1)} %get-tuple-element.921.w_ref), custom_call_target="tpu_custom_call" | custom-call | flops 335544320 | bytes 11091968 | tf_op jit(solution)/shard_map/while/body/eval_jaxpr/pallas_call | solution.py:38
  443.2 8.3 %fusion.29 = (f32[32]{0:T(128)S(1)}, bf16[32,8192]{1,0:T(8,128)(2,1)}) fusion(f32[2,64,8192]{2,1,0:T(8,128)} %get-tuple-element.925, s32[]{:T(128)S(6)} %select_n.293, s32[]{:T(128)S(6)} %select_n.294, f32[8192]{0:T(1024)S(1)} %bitcast.88, bf16[8192,640]{1,0:T(8,128)(2,1)} %get-tuple-element.923, f32[32,640]{1,0:T(8,128)S(1)} %get-tuple-element.841, ...), kind=kOutput, calls=%fused_computation.2.clone.1 | convolution fusion | flops 337080288 | bytes 12191368 | tf_op jit(solution)/shard_map/while/body/eval_jaxpr/dot_general | solution.py:265
  454.2 1.6 dynamic-slice_bitcast_fusion.2.normed_ref
  456.6 25.4 %eval_jaxpr.19 = (bf16[32,512]{1,0:T(8,128)(2,1)}, bf16[32,8192]{1,0:T(8,128)(2,1)S(1)}, f32[1,512]{1,0:T(1,128)}) custom-call(bf16[32,8192]{1,0:T(8,128)(2,1)} %get-tuple-element.843.x_ref, f32[32,128]{1,0:T(8,128)} %scatter.7.s_ref, f32[32,512]{1,0:T(8,128)} %dynamic-slice_bitcast_fusion.2.normed_ref, f32[32,1]{1,0:T(8,128)} %copy.25.inv_ref, ...), custom_call_target="tpu_custom_call" | custom-call | tf_op jit(solution)/shard_map/while/body/eval_jaxpr/pallas_call | solution.py:162
  483.0 6.3 %eval_jaxpr.18 = f32[32,640]{1,0:T(8,128)S(1)} custom-call(bf16[32,8192]{1,0:T(8,128)(2,1)S(1)} %bitcast_select_fusion.3.x_ref, bf16[640,8192]{1,0:T(8,128)(2,1)} %get-tuple-element.921.w_ref), custom_call_target="tpu_custom_call" | custom-call | flops 335544320 | bytes 11091968 | tf_op jit(solution)/shard_map/while/body/eval_jaxpr/pallas_call | solution.py:38
  489.6 8.3 %fusion.29 = (f32[32]{0:T(128)S(1)}, bf16[32,8192]{1,0:T(8,128)(2,1)}) fusion(f32[2,64,8192]{2,1,0:T(8,128)} %get-tuple-element.925, s32[]{:T(128)S(6)} %select_n.293, s32[]{:T(128)S(6)} %select_n.294, f32[8192]{0:T(1024)S(1)} %bitcast.88, bf16[8192,640]{1,0:T(8,128)(2,1)} %get-tuple-element.923, f32[32,640]{1,0:T(8,128)S(1)} %get-tuple-element.841, ...), kind=kOutput, calls=%fused_computation.2.clone.1 | convolution fusion | flops 337080288 | bytes 12191368 | tf_op jit(solution)/shard_map/while/body/eval_jaxpr/dot_general | solution.py:265
  500.6 1.6 dynamic-slice_bitcast_fusion.2.normed_ref
  502.9 25.7 %eval_jaxpr.19 = (bf16[32,512]{1,0:T(8,128)(2,1)}, bf16[32,8192]{1,0:T(8,128)(2,1)S(1)}, f32[1,512]{1,0:T(1,128)}) custom-call(bf16[32,8192]{1,0:T(8,128)(2,1)} %get-tuple-element.843.x_ref, f32[32,128]{1,0:T(8,128)} %scatter.7.s_ref, f32[32,512]{1,0:T(8,128)} %dynamic-slice_bitcast_fusion.2.normed_ref, f32[32,1]{1,0:T(8,128)} %copy.25.inv_ref, ...), custom_call_target="tpu_custom_call" | custom-call | tf_op jit(solution)/shard_map/while/body/eval_jaxpr/pallas_call | solution.py:162
  529.5 14.2 %all_to_all.11 = f32[16,1,512]{2,1,0:T(1,128)S(1)} all-to-all(f32[16,1,512]{2,1,0:T(1,128)S(1)} %broadcast_in_dim.97), channel_id=1, replica_groups=mesh['section'=8,'tensor'=16] {'tensor'}, dimensions={0} | all-to-all | bytes 65536 | tf_op jit(solution)/shard_map/all_to_all | solution.py:17
  545.3 3.7 all-to-all-start
  549.0 27.0 %all-to-all-done = bf16[16,2,2,32,512]{4,3,2,1,0:T(8,128)(2,1)S(1)} async-done(((bf16[16,2,2,32,512]{4,3,2,1,0:T(8,128)(2,1)}), bf16[16,2,2,32,512]{4,3,2,1,0:T(8,128)(2,1)S(1)}, u32[]{:S(2)}, u32[]{:S(2)}) %all-to-all-start) | async-done | bytes 2097184 | tf_op jit(solution)/shard_map/all_to_all | solution.py:17
  576.0 2.5 copy.21
  578.6 4.2 broadcast_in_dim_reshape.6
  (251 shorter events, 62.1 us)
Async XLA Ops:
  1.4 6.3 %copy-start.5 = (s32[2,64]{1,0:T(2,128)S(1)}, s32[2,64]{1,0:T(2,128)}, u32[]{:S(2)}) copy-start(s32[2,64]{1,0:T(2,128)} %param.14) | copy-start | bytes 1540
  1.4 6.3 %copy-start.6 = (s32[2]{0:T(128)S(1)}, s32[2]{0:T(128)}, u32[]{:S(2)}) copy-start(s32[2]{0:T(128)} %param.15) | copy-start | bytes 28
  1.4 6.4 %copy-start = (bf16[2,64,8192]{2,1,0:T(8,128)(2,1)S(1)}, bf16[2,64,8192]{2,1,0:T(8,128)(2,1)}, u32[]{:S(2)}) copy-start(bf16[2,64,8192]{2,1,0:T(8,128)(2,1)} %param.13) | copy-start | bytes 6291460
  3.6 4.4 copy-start.4
  3.6 4.5 copy-start.1
  3.6 4.5 copy-start.2
  529.5 49.1 %copy-start.3 = (f32[4,640]{1,0:T(4,128)}, f32[4,640]{1,0:T(4,128)S(1)}, u32[]{:S(2)}) copy-start(f32[4,640]{1,0:T(4,128)S(1)} %get-tuple-element.534) | copy-start | bytes 30724
  545.3 30.7 %all-to-all-start = ((bf16[16,2,2,32,512]{4,3,2,1,0:T(8,128)(2,1)}), bf16[16,2,2,32,512]{4,3,2,1,0:T(8,128)(2,1)S(1)}, u32[]{:S(2)}, u32[]{:S(2)}) async-start(bf16[16,2,2,32,512]{4,3,2,1,0:T(8,128)(2,1)} %broadcast_in_dim.96), calls=%async_computation | async-start | bytes 4194304 | tf_op jit(solution)/shard_map/all_to_all | solution.py:17

commit v7 on v6

--- a/solution.py
+++ b/solution.py
@@ -45,7 +45,7 @@
         ],
         out_specs=pl.BlockSpec((rows, block_n), lambda n, k: (0, n)),
         compiler_params=pltpu.CompilerParams(
-            dimension_semantics=("arbitrary", "arbitrary"), vmem_limit_bytes=48 * 1024 * 1024
+            dimension_semantics=("arbitrary", "arbitrary"), vmem_limit_bytes=16 * 1024 * 1024
         ),
         cost_estimate=pl.CostEstimate(
             flops=2 * rows * cols * depth,
@@ -116,7 +116,7 @@
     row_mean = stat_total[:, 0:1] * (1.0 / (n * width))
     normed = normed_ref[...]
     d_in = inv_ref[...] * (total * gain_ref[...] - normed * row_mean)
-    result = (up_ref[...].astype(jnp.float32) + d_in).astype(g_ref.dtype)
+    result = (up_ref[:, mine].astype(jnp.float32) + d_in).astype(g_ref.dtype)
     gbuf[...] = result
     g_ref[...] = result
     gain_out_ref[...] = jnp.sum(total * normed, axis=0, keepdims=True)
@@ -180,7 +180,9 @@
             pltpu.SemaphoreType.DMA((n,)),
             pltpu.SemaphoreType.DMA((n,)),
         ],
-        compiler_params=pltpu.CompilerParams(collective_id=2, has_side_effects=True),
+        compiler_params=pltpu.CompilerParams(
+            collective_id=2, has_side_effects=True, vmem_limit_bytes=16 * 1024 * 1024
+        ),
     )(partial, stats, normed, inv_rms, gain_own, upstream)
 
 
@@ -233,6 +235,7 @@
     inv_rms_all = lax.rsqrt(jnp.mean(values * values, axis=-1, keepdims=True) + EPSILON)
     normed_all = values * inv_rms_all
     gain_own = lax.dynamic_slice(gain_vec, (tensor_idx * width,), (width,))
+    normed_own_all = lax.dynamic_slice(normed_all, (0, 0, tensor_idx * width), (batches, seq_len, width))
 
     halves = CHUNKS_PER_BATCH
     chunk_len = seq_len // halves
@@ -267,10 +270,9 @@
         inv_rms = rows_of(inv_rms_all, batch_slot, row_start, chunk_len)
         row_part = jnp.sum(partial.astype(jnp.float32) * gain_vec * normed, axis=-1)
         stats = jnp.zeros((chunk_len, 128), jnp.float32).at[:, 0].set(row_part)
-        normed_own = lax.dynamic_slice(normed, (0, tensor_idx * width), (chunk_len, width))
-        upstream_own = lax.dynamic_slice(full_chunk, (0, tensor_idx * width), (chunk_len, width))
+        normed_own = rows_of(normed_own_all, batch_slot, row_start, chunk_len)
         grad_out, incoming_next, gain_part = layer_exchange(
-            partial, stats, normed_own, inv_rms, gain_own[None, :], upstream_own, tensors, sections, width
+            partial, stats, normed_own, inv_rms, gain_own[None, :], full_chunk, tensors, sections, width
         )
         gain_part = gain_part[0]
         previous = lax.dynamic_slice(results, (batch_slot, half_now, 0, 0), (1, 1, chunk_len, width))

time: 589 us -> 497 us (0.84)
  matrix products: 91.6 us -> 50 us
  local copies, waits for them, and re-layouts: 50.7 us -> 16.4 us
  Pallas kernels: 358 us -> 343 us
    dot_general x11, matrix products: 91.6 us -> 50 us  [step_rows(): lax.dot_general(d_vals, w_in, contract, preferred_element_type=jnp.float32)]
    dynamic_slice x22 -> x1, local copies, waits for them, and re-layouts: 24.5 us -> 0.98 us  [local(): lax.dynamic_slice(normed_all, (0, 0, tensor_idx * width), (batches, seq_l...]
    pallas_call x11, Pallas kernels: 288 us -> 270 us  [layer_exchange(): pl.pallas_call(functools.partial(layer_exchange_kernel, n, n_sec, width),...]
    select_n x11, other arithmetic: 1.39 us -> 12.9 us  [step_rows(): jnp.where(is_last, rows_of(top_grads, batch_slot, row_start, chunk_len),...]
    dynamic_update_slice x11, other arithmetic: 8.54 us -> 0.21 us  [step_rows(): lax.dynamic_update_slice(results, updated, (batch_slot, half_now, 0, 0))]
    scatter x11, local copies, waits for them, and re-layouts: 6.66 us -> 0.08 us  [step_rows(): stats = jnp.zeros((chunk_len, 128), jnp.float32).at[:, 0].set(row_part)]
    squeeze x22 -> x33, local copies, waits for them, and re-layouts: 8.32 us -> 1.96 us  [rows_of(): lax.dynamic_slice(array, (batch_slot, first_row, 0), (1, row_count, array...]
where the time goes in v7:
time: 497 us; the launch traced here: 495 us
  Pallas kernels  343 us (69%)
  matrix products  50 us (10%)
  other arithmetic  37.4 us (8%)
  waiting for transfers between devices  27.9 us (6%)
  local copies, waits for them, and re-layouts  16.4 us (3%)
  blocking collectives  14.7 us (3%)
    pallas_call x11, Pallas kernels, layer_exchange(): pl.pallas_call(functools.partial(layer_exchange_kernel, n, n_sec, width),...  270 us
    pallas_call x11, Pallas kernels, matmul_nt(): pl.pallas_call(matmul_nt_kernel, out_shape=jax.ShapeDtypeStruct((rows, co...  73.1 us
    dot_general x11, matrix products, step_rows(): lax.dot_general(d_vals, w_in, contract, preferred_element_type=jnp.float32)  50 us
    all_to_all x1, waiting for transfers between devices, sent_to_all(): return lax.all_to_all(copies, axis, split_axis=0, concat_axis=0, tiled=True)  27.9 us
    all_to_all x1, blocking collectives, sent_to_all(): return lax.all_to_all(copies, axis, split_axis=0, concat_axis=0, tiled=True)  14.7 us
    another operation x22, other arithmetic  14.2 us
    select_n x11, other arithmetic, step_rows(): jnp.where(is_last, rows_of(top_grads, batch_slot, row_start, chunk_len),...  12.9 us
  transfers between devices with their start and end apart: 1, of which 1 were waited for; matrix products, arithmetic and copies ran while one was open for 0% of the time, Pallas kernels for 0%

profile of v7, /device:TPU:32, one launch (start us, length us, event | category | flops | bytes accessed | tf_op | source)
XLA Modules:
  0.0 495.2 jit_solution(4880186756519188163)
XLA Ops:
  0.7 2.3 fusion.20
  3.0 4.0 convert_multiply_fusion
  8.2 1.5 broadcast_select_fusion.2
  9.7 430.1 %while.25 = (s32[]{:T(128)}, bf16[32,8192]{1,0:T(8,128)(2,1)S(1)}, bf16[2,2,32,512]{3,2,1,0:T(8,128)(2,1)S(1)}, f32[512]{0:T(512)S(1)}, f32[4,640]{1,0:T(4,128)S...) while((s32[]{:T(128)}, bf16[32,8192]{1,0:T(8,128)(2,1)S(1)}, ...), condition=%wide.region_8.9_spmd.clone, body=%wide.region_1.8_spmd.clone.sunk | while | flops 673416704 | bytes 67805824 | solution.py:294
  10.7 1.2 bitcast_select_fusion.3.x_ref.up_ref
  11.9 6.6 %eval_jaxpr.16 = f32[32,640]{1,0:T(8,128)S(1)} custom-call(bf16[32,8192]{1,0:T(8,128)(2,1)S(1)} %bitcast_select_fusion.3.x_ref.up_ref, bf16[640,8192]{1,0:T(8,128)(2,1)} %get-tuple-element.827.w_ref), custom_call_target="tpu_custom_call" | custom-call | flops 335544320 | bytes 11091968 | tf_op jit(solution)/shard_map/while/body/eval_jaxpr/pallas_call | solution.py:38
  19.0 4.5 fusion.29
  24.3 26.2 %eval_jaxpr.17 = (bf16[32,512]{1,0:T(8,128)(2,1)S(1)}, bf16[32,8192]{1,0:T(8,128)(2,1)S(1)}, f32[1,512]{1,0:T(1,128)S(1)}) custom-call(bf16[32,8192]{1,0:T(8,128)(2,1)S(1)} %get-tuple-element.751.x_ref, f32[32,128]{1,0:T(8,128)S(1)} %scatter.7.s_ref, f32[32,512]{1,0:T(8,128)S(1)} %dynamic-slice_bitcast_fusion.2.normed_ref, f32[32,1]{1,0:T(8,128)S(1)} %copy.25.inv_ref, ...), custom_call_target="tpu_custom_call" | custom-call | tf_op jit(solution)/shard_map/while/body/eval_jaxpr/pallas_call | solution.py:162
  51.5 1.2 bitcast_select_fusion.3.x_ref.up_ref
  52.6 6.6 %eval_jaxpr.16 = f32[32,640]{1,0:T(8,128)S(1)} custom-call(bf16[32,8192]{1,0:T(8,128)(2,1)S(1)} %bitcast_select_fusion.3.x_ref.up_ref, bf16[640,8192]{1,0:T(8,128)(2,1)} %get-tuple-element.827.w_ref), custom_call_target="tpu_custom_call" | custom-call | flops 335544320 | bytes 11091968 | tf_op jit(solution)/shard_map/while/body/eval_jaxpr/pallas_call | solution.py:38
  59.8 4.5 fusion.29
  65.0 27.9 %eval_jaxpr.17 = (bf16[32,512]{1,0:T(8,128)(2,1)S(1)}, bf16[32,8192]{1,0:T(8,128)(2,1)S(1)}, f32[1,512]{1,0:T(1,128)S(1)}) custom-call(bf16[32,8192]{1,0:T(8,128)(2,1)S(1)} %get-tuple-element.751.x_ref, f32[32,128]{1,0:T(8,128)S(1)} %scatter.7.s_ref, f32[32,512]{1,0:T(8,128)S(1)} %dynamic-slice_bitcast_fusion.2.normed_ref, f32[32,1]{1,0:T(8,128)S(1)} %copy.25.inv_ref, ...), custom_call_target="tpu_custom_call" | custom-call | tf_op jit(solution)/shard_map/while/body/eval_jaxpr/pallas_call | solution.py:162
  93.9 1.2 bitcast_select_fusion.3.x_ref.up_ref
  95.1 6.6 %eval_jaxpr.16 = f32[32,640]{1,0:T(8,128)S(1)} custom-call(bf16[32,8192]{1,0:T(8,128)(2,1)S(1)} %bitcast_select_fusion.3.x_ref.up_ref, bf16[640,8192]{1,0:T(8,128)(2,1)} %get-tuple-element.827.w_ref), custom_call_target="tpu_custom_call" | custom-call | flops 335544320 | bytes 11091968 | tf_op jit(solution)/shard_map/while/body/eval_jaxpr/pallas_call | solution.py:38
  102.2 4.5 fusion.29
  107.5 26.4 %eval_jaxpr.17 = (bf16[32,512]{1,0:T(8,128)(2,1)S(1)}, bf16[32,8192]{1,0:T(8,128)(2,1)S(1)}, f32[1,512]{1,0:T(1,128)S(1)}) custom-call(bf16[32,8192]{1,0:T(8,128)(2,1)S(1)} %get-tuple-element.751.x_ref, f32[32,128]{1,0:T(8,128)S(1)} %scatter.7.s_ref, f32[32,512]{1,0:T(8,128)S(1)} %dynamic-slice_bitcast_fusion.2.normed_ref, f32[32,1]{1,0:T(8,128)S(1)} %copy.25.inv_ref, ...), custom_call_target="tpu_custom_call" | custom-call | tf_op jit(solution)/shard_map/while/body/eval_jaxpr/pallas_call | solution.py:162
  134.9 1.2 bitcast_select_fusion.3.x_ref.up_ref
  136.1 6.6 %eval_jaxpr.16 = f32[32,640]{1,0:T(8,128)S(1)} custom-call(bf16[32,8192]{1,0:T(8,128)(2,1)S(1)} %bitcast_select_fusion.3.x_ref.up_ref, bf16[640,8192]{1,0:T(8,128)(2,1)} %get-tuple-element.827.w_ref), custom_call_target="tpu_custom_call" | custom-call | flops 335544320 | bytes 11091968 | tf_op jit(solution)/shard_map/while/body/eval_jaxpr/pallas_call | solution.py:38
  143.2 4.5 fusion.29
  148.5 22.0 %eval_jaxpr.17 = (bf16[32,512]{1,0:T(8,128)(2,1)S(1)}, bf16[32,8192]{1,0:T(8,128)(2,1)S(1)}, f32[1,512]{1,0:T(1,128)S(1)}) custom-call(bf16[32,8192]{1,0:T(8,128)(2,1)S(1)} %get-tuple-element.751.x_ref, f32[32,128]{1,0:T(8,128)S(1)} %scatter.7.s_ref, f32[32,512]{1,0:T(8,128)S(1)} %dynamic-slice_bitcast_fusion.2.normed_ref, f32[32,1]{1,0:T(8,128)S(1)} %copy.25.inv_ref, ...), custom_call_target="tpu_custom_call" | custom-call | tf_op jit(solution)/shard_map/while/body/eval_jaxpr/pallas_call | solution.py:162
  171.5 1.2 bitcast_select_fusion.3.x_ref.up_ref
  172.7 6.6 %eval_jaxpr.16 = f32[32,640]{1,0:T(8,128)S(1)} custom-call(bf16[32,8192]{1,0:T(8,128)(2,1)S(1)} %bitcast_select_fusion.3.x_ref.up_ref, bf16[640,8192]{1,0:T(8,128)(2,1)} %get-tuple-element.827.w_ref), custom_call_target="tpu_custom_call" | custom-call | flops 335544320 | bytes 11091968 | tf_op jit(solution)/shard_map/while/body/eval_jaxpr/pallas_call | solution.py:38
  179.8 4.5 fusion.29
  185.1 21.8 %eval_jaxpr.17 = (bf16[32,512]{1,0:T(8,128)(2,1)S(1)}, bf16[32,8192]{1,0:T(8,128)(2,1)S(1)}, f32[1,512]{1,0:T(1,128)S(1)}) custom-call(bf16[32,8192]{1,0:T(8,128)(2,1)S(1)} %get-tuple-element.751.x_ref, f32[32,128]{1,0:T(8,128)S(1)} %scatter.7.s_ref, f32[32,512]{1,0:T(8,128)S(1)} %dynamic-slice_bitcast_fusion.2.normed_ref, f32[32,1]{1,0:T(8,128)S(1)} %copy.25.inv_ref, ...), custom_call_target="tpu_custom_call" | custom-call | tf_op jit(solution)/shard_map/while/body/eval_jaxpr/pallas_call | solution.py:162
  209.1 6.6 %eval_jaxpr.16 = f32[32,640]{1,0:T(8,128)S(1)} custom-call(bf16[32,8192]{1,0:T(8,128)(2,1)S(1)} %bitcast_select_fusion.3.x_ref.up_ref, bf16[640,8192]{1,0:T(8,128)(2,1)} %get-tuple-element.827.w_ref), custom_call_target="tpu_custom_call" | custom-call | flops 335544320 | bytes 11091968 | tf_op jit(solution)/shard_map/while/body/eval_jaxpr/pallas_call | solution.py:38
  216.2 4.5 fusion.29
  221.5 25.8 %eval_jaxpr.17 = (bf16[32,512]{1,0:T(8,128)(2,1)S(1)}, bf16[32,8192]{1,0:T(8,128)(2,1)S(1)}, f32[1,512]{1,0:T(1,128)S(1)}) custom-call(bf16[32,8192]{1,0:T(8,128)(2,1)S(1)} %get-tuple-element.751.x_ref, f32[32,128]{1,0:T(8,128)S(1)} %scatter.7.s_ref, f32[32,512]{1,0:T(8,128)S(1)} %dynamic-slice_bitcast_fusion.2.normed_ref, f32[32,1]{1,0:T(8,128)S(1)} %copy.25.inv_ref, ...), custom_call_target="tpu_custom_call" | custom-call | tf_op jit(solution)/shard_map/while/body/eval_jaxpr/pallas_call | solution.py:162
  249.5 6.6 %eval_jaxpr.16 = f32[32,640]{1,0:T(8,128)S(1)} custom-call(bf16[32,8192]{1,0:T(8,128)(2,1)S(1)} %bitcast_select_fusion.3.x_ref.up_ref, bf16[640,8192]{1,0:T(8,128)(2,1)} %get-tuple-element.827.w_ref), custom_call_target="tpu_custom_call" | custom-call | flops 335544320 | bytes 11091968 | tf_op jit(solution)/shard_map/while/body/eval_jaxpr/pallas_call | solution.py:38
  256.6 4.5 fusion.29
  261.8 24.1 %eval_jaxpr.17 = (bf16[32,512]{1,0:T(8,128)(2,1)S(1)}, bf16[32,8192]{1,0:T(8,128)(2,1)S(1)}, f32[1,512]{1,0:T(1,128)S(1)}) custom-call(bf16[32,8192]{1,0:T(8,128)(2,1)S(1)} %get-tuple-element.751.x_ref, f32[32,128]{1,0:T(8,128)S(1)} %scatter.7.s_ref, f32[32,512]{1,0:T(8,128)S(1)} %dynamic-slice_bitcast_fusion.2.normed_ref, f32[32,1]{1,0:T(8,128)S(1)} %copy.25.inv_ref, ...), custom_call_target="tpu_custom_call" | custom-call | tf_op jit(solution)/shard_map/while/body/eval_jaxpr/pallas_call | solution.py:162
  288.1 6.6 %eval_jaxpr.16 = f32[32,640]{1,0:T(8,128)S(1)} custom-call(bf16[32,8192]{1,0:T(8,128)(2,1)S(1)} %bitcast_select_fusion.3.x_ref.up_ref, bf16[640,8192]{1,0:T(8,128)(2,1)} %get-tuple-element.827.w_ref), custom_call_target="tpu_custom_call" | custom-call | flops 335544320 | bytes 11091968 | tf_op jit(solution)/shard_map/while/body/eval_jaxpr/pallas_call | solution.py:38
  295.3 4.5 fusion.29
  300.5 24.1 %eval_jaxpr.17 = (bf16[32,512]{1,0:T(8,128)(2,1)S(1)}, bf16[32,8192]{1,0:T(8,128)(2,1)S(1)}, f32[1,512]{1,0:T(1,128)S(1)}) custom-call(bf16[32,8192]{1,0:T(8,128)(2,1)S(1)} %get-tuple-element.751.x_ref, f32[32,128]{1,0:T(8,128)S(1)} %scatter.7.s_ref, f32[32,512]{1,0:T(8,128)S(1)} %dynamic-slice_bitcast_fusion.2.normed_ref, f32[32,1]{1,0:T(8,128)S(1)} %copy.25.inv_ref, ...), custom_call_target="tpu_custom_call" | custom-call | tf_op jit(solution)/shard_map/while/body/eval_jaxpr/pallas_call | solution.py:162
  326.8 6.6 %eval_jaxpr.16 = f32[32,640]{1,0:T(8,128)S(1)} custom-call(bf16[32,8192]{1,0:T(8,128)(2,1)S(1)} %bitcast_select_fusion.3.x_ref.up_ref, bf16[640,8192]{1,0:T(8,128)(2,1)} %get-tuple-element.827.w_ref), custom_call_target="tpu_custom_call" | custom-call | flops 335544320 | bytes 11091968 | tf_op jit(solution)/shard_map/while/body/eval_jaxpr/pallas_call | solution.py:38
  333.9 4.5 fusion.29
  339.2 23.9 %eval_jaxpr.17 = (bf16[32,512]{1,0:T(8,128)(2,1)S(1)}, bf16[32,8192]{1,0:T(8,128)(2,1)S(1)}, f32[1,512]{1,0:T(1,128)S(1)}) custom-call(bf16[32,8192]{1,0:T(8,128)(2,1)S(1)} %get-tuple-element.751.x_ref, f32[32,128]{1,0:T(8,128)S(1)} %scatter.7.s_ref, f32[32,512]{1,0:T(8,128)S(1)} %dynamic-slice_bitcast_fusion.2.normed_ref, f32[32,1]{1,0:T(8,128)S(1)} %copy.25.inv_ref, ...), custom_call_target="tpu_custom_call" | custom-call | tf_op jit(solution)/shard_map/while/body/eval_jaxpr/pallas_call | solution.py:162
  365.3 6.6 %eval_jaxpr.16 = f32[32,640]{1,0:T(8,128)S(1)} custom-call(bf16[32,8192]{1,0:T(8,128)(2,1)S(1)} %bitcast_select_fusion.3.x_ref.up_ref, bf16[640,8192]{1,0:T(8,128)(2,1)} %get-tuple-element.827.w_ref), custom_call_target="tpu_custom_call" | custom-call | flops 335544320 | bytes 11091968 | tf_op jit(solution)/shard_map/while/body/eval_jaxpr/pallas_call | solution.py:38
  372.4 4.5 fusion.29
  377.7 22.4 %eval_jaxpr.17 = (bf16[32,512]{1,0:T(8,128)(2,1)S(1)}, bf16[32,8192]{1,0:T(8,128)(2,1)S(1)}, f32[1,512]{1,0:T(1,128)S(1)}) custom-call(bf16[32,8192]{1,0:T(8,128)(2,1)S(1)} %get-tuple-element.751.x_ref, f32[32,128]{1,0:T(8,128)S(1)} %scatter.7.s_ref, f32[32,512]{1,0:T(8,128)S(1)} %dynamic-slice_bitcast_fusion.2.normed_ref, f32[32,1]{1,0:T(8,128)S(1)} %copy.25.inv_ref, ...), custom_call_target="tpu_custom_call" | custom-call | tf_op jit(solution)/shard_map/while/body/eval_jaxpr/pallas_call | solution.py:162
  402.3 6.6 %eval_jaxpr.16 = f32[32,640]{1,0:T(8,128)S(1)} custom-call(bf16[32,8192]{1,0:T(8,128)(2,1)S(1)} %bitcast_select_fusion.3.x_ref.up_ref, bf16[640,8192]{1,0:T(8,128)(2,1)} %get-tuple-element.827.w_ref), custom_call_target="tpu_custom_call" | custom-call | flops 335544320 | bytes 11091968 | tf_op jit(solution)/shard_map/while/body/eval_jaxpr/pallas_call | solution.py:38
  409.4 4.5 fusion.29
  414.7 25.1 %eval_jaxpr.17 = (bf16[32,512]{1,0:T(8,128)(2,1)S(1)}, bf16[32,8192]{1,0:T(8,128)(2,1)S(1)}, f32[1,512]{1,0:T(1,128)S(1)}) custom-call(bf16[32,8192]{1,0:T(8,128)(2,1)S(1)} %get-tuple-element.751.x_ref, f32[32,128]{1,0:T(8,128)S(1)} %scatter.7.s_ref, f32[32,512]{1,0:T(8,128)S(1)} %dynamic-slice_bitcast_fusion.2.normed_ref, f32[32,1]{1,0:T(8,128)S(1)} %copy.25.inv_ref, ...), custom_call_target="tpu_custom_call" | custom-call | tf_op jit(solution)/shard_map/while/body/eval_jaxpr/pallas_call | solution.py:162
  439.9 14.7 %all_to_all.11 = f32[16,1,512]{2,1,0:T(1,128)S(1)} all-to-all(f32[16,1,512]{2,1,0:T(1,128)S(1)} %broadcast_in_dim.93), channel_id=1, replica_groups=mesh['section'=8,'tensor'=16] {'tensor'}, dimensions={0} | all-to-all | bytes 65536 | tf_op jit(solution)/shard_map/all_to_all | solution.py:17
  454.6 1.6 broadcast_in_dim.92
  456.2 3.7 all-to-all-start
  459.9 27.9 %all-to-all-done = bf16[16,2,2,32,512]{4,3,2,1,0:T(8,128)(2,1)S(1)} async-done(((bf16[16,2,2,32,512]{4,3,2,1,0:T(8,128)(2,1)}), bf16[16,2,2,32,512]{4,3,2,1,0:T(8,128)(2,1)S(1)}, u32[]{:S(2)}, u32[]{:S(2)}) %all-to-all-start) | async-done | bytes 2097184 | tf_op jit(solution)/shard_map/all_to_all | solution.py:17
  487.8 2.5 copy.21
  490.4 4.2 broadcast_in_dim_reshape.6
  (263 shorter events, 31.8 us)
Async XLA Ops:
  0.7 6.3 %copy-start.2 = (f32[1,8192]{1,0:T(1,128)S(1)}, f32[1,8192]{1,0:T(1,128)}, u32[]{:S(2)}) copy-start(f32[1,8192]{1,0:T(1,128)} %param.18) | copy-start | bytes 98308
  0.7 7.3 %copy-start.6 = (s32[2,64]{1,0:T(2,128)S(1)}, s32[2,64]{1,0:T(2,128)}, u32[]{:S(2)}) copy-start(s32[2,64]{1,0:T(2,128)} %param.14) | copy-start | bytes 1540
  0.7 7.3 %copy-start.7 = (s32[2]{0:T(128)S(1)}, s32[2]{0:T(128)}, u32[]{:S(2)}) copy-start(s32[2]{0:T(128)} %param.15) | copy-start | bytes 28
  0.7 7.4 %copy-start.5 = (bf16[1,2,64,640]{3,2,1,0:T(8,128)(2,1)S(1)}, bf16[1,2,64,640]{3,2,1,0:T(8,128)(2,1)}, u32[]{:S(2)}) copy-start(bf16[1,2,64,640]{3,2,1,0:T(8,128)(2,1)} %param.17) | copy-start | bytes 491524
  0.7 7.4 %copy-start.1 = (bf16[2,64,8192]{2,1,0:T(8,128)(2,1)S(1)}, bf16[2,64,8192]{2,1,0:T(8,128)(2,1)}, u32[]{:S(2)}) copy-start(bf16[2,64,8192]{2,1,0:T(8,128)(2,1)} %param.13) | copy-start | bytes 6291460
  7.0 2.7 copy-start.3
  11.9 7.1 %copy-start = (bf16[8192,640]{1,0:T(8,128)(2,1)S(1)}, bf16[8192,640]{1,0:T(8,128)(2,1)}, u32[]{:S(2)}) copy-start(bf16[8192,640]{1,0:T(8,128)(2,1)} %get-tuple-element.829) | copy-start | bytes 31457284 | tf_op jit(solution)/shard_map/while
  52.6 7.1 %copy-start = (bf16[8192,640]{1,0:T(8,128)(2,1)S(1)}, bf16[8192,640]{1,0:T(8,128)(2,1)}, u32[]{:S(2)}) copy-start(bf16[8192,640]{1,0:T(8,128)(2,1)} %get-tuple-element.829) | copy-start | bytes 31457284 | tf_op jit(solution)/shard_map/while
  95.1 7.1 %copy-start = (bf16[8192,640]{1,0:T(8,128)(2,1)S(1)}, bf16[8192,640]{1,0:T(8,128)(2,1)}, u32[]{:S(2)}) copy-start(bf16[8192,640]{1,0:T(8,128)(2,1)} %get-tuple-element.829) | copy-start | bytes 31457284 | tf_op jit(solution)/shard_map/while
  136.1 7.1 %copy-start = (bf16[8192,640]{1,0:T(8,128)(2,1)S(1)}, bf16[8192,640]{1,0:T(8,128)(2,1)}, u32[]{:S(2)}) copy-start(bf16[8192,640]{1,0:T(8,128)(2,1)} %get-tuple-element.829) | copy-start | bytes 31457284 | tf_op jit(solution)/shard_map/while
  172.7 7.1 %copy-start = (bf16[8192,640]{1,0:T(8,128)(2,1)S(1)}, bf16[8192,640]{1,0:T(8,128)(2,1)}, u32[]{:S(2)}) copy-start(bf16[8192,640]{1,0:T(8,128)(2,1)} %get-tuple-element.829) | copy-start | bytes 31457284 | tf_op jit(solution)/shard_map/while
  209.1 7.1 %copy-start = (bf16[8192,640]{1,0:T(8,128)(2,1)S(1)}, bf16[8192,640]{1,0:T(8,128)(2,1)}, u32[]{:S(2)}) copy-start(bf16[8192,640]{1,0:T(8,128)(2,1)} %get-tuple-element.829) | copy-start | bytes 31457284 | tf_op jit(solution)/shard_map/while
  249.4 7.1 %copy-start = (bf16[8192,640]{1,0:T(8,128)(2,1)S(1)}, bf16[8192,640]{1,0:T(8,128)(2,1)}, u32[]{:S(2)}) copy-start(bf16[8192,640]{1,0:T(8,128)(2,1)} %get-tuple-element.829) | copy-start | bytes 31457284 | tf_op jit(solution)/shard_map/while
  288.1 7.1 %copy-start = (bf16[8192,640]{1,0:T(8,128)(2,1)S(1)}, bf16[8192,640]{1,0:T(8,128)(2,1)}, u32[]{:S(2)}) copy-start(bf16[8192,640]{1,0:T(8,128)(2,1)} %get-tuple-element.829) | copy-start | bytes 31457284 | tf_op jit(solution)/shard_map/while
  326.8 7.1 %copy-start = (bf16[8192,640]{1,0:T(8,128)(2,1)S(1)}, bf16[8192,640]{1,0:T(8,128)(2,1)}, u32[]{:S(2)}) copy-start(bf16[8192,640]{1,0:T(8,128)(2,1)} %get-tuple-element.829) | copy-start | bytes 31457284 | tf_op jit(solution)/shard_map/while
  365.3 7.1 %copy-start = (bf16[8192,640]{1,0:T(8,128)(2,1)S(1)}, bf16[8192,640]{1,0:T(8,128)(2,1)}, u32[]{:S(2)}) copy-start(bf16[8192,640]{1,0:T(8,128)(2,1)} %get-tuple-element.829) | copy-start | bytes 31457284 | tf_op jit(solution)/shard_map/while
  402.3 7.1 %copy-start = (bf16[8192,640]{1,0:T(8,128)(2,1)S(1)}, bf16[8192,640]{1,0:T(8,128)(2,1)}, u32[]{:S(2)}) copy-start(bf16[8192,640]{1,0:T(8,128)(2,1)} %get-tuple-element.829) | copy-start | bytes 31457284 | tf_op jit(solution)/shard_map/while
  439.9 50.5 %copy-start.4 = (f32[4,640]{1,0:T(4,128)}, f32[4,640]{1,0:T(4,128)S(1)}, u32[]{:S(2)}) copy-start(f32[4,640]{1,0:T(4,128)S(1)} %get-tuple-element.456) | copy-start | bytes 30724
  456.2 31.6 %all-to-all-start = ((bf16[16,2,2,32,512]{4,3,2,1,0:T(8,128)(2,1)}), bf16[16,2,2,32,512]{4,3,2,1,0:T(8,128)(2,1)S(1)}, u32[]{:S(2)}, u32[]{:S(2)}) async-start(bf16[16,2,2,32,512]{4,3,2,1,0:T(8,128)(2,1)} %broadcast_in_dim.92), calls=%async_computation | async-start | bytes 4194304 | tf_op jit(solution)/shard_map/all_to_all | solution.py:17

commit v8 on v7

--- a/solution.py
+++ b/solution.py
@@ -292,8 +292,9 @@
         tail_init,
     )
     last_state = lax.fori_loop(0, total_steps, step_rows, initial)
-    gathered = sent_to_all(last_state[1], "tensor")
-    results = jnp.transpose(gathered, (1, 2, 3, 0, 4)).reshape(batches, seq_len, model_width)
+    own = last_state[1].reshape(batches, seq_len, width)
+    copies = jnp.broadcast_to(own, (tensors, batches, seq_len, width))
+    results = lax.all_to_all(copies, "tensor", split_axis=0, concat_axis=3, tiled=True)[0]
     conv_acc = last_state[3]
     gain_total = sent_to_all(last_state[2], "tensor").reshape(model_width)
     return (results[None], gain_total[None], conv_acc[None])

time: 497 us -> 492 us (0.990)
  local copies, waits for them, and re-layouts: 16.4 us -> 11.2 us
where the time goes in v8:
time: 492 us; the launch traced here: 490 us
  Pallas kernels  343 us (70%)
  matrix products  50 us (10%)
  other arithmetic  37.4 us (8%)
  waiting for transfers between devices  27.9 us (6%)
  blocking collectives  14.7 us (3%)
  local copies, waits for them, and re-layouts  11.2 us (2%)
    pallas_call x11, Pallas kernels, layer_exchange(): pl.pallas_call(functools.partial(layer_exchange_kernel, n, n_sec, width),...  270 us
    pallas_call x11, Pallas kernels, matmul_nt(): pl.pallas_call(matmul_nt_kernel, out_shape=jax.ShapeDtypeStruct((rows, co...  73.1 us
    dot_general x11, matrix products, step_rows(): lax.dot_general(d_vals, w_in, contract, preferred_element_type=jnp.float32)  50 us
    all_to_all x1, waiting for transfers between devices, local(): lax.all_to_all(copies, 'tensor', split_axis=0, concat_axis=3, tiled=True)[0]  27.9 us
    all_to_all x1, blocking collectives, sent_to_all(): return lax.all_to_all(copies, axis, split_axis=0, concat_axis=0, tiled=True)  14.7 us
    another operation x22, other arithmetic  14.2 us
    select_n x11, other arithmetic, step_rows(): jnp.where(is_last, rows_of(top_grads, batch_slot, row_start, chunk_len),...  12.9 us
  transfers between devices with their start and end apart: 1, of which 1 were waited for; matrix products, arithmetic and copies ran while one was open for 0% of the time, Pallas kernels for 0%

profile of v8, /device:TPU:32, one launch (start us, length us, event | category | flops | bytes accessed | tf_op | source)
XLA Modules:
  0.0 490.0 jit_solution(4638324529530647075)
XLA Ops:
  0.7 2.3 fusion.20
  3.0 4.0 convert_multiply_fusion
  8.2 1.5 broadcast_select_fusion.2
  9.7 430.1 %while.25 = (s32[]{:T(128)}, bf16[32,8192]{1,0:T(8,128)(2,1)S(1)}, bf16[2,2,32,512]{3,2,1,0:T(8,128)(2,1)S(1)}, f32[512]{0:T(512)S(1)}, f32[4,640]{1,0:T(4,128)S...) while((s32[]{:T(128)}, bf16[32,8192]{1,0:T(8,128)(2,1)S(1)}, ...), condition=%wide.region_8.9_spmd.clone, body=%wide.region_1.8_spmd.clone.sunk | while | flops 673416704 | bytes 67805824 | solution.py:294
  10.7 1.2 bitcast_select_fusion.3.x_ref.up_ref
  11.9 6.6 %eval_jaxpr.16 = f32[32,640]{1,0:T(8,128)S(1)} custom-call(bf16[32,8192]{1,0:T(8,128)(2,1)S(1)} %bitcast_select_fusion.3.x_ref.up_ref, bf16[640,8192]{1,0:T(8,128)(2,1)} %get-tuple-element.827.w_ref), custom_call_target="tpu_custom_call" | custom-call | flops 335544320 | bytes 11091968 | tf_op jit(solution)/shard_map/while/body/eval_jaxpr/pallas_call | solution.py:38
  19.0 4.5 fusion.29
  24.3 26.2 %eval_jaxpr.17 = (bf16[32,512]{1,0:T(8,128)(2,1)S(1)}, bf16[32,8192]{1,0:T(8,128)(2,1)S(1)}, f32[1,512]{1,0:T(1,128)S(1)}) custom-call(bf16[32,8192]{1,0:T(8,128)(2,1)S(1)} %get-tuple-element.751.x_ref, f32[32,128]{1,0:T(8,128)S(1)} %scatter.7.s_ref, f32[32,512]{1,0:T(8,128)S(1)} %dynamic-slice_bitcast_fusion.2.normed_ref, f32[32,1]{1,0:T(8,128)S(1)} %copy.26.inv_ref, ...), custom_call_target="tpu_custom_call" | custom-call | tf_op jit(solution)/shard_map/while/body/eval_jaxpr/pallas_call | solution.py:162
  51.5 1.2 bitcast_select_fusion.3.x_ref.up_ref
  52.6 6.6 %eval_jaxpr.16 = f32[32,640]{1,0:T(8,128)S(1)} custom-call(bf16[32,8192]{1,0:T(8,128)(2,1)S(1)} %bitcast_select_fusion.3.x_ref.up_ref, bf16[640,8192]{1,0:T(8,128)(2,1)} %get-tuple-element.827.w_ref), custom_call_target="tpu_custom_call" | custom-call | flops 335544320 | bytes 11091968 | tf_op jit(solution)/shard_map/while/body/eval_jaxpr/pallas_call | solution.py:38
  59.8 4.5 fusion.29
  65.0 27.9 %eval_jaxpr.17 = (bf16[32,512]{1,0:T(8,128)(2,1)S(1)}, bf16[32,8192]{1,0:T(8,128)(2,1)S(1)}, f32[1,512]{1,0:T(1,128)S(1)}) custom-call(bf16[32,8192]{1,0:T(8,128)(2,1)S(1)} %get-tuple-element.751.x_ref, f32[32,128]{1,0:T(8,128)S(1)} %scatter.7.s_ref, f32[32,512]{1,0:T(8,128)S(1)} %dynamic-slice_bitcast_fusion.2.normed_ref, f32[32,1]{1,0:T(8,128)S(1)} %copy.26.inv_ref, ...), custom_call_target="tpu_custom_call" | custom-call | tf_op jit(solution)/shard_map/while/body/eval_jaxpr/pallas_call | solution.py:162
  93.9 1.2 bitcast_select_fusion.3.x_ref.up_ref
  95.1 6.6 %eval_jaxpr.16 = f32[32,640]{1,0:T(8,128)S(1)} custom-call(bf16[32,8192]{1,0:T(8,128)(2,1)S(1)} %bitcast_select_fusion.3.x_ref.up_ref, bf16[640,8192]{1,0:T(8,128)(2,1)} %get-tuple-element.827.w_ref), custom_call_target="tpu_custom_call" | custom-call | flops 335544320 | bytes 11091968 | tf_op jit(solution)/shard_map/while/body/eval_jaxpr/pallas_call | solution.py:38
  102.2 4.5 fusion.29
  107.5 26.4 %eval_jaxpr.17 = (bf16[32,512]{1,0:T(8,128)(2,1)S(1)}, bf16[32,8192]{1,0:T(8,128)(2,1)S(1)}, f32[1,512]{1,0:T(1,128)S(1)}) custom-call(bf16[32,8192]{1,0:T(8,128)(2,1)S(1)} %get-tuple-element.751.x_ref, f32[32,128]{1,0:T(8,128)S(1)} %scatter.7.s_ref, f32[32,512]{1,0:T(8,128)S(1)} %dynamic-slice_bitcast_fusion.2.normed_ref, f32[32,1]{1,0:T(8,128)S(1)} %copy.26.inv_ref, ...), custom_call_target="tpu_custom_call" | custom-call | tf_op jit(solution)/shard_map/while/body/eval_jaxpr/pallas_call | solution.py:162
  134.9 1.2 bitcast_select_fusion.3.x_ref.up_ref
  136.1 6.6 %eval_jaxpr.16 = f32[32,640]{1,0:T(8,128)S(1)} custom-call(bf16[32,8192]{1,0:T(8,128)(2,1)S(1)} %bitcast_select_fusion.3.x_ref.up_ref, bf16[640,8192]{1,0:T(8,128)(2,1)} %get-tuple-element.827.w_ref), custom_call_target="tpu_custom_call" | custom-call | flops 335544320 | bytes 11091968 | tf_op jit(solution)/shard_map/while/body/eval_jaxpr/pallas_call | solution.py:38
  143.2 4.5 fusion.29
  148.5 22.0 %eval_jaxpr.17 = (bf16[32,512]{1,0:T(8,128)(2,1)S(1)}, bf16[32,8192]{1,0:T(8,128)(2,1)S(1)}, f32[1,512]{1,0:T(1,128)S(1)}) custom-call(bf16[32,8192]{1,0:T(8,128)(2,1)S(1)} %get-tuple-element.751.x_ref, f32[32,128]{1,0:T(8,128)S(1)} %scatter.7.s_ref, f32[32,512]{1,0:T(8,128)S(1)} %dynamic-slice_bitcast_fusion.2.normed_ref, f32[32,1]{1,0:T(8,128)S(1)} %copy.26.inv_ref, ...), custom_call_target="tpu_custom_call" | custom-call | tf_op jit(solution)/shard_map/while/body/eval_jaxpr/pallas_call | solution.py:162
  171.5 1.2 bitcast_select_fusion.3.x_ref.up_ref
  172.7 6.6 %eval_jaxpr.16 = f32[32,640]{1,0:T(8,128)S(1)} custom-call(bf16[32,8192]{1,0:T(8,128)(2,1)S(1)} %bitcast_select_fusion.3.x_ref.up_ref, bf16[640,8192]{1,0:T(8,128)(2,1)} %get-tuple-element.827.w_ref), custom_call_target="tpu_custom_call" | custom-call | flops 335544320 | bytes 11091968 | tf_op jit(solution)/shard_map/while/body/eval_jaxpr/pallas_call | solution.py:38
  179.8 4.5 fusion.29
  185.1 21.8 %eval_jaxpr.17 = (bf16[32,512]{1,0:T(8,128)(2,1)S(1)}, bf16[32,8192]{1,0:T(8,128)(2,1)S(1)}, f32[1,512]{1,0:T(1,128)S(1)}) custom-call(bf16[32,8192]{1,0:T(8,128)(2,1)S(1)} %get-tuple-element.751.x_ref, f32[32,128]{1,0:T(8,128)S(1)} %scatter.7.s_ref, f32[32,512]{1,0:T(8,128)S(1)} %dynamic-slice_bitcast_fusion.2.normed_ref, f32[32,1]{1,0:T(8,128)S(1)} %copy.26.inv_ref, ...), custom_call_target="tpu_custom_call" | custom-call | tf_op jit(solution)/shard_map/while/body/eval_jaxpr/pallas_call | solution.py:162
  207.9 1.2 bitcast_select_fusion.3.x_ref.up_ref
  209.1 6.6 %eval_jaxpr.16 = f32[32,640]{1,0:T(8,128)S(1)} custom-call(bf16[32,8192]{1,0:T(8,128)(2,1)S(1)} %bitcast_select_fusion.3.x_ref.up_ref, bf16[640,8192]{1,0:T(8,128)(2,1)} %get-tuple-element.827.w_ref), custom_call_target="tpu_custom_call" | custom-call | flops 335544320 | bytes 11091968 | tf_op jit(solution)/shard_map/while/body/eval_jaxpr/pallas_call | solution.py:38
  216.2 4.5 fusion.29
  221.5 25.8 %eval_jaxpr.17 = (bf16[32,512]{1,0:T(8,128)(2,1)S(1)}, bf16[32,8192]{1,0:T(8,128)(2,1)S(1)}, f32[1,512]{1,0:T(1,128)S(1)}) custom-call(bf16[32,8192]{1,0:T(8,128)(2,1)S(1)} %get-tuple-element.751.x_ref, f32[32,128]{1,0:T(8,128)S(1)} %scatter.7.s_ref, f32[32,512]{1,0:T(8,128)S(1)} %dynamic-slice_bitcast_fusion.2.normed_ref, f32[32,1]{1,0:T(8,128)S(1)} %copy.26.inv_ref, ...), custom_call_target="tpu_custom_call" | custom-call | tf_op jit(solution)/shard_map/while/body/eval_jaxpr/pallas_call | solution.py:162
  249.5 6.6 %eval_jaxpr.16 = f32[32,640]{1,0:T(8,128)S(1)} custom-call(bf16[32,8192]{1,0:T(8,128)(2,1)S(1)} %bitcast_select_fusion.3.x_ref.up_ref, bf16[640,8192]{1,0:T(8,128)(2,1)} %get-tuple-element.827.w_ref), custom_call_target="tpu_custom_call" | custom-call | flops 335544320 | bytes 11091968 | tf_op jit(solution)/shard_map/while/body/eval_jaxpr/pallas_call | solution.py:38
  256.6 4.5 fusion.29
  261.8 24.1 %eval_jaxpr.17 = (bf16[32,512]{1,0:T(8,128)(2,1)S(1)}, bf16[32,8192]{1,0:T(8,128)(2,1)S(1)}, f32[1,512]{1,0:T(1,128)S(1)}) custom-call(bf16[32,8192]{1,0:T(8,128)(2,1)S(1)} %get-tuple-element.751.x_ref, f32[32,128]{1,0:T(8,128)S(1)} %scatter.7.s_ref, f32[32,512]{1,0:T(8,128)S(1)} %dynamic-slice_bitcast_fusion.2.normed_ref, f32[32,1]{1,0:T(8,128)S(1)} %copy.26.inv_ref, ...), custom_call_target="tpu_custom_call" | custom-call | tf_op jit(solution)/shard_map/while/body/eval_jaxpr/pallas_call | solution.py:162
  288.1 6.6 %eval_jaxpr.16 = f32[32,640]{1,0:T(8,128)S(1)} custom-call(bf16[32,8192]{1,0:T(8,128)(2,1)S(1)} %bitcast_select_fusion.3.x_ref.up_ref, bf16[640,8192]{1,0:T(8,128)(2,1)} %get-tuple-element.827.w_ref), custom_call_target="tpu_custom_call" | custom-call | flops 335544320 | bytes 11091968 | tf_op jit(solution)/shard_map/while/body/eval_jaxpr/pallas_call | solution.py:38
  295.3 4.5 fusion.29
  300.5 24.1 %eval_jaxpr.17 = (bf16[32,512]{1,0:T(8,128)(2,1)S(1)}, bf16[32,8192]{1,0:T(8,128)(2,1)S(1)}, f32[1,512]{1,0:T(1,128)S(1)}) custom-call(bf16[32,8192]{1,0:T(8,128)(2,1)S(1)} %get-tuple-element.751.x_ref, f32[32,128]{1,0:T(8,128)S(1)} %scatter.7.s_ref, f32[32,512]{1,0:T(8,128)S(1)} %dynamic-slice_bitcast_fusion.2.normed_ref, f32[32,1]{1,0:T(8,128)S(1)} %copy.26.inv_ref, ...), custom_call_target="tpu_custom_call" | custom-call | tf_op jit(solution)/shard_map/while/body/eval_jaxpr/pallas_call | solution.py:162
  326.8 6.6 %eval_jaxpr.16 = f32[32,640]{1,0:T(8,128)S(1)} custom-call(bf16[32,8192]{1,0:T(8,128)(2,1)S(1)} %bitcast_select_fusion.3.x_ref.up_ref, bf16[640,8192]{1,0:T(8,128)(2,1)} %get-tuple-element.827.w_ref), custom_call_target="tpu_custom_call" | custom-call | flops 335544320 | bytes 11091968 | tf_op jit(solution)/shard_map/while/body/eval_jaxpr/pallas_call | solution.py:38
  333.9 4.5 fusion.29
  339.2 23.9 %eval_jaxpr.17 = (bf16[32,512]{1,0:T(8,128)(2,1)S(1)}, bf16[32,8192]{1,0:T(8,128)(2,1)S(1)}, f32[1,512]{1,0:T(1,128)S(1)}) custom-call(bf16[32,8192]{1,0:T(8,128)(2,1)S(1)} %get-tuple-element.751.x_ref, f32[32,128]{1,0:T(8,128)S(1)} %scatter.7.s_ref, f32[32,512]{1,0:T(8,128)S(1)} %dynamic-slice_bitcast_fusion.2.normed_ref, f32[32,1]{1,0:T(8,128)S(1)} %copy.26.inv_ref, ...), custom_call_target="tpu_custom_call" | custom-call | tf_op jit(solution)/shard_map/while/body/eval_jaxpr/pallas_call | solution.py:162
  365.3 6.6 %eval_jaxpr.16 = f32[32,640]{1,0:T(8,128)S(1)} custom-call(bf16[32,8192]{1,0:T(8,128)(2,1)S(1)} %bitcast_select_fusion.3.x_ref.up_ref, bf16[640,8192]{1,0:T(8,128)(2,1)} %get-tuple-element.827.w_ref), custom_call_target="tpu_custom_call" | custom-call | flops 335544320 | bytes 11091968 | tf_op jit(solution)/shard_map/while/body/eval_jaxpr/pallas_call | solution.py:38
  372.4 4.5 fusion.29
  377.7 22.4 %eval_jaxpr.17 = (bf16[32,512]{1,0:T(8,128)(2,1)S(1)}, bf16[32,8192]{1,0:T(8,128)(2,1)S(1)}, f32[1,512]{1,0:T(1,128)S(1)}) custom-call(bf16[32,8192]{1,0:T(8,128)(2,1)S(1)} %get-tuple-element.751.x_ref, f32[32,128]{1,0:T(8,128)S(1)} %scatter.7.s_ref, f32[32,512]{1,0:T(8,128)S(1)} %dynamic-slice_bitcast_fusion.2.normed_ref, f32[32,1]{1,0:T(8,128)S(1)} %copy.26.inv_ref, ...), custom_call_target="tpu_custom_call" | custom-call | tf_op jit(solution)/shard_map/while/body/eval_jaxpr/pallas_call | solution.py:162
  402.3 6.6 %eval_jaxpr.16 = f32[32,640]{1,0:T(8,128)S(1)} custom-call(bf16[32,8192]{1,0:T(8,128)(2,1)S(1)} %bitcast_select_fusion.3.x_ref.up_ref, bf16[640,8192]{1,0:T(8,128)(2,1)} %get-tuple-element.827.w_ref), custom_call_target="tpu_custom_call" | custom-call | flops 335544320 | bytes 11091968 | tf_op jit(solution)/shard_map/while/body/eval_jaxpr/pallas_call | solution.py:38
  409.4 4.5 fusion.29
  414.7 25.1 %eval_jaxpr.17 = (bf16[32,512]{1,0:T(8,128)(2,1)S(1)}, bf16[32,8192]{1,0:T(8,128)(2,1)S(1)}, f32[1,512]{1,0:T(1,128)S(1)}) custom-call(bf16[32,8192]{1,0:T(8,128)(2,1)S(1)} %get-tuple-element.751.x_ref, f32[32,128]{1,0:T(8,128)S(1)} %scatter.7.s_ref, f32[32,512]{1,0:T(8,128)S(1)} %dynamic-slice_bitcast_fusion.2.normed_ref, f32[32,1]{1,0:T(8,128)S(1)} %copy.26.inv_ref, ...), custom_call_target="tpu_custom_call" | custom-call | tf_op jit(solution)/shard_map/while/body/eval_jaxpr/pallas_call | solution.py:162
  439.9 14.7 %all_to_all.24 = f32[16,1,512]{2,1,0:T(1,128)S(1)} all-to-all(f32[16,1,512]{2,1,0:T(1,128)S(1)} %broadcast_in_dim.93), channel_id=1, replica_groups=mesh['section'=8,'tensor'=16] {'tensor'}, dimensions={0} | all-to-all | bytes 65536 | tf_op jit(solution)/shard_map/all_to_all | solution.py:17
  454.6 1.6 broadcast_in_dim.92
  456.2 3.7 all-to-all-start
  459.9 27.9 %all-to-all-done = bf16[16,2,64,512]{3,2,1,0:T(8,128)(2,1)S(1)} async-done(((bf16[16,2,64,512]{3,2,1,0:T(8,128)(2,1)}), bf16[16,2,64,512]{3,2,1,0:T(8,128)(2,1)S(1)}, u32[]{:S(2)}, u32[]{:S(2)}) %all-to-all-start) | async-done | bytes 2097184 | tf_op jit(solution)/shard_map/all_to_all | solution.py:297
  487.8 1.5 copy.22
  (262 shorter events, 30.7 us)
Async XLA Ops:
  0.7 6.3 %copy-start.2 = (f32[1,8192]{1,0:T(1,128)S(1)}, f32[1,8192]{1,0:T(1,128)}, u32[]{:S(2)}) copy-start(f32[1,8192]{1,0:T(1,128)} %param.18) | copy-start | bytes 98308
  0.7 7.3 %copy-start.6 = (s32[2,64]{1,0:T(2,128)S(1)}, s32[2,64]{1,0:T(2,128)}, u32[]{:S(2)}) copy-start(s32[2,64]{1,0:T(2,128)} %param.14) | copy-start | bytes 1540
  0.7 7.3 %copy-start.7 = (s32[2]{0:T(128)S(1)}, s32[2]{0:T(128)}, u32[]{:S(2)}) copy-start(s32[2]{0:T(128)} %param.15) | copy-start | bytes 28
  0.7 7.4 %copy-start.5 = (bf16[1,2,64,640]{3,2,1,0:T(8,128)(2,1)S(1)}, bf16[1,2,64,640]{3,2,1,0:T(8,128)(2,1)}, u32[]{:S(2)}) copy-start(bf16[1,2,64,640]{3,2,1,0:T(8,128)(2,1)} %param.17) | copy-start | bytes 491524
  0.7 7.4 %copy-start.1 = (bf16[2,64,8192]{2,1,0:T(8,128)(2,1)S(1)}, bf16[2,64,8192]{2,1,0:T(8,128)(2,1)}, u32[]{:S(2)}) copy-start(bf16[2,64,8192]{2,1,0:T(8,128)(2,1)} %param.13) | copy-start | bytes 6291460
  7.0 2.7 copy-start.3
  11.9 7.1 %copy-start = (bf16[8192,640]{1,0:T(8,128)(2,1)S(1)}, bf16[8192,640]{1,0:T(8,128)(2,1)}, u32[]{:S(2)}) copy-start(bf16[8192,640]{1,0:T(8,128)(2,1)} %get-tuple-element.829) | copy-start | bytes 31457284 | tf_op jit(solution)/shard_map/while
  52.6 7.1 %copy-start = (bf16[8192,640]{1,0:T(8,128)(2,1)S(1)}, bf16[8192,640]{1,0:T(8,128)(2,1)}, u32[]{:S(2)}) copy-start(bf16[8192,640]{1,0:T(8,128)(2,1)} %get-tuple-element.829) | copy-start | bytes 31457284 | tf_op jit(solution)/shard_map/while
  95.1 7.1 %copy-start = (bf16[8192,640]{1,0:T(8,128)(2,1)S(1)}, bf16[8192,640]{1,0:T(8,128)(2,1)}, u32[]{:S(2)}) copy-start(bf16[8192,640]{1,0:T(8,128)(2,1)} %get-tuple-element.829) | copy-start | bytes 31457284 | tf_op jit(solution)/shard_map/while
  136.1 7.1 %copy-start = (bf16[8192,640]{1,0:T(8,128)(2,1)S(1)}, bf16[8192,640]{1,0:T(8,128)(2,1)}, u32[]{:S(2)}) copy-start(bf16[8192,640]{1,0:T(8,128)(2,1)} %get-tuple-element.829) | copy-start | bytes 31457284 | tf_op jit(solution)/shard_map/while
  172.7 7.1 %copy-start = (bf16[8192,640]{1,0:T(8,128)(2,1)S(1)}, bf16[8192,640]{1,0:T(8,128)(2,1)}, u32[]{:S(2)}) copy-start(bf16[8192,640]{1,0:T(8,128)(2,1)} %get-tuple-element.829) | copy-start | bytes 31457284 | tf_op jit(solution)/shard_map/while
  209.1 7.1 %copy-start = (bf16[8192,640]{1,0:T(8,128)(2,1)S(1)}, bf16[8192,640]{1,0:T(8,128)(2,1)}, u32[]{:S(2)}) copy-start(bf16[8192,640]{1,0:T(8,128)(2,1)} %get-tuple-element.829) | copy-start | bytes 31457284 | tf_op jit(solution)/shard_map/while
  249.4 7.1 %copy-start = (bf16[8192,640]{1,0:T(8,128)(2,1)S(1)}, bf16[8192,640]{1,0:T(8,128)(2,1)}, u32[]{:S(2)}) copy-start(bf16[8192,640]{1,0:T(8,128)(2,1)} %get-tuple-element.829) | copy-start | bytes 31457284 | tf_op jit(solution)/shard_map/while
  288.1 7.1 %copy-start = (bf16[8192,640]{1,0:T(8,128)(2,1)S(1)}, bf16[8192,640]{1,0:T(8,128)(2,1)}, u32[]{:S(2)}) copy-start(bf16[8192,640]{1,0:T(8,128)(2,1)} %get-tuple-element.829) | copy-start | bytes 31457284 | tf_op jit(solution)/shard_map/while
  326.8 7.1 %copy-start = (bf16[8192,640]{1,0:T(8,128)(2,1)S(1)}, bf16[8192,640]{1,0:T(8,128)(2,1)}, u32[]{:S(2)}) copy-start(bf16[8192,640]{1,0:T(8,128)(2,1)} %get-tuple-element.829) | copy-start | bytes 31457284 | tf_op jit(solution)/shard_map/while
  365.3 7.1 %copy-start = (bf16[8192,640]{1,0:T(8,128)(2,1)S(1)}, bf16[8192,640]{1,0:T(8,128)(2,1)}, u32[]{:S(2)}) copy-start(bf16[8192,640]{1,0:T(8,128)(2,1)} %get-tuple-element.829) | copy-start | bytes 31457284 | tf_op jit(solution)/shard_map/while
  402.3 7.1 %copy-start = (bf16[8192,640]{1,0:T(8,128)(2,1)S(1)}, bf16[8192,640]{1,0:T(8,128)(2,1)}, u32[]{:S(2)}) copy-start(bf16[8192,640]{1,0:T(8,128)(2,1)} %get-tuple-element.829) | copy-start | bytes 31457284 | tf_op jit(solution)/shard_map/while
  439.9 49.5 %copy-start.4 = (f32[4,640]{1,0:T(4,128)}, f32[4,640]{1,0:T(4,128)S(1)}, u32[]{:S(2)}) copy-start(f32[4,640]{1,0:T(4,128)S(1)} %get-tuple-element.456) | copy-start | bytes 30724
  456.2 31.6 %all-to-all-start = ((bf16[16,2,64,512]{3,2,1,0:T(8,128)(2,1)}), bf16[16,2,64,512]{3,2,1,0:T(8,128)(2,1)S(1)}, u32[]{:S(2)}, u32[]{:S(2)}) async-start(bf16[16,2,64,512]{3,2,1,0:T(8,128)(2,1)} %broadcast_in_dim.92), calls=%async_computation | async-start | bytes 4194304 | tf_op jit(solution)/shard_map/all_to_all | solution.py:297

commit v9 on v7

--- a/solution.py
+++ b/solution.py
@@ -292,10 +292,17 @@
         tail_init,
     )
     last_state = lax.fori_loop(0, total_steps, step_rows, initial)
-    gathered = sent_to_all(last_state[1], "tensor")
-    results = jnp.transpose(gathered, (1, 2, 3, 0, 4)).reshape(batches, seq_len, model_width)
+    own = last_state[1].reshape(batches * seq_len, width)
+    gain_hi = last_state[2].astype(jnp.bfloat16)
+    gain_lo = (last_state[2] - gain_hi.astype(jnp.float32)).astype(jnp.bfloat16)
+    extra = jnp.zeros((16, width), jnp.bfloat16).at[0].set(gain_hi).at[1].set(gain_lo)
+    own = jnp.concatenate([own, extra], axis=0)
+    copies = jnp.broadcast_to(own, (tensors, *own.shape))
+    gathered = lax.all_to_all(copies, "tensor", split_axis=0, concat_axis=2, tiled=True)[0]
+    rows = batches * seq_len
+    results = gathered[:rows].reshape(batches, seq_len, model_width)
+    gain_total = gathered[rows].astype(jnp.float32) + gathered[rows + 1].astype(jnp.float32)
     conv_acc = last_state[3]
-    gain_total = sent_to_all(last_state[2], "tensor").reshape(model_width)
     return (results[None], gain_total[None], conv_acc[None])
 
 

time: 497 us -> 483 us (0.972)
  waiting for transfers between devices: 27.9 us -> 0 us
  blocking collectives: 14.7 us -> 37.6 us
    all_to_all x1 -> x0, waiting for transfers between devices: 27.9 us -> none  [sent_to_all(): return lax.all_to_all(copies, axis, split_axis=0, concat_axis=0, tiled=True)]
    all_to_all x1, blocking collectives: 14.7 us -> 37.6 us  [local(): lax.all_to_all(copies, 'tensor', split_axis=0, concat_axis=2, tiled=True)[0]]
  transfers between devices with their start and end apart: 1 -> 0, of which waited for: 1 -> 0; matrix products, arithmetic and copies ran while one was open for 0% -> 0% of each run, Pallas kernels for 0% -> 0%
where the time goes in v9:
time: 483 us; the launch traced here: 482 us
  Pallas kernels  342 us (71%)
  matrix products  50 us (10%)
  other arithmetic  38 us (8%)
  blocking collectives  37.6 us (8%)
  local copies, waits for them, and re-layouts  11.5 us (2%)
    pallas_call x11, Pallas kernels, layer_exchange(): pl.pallas_call(functools.partial(layer_exchange_kernel, n, n_sec, width),...  269 us
    pallas_call x11, Pallas kernels, matmul_nt(): pl.pallas_call(matmul_nt_kernel, out_shape=jax.ShapeDtypeStruct((rows, co...  73.1 us
    dot_general x11, matrix products, step_rows(): lax.dot_general(d_vals, w_in, contract, preferred_element_type=jnp.float32)  50 us
    all_to_all x1, blocking collectives, local(): lax.all_to_all(copies, 'tensor', split_axis=0, concat_axis=2, tiled=True)[0]  37.6 us
    another operation x22, other arithmetic  14.2 us
    select_n x11, other arithmetic, step_rows(): jnp.where(is_last, rows_of(top_grads, batch_slot, row_start, chunk_len),...  12.9 us

profile of v9, /device:TPU:32, one launch (start us, length us, event | category | flops | bytes accessed | tf_op | source)
XLA Modules:
  0.0 481.8 jit_solution(9479959681228951453)
XLA Ops:
  0.7 2.2 fusion.20
  3.0 2.4 convert_multiply_fusion
  6.5 3.1 broadcast_select_fusion.2
  9.7 429.8 %while.27 = (s32[]{:T(128)}, bf16[32,8192]{1,0:T(8,128)(2,1)S(1)}, bf16[2,2,32,512]{3,2,1,0:T(8,128)(2,1)S(1)}, f32[512]{0:T(512)S(1)}, f32[4,640]{1,0:T(4,128)S...) while((s32[]{:T(128)}, bf16[32,8192]{1,0:T(8,128)(2,1)S(1)}, ...), condition=%wide.region_8.9_spmd.clone, body=%wide.region_1.8_spmd.clone.sunk | while | flops 673416704 | bytes 67805824 | solution.py:294
  10.7 1.2 bitcast_select_fusion.3.x_ref.up_ref
  11.9 6.6 %eval_jaxpr.16 = f32[32,640]{1,0:T(8,128)S(1)} custom-call(bf16[32,8192]{1,0:T(8,128)(2,1)S(1)} %bitcast_select_fusion.3.x_ref.up_ref, bf16[640,8192]{1,0:T(8,128)(2,1)} %get-tuple-element.853.w_ref), custom_call_target="tpu_custom_call" | custom-call | flops 335544320 | bytes 11091968 | tf_op jit(solution)/shard_map/while/body/eval_jaxpr/pallas_call | solution.py:38
  19.0 4.5 fusion.30
  24.2 26.1 %eval_jaxpr.17 = (bf16[32,512]{1,0:T(8,128)(2,1)S(1)}, bf16[32,8192]{1,0:T(8,128)(2,1)S(1)}, f32[1,512]{1,0:T(1,128)S(1)}) custom-call(bf16[32,8192]{1,0:T(8,128)(2,1)S(1)} %get-tuple-element.777.x_ref, f32[32,128]{1,0:T(8,128)S(1)} %scatter.19.s_ref, f32[32,512]{1,0:T(8,128)S(1)} %dynamic-slice_bitcast_fusion.2.normed_ref, f32[32,1]{1,0:T(8,128)S(1)} %copy.25.inv_ref, ...), custom_call_target="tpu_custom_call" | custom-call | tf_op jit(solution)/shard_map/while/body/eval_jaxpr/pallas_call | solution.py:162
  51.4 1.2 bitcast_select_fusion.3.x_ref.up_ref
  52.5 6.6 %eval_jaxpr.16 = f32[32,640]{1,0:T(8,128)S(1)} custom-call(bf16[32,8192]{1,0:T(8,128)(2,1)S(1)} %bitcast_select_fusion.3.x_ref.up_ref, bf16[640,8192]{1,0:T(8,128)(2,1)} %get-tuple-element.853.w_ref), custom_call_target="tpu_custom_call" | custom-call | flops 335544320 | bytes 11091968 | tf_op jit(solution)/shard_map/while/body/eval_jaxpr/pallas_call | solution.py:38
  59.7 4.5 fusion.30
  64.9 28.0 %eval_jaxpr.17 = (bf16[32,512]{1,0:T(8,128)(2,1)S(1)}, bf16[32,8192]{1,0:T(8,128)(2,1)S(1)}, f32[1,512]{1,0:T(1,128)S(1)}) custom-call(bf16[32,8192]{1,0:T(8,128)(2,1)S(1)} %get-tuple-element.777.x_ref, f32[32,128]{1,0:T(8,128)S(1)} %scatter.19.s_ref, f32[32,512]{1,0:T(8,128)S(1)} %dynamic-slice_bitcast_fusion.2.normed_ref, f32[32,1]{1,0:T(8,128)S(1)} %copy.25.inv_ref, ...), custom_call_target="tpu_custom_call" | custom-call | tf_op jit(solution)/shard_map/while/body/eval_jaxpr/pallas_call | solution.py:162
  93.9 1.2 bitcast_select_fusion.3.x_ref.up_ref
  95.1 6.6 %eval_jaxpr.16 = f32[32,640]{1,0:T(8,128)S(1)} custom-call(bf16[32,8192]{1,0:T(8,128)(2,1)S(1)} %bitcast_select_fusion.3.x_ref.up_ref, bf16[640,8192]{1,0:T(8,128)(2,1)} %get-tuple-element.853.w_ref), custom_call_target="tpu_custom_call" | custom-call | flops 335544320 | bytes 11091968 | tf_op jit(solution)/shard_map/while/body/eval_jaxpr/pallas_call | solution.py:38
  102.2 4.5 fusion.30
  107.5 26.7 %eval_jaxpr.17 = (bf16[32,512]{1,0:T(8,128)(2,1)S(1)}, bf16[32,8192]{1,0:T(8,128)(2,1)S(1)}, f32[1,512]{1,0:T(1,128)S(1)}) custom-call(bf16[32,8192]{1,0:T(8,128)(2,1)S(1)} %get-tuple-element.777.x_ref, f32[32,128]{1,0:T(8,128)S(1)} %scatter.19.s_ref, f32[32,512]{1,0:T(8,128)S(1)} %dynamic-slice_bitcast_fusion.2.normed_ref, f32[32,1]{1,0:T(8,128)S(1)} %copy.25.inv_ref, ...), custom_call_target="tpu_custom_call" | custom-call | tf_op jit(solution)/shard_map/while/body/eval_jaxpr/pallas_call | solution.py:162
  135.2 1.2 bitcast_select_fusion.3.x_ref.up_ref
  136.4 6.6 %eval_jaxpr.16 = f32[32,640]{1,0:T(8,128)S(1)} custom-call(bf16[32,8192]{1,0:T(8,128)(2,1)S(1)} %bitcast_select_fusion.3.x_ref.up_ref, bf16[640,8192]{1,0:T(8,128)(2,1)} %get-tuple-element.853.w_ref), custom_call_target="tpu_custom_call" | custom-call | flops 335544320 | bytes 11091968 | tf_op jit(solution)/shard_map/while/body/eval_jaxpr/pallas_call | solution.py:38
  143.5 4.5 fusion.30
  148.8 21.6 %eval_jaxpr.17 = (bf16[32,512]{1,0:T(8,128)(2,1)S(1)}, bf16[32,8192]{1,0:T(8,128)(2,1)S(1)}, f32[1,512]{1,0:T(1,128)S(1)}) custom-call(bf16[32,8192]{1,0:T(8,128)(2,1)S(1)} %get-tuple-element.777.x_ref, f32[32,128]{1,0:T(8,128)S(1)} %scatter.19.s_ref, f32[32,512]{1,0:T(8,128)S(1)} %dynamic-slice_bitcast_fusion.2.normed_ref, f32[32,1]{1,0:T(8,128)S(1)} %copy.25.inv_ref, ...), custom_call_target="tpu_custom_call" | custom-call | tf_op jit(solution)/shard_map/while/body/eval_jaxpr/pallas_call | solution.py:162
  171.3 1.2 bitcast_select_fusion.3.x_ref.up_ref
  172.5 6.6 %eval_jaxpr.16 = f32[32,640]{1,0:T(8,128)S(1)} custom-call(bf16[32,8192]{1,0:T(8,128)(2,1)S(1)} %bitcast_select_fusion.3.x_ref.up_ref, bf16[640,8192]{1,0:T(8,128)(2,1)} %get-tuple-element.853.w_ref), custom_call_target="tpu_custom_call" | custom-call | flops 335544320 | bytes 11091968 | tf_op jit(solution)/shard_map/while/body/eval_jaxpr/pallas_call | solution.py:38
  179.6 4.5 fusion.30
  184.9 22.2 %eval_jaxpr.17 = (bf16[32,512]{1,0:T(8,128)(2,1)S(1)}, bf16[32,8192]{1,0:T(8,128)(2,1)S(1)}, f32[1,512]{1,0:T(1,128)S(1)}) custom-call(bf16[32,8192]{1,0:T(8,128)(2,1)S(1)} %get-tuple-element.777.x_ref, f32[32,128]{1,0:T(8,128)S(1)} %scatter.19.s_ref, f32[32,512]{1,0:T(8,128)S(1)} %dynamic-slice_bitcast_fusion.2.normed_ref, f32[32,1]{1,0:T(8,128)S(1)} %copy.25.inv_ref, ...), custom_call_target="tpu_custom_call" | custom-call | tf_op jit(solution)/shard_map/while/body/eval_jaxpr/pallas_call | solution.py:162
  208.1 1.2 bitcast_select_fusion.3.x_ref.up_ref
  209.3 6.6 %eval_jaxpr.16 = f32[32,640]{1,0:T(8,128)S(1)} custom-call(bf16[32,8192]{1,0:T(8,128)(2,1)S(1)} %bitcast_select_fusion.3.x_ref.up_ref, bf16[640,8192]{1,0:T(8,128)(2,1)} %get-tuple-element.853.w_ref), custom_call_target="tpu_custom_call" | custom-call | flops 335544320 | bytes 11091968 | tf_op jit(solution)/shard_map/while/body/eval_jaxpr/pallas_call | solution.py:38
  216.4 4.5 fusion.30
  221.7 25.6 %eval_jaxpr.17 = (bf16[32,512]{1,0:T(8,128)(2,1)S(1)}, bf16[32,8192]{1,0:T(8,128)(2,1)S(1)}, f32[1,512]{1,0:T(1,128)S(1)}) custom-call(bf16[32,8192]{1,0:T(8,128)(2,1)S(1)} %get-tuple-element.777.x_ref, f32[32,128]{1,0:T(8,128)S(1)} %scatter.19.s_ref, f32[32,512]{1,0:T(8,128)S(1)} %dynamic-slice_bitcast_fusion.2.normed_ref, f32[32,1]{1,0:T(8,128)S(1)} %copy.25.inv_ref, ...), custom_call_target="tpu_custom_call" | custom-call | tf_op jit(solution)/shard_map/while/body/eval_jaxpr/pallas_call | solution.py:162
  248.3 1.2 bitcast_select_fusion.3.x_ref.up_ref
  249.5 6.6 %eval_jaxpr.16 = f32[32,640]{1,0:T(8,128)S(1)} custom-call(bf16[32,8192]{1,0:T(8,128)(2,1)S(1)} %bitcast_select_fusion.3.x_ref.up_ref, bf16[640,8192]{1,0:T(8,128)(2,1)} %get-tuple-element.853.w_ref), custom_call_target="tpu_custom_call" | custom-call | flops 335544320 | bytes 11091968 | tf_op jit(solution)/shard_map/while/body/eval_jaxpr/pallas_call | solution.py:38
  256.6 4.5 fusion.30
  261.9 24.3 %eval_jaxpr.17 = (bf16[32,512]{1,0:T(8,128)(2,1)S(1)}, bf16[32,8192]{1,0:T(8,128)(2,1)S(1)}, f32[1,512]{1,0:T(1,128)S(1)}) custom-call(bf16[32,8192]{1,0:T(8,128)(2,1)S(1)} %get-tuple-element.777.x_ref, f32[32,128]{1,0:T(8,128)S(1)} %scatter.19.s_ref, f32[32,512]{1,0:T(8,128)S(1)} %dynamic-slice_bitcast_fusion.2.normed_ref, f32[32,1]{1,0:T(8,128)S(1)} %copy.25.inv_ref, ...), custom_call_target="tpu_custom_call" | custom-call | tf_op jit(solution)/shard_map/while/body/eval_jaxpr/pallas_call | solution.py:162
  287.2 1.2 bitcast_select_fusion.3.x_ref.up_ref
  288.4 6.6 %eval_jaxpr.16 = f32[32,640]{1,0:T(8,128)S(1)} custom-call(bf16[32,8192]{1,0:T(8,128)(2,1)S(1)} %bitcast_select_fusion.3.x_ref.up_ref, bf16[640,8192]{1,0:T(8,128)(2,1)} %get-tuple-element.853.w_ref), custom_call_target="tpu_custom_call" | custom-call | flops 335544320 | bytes 11091968 | tf_op jit(solution)/shard_map/while/body/eval_jaxpr/pallas_call | solution.py:38
  295.5 4.5 fusion.30
  300.8 24.6 %eval_jaxpr.17 = (bf16[32,512]{1,0:T(8,128)(2,1)S(1)}, bf16[32,8192]{1,0:T(8,128)(2,1)S(1)}, f32[1,512]{1,0:T(1,128)S(1)}) custom-call(bf16[32,8192]{1,0:T(8,128)(2,1)S(1)} %get-tuple-element.777.x_ref, f32[32,128]{1,0:T(8,128)S(1)} %scatter.19.s_ref, f32[32,512]{1,0:T(8,128)S(1)} %dynamic-slice_bitcast_fusion.2.normed_ref, f32[32,1]{1,0:T(8,128)S(1)} %copy.25.inv_ref, ...), custom_call_target="tpu_custom_call" | custom-call | tf_op jit(solution)/shard_map/while/body/eval_jaxpr/pallas_call | solution.py:162
  326.4 1.2 bitcast_select_fusion.3.x_ref.up_ref
  327.6 6.6 %eval_jaxpr.16 = f32[32,640]{1,0:T(8,128)S(1)} custom-call(bf16[32,8192]{1,0:T(8,128)(2,1)S(1)} %bitcast_select_fusion.3.x_ref.up_ref, bf16[640,8192]{1,0:T(8,128)(2,1)} %get-tuple-element.853.w_ref), custom_call_target="tpu_custom_call" | custom-call | flops 335544320 | bytes 11091968 | tf_op jit(solution)/shard_map/while/body/eval_jaxpr/pallas_call | solution.py:38
  334.7 4.5 fusion.30
  340.0 22.6 %eval_jaxpr.17 = (bf16[32,512]{1,0:T(8,128)(2,1)S(1)}, bf16[32,8192]{1,0:T(8,128)(2,1)S(1)}, f32[1,512]{1,0:T(1,128)S(1)}) custom-call(bf16[32,8192]{1,0:T(8,128)(2,1)S(1)} %get-tuple-element.777.x_ref, f32[32,128]{1,0:T(8,128)S(1)} %scatter.19.s_ref, f32[32,512]{1,0:T(8,128)S(1)} %dynamic-slice_bitcast_fusion.2.normed_ref, f32[32,1]{1,0:T(8,128)S(1)} %copy.25.inv_ref, ...), custom_call_target="tpu_custom_call" | custom-call | tf_op jit(solution)/shard_map/while/body/eval_jaxpr/pallas_call | solution.py:162
  364.8 6.6 %eval_jaxpr.16 = f32[32,640]{1,0:T(8,128)S(1)} custom-call(bf16[32,8192]{1,0:T(8,128)(2,1)S(1)} %bitcast_select_fusion.3.x_ref.up_ref, bf16[640,8192]{1,0:T(8,128)(2,1)} %get-tuple-element.853.w_ref), custom_call_target="tpu_custom_call" | custom-call | flops 335544320 | bytes 11091968 | tf_op jit(solution)/shard_map/while/body/eval_jaxpr/pallas_call | solution.py:38
  371.9 4.5 fusion.30
  377.2 22.8 %eval_jaxpr.17 = (bf16[32,512]{1,0:T(8,128)(2,1)S(1)}, bf16[32,8192]{1,0:T(8,128)(2,1)S(1)}, f32[1,512]{1,0:T(1,128)S(1)}) custom-call(bf16[32,8192]{1,0:T(8,128)(2,1)S(1)} %get-tuple-element.777.x_ref, f32[32,128]{1,0:T(8,128)S(1)} %scatter.19.s_ref, f32[32,512]{1,0:T(8,128)S(1)} %dynamic-slice_bitcast_fusion.2.normed_ref, f32[32,1]{1,0:T(8,128)S(1)} %copy.25.inv_ref, ...), custom_call_target="tpu_custom_call" | custom-call | tf_op jit(solution)/shard_map/while/body/eval_jaxpr/pallas_call | solution.py:162
  402.2 6.6 %eval_jaxpr.16 = f32[32,640]{1,0:T(8,128)S(1)} custom-call(bf16[32,8192]{1,0:T(8,128)(2,1)S(1)} %bitcast_select_fusion.3.x_ref.up_ref, bf16[640,8192]{1,0:T(8,128)(2,1)} %get-tuple-element.853.w_ref), custom_call_target="tpu_custom_call" | custom-call | flops 335544320 | bytes 11091968 | tf_op jit(solution)/shard_map/while/body/eval_jaxpr/pallas_call | solution.py:38
  409.4 4.5 fusion.30
  414.6 24.8 %eval_jaxpr.17 = (bf16[32,512]{1,0:T(8,128)(2,1)S(1)}, bf16[32,8192]{1,0:T(8,128)(2,1)S(1)}, f32[1,512]{1,0:T(1,128)S(1)}) custom-call(bf16[32,8192]{1,0:T(8,128)(2,1)S(1)} %get-tuple-element.777.x_ref, f32[32,128]{1,0:T(8,128)S(1)} %scatter.19.s_ref, f32[32,512]{1,0:T(8,128)S(1)} %dynamic-slice_bitcast_fusion.2.normed_ref, f32[32,1]{1,0:T(8,128)S(1)} %copy.25.inv_ref, ...), custom_call_target="tpu_custom_call" | custom-call | tf_op jit(solution)/shard_map/while/body/eval_jaxpr/pallas_call | solution.py:162
  439.9 37.6 %all_to_all.15 = bf16[16,144,512]{2,1,0:T(8,128)(2,1)S(1)} all-to-all(bf16[16,144,512]{2,1,0:T(8,128)(2,1)S(1)} %broadcast_in_dim.91), channel_id=1, replica_groups=mesh['section'=8,'tensor'=16] {'tensor'}, dimensions={0} | all-to-all | bytes 4718592 | tf_op jit(solution)/shard_map/all_to_all | solution.py:301
  479.5 2.3 broadcast_in_dim_reshape.3
  (267 shorter events, 28.8 us)
Async XLA Ops:
  0.6 2.3 copy-start.1
  2.9 2.5 copy-start.2
  3.0 3.4 copy-start.6
  3.0 3.4 copy-start.7
  3.0 3.5 copy-start.5
  6.5 3.2 copy-start.3
  11.8 7.1 %copy-start = (bf16[8192,640]{1,0:T(8,128)(2,1)S(1)}, bf16[8192,640]{1,0:T(8,128)(2,1)}, u32[]{:S(2)}) copy-start(bf16[8192,640]{1,0:T(8,128)(2,1)} %get-tuple-element.855) | copy-start | bytes 31457284 | tf_op jit(solution)/shard_map/while
  52.5 7.1 %copy-start = (bf16[8192,640]{1,0:T(8,128)(2,1)S(1)}, bf16[8192,640]{1,0:T(8,128)(2,1)}, u32[]{:S(2)}) copy-start(bf16[8192,640]{1,0:T(8,128)(2,1)} %get-tuple-element.855) | copy-start | bytes 31457284 | tf_op jit(solution)/shard_map/while
  95.1 7.1 %copy-start = (bf16[8192,640]{1,0:T(8,128)(2,1)S(1)}, bf16[8192,640]{1,0:T(8,128)(2,1)}, u32[]{:S(2)}) copy-start(bf16[8192,640]{1,0:T(8,128)(2,1)} %get-tuple-element.855) | copy-start | bytes 31457284 | tf_op jit(solution)/shard_map/while
  136.3 7.1 %copy-start = (bf16[8192,640]{1,0:T(8,128)(2,1)S(1)}, bf16[8192,640]{1,0:T(8,128)(2,1)}, u32[]{:S(2)}) copy-start(bf16[8192,640]{1,0:T(8,128)(2,1)} %get-tuple-element.855) | copy-start | bytes 31457284 | tf_op jit(solution)/shard_map/while
  172.5 7.1 %copy-start = (bf16[8192,640]{1,0:T(8,128)(2,1)S(1)}, bf16[8192,640]{1,0:T(8,128)(2,1)}, u32[]{:S(2)}) copy-start(bf16[8192,640]{1,0:T(8,128)(2,1)} %get-tuple-element.855) | copy-start | bytes 31457284 | tf_op jit(solution)/shard_map/while
  209.3 7.1 %copy-start = (bf16[8192,640]{1,0:T(8,128)(2,1)S(1)}, bf16[8192,640]{1,0:T(8,128)(2,1)}, u32[]{:S(2)}) copy-start(bf16[8192,640]{1,0:T(8,128)(2,1)} %get-tuple-element.855) | copy-start | bytes 31457284 | tf_op jit(solution)/shard_map/while
  249.5 7.1 %copy-start = (bf16[8192,640]{1,0:T(8,128)(2,1)S(1)}, bf16[8192,640]{1,0:T(8,128)(2,1)}, u32[]{:S(2)}) copy-start(bf16[8192,640]{1,0:T(8,128)(2,1)} %get-tuple-element.855) | copy-start | bytes 31457284 | tf_op jit(solution)/shard_map/while
  288.4 7.1 %copy-start = (bf16[8192,640]{1,0:T(8,128)(2,1)S(1)}, bf16[8192,640]{1,0:T(8,128)(2,1)}, u32[]{:S(2)}) copy-start(bf16[8192,640]{1,0:T(8,128)(2,1)} %get-tuple-element.855) | copy-start | bytes 31457284 | tf_op jit(solution)/shard_map/while
  327.6 7.1 %copy-start = (bf16[8192,640]{1,0:T(8,128)(2,1)S(1)}, bf16[8192,640]{1,0:T(8,128)(2,1)}, u32[]{:S(2)}) copy-start(bf16[8192,640]{1,0:T(8,128)(2,1)} %get-tuple-element.855) | copy-start | bytes 31457284 | tf_op jit(solution)/shard_map/while
  364.8 7.1 %copy-start = (bf16[8192,640]{1,0:T(8,128)(2,1)S(1)}, bf16[8192,640]{1,0:T(8,128)(2,1)}, u32[]{:S(2)}) copy-start(bf16[8192,640]{1,0:T(8,128)(2,1)} %get-tuple-element.855) | copy-start | bytes 31457284 | tf_op jit(solution)/shard_map/while
  402.2 7.1 %copy-start = (bf16[8192,640]{1,0:T(8,128)(2,1)S(1)}, bf16[8192,640]{1,0:T(8,128)(2,1)}, u32[]{:S(2)}) copy-start(bf16[8192,640]{1,0:T(8,128)(2,1)} %get-tuple-element.855) | copy-start | bytes 31457284 | tf_op jit(solution)/shard_map/while
  439.5 38.0 %copy-start.4 = (f32[4,640]{1,0:T(4,128)}, f32[4,640]{1,0:T(4,128)S(1)}, u32[]{:S(2)}) copy-start(f32[4,640]{1,0:T(4,128)S(1)} %get-tuple-element.480) | copy-start | bytes 30724

commit v10 on v9

--- a/solution.py
+++ b/solution.py
@@ -17,10 +17,9 @@
     return lax.all_to_all(copies, axis, split_axis=0, concat_axis=0, tiled=True)
 
 
-def matmul_nt_kernel(x_ref, w_ref, out_ref):
-    product = lax.dot_general(
-        x_ref[...], w_ref[...], (((1,), (1,)), ((), ())), preferred_element_type=jnp.float32
-    )
+def matmul_nt_kernel(n_sec, top_ref, x_ref, w_ref, out_ref):
+    lhs = jnp.where(lax.axis_index("section") == n_sec - 1, top_ref[...], x_ref[...])
+    product = lax.dot_general(lhs, w_ref[...], (((1,), (1,)), ((), ())), preferred_element_type=jnp.float32)
 
     @pl.when(pl.program_id(1) == 0)
     def _():
@@ -31,15 +30,16 @@
         out_ref[...] += product.astype(out_ref.dtype)
 
 
-def matmul_nt(x, w, block_n, block_k, out_dtype):
+def matmul_nt(top, x, w, block_n, block_k, out_dtype, n_sec):
     rows, depth = x.shape
     cols = w.shape[0]
     grid = (cols // block_n, depth // block_k)
     return pl.pallas_call(
-        matmul_nt_kernel,
+        functools.partial(matmul_nt_kernel, n_sec),
         out_shape=jax.ShapeDtypeStruct((rows, cols), out_dtype),
         grid=grid,
         in_specs=[
+            pl.BlockSpec((rows, block_k), lambda n, k: (0, k)),
             pl.BlockSpec((rows, block_k), lambda n, k: (0, k)),
             pl.BlockSpec((block_n, block_k), lambda n, k: (n, k)),
         ],
@@ -49,14 +49,14 @@
         ),
         cost_estimate=pl.CostEstimate(
             flops=2 * rows * cols * depth,
-            bytes_accessed=2 * (rows * depth + cols * depth) + rows * cols * jnp.dtype(out_dtype).itemsize,
+            bytes_accessed=2 * (2 * rows * depth + cols * depth) + rows * cols * jnp.dtype(out_dtype).itemsize,
             transcendentals=0,
         ),
-    )(x, w)
+    )(top, x, w)
 
 
 def layer_exchange_kernel(
-    n, n_sec, width, x_ref, s_ref, normed_ref, inv_ref, gain_ref, up_ref,
+    n, n_sec, width, x_ref, s_ref, normed_ref, inv_ref, gain_ref, top_ref, up_ref,
     g_ref, next_ref, gain_out_ref,
     recv, srecv, gbuf, down, send_sem, recv_sem, ssend_sem, srecv_sem, dsend_sem, drecv_sem,
 ):
@@ -116,7 +116,8 @@
     row_mean = stat_total[:, 0:1] * (1.0 / (n * width))
     normed = normed_ref[...]
     d_in = inv_ref[...] * (total * gain_ref[...] - normed * row_mean)
-    result = (up_ref[:, mine].astype(jnp.float32) + d_in).astype(g_ref.dtype)
+    upstream = jnp.where(sec == n_sec - 1, top_ref[:, mine], up_ref[:, mine])
+    result = (upstream.astype(jnp.float32) + d_in).astype(g_ref.dtype)
     gbuf[...] = result
     g_ref[...] = result
     gain_out_ref[...] = jnp.sum(total * normed, axis=0, keepdims=True)
@@ -156,7 +157,7 @@
         next_ref[...] = jnp.zeros_like(next_ref)
 
 
-def layer_exchange(partial, stats, normed, inv_rms, gain_own, upstream, n, n_sec, width):
+def layer_exchange(partial, stats, normed, inv_rms, gain_own, top, upstream, n, n_sec, width):
     rows = partial.shape[0]
     vmem = pl.BlockSpec(memory_space=pltpu.VMEM)
     return pl.pallas_call(
@@ -166,7 +167,7 @@
             jax.ShapeDtypeStruct((rows, n * width), jnp.bfloat16),
             jax.ShapeDtypeStruct((1, width), jnp.float32),
         ),
-        in_specs=[vmem] * 6,
+        in_specs=[vmem] * 7,
         out_specs=(vmem, vmem, vmem),
         scratch_shapes=[
             pltpu.VMEM((n, rows, width), partial.dtype),
@@ -183,7 +184,7 @@
         compiler_params=pltpu.CompilerParams(
             collective_id=2, has_side_effects=True, vmem_limit_bytes=16 * 1024 * 1024
         ),
-    )(partial, stats, normed, inv_rms, gain_own, upstream)
+    )(partial, stats, normed, inv_rms, gain_own, top, upstream)
 
 
 def conv_block(weights, ext_vals, tail_rows, d_act):
@@ -258,8 +259,8 @@
         incoming, results, gain_acc, conv_acc, tail_carry = loop_state
         batch_slot, half_now, join_now, active = pick_block(step_idx)
         row_start = half_now * chunk_len
-        full_chunk = jnp.where(is_last, rows_of(top_grads, batch_slot, row_start, chunk_len), incoming)
-        d_act = matmul_nt(full_chunk, w_out, w_out.shape[0], 2048, jnp.float32)
+        top_chunk = rows_of(top_grads, batch_slot, row_start, chunk_len)
+        d_act = matmul_nt(top_chunk, incoming, w_out, w_out.shape[0], 2048, jnp.float32, sections)
         ext_vals = lax.dynamic_slice(
             conv_padded, (batch_slot, row_start, 0), (1, chunk_len + kernel_width - 1, local_channels)
         )[0].astype(jnp.float32)
@@ -272,7 +273,7 @@
         stats = jnp.zeros((chunk_len, 128), jnp.float32).at[:, 0].set(row_part)
         normed_own = rows_of(normed_own_all, batch_slot, row_start, chunk_len)
         grad_out, incoming_next, gain_part = layer_exchange(
-            partial, stats, normed_own, inv_rms, gain_own[None, :], full_chunk, tensors, sections, width
+            partial, stats, normed_own, inv_rms, gain_own[None, :], top_chunk, incoming, tensors, sections, width
         )
         gain_part = gain_part[0]
         previous = lax.dynamic_slice(results, (batch_slot, half_now, 0, 0), (1, 1, chunk_len, width))

time: 483 us -> 482 us (level)
  other arithmetic: 38 us -> 25 us
  local copies, waits for them, and re-layouts: 11.5 us -> 23.5 us
    select_n x11 -> x0, other arithmetic: 12.9 us -> none  [step_rows(): jnp.where(is_last, rows_of(top_grads, batch_slot, row_start, chunk_len),...]
    squeeze x33 -> x44, local copies, waits for them, and re-layouts: 1.96 us -> 14 us  [rows_of(): lax.dynamic_slice(array, (batch_slot, first_row, 0), (1, row_count, array...]
where the time goes in v10:
time: 482 us; the launch traced here: 481 us
  Pallas kernels  343 us (71%)
  matrix products  50 us (10%)
  blocking collectives  36.3 us (8%)
  other arithmetic  25 us (5%)
  local copies, waits for them, and re-layouts  23.5 us (5%)
    pallas_call x11, Pallas kernels, layer_exchange(): pl.pallas_call(functools.partial(layer_exchange_kernel, n, n_sec, width),...  270 us
    pallas_call x11, Pallas kernels, matmul_nt(): pl.pallas_call(functools.partial(matmul_nt_kernel, n_sec), out_shape=jax....  73.4 us
    dot_general x11, matrix products, step_rows(): lax.dot_general(d_vals, w_in, contract, preferred_element_type=jnp.float32)  50 us
    all_to_all x1, blocking collectives, local(): lax.all_to_all(copies, 'tensor', split_axis=0, concat_axis=2, tiled=True)[0]  36.3 us
    another operation x22, other arithmetic  14 us
    squeeze x44, local copies, waits for them, and re-layouts, rows_of(): lax.dynamic_slice(array, (batch_slot, first_row, 0), (1, row_count, array...  14 us

profile of v10, /device:TPU:32, one launch (start us, length us, event | category | flops | bytes accessed | tf_op | source)
XLA Modules:
  0.0 480.5 jit_solution(15802394530307734838)
XLA Ops:
  0.7 2.3 fusion.20
  3.0 2.4 convert_multiply_fusion
  6.5 3.1 broadcast_select_fusion.2
  9.7 429.8 %while.27 = (s32[]{:T(128)}, bf16[32,8192]{1,0:T(8,128)(2,1)S(1)}, bf16[2,2,32,512]{3,2,1,0:T(8,128)(2,1)S(1)}, f32[512]{0:T(512)S(1)}, f32[4,640]{1,0:T(4,128)S...) while((s32[]{:T(128)}, bf16[32,8192]{1,0:T(8,128)(2,1)S(1)}, ...), condition=%wide.region_8.9_spmd.clone, body=%wide.region_1.8_spmd.clone.sunk | while | flops 673154560 | bytes 68854392 | solution.py:295
  10.7 1.1 dynamic-slice_bitcast_fusion.4.top_ref
  11.8 6.7 %eval_jaxpr.16 = f32[32,640]{1,0:T(8,128)S(1)} custom-call(bf16[32,8192]{1,0:T(8,128)(2,1)S(1)} %dynamic-slice_bitcast_fusion.4.top_ref, bf16[32,8192]{1,0:T(8,128)(2,1)S(1)} %copy.47.x_ref.up_ref, bf16[640,8192]{1,0:T(8,128)(2,1)} %get-tuple-element.811.w_ref), custom_call_target="tpu_custom_call" | custom-call | flops 335544320 | bytes 11616256 | tf_op jit(solution)/shard_map/while/body/eval_jaxpr/pallas_call | solution.py:37
  18.9 4.5 fusion.30
  24.2 26.2 %eval_jaxpr.17 = (bf16[32,512]{1,0:T(8,128)(2,1)S(1)}, bf16[32,8192]{1,0:T(8,128)(2,1)S(1)}, f32[1,512]{1,0:T(1,128)S(1)}) custom-call(bf16[32,8192]{1,0:T(8,128)(2,1)S(1)} %get-tuple-element.738.x_ref, f32[32,128]{1,0:T(8,128)S(1)} %scatter.19.s_ref, f32[32,512]{1,0:T(8,128)S(1)} %dynamic-slice_bitcast_fusion.5.normed_ref, f32[32,1]{1,0:T(8,128)S(1)} %copy.25.inv_ref, ...), custom_call_target="tpu_custom_call" | custom-call | tf_op jit(solution)/shard_map/while/body/eval_jaxpr/pallas_call | solution.py:163
  51.4 1.1 dynamic-slice_bitcast_fusion.4.top_ref
  52.5 6.7 %eval_jaxpr.16 = f32[32,640]{1,0:T(8,128)S(1)} custom-call(bf16[32,8192]{1,0:T(8,128)(2,1)S(1)} %dynamic-slice_bitcast_fusion.4.top_ref, bf16[32,8192]{1,0:T(8,128)(2,1)S(1)} %copy.47.x_ref.up_ref, bf16[640,8192]{1,0:T(8,128)(2,1)} %get-tuple-element.811.w_ref), custom_call_target="tpu_custom_call" | custom-call | flops 335544320 | bytes 11616256 | tf_op jit(solution)/shard_map/while/body/eval_jaxpr/pallas_call | solution.py:37
  59.6 4.5 fusion.30
  64.9 27.9 %eval_jaxpr.17 = (bf16[32,512]{1,0:T(8,128)(2,1)S(1)}, bf16[32,8192]{1,0:T(8,128)(2,1)S(1)}, f32[1,512]{1,0:T(1,128)S(1)}) custom-call(bf16[32,8192]{1,0:T(8,128)(2,1)S(1)} %get-tuple-element.738.x_ref, f32[32,128]{1,0:T(8,128)S(1)} %scatter.19.s_ref, f32[32,512]{1,0:T(8,128)S(1)} %dynamic-slice_bitcast_fusion.5.normed_ref, f32[32,1]{1,0:T(8,128)S(1)} %copy.25.inv_ref, ...), custom_call_target="tpu_custom_call" | custom-call | tf_op jit(solution)/shard_map/while/body/eval_jaxpr/pallas_call | solution.py:163
  93.8 1.1 dynamic-slice_bitcast_fusion.4.top_ref
  94.9 6.7 %eval_jaxpr.16 = f32[32,640]{1,0:T(8,128)S(1)} custom-call(bf16[32,8192]{1,0:T(8,128)(2,1)S(1)} %dynamic-slice_bitcast_fusion.4.top_ref, bf16[32,8192]{1,0:T(8,128)(2,1)S(1)} %copy.47.x_ref.up_ref, bf16[640,8192]{1,0:T(8,128)(2,1)} %get-tuple-element.811.w_ref), custom_call_target="tpu_custom_call" | custom-call | flops 335544320 | bytes 11616256 | tf_op jit(solution)/shard_map/while/body/eval_jaxpr/pallas_call | solution.py:37
  102.0 4.5 fusion.30
  107.3 26.7 %eval_jaxpr.17 = (bf16[32,512]{1,0:T(8,128)(2,1)S(1)}, bf16[32,8192]{1,0:T(8,128)(2,1)S(1)}, f32[1,512]{1,0:T(1,128)S(1)}) custom-call(bf16[32,8192]{1,0:T(8,128)(2,1)S(1)} %get-tuple-element.738.x_ref, f32[32,128]{1,0:T(8,128)S(1)} %scatter.19.s_ref, f32[32,512]{1,0:T(8,128)S(1)} %dynamic-slice_bitcast_fusion.5.normed_ref, f32[32,1]{1,0:T(8,128)S(1)} %copy.25.inv_ref, ...), custom_call_target="tpu_custom_call" | custom-call | tf_op jit(solution)/shard_map/while/body/eval_jaxpr/pallas_call | solution.py:163
  135.1 1.1 dynamic-slice_bitcast_fusion.4.top_ref
  136.2 6.7 %eval_jaxpr.16 = f32[32,640]{1,0:T(8,128)S(1)} custom-call(bf16[32,8192]{1,0:T(8,128)(2,1)S(1)} %dynamic-slice_bitcast_fusion.4.top_ref, bf16[32,8192]{1,0:T(8,128)(2,1)S(1)} %copy.47.x_ref.up_ref, bf16[640,8192]{1,0:T(8,128)(2,1)} %get-tuple-element.811.w_ref), custom_call_target="tpu_custom_call" | custom-call | flops 335544320 | bytes 11616256 | tf_op jit(solution)/shard_map/while/body/eval_jaxpr/pallas_call | solution.py:37
  143.3 4.5 fusion.30
  148.6 21.5 %eval_jaxpr.17 = (bf16[32,512]{1,0:T(8,128)(2,1)S(1)}, bf16[32,8192]{1,0:T(8,128)(2,1)S(1)}, f32[1,512]{1,0:T(1,128)S(1)}) custom-call(bf16[32,8192]{1,0:T(8,128)(2,1)S(1)} %get-tuple-element.738.x_ref, f32[32,128]{1,0:T(8,128)S(1)} %scatter.19.s_ref, f32[32,512]{1,0:T(8,128)S(1)} %dynamic-slice_bitcast_fusion.5.normed_ref, f32[32,1]{1,0:T(8,128)S(1)} %copy.25.inv_ref, ...), custom_call_target="tpu_custom_call" | custom-call | tf_op jit(solution)/shard_map/while/body/eval_jaxpr/pallas_call | solution.py:163
  172.2 6.7 %eval_jaxpr.16 = f32[32,640]{1,0:T(8,128)S(1)} custom-call(bf16[32,8192]{1,0:T(8,128)(2,1)S(1)} %dynamic-slice_bitcast_fusion.4.top_ref, bf16[32,8192]{1,0:T(8,128)(2,1)S(1)} %copy.47.x_ref.up_ref, bf16[640,8192]{1,0:T(8,128)(2,1)} %get-tuple-element.811.w_ref), custom_call_target="tpu_custom_call" | custom-call | flops 335544320 | bytes 11616256 | tf_op jit(solution)/shard_map/while/body/eval_jaxpr/pallas_call | solution.py:37
  179.4 4.5 fusion.30
  184.6 22.4 %eval_jaxpr.17 = (bf16[32,512]{1,0:T(8,128)(2,1)S(1)}, bf16[32,8192]{1,0:T(8,128)(2,1)S(1)}, f32[1,512]{1,0:T(1,128)S(1)}) custom-call(bf16[32,8192]{1,0:T(8,128)(2,1)S(1)} %get-tuple-element.738.x_ref, f32[32,128]{1,0:T(8,128)S(1)} %scatter.19.s_ref, f32[32,512]{1,0:T(8,128)S(1)} %dynamic-slice_bitcast_fusion.5.normed_ref, f32[32,1]{1,0:T(8,128)S(1)} %copy.25.inv_ref, ...), custom_call_target="tpu_custom_call" | custom-call | tf_op jit(solution)/shard_map/while/body/eval_jaxpr/pallas_call | solution.py:163
  208.0 1.1 dynamic-slice_bitcast_fusion.4.top_ref
  209.1 6.7 %eval_jaxpr.16 = f32[32,640]{1,0:T(8,128)S(1)} custom-call(bf16[32,8192]{1,0:T(8,128)(2,1)S(1)} %dynamic-slice_bitcast_fusion.4.top_ref, bf16[32,8192]{1,0:T(8,128)(2,1)S(1)} %copy.47.x_ref.up_ref, bf16[640,8192]{1,0:T(8,128)(2,1)} %get-tuple-element.811.w_ref), custom_call_target="tpu_custom_call" | custom-call | flops 335544320 | bytes 11616256 | tf_op jit(solution)/shard_map/while/body/eval_jaxpr/pallas_call | solution.py:37
  216.2 4.5 fusion.30
  221.5 25.8 %eval_jaxpr.17 = (bf16[32,512]{1,0:T(8,128)(2,1)S(1)}, bf16[32,8192]{1,0:T(8,128)(2,1)S(1)}, f32[1,512]{1,0:T(1,128)S(1)}) custom-call(bf16[32,8192]{1,0:T(8,128)(2,1)S(1)} %get-tuple-element.738.x_ref, f32[32,128]{1,0:T(8,128)S(1)} %scatter.19.s_ref, f32[32,512]{1,0:T(8,128)S(1)} %dynamic-slice_bitcast_fusion.5.normed_ref, f32[32,1]{1,0:T(8,128)S(1)} %copy.25.inv_ref, ...), custom_call_target="tpu_custom_call" | custom-call | tf_op jit(solution)/shard_map/while/body/eval_jaxpr/pallas_call | solution.py:163
  249.4 6.7 %eval_jaxpr.16 = f32[32,640]{1,0:T(8,128)S(1)} custom-call(bf16[32,8192]{1,0:T(8,128)(2,1)S(1)} %dynamic-slice_bitcast_fusion.4.top_ref, bf16[32,8192]{1,0:T(8,128)(2,1)S(1)} %copy.47.x_ref.up_ref, bf16[640,8192]{1,0:T(8,128)(2,1)} %get-tuple-element.811.w_ref), custom_call_target="tpu_custom_call" | custom-call | flops 335544320 | bytes 11616256 | tf_op jit(solution)/shard_map/while/body/eval_jaxpr/pallas_call | solution.py:37
  256.6 4.5 fusion.30
  261.8 23.6 %eval_jaxpr.17 = (bf16[32,512]{1,0:T(8,128)(2,1)S(1)}, bf16[32,8192]{1,0:T(8,128)(2,1)S(1)}, f32[1,512]{1,0:T(1,128)S(1)}) custom-call(bf16[32,8192]{1,0:T(8,128)(2,1)S(1)} %get-tuple-element.738.x_ref, f32[32,128]{1,0:T(8,128)S(1)} %scatter.19.s_ref, f32[32,512]{1,0:T(8,128)S(1)} %dynamic-slice_bitcast_fusion.5.normed_ref, f32[32,1]{1,0:T(8,128)S(1)} %copy.25.inv_ref, ...), custom_call_target="tpu_custom_call" | custom-call | tf_op jit(solution)/shard_map/while/body/eval_jaxpr/pallas_call | solution.py:163
  286.5 1.1 dynamic-slice_bitcast_fusion.4.top_ref
  287.6 6.7 %eval_jaxpr.16 = f32[32,640]{1,0:T(8,128)S(1)} custom-call(bf16[32,8192]{1,0:T(8,128)(2,1)S(1)} %dynamic-slice_bitcast_fusion.4.top_ref, bf16[32,8192]{1,0:T(8,128)(2,1)S(1)} %copy.47.x_ref.up_ref, bf16[640,8192]{1,0:T(8,128)(2,1)} %get-tuple-element.811.w_ref), custom_call_target="tpu_custom_call" | custom-call | flops 335544320 | bytes 11616256 | tf_op jit(solution)/shard_map/while/body/eval_jaxpr/pallas_call | solution.py:37
  294.7 4.5 fusion.30
  300.0 24.0 %eval_jaxpr.17 = (bf16[32,512]{1,0:T(8,128)(2,1)S(1)}, bf16[32,8192]{1,0:T(8,128)(2,1)S(1)}, f32[1,512]{1,0:T(1,128)S(1)}) custom-call(bf16[32,8192]{1,0:T(8,128)(2,1)S(1)} %get-tuple-element.738.x_ref, f32[32,128]{1,0:T(8,128)S(1)} %scatter.19.s_ref, f32[32,512]{1,0:T(8,128)S(1)} %dynamic-slice_bitcast_fusion.5.normed_ref, f32[32,1]{1,0:T(8,128)S(1)} %copy.25.inv_ref, ...), custom_call_target="tpu_custom_call" | custom-call | tf_op jit(solution)/shard_map/while/body/eval_jaxpr/pallas_call | solution.py:163
  326.1 6.7 %eval_jaxpr.16 = f32[32,640]{1,0:T(8,128)S(1)} custom-call(bf16[32,8192]{1,0:T(8,128)(2,1)S(1)} %dynamic-slice_bitcast_fusion.4.top_ref, bf16[32,8192]{1,0:T(8,128)(2,1)S(1)} %copy.47.x_ref.up_ref, bf16[640,8192]{1,0:T(8,128)(2,1)} %get-tuple-element.811.w_ref), custom_call_target="tpu_custom_call" | custom-call | flops 335544320 | bytes 11616256 | tf_op jit(solution)/shard_map/while/body/eval_jaxpr/pallas_call | solution.py:37
  333.2 4.5 fusion.30
  338.5 24.8 %eval_jaxpr.17 = (bf16[32,512]{1,0:T(8,128)(2,1)S(1)}, bf16[32,8192]{1,0:T(8,128)(2,1)S(1)}, f32[1,512]{1,0:T(1,128)S(1)}) custom-call(bf16[32,8192]{1,0:T(8,128)(2,1)S(1)} %get-tuple-element.738.x_ref, f32[32,128]{1,0:T(8,128)S(1)} %scatter.19.s_ref, f32[32,512]{1,0:T(8,128)S(1)} %dynamic-slice_bitcast_fusion.5.normed_ref, f32[32,1]{1,0:T(8,128)S(1)} %copy.25.inv_ref, ...), custom_call_target="tpu_custom_call" | custom-call | tf_op jit(solution)/shard_map/while/body/eval_jaxpr/pallas_call | solution.py:163
  364.4 1.1 dynamic-slice_bitcast_fusion.4.top_ref
  365.5 6.7 %eval_jaxpr.16 = f32[32,640]{1,0:T(8,128)S(1)} custom-call(bf16[32,8192]{1,0:T(8,128)(2,1)S(1)} %dynamic-slice_bitcast_fusion.4.top_ref, bf16[32,8192]{1,0:T(8,128)(2,1)S(1)} %copy.47.x_ref.up_ref, bf16[640,8192]{1,0:T(8,128)(2,1)} %get-tuple-element.811.w_ref), custom_call_target="tpu_custom_call" | custom-call | flops 335544320 | bytes 11616256 | tf_op jit(solution)/shard_map/while/body/eval_jaxpr/pallas_call | solution.py:37
  372.6 4.5 fusion.30
  377.9 22.6 %eval_jaxpr.17 = (bf16[32,512]{1,0:T(8,128)(2,1)S(1)}, bf16[32,8192]{1,0:T(8,128)(2,1)S(1)}, f32[1,512]{1,0:T(1,128)S(1)}) custom-call(bf16[32,8192]{1,0:T(8,128)(2,1)S(1)} %get-tuple-element.738.x_ref, f32[32,128]{1,0:T(8,128)S(1)} %scatter.19.s_ref, f32[32,512]{1,0:T(8,128)S(1)} %dynamic-slice_bitcast_fusion.5.normed_ref, f32[32,1]{1,0:T(8,128)S(1)} %copy.25.inv_ref, ...), custom_call_target="tpu_custom_call" | custom-call | tf_op jit(solution)/shard_map/while/body/eval_jaxpr/pallas_call | solution.py:163
  401.5 1.1 dynamic-slice_bitcast_fusion.4.top_ref
  402.6 6.7 %eval_jaxpr.16 = f32[32,640]{1,0:T(8,128)S(1)} custom-call(bf16[32,8192]{1,0:T(8,128)(2,1)S(1)} %dynamic-slice_bitcast_fusion.4.top_ref, bf16[32,8192]{1,0:T(8,128)(2,1)S(1)} %copy.47.x_ref.up_ref, bf16[640,8192]{1,0:T(8,128)(2,1)} %get-tuple-element.811.w_ref), custom_call_target="tpu_custom_call" | custom-call | flops 335544320 | bytes 11616256 | tf_op jit(solution)/shard_map/while/body/eval_jaxpr/pallas_call | solution.py:37
  409.7 4.5 fusion.30
  415.0 24.4 %eval_jaxpr.17 = (bf16[32,512]{1,0:T(8,128)(2,1)S(1)}, bf16[32,8192]{1,0:T(8,128)(2,1)S(1)}, f32[1,512]{1,0:T(1,128)S(1)}) custom-call(bf16[32,8192]{1,0:T(8,128)(2,1)S(1)} %get-tuple-element.738.x_ref, f32[32,128]{1,0:T(8,128)S(1)} %scatter.19.s_ref, f32[32,512]{1,0:T(8,128)S(1)} %dynamic-slice_bitcast_fusion.5.normed_ref, f32[32,1]{1,0:T(8,128)S(1)} %copy.25.inv_ref, ...), custom_call_target="tpu_custom_call" | custom-call | tf_op jit(solution)/shard_map/while/body/eval_jaxpr/pallas_call | solution.py:163
  439.9 36.3 %all_to_all.15 = bf16[16,144,512]{2,1,0:T(8,128)(2,1)S(1)} all-to-all(bf16[16,144,512]{2,1,0:T(8,128)(2,1)S(1)} %broadcast_in_dim.91), channel_id=1, replica_groups=mesh['section'=8,'tensor'=16] {'tensor'}, dimensions={0} | all-to-all | bytes 4718592 | tf_op jit(solution)/shard_map/all_to_all | solution.py:302
  477.0 1.2 copy.21
  478.2 2.3 broadcast_in_dim_reshape.3
  (278 shorter events, 28.5 us)
Async XLA Ops:
  0.6 2.3 copy-start.1
  2.9 2.5 copy-start.2
  2.9 3.4 copy-start.6
  3.0 3.4 copy-start.7
  3.0 3.5 copy-start.5
  6.5 3.2 copy-start.3
  11.8 7.1 %copy-start = (bf16[8192,640]{1,0:T(8,128)(2,1)S(1)}, bf16[8192,640]{1,0:T(8,128)(2,1)}, u32[]{:S(2)}) copy-start(bf16[8192,640]{1,0:T(8,128)(2,1)} %get-tuple-element.813) | copy-start | bytes 31457284 | tf_op jit(solution)/shard_map/while
  52.5 7.1 %copy-start = (bf16[8192,640]{1,0:T(8,128)(2,1)S(1)}, bf16[8192,640]{1,0:T(8,128)(2,1)}, u32[]{:S(2)}) copy-start(bf16[8192,640]{1,0:T(8,128)(2,1)} %get-tuple-element.813) | copy-start | bytes 31457284 | tf_op jit(solution)/shard_map/while
  94.9 7.1 %copy-start = (bf16[8192,640]{1,0:T(8,128)(2,1)S(1)}, bf16[8192,640]{1,0:T(8,128)(2,1)}, u32[]{:S(2)}) copy-start(bf16[8192,640]{1,0:T(8,128)(2,1)} %get-tuple-element.813) | copy-start | bytes 31457284 | tf_op jit(solution)/shard_map/while
  136.2 7.1 %copy-start = (bf16[8192,640]{1,0:T(8,128)(2,1)S(1)}, bf16[8192,640]{1,0:T(8,128)(2,1)}, u32[]{:S(2)}) copy-start(bf16[8192,640]{1,0:T(8,128)(2,1)} %get-tuple-element.813) | copy-start | bytes 31457284 | tf_op jit(solution)/shard_map/while
  172.2 7.1 %copy-start = (bf16[8192,640]{1,0:T(8,128)(2,1)S(1)}, bf16[8192,640]{1,0:T(8,128)(2,1)}, u32[]{:S(2)}) copy-start(bf16[8192,640]{1,0:T(8,128)(2,1)} %get-tuple-element.813) | copy-start | bytes 31457284 | tf_op jit(solution)/shard_map/while
  209.1 7.1 %copy-start = (bf16[8192,640]{1,0:T(8,128)(2,1)S(1)}, bf16[8192,640]{1,0:T(8,128)(2,1)}, u32[]{:S(2)}) copy-start(bf16[8192,640]{1,0:T(8,128)(2,1)} %get-tuple-element.813) | copy-start | bytes 31457284 | tf_op jit(solution)/shard_map/while
  249.4 7.1 %copy-start = (bf16[8192,640]{1,0:T(8,128)(2,1)S(1)}, bf16[8192,640]{1,0:T(8,128)(2,1)}, u32[]{:S(2)}) copy-start(bf16[8192,640]{1,0:T(8,128)(2,1)} %get-tuple-element.813) | copy-start | bytes 31457284 | tf_op jit(solution)/shard_map/while
  287.6 7.1 %copy-start = (bf16[8192,640]{1,0:T(8,128)(2,1)S(1)}, bf16[8192,640]{1,0:T(8,128)(2,1)}, u32[]{:S(2)}) copy-start(bf16[8192,640]{1,0:T(8,128)(2,1)} %get-tuple-element.813) | copy-start | bytes 31457284 | tf_op jit(solution)/shard_map/while
  326.1 7.1 %copy-start = (bf16[8192,640]{1,0:T(8,128)(2,1)S(1)}, bf16[8192,640]{1,0:T(8,128)(2,1)}, u32[]{:S(2)}) copy-start(bf16[8192,640]{1,0:T(8,128)(2,1)} %get-tuple-element.813) | copy-start | bytes 31457284 | tf_op jit(solution)/shard_map/while
  365.4 7.1 %copy-start = (bf16[8192,640]{1,0:T(8,128)(2,1)S(1)}, bf16[8192,640]{1,0:T(8,128)(2,1)}, u32[]{:S(2)}) copy-start(bf16[8192,640]{1,0:T(8,128)(2,1)} %get-tuple-element.813) | copy-start | bytes 31457284 | tf_op jit(solution)/shard_map/while
  402.6 7.1 %copy-start = (bf16[8192,640]{1,0:T(8,128)(2,1)S(1)}, bf16[8192,640]{1,0:T(8,128)(2,1)}, u32[]{:S(2)}) copy-start(bf16[8192,640]{1,0:T(8,128)(2,1)} %get-tuple-element.813) | copy-start | bytes 31457284 | tf_op jit(solution)/shard_map/while
  439.5 36.7 %copy-start.4 = (f32[4,640]{1,0:T(4,128)}, f32[4,640]{1,0:T(4,128)S(1)}, u32[]{:S(2)}) copy-start(f32[4,640]{1,0:T(4,128)S(1)} %get-tuple-element.455) | copy-start | bytes 30724

commit v11 on v10

--- a/solution.py
+++ b/solution.py
@@ -113,7 +113,7 @@
         total = total + recv[src].astype(jnp.float32)
         stat_total = stat_total + srecv[src]
     rows = total.shape[0]
-    row_mean = stat_total[:, 0:1] * (1.0 / (n * width))
+    row_mean = jnp.transpose(stat_total)[:rows, 0:1] * (1.0 / (n * width))
     normed = normed_ref[...]
     d_in = inv_ref[...] * (total * gain_ref[...] - normed * row_mean)
     upstream = jnp.where(sec == n_sec - 1, top_ref[:, mine], up_ref[:, mine])
@@ -270,7 +270,7 @@
         normed = rows_of(normed_all, batch_slot, row_start, chunk_len)
         inv_rms = rows_of(inv_rms_all, batch_slot, row_start, chunk_len)
         row_part = jnp.sum(partial.astype(jnp.float32) * gain_vec * normed, axis=-1)
-        stats = jnp.zeros((chunk_len, 128), jnp.float32).at[:, 0].set(row_part)
+        stats = jnp.zeros((8, 128), jnp.float32).at[0, :chunk_len].set(row_part)
         normed_own = rows_of(normed_own_all, batch_slot, row_start, chunk_len)
         grad_out, incoming_next, gain_part = layer_exchange(
             partial, stats, normed_own, inv_rms, gain_own[None, :], top_chunk, incoming, tensors, sections, width

time: 482 us -> 472 us (0.979)
  Pallas kernels: 343 us -> 323 us
  local copies, waits for them, and re-layouts: 23.5 us -> 35.2 us
    pallas_call x11, Pallas kernels: 270 us -> 250 us  [layer_exchange(): pl.pallas_call(functools.partial(layer_exchange_kernel, n, n_sec, width),...]
    another operation x22 -> x0, other arithmetic: 14 us -> none
    slice x11, local copies, waits for them, and re-layouts: 0.36 us -> 9.7 us  [conv_block(): d_vals = d_vals + weights[lag_idx] * padded_back[lag_idx:lag_idx + length]]
    convert_element_type x11, other arithmetic: 0.28 us -> 9.23 us  [step_rows(): ext_vals = lax.dynamic_slice(conv_padded, (batch_slot, row_start, 0), (1,...]
    while x33 -> x165, local copies, waits for them, and re-layouts: 2.92 us -> 8.73 us
where the time goes in v11:
time: 472 us; the launch traced here: 469 us
  Pallas kernels  323 us (68%)
  matrix products  50 us (11%)
  blocking collectives  37.2 us (8%)
  local copies, waits for them, and re-layouts  35.2 us (7%)
  other arithmetic  20.6 us (4%)
    pallas_call x11, Pallas kernels, layer_exchange(): pl.pallas_call(functools.partial(layer_exchange_kernel, n, n_sec, width),...  250 us
    pallas_call x11, Pallas kernels, matmul_nt(): pl.pallas_call(functools.partial(matmul_nt_kernel, n_sec), out_shape=jax....  73.4 us
    dot_general x11, matrix products, step_rows(): lax.dot_general(d_vals, w_in, contract, preferred_element_type=jnp.float32)  50 us
    all_to_all x1, blocking collectives, local(): lax.all_to_all(copies, 'tensor', split_axis=0, concat_axis=2, tiled=True)[0]  37.2 us
    slice x11, local copies, waits for them, and re-layouts, conv_block(): d_vals = d_vals + weights[lag_idx] * padded_back[lag_idx:lag_idx + length]  9.7 us
    squeeze x44, local copies, waits for them, and re-layouts, rows_of(): lax.dynamic_slice(array, (batch_slot, first_row, 0), (1, row_count, array...  9.55 us

profile of v11, /device:TPU:32, one launch (start us, length us, event | category | flops | bytes accessed | tf_op | source)
XLA Modules:
  0.0 469.0 jit_solution(17775291131458429243)
XLA Ops:
  0.7 2.3 fusion.19
  3.5 3.1 convert_multiply_fusion
  6.7 1.3 constant_dynamic-slice_fusion.1
  7.9 1.0 constant_dynamic-slice_fusion.2
  9.7 1.8 broadcast_select_fusion.1
  11.6 414.8 %while.27 = (s32[]{:T(128)}, bf16[32,8192]{1,0:T(8,128)(2,1)S(1)}, bf16[2,2,32,512]{3,2,1,0:T(8,128)(2,1)S(1)}, f32[512]{0:T(512)}, f32[4,640]{1,0:T(4,128)}, /*...) while((s32[]{:T(128)}, bf16[32,8192]{1,0:T(8,128)(2,1)S(1)}, ...), condition=%wide.region_7.8_spmd.clone, body=%wide.region_1.7_spmd.clone.sunk | while | flops 673154560 | bytes 69001512 | solution.py:295
  12.5 0.9 slice_reduce_fusion.5
  14.4 6.7 %eval_jaxpr.16 = f32[32,640]{1,0:T(8,128)S(1)} custom-call(bf16[32,8192]{1,0:T(8,128)(2,1)S(1)} %dynamic-slice_bitcast_fusion.4.top_ref, bf16[32,8192]{1,0:T(8,128)(2,1)S(1)} %copy.42.x_ref.up_ref, bf16[640,8192]{1,0:T(8,128)(2,1)} %get-tuple-element.812.w_ref), custom_call_target="tpu_custom_call" | custom-call | flops 335544320 | bytes 11616256 | tf_op jit(solution)/shard_map/while/body/eval_jaxpr/pallas_call | solution.py:37
  21.5 4.5 fusion.28
  26.1 23.8 %eval_jaxpr.17 = (bf16[32,512]{1,0:T(8,128)(2,1)S(1)}, bf16[32,8192]{1,0:T(8,128)(2,1)S(1)}, f32[1,512]{1,0:T(1,128)S(1)}) custom-call(bf16[32,8192]{1,0:T(8,128)(2,1)S(1)} %get-tuple-element.739.x_ref, f32[8,128]{1,0:T(8,128)S(1)} %scatter.19.s_ref, f32[32,512]{1,0:T(8,128)S(1)} %dynamic-slice_bitcast_fusion.5.normed_ref, f32[32,1]{1,0:T(8,128)S(1)} %copy.20.inv_ref, ...), custom_call_target="tpu_custom_call" | custom-call | tf_op jit(solution)/shard_map/while/body/eval_jaxpr/pallas_call | solution.py:163
  51.3 0.9 slice_reduce_fusion.5
  53.2 6.7 %eval_jaxpr.16 = f32[32,640]{1,0:T(8,128)S(1)} custom-call(bf16[32,8192]{1,0:T(8,128)(2,1)S(1)} %dynamic-slice_bitcast_fusion.4.top_ref, bf16[32,8192]{1,0:T(8,128)(2,1)S(1)} %copy.42.x_ref.up_ref, bf16[640,8192]{1,0:T(8,128)(2,1)} %get-tuple-element.812.w_ref), custom_call_target="tpu_custom_call" | custom-call | flops 335544320 | bytes 11616256 | tf_op jit(solution)/shard_map/while/body/eval_jaxpr/pallas_call | solution.py:37
  60.3 4.5 fusion.28
  64.9 26.5 %eval_jaxpr.17 = (bf16[32,512]{1,0:T(8,128)(2,1)S(1)}, bf16[32,8192]{1,0:T(8,128)(2,1)S(1)}, f32[1,512]{1,0:T(1,128)S(1)}) custom-call(bf16[32,8192]{1,0:T(8,128)(2,1)S(1)} %get-tuple-element.739.x_ref, f32[8,128]{1,0:T(8,128)S(1)} %scatter.19.s_ref, f32[32,512]{1,0:T(8,128)S(1)} %dynamic-slice_bitcast_fusion.5.normed_ref, f32[32,1]{1,0:T(8,128)S(1)} %copy.20.inv_ref, ...), custom_call_target="tpu_custom_call" | custom-call | tf_op jit(solution)/shard_map/while/body/eval_jaxpr/pallas_call | solution.py:163
  92.9 0.9 slice_reduce_fusion.5
  94.8 6.7 %eval_jaxpr.16 = f32[32,640]{1,0:T(8,128)S(1)} custom-call(bf16[32,8192]{1,0:T(8,128)(2,1)S(1)} %dynamic-slice_bitcast_fusion.4.top_ref, bf16[32,8192]{1,0:T(8,128)(2,1)S(1)} %copy.42.x_ref.up_ref, bf16[640,8192]{1,0:T(8,128)(2,1)} %get-tuple-element.812.w_ref), custom_call_target="tpu_custom_call" | custom-call | flops 335544320 | bytes 11616256 | tf_op jit(solution)/shard_map/while/body/eval_jaxpr/pallas_call | solution.py:37
  101.9 4.5 fusion.28
  106.5 22.3 %eval_jaxpr.17 = (bf16[32,512]{1,0:T(8,128)(2,1)S(1)}, bf16[32,8192]{1,0:T(8,128)(2,1)S(1)}, f32[1,512]{1,0:T(1,128)S(1)}) custom-call(bf16[32,8192]{1,0:T(8,128)(2,1)S(1)} %get-tuple-element.739.x_ref, f32[8,128]{1,0:T(8,128)S(1)} %scatter.19.s_ref, f32[32,512]{1,0:T(8,128)S(1)} %dynamic-slice_bitcast_fusion.5.normed_ref, f32[32,1]{1,0:T(8,128)S(1)} %copy.20.inv_ref, ...), custom_call_target="tpu_custom_call" | custom-call | tf_op jit(solution)/shard_map/while/body/eval_jaxpr/pallas_call | solution.py:163
  130.3 0.9 slice_reduce_fusion.5
  132.1 6.7 %eval_jaxpr.16 = f32[32,640]{1,0:T(8,128)S(1)} custom-call(bf16[32,8192]{1,0:T(8,128)(2,1)S(1)} %dynamic-slice_bitcast_fusion.4.top_ref, bf16[32,8192]{1,0:T(8,128)(2,1)S(1)} %copy.42.x_ref.up_ref, bf16[640,8192]{1,0:T(8,128)(2,1)} %get-tuple-element.812.w_ref), custom_call_target="tpu_custom_call" | custom-call | flops 335544320 | bytes 11616256 | tf_op jit(solution)/shard_map/while/body/eval_jaxpr/pallas_call | solution.py:37
  139.2 4.5 fusion.28
  143.8 20.9 %eval_jaxpr.17 = (bf16[32,512]{1,0:T(8,128)(2,1)S(1)}, bf16[32,8192]{1,0:T(8,128)(2,1)S(1)}, f32[1,512]{1,0:T(1,128)S(1)}) custom-call(bf16[32,8192]{1,0:T(8,128)(2,1)S(1)} %get-tuple-element.739.x_ref, f32[8,128]{1,0:T(8,128)S(1)} %scatter.19.s_ref, f32[32,512]{1,0:T(8,128)S(1)} %dynamic-slice_bitcast_fusion.5.normed_ref, f32[32,1]{1,0:T(8,128)S(1)} %copy.20.inv_ref, ...), custom_call_target="tpu_custom_call" | custom-call | tf_op jit(solution)/shard_map/while/body/eval_jaxpr/pallas_call | solution.py:163
  166.2 0.9 slice_reduce_fusion.5
  168.1 6.7 %eval_jaxpr.16 = f32[32,640]{1,0:T(8,128)S(1)} custom-call(bf16[32,8192]{1,0:T(8,128)(2,1)S(1)} %dynamic-slice_bitcast_fusion.4.top_ref, bf16[32,8192]{1,0:T(8,128)(2,1)S(1)} %copy.42.x_ref.up_ref, bf16[640,8192]{1,0:T(8,128)(2,1)} %get-tuple-element.812.w_ref), custom_call_target="tpu_custom_call" | custom-call | flops 335544320 | bytes 11616256 | tf_op jit(solution)/shard_map/while/body/eval_jaxpr/pallas_call | solution.py:37
  175.2 4.5 fusion.28
  179.8 23.6 %eval_jaxpr.17 = (bf16[32,512]{1,0:T(8,128)(2,1)S(1)}, bf16[32,8192]{1,0:T(8,128)(2,1)S(1)}, f32[1,512]{1,0:T(1,128)S(1)}) custom-call(bf16[32,8192]{1,0:T(8,128)(2,1)S(1)} %get-tuple-element.739.x_ref, f32[8,128]{1,0:T(8,128)S(1)} %scatter.19.s_ref, f32[32,512]{1,0:T(8,128)S(1)} %dynamic-slice_bitcast_fusion.5.normed_ref, f32[32,1]{1,0:T(8,128)S(1)} %copy.20.inv_ref, ...), custom_call_target="tpu_custom_call" | custom-call | tf_op jit(solution)/shard_map/while/body/eval_jaxpr/pallas_call | solution.py:163
  204.8 0.9 slice_reduce_fusion.5
  206.7 6.7 %eval_jaxpr.16 = f32[32,640]{1,0:T(8,128)S(1)} custom-call(bf16[32,8192]{1,0:T(8,128)(2,1)S(1)} %dynamic-slice_bitcast_fusion.4.top_ref, bf16[32,8192]{1,0:T(8,128)(2,1)S(1)} %copy.42.x_ref.up_ref, bf16[640,8192]{1,0:T(8,128)(2,1)} %get-tuple-element.812.w_ref), custom_call_target="tpu_custom_call" | custom-call | flops 335544320 | bytes 11616256 | tf_op jit(solution)/shard_map/while/body/eval_jaxpr/pallas_call | solution.py:37
  213.8 4.5 fusion.28
  218.4 19.9 %eval_jaxpr.17 = (bf16[32,512]{1,0:T(8,128)(2,1)S(1)}, bf16[32,8192]{1,0:T(8,128)(2,1)S(1)}, f32[1,512]{1,0:T(1,128)S(1)}) custom-call(bf16[32,8192]{1,0:T(8,128)(2,1)S(1)} %get-tuple-element.739.x_ref, f32[8,128]{1,0:T(8,128)S(1)} %scatter.19.s_ref, f32[32,512]{1,0:T(8,128)S(1)} %dynamic-slice_bitcast_fusion.5.normed_ref, f32[32,1]{1,0:T(8,128)S(1)} %copy.20.inv_ref, ...), custom_call_target="tpu_custom_call" | custom-call | tf_op jit(solution)/shard_map/while/body/eval_jaxpr/pallas_call | solution.py:163
  241.6 6.7 %eval_jaxpr.16 = f32[32,640]{1,0:T(8,128)S(1)} custom-call(bf16[32,8192]{1,0:T(8,128)(2,1)S(1)} %dynamic-slice_bitcast_fusion.4.top_ref, bf16[32,8192]{1,0:T(8,128)(2,1)S(1)} %copy.42.x_ref.up_ref, bf16[640,8192]{1,0:T(8,128)(2,1)} %get-tuple-element.812.w_ref), custom_call_target="tpu_custom_call" | custom-call | flops 335544320 | bytes 11616256 | tf_op jit(solution)/shard_map/while/body/eval_jaxpr/pallas_call | solution.py:37
  248.8 4.5 fusion.28
  253.4 24.8 %eval_jaxpr.17 = (bf16[32,512]{1,0:T(8,128)(2,1)S(1)}, bf16[32,8192]{1,0:T(8,128)(2,1)S(1)}, f32[1,512]{1,0:T(1,128)S(1)}) custom-call(bf16[32,8192]{1,0:T(8,128)(2,1)S(1)} %get-tuple-element.739.x_ref, f32[8,128]{1,0:T(8,128)S(1)} %scatter.19.s_ref, f32[32,512]{1,0:T(8,128)S(1)} %dynamic-slice_bitcast_fusion.5.normed_ref, f32[32,1]{1,0:T(8,128)S(1)} %copy.20.inv_ref, ...), custom_call_target="tpu_custom_call" | custom-call | tf_op jit(solution)/shard_map/while/body/eval_jaxpr/pallas_call | solution.py:163
  281.4 6.7 %eval_jaxpr.16 = f32[32,640]{1,0:T(8,128)S(1)} custom-call(bf16[32,8192]{1,0:T(8,128)(2,1)S(1)} %dynamic-slice_bitcast_fusion.4.top_ref, bf16[32,8192]{1,0:T(8,128)(2,1)S(1)} %copy.42.x_ref.up_ref, bf16[640,8192]{1,0:T(8,128)(2,1)} %get-tuple-element.812.w_ref), custom_call_target="tpu_custom_call" | custom-call | flops 335544320 | bytes 11616256 | tf_op jit(solution)/shard_map/while/body/eval_jaxpr/pallas_call | solution.py:37
  288.5 4.5 fusion.28
  293.1 20.0 %eval_jaxpr.17 = (bf16[32,512]{1,0:T(8,128)(2,1)S(1)}, bf16[32,8192]{1,0:T(8,128)(2,1)S(1)}, f32[1,512]{1,0:T(1,128)S(1)}) custom-call(bf16[32,8192]{1,0:T(8,128)(2,1)S(1)} %get-tuple-element.739.x_ref, f32[8,128]{1,0:T(8,128)S(1)} %scatter.19.s_ref, f32[32,512]{1,0:T(8,128)S(1)} %dynamic-slice_bitcast_fusion.5.normed_ref, f32[32,1]{1,0:T(8,128)S(1)} %copy.20.inv_ref, ...), custom_call_target="tpu_custom_call" | custom-call | tf_op jit(solution)/shard_map/while/body/eval_jaxpr/pallas_call | solution.py:163
  316.4 6.7 %eval_jaxpr.16 = f32[32,640]{1,0:T(8,128)S(1)} custom-call(bf16[32,8192]{1,0:T(8,128)(2,1)S(1)} %dynamic-slice_bitcast_fusion.4.top_ref, bf16[32,8192]{1,0:T(8,128)(2,1)S(1)} %copy.42.x_ref.up_ref, bf16[640,8192]{1,0:T(8,128)(2,1)} %get-tuple-element.812.w_ref), custom_call_target="tpu_custom_call" | custom-call | flops 335544320 | bytes 11616256 | tf_op jit(solution)/shard_map/while/body/eval_jaxpr/pallas_call | solution.py:37
  323.5 4.5 fusion.28
  328.1 22.9 %eval_jaxpr.17 = (bf16[32,512]{1,0:T(8,128)(2,1)S(1)}, bf16[32,8192]{1,0:T(8,128)(2,1)S(1)}, f32[1,512]{1,0:T(1,128)S(1)}) custom-call(bf16[32,8192]{1,0:T(8,128)(2,1)S(1)} %get-tuple-element.739.x_ref, f32[8,128]{1,0:T(8,128)S(1)} %scatter.19.s_ref, f32[32,512]{1,0:T(8,128)S(1)} %dynamic-slice_bitcast_fusion.5.normed_ref, f32[32,1]{1,0:T(8,128)S(1)} %copy.20.inv_ref, ...), custom_call_target="tpu_custom_call" | custom-call | tf_op jit(solution)/shard_map/while/body/eval_jaxpr/pallas_call | solution.py:163
  354.3 6.7 %eval_jaxpr.16 = f32[32,640]{1,0:T(8,128)S(1)} custom-call(bf16[32,8192]{1,0:T(8,128)(2,1)S(1)} %dynamic-slice_bitcast_fusion.4.top_ref, bf16[32,8192]{1,0:T(8,128)(2,1)S(1)} %copy.42.x_ref.up_ref, bf16[640,8192]{1,0:T(8,128)(2,1)} %get-tuple-element.812.w_ref), custom_call_target="tpu_custom_call" | custom-call | flops 335544320 | bytes 11616256 | tf_op jit(solution)/shard_map/while/body/eval_jaxpr/pallas_call | solution.py:37
  361.4 4.5 fusion.28
  366.0 21.8 %eval_jaxpr.17 = (bf16[32,512]{1,0:T(8,128)(2,1)S(1)}, bf16[32,8192]{1,0:T(8,128)(2,1)S(1)}, f32[1,512]{1,0:T(1,128)S(1)}) custom-call(bf16[32,8192]{1,0:T(8,128)(2,1)S(1)} %get-tuple-element.739.x_ref, f32[8,128]{1,0:T(8,128)S(1)} %scatter.19.s_ref, f32[32,512]{1,0:T(8,128)S(1)} %dynamic-slice_bitcast_fusion.5.normed_ref, f32[32,1]{1,0:T(8,128)S(1)} %copy.20.inv_ref, ...), custom_call_target="tpu_custom_call" | custom-call | tf_op jit(solution)/shard_map/while/body/eval_jaxpr/pallas_call | solution.py:163
  391.1 6.7 %eval_jaxpr.16 = f32[32,640]{1,0:T(8,128)S(1)} custom-call(bf16[32,8192]{1,0:T(8,128)(2,1)S(1)} %dynamic-slice_bitcast_fusion.4.top_ref, bf16[32,8192]{1,0:T(8,128)(2,1)S(1)} %copy.42.x_ref.up_ref, bf16[640,8192]{1,0:T(8,128)(2,1)} %get-tuple-element.812.w_ref), custom_call_target="tpu_custom_call" | custom-call | flops 335544320 | bytes 11616256 | tf_op jit(solution)/shard_map/while/body/eval_jaxpr/pallas_call | solution.py:37
  398.2 4.5 fusion.28
  402.8 23.0 %eval_jaxpr.17 = (bf16[32,512]{1,0:T(8,128)(2,1)S(1)}, bf16[32,8192]{1,0:T(8,128)(2,1)S(1)}, f32[1,512]{1,0:T(1,128)S(1)}) custom-call(bf16[32,8192]{1,0:T(8,128)(2,1)S(1)} %get-tuple-element.739.x_ref, f32[8,128]{1,0:T(8,128)S(1)} %scatter.19.s_ref, f32[32,512]{1,0:T(8,128)S(1)} %dynamic-slice_bitcast_fusion.5.normed_ref, f32[32,1]{1,0:T(8,128)S(1)} %copy.20.inv_ref, ...), custom_call_target="tpu_custom_call" | custom-call | tf_op jit(solution)/shard_map/while/body/eval_jaxpr/pallas_call | solution.py:163
  427.5 37.2 %all_to_all.15 = bf16[16,144,512]{2,1,0:T(8,128)(2,1)S(1)} all-to-all(bf16[16,144,512]{2,1,0:T(8,128)(2,1)S(1)} %broadcast_in_dim.91), channel_id=1, replica_groups=mesh['section'=8,'tensor'=16] {'tensor'}, dimensions={0} | all-to-all | bytes 4718592 | tf_op jit(solution)/shard_map/all_to_all | solution.py:302
  465.5 1.2 copy.18
  466.7 2.3 broadcast_in_dim_reshape.3
  (371 shorter events, 37.6 us)
Async XLA Ops:
  3.5 5.4 %copy-start.9 = (s32[2,64]{1,0:T(2,128)S(1)}, s32[2,64]{1,0:T(2,128)}, u32[]{:S(2)}) copy-start(s32[2,64]{1,0:T(2,128)} %param.18) | copy-start | bytes 1540
  3.5 5.4 %copy-start.10 = (s32[2]{0:T(128)S(1)}, s32[2]{0:T(128)}, u32[]{:S(2)}) copy-start(s32[2]{0:T(128)} %param.19) | copy-start | bytes 28
  3.5 5.5 %copy-start.6 = (bf16[1,2,64,640]{3,2,1,0:T(8,128)(2,1)S(1)}, bf16[1,2,64,640]{3,2,1,0:T(8,128)(2,1)}, u32[]{:S(2)}) copy-start(bf16[1,2,64,640]{3,2,1,0:T(8,128)(2,1)} %param.21) | copy-start | bytes 491524
  14.3 6.9 %copy-start.2 = (f32[4,640]{1,0:T(4,128)S(1)}, f32[4,640]{1,0:T(4,128)}, u32[]{:S(2)}) copy-start(f32[4,640]{1,0:T(4,128)} %get-tuple-element.780) | copy-start | bytes 30724 | tf_op jit(solution)/shard_map/while
  14.3 6.9 %copy-start.4 = (f32[3,640]{1,0:T(4,128)S(1)}, f32[3,640]{1,0:T(4,128)}, u32[]{:S(2)}) copy-start(f32[3,640]{1,0:T(4,128)} %get-tuple-element.781) | copy-start | bytes 23044 | tf_op jit(solution)/shard_map/while
  14.3 7.1 %copy-start = (bf16[8192,640]{1,0:T(8,128)(2,1)S(1)}, bf16[8192,640]{1,0:T(8,128)(2,1)}, u32[]{:S(2)}) copy-start(bf16[8192,640]{1,0:T(8,128)(2,1)} %get-tuple-element.814) | copy-start | bytes 31457284 | tf_op jit(solution)/shard_map/while
  21.5 28.4 %copy-start.7 = (f32[512]{0:T(512)S(1)}, f32[512]{0:T(512)}, u32[]{:S(2)}) copy-start(f32[512]{0:T(512)} %get-tuple-element.779) | copy-start | bytes 6148 | tf_op jit(solution)/shard_map/while
  53.1 6.9 %copy-start.2 = (f32[4,640]{1,0:T(4,128)S(1)}, f32[4,640]{1,0:T(4,128)}, u32[]{:S(2)}) copy-start(f32[4,640]{1,0:T(4,128)} %get-tuple-element.780) | copy-start | bytes 30724 | tf_op jit(solution)/shard_map/while
  53.1 6.9 %copy-start.4 = (f32[3,640]{1,0:T(4,128)S(1)}, f32[3,640]{1,0:T(4,128)}, u32[]{:S(2)}) copy-start(f32[3,640]{1,0:T(4,128)} %get-tuple-element.781) | copy-start | bytes 23044 | tf_op jit(solution)/shard_map/while
  53.1 7.1 %copy-start = (bf16[8192,640]{1,0:T(8,128)(2,1)S(1)}, bf16[8192,640]{1,0:T(8,128)(2,1)}, u32[]{:S(2)}) copy-start(bf16[8192,640]{1,0:T(8,128)(2,1)} %get-tuple-element.814) | copy-start | bytes 31457284 | tf_op jit(solution)/shard_map/while
  60.3 31.2 %copy-start.7 = (f32[512]{0:T(512)S(1)}, f32[512]{0:T(512)}, u32[]{:S(2)}) copy-start(f32[512]{0:T(512)} %get-tuple-element.779) | copy-start | bytes 6148 | tf_op jit(solution)/shard_map/while
  94.7 6.9 %copy-start.2 = (f32[4,640]{1,0:T(4,128)S(1)}, f32[4,640]{1,0:T(4,128)}, u32[]{:S(2)}) copy-start(f32[4,640]{1,0:T(4,128)} %get-tuple-element.780) | copy-start | bytes 30724 | tf_op jit(solution)/shard_map/while
  94.7 6.9 %copy-start.4 = (f32[3,640]{1,0:T(4,128)S(1)}, f32[3,640]{1,0:T(4,128)}, u32[]{:S(2)}) copy-start(f32[3,640]{1,0:T(4,128)} %get-tuple-element.781) | copy-start | bytes 23044 | tf_op jit(solution)/shard_map/while
  94.7 7.1 %copy-start = (bf16[8192,640]{1,0:T(8,128)(2,1)S(1)}, bf16[8192,640]{1,0:T(8,128)(2,1)}, u32[]{:S(2)}) copy-start(bf16[8192,640]{1,0:T(8,128)(2,1)} %get-tuple-element.814) | copy-start | bytes 31457284 | tf_op jit(solution)/shard_map/while
  101.9 26.9 %copy-start.7 = (f32[512]{0:T(512)S(1)}, f32[512]{0:T(512)}, u32[]{:S(2)}) copy-start(f32[512]{0:T(512)} %get-tuple-element.779) | copy-start | bytes 6148 | tf_op jit(solution)/shard_map/while
  132.1 6.9 %copy-start.2 = (f32[4,640]{1,0:T(4,128)S(1)}, f32[4,640]{1,0:T(4,128)}, u32[]{:S(2)}) copy-start(f32[4,640]{1,0:T(4,128)} %get-tuple-element.780) | copy-start | bytes 30724 | tf_op jit(solution)/shard_map/while
  132.1 6.9 %copy-start.4 = (f32[3,640]{1,0:T(4,128)S(1)}, f32[3,640]{1,0:T(4,128)}, u32[]{:S(2)}) copy-start(f32[3,640]{1,0:T(4,128)} %get-tuple-element.781) | copy-start | bytes 23044 | tf_op jit(solution)/shard_map/while
  132.1 7.1 %copy-start = (bf16[8192,640]{1,0:T(8,128)(2,1)S(1)}, bf16[8192,640]{1,0:T(8,128)(2,1)}, u32[]{:S(2)}) copy-start(bf16[8192,640]{1,0:T(8,128)(2,1)} %get-tuple-element.814) | copy-start | bytes 31457284 | tf_op jit(solution)/shard_map/while
  139.0 4.8 %copy-start.3 = (f32[4,640]{1,0:T(4,128)}, f32[4,640]{1,0:T(4,128)S(1)}, u32[]{:S(2)}) copy-start(f32[4,640]{1,0:T(4,128)S(1)} %fusion.31) | copy-start | bytes 30724 | tf_op jit(solution)/shard_map/while
  139.2 25.5 %copy-start.7 = (f32[512]{0:T(512)S(1)}, f32[512]{0:T(512)}, u32[]{:S(2)}) copy-start(f32[512]{0:T(512)} %get-tuple-element.779) | copy-start | bytes 6148 | tf_op jit(solution)/shard_map/while
  168.0 6.9 %copy-start.2 = (f32[4,640]{1,0:T(4,128)S(1)}, f32[4,640]{1,0:T(4,128)}, u32[]{:S(2)}) copy-start(f32[4,640]{1,0:T(4,128)} %get-tuple-element.780) | copy-start | bytes 30724 | tf_op jit(solution)/shard_map/while
  168.0 6.9 %copy-start.4 = (f32[3,640]{1,0:T(4,128)S(1)}, f32[3,640]{1,0:T(4,128)}, u32[]{:S(2)}) copy-start(f32[3,640]{1,0:T(4,128)} %get-tuple-element.781) | copy-start | bytes 23044 | tf_op jit(solution)/shard_map/while
  168.0 7.1 %copy-start = (bf16[8192,640]{1,0:T(8,128)(2,1)S(1)}, bf16[8192,640]{1,0:T(8,128)(2,1)}, u32[]{:S(2)}) copy-start(bf16[8192,640]{1,0:T(8,128)(2,1)} %get-tuple-element.814) | copy-start | bytes 31457284 | tf_op jit(solution)/shard_map/while
  175.2 28.2 %copy-start.7 = (f32[512]{0:T(512)S(1)}, f32[512]{0:T(512)}, u32[]{:S(2)}) copy-start(f32[512]{0:T(512)} %get-tuple-element.779) | copy-start | bytes 6148 | tf_op jit(solution)/shard_map/while
  206.6 6.9 %copy-start.2 = (f32[4,640]{1,0:T(4,128)S(1)}, f32[4,640]{1,0:T(4,128)}, u32[]{:S(2)}) copy-start(f32[4,640]{1,0:T(4,128)} %get-tuple-element.780) | copy-start | bytes 30724 | tf_op jit(solution)/shard_map/while
  206.6 6.9 %copy-start.4 = (f32[3,640]{1,0:T(4,128)S(1)}, f32[3,640]{1,0:T(4,128)}, u32[]{:S(2)}) copy-start(f32[3,640]{1,0:T(4,128)} %get-tuple-element.781) | copy-start | bytes 23044 | tf_op jit(solution)/shard_map/while
  206.7 7.1 %copy-start = (bf16[8192,640]{1,0:T(8,128)(2,1)S(1)}, bf16[8192,640]{1,0:T(8,128)(2,1)}, u32[]{:S(2)}) copy-start(bf16[8192,640]{1,0:T(8,128)(2,1)} %get-tuple-element.814) | copy-start | bytes 31457284 | tf_op jit(solution)/shard_map/while
  213.8 24.5 %copy-start.7 = (f32[512]{0:T(512)S(1)}, f32[512]{0:T(512)}, u32[]{:S(2)}) copy-start(f32[512]{0:T(512)} %get-tuple-element.779) | copy-start | bytes 6148 | tf_op jit(solution)/shard_map/while
  241.6 6.9 %copy-start.2 = (f32[4,640]{1,0:T(4,128)S(1)}, f32[4,640]{1,0:T(4,128)}, u32[]{:S(2)}) copy-start(f32[4,640]{1,0:T(4,128)} %get-tuple-element.780) | copy-start | bytes 30724 | tf_op jit(solution)/shard_map/while
  241.6 6.9 %copy-start.4 = (f32[3,640]{1,0:T(4,128)S(1)}, f32[3,640]{1,0:T(4,128)}, u32[]{:S(2)}) copy-start(f32[3,640]{1,0:T(4,128)} %get-tuple-element.781) | copy-start | bytes 23044 | tf_op jit(solution)/shard_map/while
  241.6 7.1 %copy-start = (bf16[8192,640]{1,0:T(8,128)(2,1)S(1)}, bf16[8192,640]{1,0:T(8,128)(2,1)}, u32[]{:S(2)}) copy-start(bf16[8192,640]{1,0:T(8,128)(2,1)} %get-tuple-element.814) | copy-start | bytes 31457284 | tf_op jit(solution)/shard_map/while
  248.8 29.4 %copy-start.7 = (f32[512]{0:T(512)S(1)}, f32[512]{0:T(512)}, u32[]{:S(2)}) copy-start(f32[512]{0:T(512)} %get-tuple-element.779) | copy-start | bytes 6148 | tf_op jit(solution)/shard_map/while
  281.3 6.9 %copy-start.2 = (f32[4,640]{1,0:T(4,128)S(1)}, f32[4,640]{1,0:T(4,128)}, u32[]{:S(2)}) copy-start(f32[4,640]{1,0:T(4,128)} %get-tuple-element.780) | copy-start | bytes 30724 | tf_op jit(solution)/shard_map/while
  281.4 6.9 %copy-start.4 = (f32[3,640]{1,0:T(4,128)S(1)}, f32[3,640]{1,0:T(4,128)}, u32[]{:S(2)}) copy-start(f32[3,640]{1,0:T(4,128)} %get-tuple-element.781) | copy-start | bytes 23044 | tf_op jit(solution)/shard_map/while
  281.4 7.1 %copy-start = (bf16[8192,640]{1,0:T(8,128)(2,1)S(1)}, bf16[8192,640]{1,0:T(8,128)(2,1)}, u32[]{:S(2)}) copy-start(bf16[8192,640]{1,0:T(8,128)(2,1)} %get-tuple-element.814) | copy-start | bytes 31457284 | tf_op jit(solution)/shard_map/while
  288.5 24.6 %copy-start.7 = (f32[512]{0:T(512)S(1)}, f32[512]{0:T(512)}, u32[]{:S(2)}) copy-start(f32[512]{0:T(512)} %get-tuple-element.779) | copy-start | bytes 6148 | tf_op jit(solution)/shard_map/while
  316.3 6.9 %copy-start.2 = (f32[4,640]{1,0:T(4,128)S(1)}, f32[4,640]{1,0:T(4,128)}, u32[]{:S(2)}) copy-start(f32[4,640]{1,0:T(4,128)} %get-tuple-element.780) | copy-start | bytes 30724 | tf_op jit(solution)/shard_map/while
  316.3 6.9 %copy-start.4 = (f32[3,640]{1,0:T(4,128)S(1)}, f32[3,640]{1,0:T(4,128)}, u32[]{:S(2)}) copy-start(f32[3,640]{1,0:T(4,128)} %get-tuple-element.781) | copy-start | bytes 23044 | tf_op jit(solution)/shard_map/while
  316.4 7.1 %copy-start = (bf16[8192,640]{1,0:T(8,128)(2,1)S(1)}, bf16[8192,640]{1,0:T(8,128)(2,1)}, u32[]{:S(2)}) copy-start(bf16[8192,640]{1,0:T(8,128)(2,1)} %get-tuple-element.814) | copy-start | bytes 31457284 | tf_op jit(solution)/shard_map/while
  323.5 27.5 %copy-start.7 = (f32[512]{0:T(512)S(1)}, f32[512]{0:T(512)}, u32[]{:S(2)}) copy-start(f32[512]{0:T(512)} %get-tuple-element.779) | copy-start | bytes 6148 | tf_op jit(solution)/shard_map/while
  354.2 6.9 %copy-start.2 = (f32[4,640]{1,0:T(4,128)S(1)}, f32[4,640]{1,0:T(4,128)}, u32[]{:S(2)}) copy-start(f32[4,640]{1,0:T(4,128)} %get-tuple-element.780) | copy-start | bytes 30724 | tf_op jit(solution)/shard_map/while
  354.2 6.9 %copy-start.4 = (f32[3,640]{1,0:T(4,128)S(1)}, f32[3,640]{1,0:T(4,128)}, u32[]{:S(2)}) copy-start(f32[3,640]{1,0:T(4,128)} %get-tuple-element.781) | copy-start | bytes 23044 | tf_op jit(solution)/shard_map/while
  354.2 7.1 %copy-start = (bf16[8192,640]{1,0:T(8,128)(2,1)S(1)}, bf16[8192,640]{1,0:T(8,128)(2,1)}, u32[]{:S(2)}) copy-start(bf16[8192,640]{1,0:T(8,128)(2,1)} %get-tuple-element.814) | copy-start | bytes 31457284 | tf_op jit(solution)/shard_map/while
  361.4 26.4 %copy-start.7 = (f32[512]{0:T(512)S(1)}, f32[512]{0:T(512)}, u32[]{:S(2)}) copy-start(f32[512]{0:T(512)} %get-tuple-element.779) | copy-start | bytes 6148 | tf_op jit(solution)/shard_map/while
  391.0 6.9 %copy-start.2 = (f32[4,640]{1,0:T(4,128)S(1)}, f32[4,640]{1,0:T(4,128)}, u32[]{:S(2)}) copy-start(f32[4,640]{1,0:T(4,128)} %get-tuple-element.780) | copy-start | bytes 30724 | tf_op jit(solution)/shard_map/while
  391.0 6.9 %copy-start.4 = (f32[3,640]{1,0:T(4,128)S(1)}, f32[3,640]{1,0:T(4,128)}, u32[]{:S(2)}) copy-start(f32[3,640]{1,0:T(4,128)} %get-tuple-element.781) | copy-start | bytes 23044 | tf_op jit(solution)/shard_map/while
  391.0 7.1 %copy-start = (bf16[8192,640]{1,0:T(8,128)(2,1)S(1)}, bf16[8192,640]{1,0:T(8,128)(2,1)}, u32[]{:S(2)}) copy-start(bf16[8192,640]{1,0:T(8,128)(2,1)} %get-tuple-element.814) | copy-start | bytes 31457284 | tf_op jit(solution)/shard_map/while
  398.2 27.6 %copy-start.7 = (f32[512]{0:T(512)S(1)}, f32[512]{0:T(512)}, u32[]{:S(2)}) copy-start(f32[512]{0:T(512)} %get-tuple-element.779) | copy-start | bytes 6148 | tf_op jit(solution)/shard_map/while
  (33 other events, 109.4 us)

commit v12 on v11

--- a/solution.py
+++ b/solution.py
@@ -56,7 +56,7 @@
 
 
 def layer_exchange_kernel(
-    n, n_sec, width, x_ref, s_ref, normed_ref, inv_ref, gain_ref, top_ref, up_ref,
+    n, n_sec, width, x_ref, s_ref, aux_ref, gain_ref, top_ref, up_ref,
     g_ref, next_ref, gain_out_ref,
     recv, srecv, gbuf, down, send_sem, recv_sem, ssend_sem, srecv_sem, dsend_sem, drecv_sem,
 ):
@@ -114,8 +114,9 @@
         stat_total = stat_total + srecv[src]
     rows = total.shape[0]
     row_mean = jnp.transpose(stat_total)[:rows, 0:1] * (1.0 / (n * width))
-    normed = normed_ref[...]
-    d_in = inv_ref[...] * (total * gain_ref[...] - normed * row_mean)
+    normed = aux_ref[:, :width]
+    inv_rms = aux_ref[:, width : width + 1]
+    d_in = inv_rms * (total * gain_ref[...] - normed * row_mean)
     upstream = jnp.where(sec == n_sec - 1, top_ref[:, mine], up_ref[:, mine])
     result = (upstream.astype(jnp.float32) + d_in).astype(g_ref.dtype)
     gbuf[...] = result
@@ -157,7 +158,7 @@
         next_ref[...] = jnp.zeros_like(next_ref)
 
 
-def layer_exchange(partial, stats, normed, inv_rms, gain_own, top, upstream, n, n_sec, width):
+def layer_exchange(partial, stats, aux, gain_own, top, upstream, n, n_sec, width):
     rows = partial.shape[0]
     vmem = pl.BlockSpec(memory_space=pltpu.VMEM)
     return pl.pallas_call(
@@ -167,7 +168,7 @@
             jax.ShapeDtypeStruct((rows, n * width), jnp.bfloat16),
             jax.ShapeDtypeStruct((1, width), jnp.float32),
         ),
-        in_specs=[vmem] * 7,
+        in_specs=[vmem] * 6,
         out_specs=(vmem, vmem, vmem),
         scratch_shapes=[
             pltpu.VMEM((n, rows, width), partial.dtype),
@@ -184,7 +185,7 @@
         compiler_params=pltpu.CompilerParams(
             collective_id=2, has_side_effects=True, vmem_limit_bytes=16 * 1024 * 1024
         ),
-    )(partial, stats, normed, inv_rms, gain_own, top, upstream)
+    )(partial, stats, aux, gain_own, top, upstream)
 
 
 def conv_block(weights, ext_vals, tail_rows, d_act):
@@ -237,6 +238,9 @@
     normed_all = values * inv_rms_all
     gain_own = lax.dynamic_slice(gain_vec, (tensor_idx * width,), (width,))
     normed_own_all = lax.dynamic_slice(normed_all, (0, 0, tensor_idx * width), (batches, seq_len, width))
+    aux_all = jnp.concatenate(
+        [normed_own_all, jnp.broadcast_to(inv_rms_all, (batches, seq_len, 128))], axis=-1
+    )
 
     halves = CHUNKS_PER_BATCH
     chunk_len = seq_len // halves
@@ -268,12 +272,11 @@
         d_vals, conv_part, new_tail = conv_block(weights, ext_vals, tail_rows, d_act)
         partial = lax.dot_general(d_vals, w_in, contract, preferred_element_type=jnp.float32).astype(jnp.bfloat16)
         normed = rows_of(normed_all, batch_slot, row_start, chunk_len)
-        inv_rms = rows_of(inv_rms_all, batch_slot, row_start, chunk_len)
         row_part = jnp.sum(partial.astype(jnp.float32) * gain_vec * normed, axis=-1)
         stats = jnp.zeros((8, 128), jnp.float32).at[0, :chunk_len].set(row_part)
-        normed_own = rows_of(normed_own_all, batch_slot, row_start, chunk_len)
+        aux = rows_of(aux_all, batch_slot, row_start, chunk_len)
         grad_out, incoming_next, gain_part = layer_exchange(
-            partial, stats, normed_own, inv_rms, gain_own[None, :], top_chunk, incoming, tensors, sections, width
+            partial, stats, aux, gain_own[None, :], top_chunk, incoming, tensors, sections, width
         )
         gain_part = gain_part[0]
         previous = lax.dynamic_slice(results, (batch_slot, half_now, 0, 0), (1, 1, chunk_len, width))

time: 472 us -> 428 us (0.907)
  local copies, waits for them, and re-layouts: 35.2 us -> 9.39 us
  other arithmetic: 20.6 us -> 9.67 us
  Pallas kernels: 323 us -> 317 us
    slice x11, local copies, waits for them, and re-layouts: 9.7 us -> 0.38 us  [conv_block(): d_vals = d_vals + weights[lag_idx] * padded_back[lag_idx:lag_idx + length]]
    convert_element_type x11, other arithmetic: 9.23 us -> 0.28 us  [step_rows(): ext_vals = lax.dynamic_slice(conv_padded, (batch_slot, row_start, 0), (1,...]
    squeeze x44 -> x22, local copies, waits for them, and re-layouts: 9.55 us -> 0.69 us  [rows_of(): lax.dynamic_slice(array, (batch_slot, first_row, 0), (1, row_count, array...]
    pallas_call x11, Pallas kernels: 250 us -> 243 us  [layer_exchange(): pl.pallas_call(functools.partial(layer_exchange_kernel, n, n_sec, width),...]
    while x165 -> x33, local copies, waits for them, and re-layouts: 8.73 us -> 2.93 us
where the time goes in v12:
time: 428 us
  Pallas kernels  317 us (74%)
  matrix products  50 us (12%)
  blocking collectives  38.8 us (9%)
  other arithmetic  9.67 us (2%)
  local copies, waits for them, and re-layouts  9.39 us (2%)
    pallas_call x11, Pallas kernels, layer_exchange(): pl.pallas_call(functools.partial(layer_exchange_kernel, n, n_sec, width),...  243 us
    pallas_call x11, Pallas kernels, matmul_nt(): pl.pallas_call(functools.partial(matmul_nt_kernel, n_sec), out_shape=jax....  73.4 us
    dot_general x11, matrix products, step_rows(): lax.dot_general(d_vals, w_in, contract, preferred_element_type=jnp.float32)  50 us
    all_to_all x1, blocking collectives, local(): lax.all_to_all(copies, 'tensor', split_axis=0, concat_axis=2, tiled=True)[0]  38.8 us

profile of v12, /device:TPU:32, one launch (start us, length us, event | category | flops | bytes accessed | tf_op | source)
XLA Modules:
  0.0 427.5 jit_solution(2651155258957939371)
XLA Ops:
  0.7 2.3 fusion.18
  3.0 2.4 convert_multiply_fusion
  5.4 1.0 constant_dynamic-slice_fusion.1
  6.5 1.8 broadcast_select_fusion.1
  8.5 375.5 %while.27 = (s32[]{:T(128)}, bf16[32,8192]{1,0:T(8,128)(2,1)S(1)}, bf16[2,2,32,512]{3,2,1,0:T(8,128)(2,1)S(1)}, f32[512]{0:T(512)S(1)}, f32[4,640]{1,0:T(4,128)S...) while((s32[]{:T(128)}, bf16[32,8192]{1,0:T(8,128)(2,1)S(1)}, ...), condition=%wide.region_7.8_spmd.clone, body=%wide.region_1.7_spmd.clone.sunk | while | flops 673154560 | bytes 68873840 | solution.py:298
  8.8 6.7 %eval_jaxpr.16 = f32[32,640]{1,0:T(8,128)S(1)} custom-call(bf16[32,8192]{1,0:T(8,128)(2,1)S(1)} %dynamic-slice_bitcast_fusion.4.top_ref, bf16[32,8192]{1,0:T(8,128)(2,1)S(1)} %copy.34.x_ref.up_ref, bf16[640,8192]{1,0:T(8,128)(2,1)} %get-tuple-element.726.w_ref), custom_call_target="tpu_custom_call" | custom-call | flops 335544320 | bytes 11616256 | tf_op jit(solution)/shard_map/while/body/eval_jaxpr/pallas_call | solution.py:37
  15.7 0.2 copy-done
  15.9 4.5 %fusion.26 = (f32[32]{0:T(128)S(1)}, bf16[32,8192]{1,0:T(8,128)(2,1)S(1)}) fusion(f32[2,64,8192]{2,1,0:T(8,128)} %get-tuple-element.730, s32[]{:T(128)S(6)} %select_n.236, s32[]{:T(128)S(6)} %select_n.237, f32[8192]{0:T(1024)S(1)} %bitcast.85, bf16[8192,640]{1,0:T(8,128)(2,1)S(1)} %copy-done, f32[32,640]{1,0:T(8,128)S(1)} %get-tuple-element.653, ...), kind=kOutput, calls=%fused_computation.2.clone.1 | convolution fusion | flops 337080288 | bytes 12191368 | tf_op jit(solution)/shard_map/while/body/eval_jaxpr/dot_general | solution.py:273
  20.5 24.2 %eval_jaxpr.17 = (bf16[32,512]{1,0:T(8,128)(2,1)S(1)}, bf16[32,8192]{1,0:T(8,128)(2,1)S(1)}, f32[1,512]{1,0:T(1,128)S(1)}) custom-call(bf16[32,8192]{1,0:T(8,128)(2,1)S(1)} %get-tuple-element.655.x_ref, f32[8,128]{1,0:T(8,128)S(1)} %scatter.19.s_ref, f32[32,640]{1,0:T(8,128)S(1)} %dynamic-slice_bitcast_fusion.5.aux_ref, f32[1,512]{1,0:T(1,128)S(1)} %bitcast.91, ...), custom_call_target="tpu_custom_call" | custom-call | tf_op jit(solution)/shard_map/while/body/eval_jaxpr/pallas_call | solution.py:164
  45.0 6.7 %eval_jaxpr.16 = f32[32,640]{1,0:T(8,128)S(1)} custom-call(bf16[32,8192]{1,0:T(8,128)(2,1)S(1)} %dynamic-slice_bitcast_fusion.4.top_ref, bf16[32,8192]{1,0:T(8,128)(2,1)S(1)} %copy.34.x_ref.up_ref, bf16[640,8192]{1,0:T(8,128)(2,1)} %get-tuple-element.726.w_ref), custom_call_target="tpu_custom_call" | custom-call | flops 335544320 | bytes 11616256 | tf_op jit(solution)/shard_map/while/body/eval_jaxpr/pallas_call | solution.py:37
  52.1 4.5 %fusion.26 = (f32[32]{0:T(128)S(1)}, bf16[32,8192]{1,0:T(8,128)(2,1)S(1)}) fusion(f32[2,64,8192]{2,1,0:T(8,128)} %get-tuple-element.730, s32[]{:T(128)S(6)} %select_n.236, s32[]{:T(128)S(6)} %select_n.237, f32[8192]{0:T(1024)S(1)} %bitcast.85, bf16[8192,640]{1,0:T(8,128)(2,1)S(1)} %copy-done, f32[32,640]{1,0:T(8,128)S(1)} %get-tuple-element.653, ...), kind=kOutput, calls=%fused_computation.2.clone.1 | convolution fusion | flops 337080288 | bytes 12191368 | tf_op jit(solution)/shard_map/while/body/eval_jaxpr/dot_general | solution.py:273
  56.7 25.1 %eval_jaxpr.17 = (bf16[32,512]{1,0:T(8,128)(2,1)S(1)}, bf16[32,8192]{1,0:T(8,128)(2,1)S(1)}, f32[1,512]{1,0:T(1,128)S(1)}) custom-call(bf16[32,8192]{1,0:T(8,128)(2,1)S(1)} %get-tuple-element.655.x_ref, f32[8,128]{1,0:T(8,128)S(1)} %scatter.19.s_ref, f32[32,640]{1,0:T(8,128)S(1)} %dynamic-slice_bitcast_fusion.5.aux_ref, f32[1,512]{1,0:T(1,128)S(1)} %bitcast.91, ...), custom_call_target="tpu_custom_call" | custom-call | tf_op jit(solution)/shard_map/while/body/eval_jaxpr/pallas_call | solution.py:164
  82.1 6.7 %eval_jaxpr.16 = f32[32,640]{1,0:T(8,128)S(1)} custom-call(bf16[32,8192]{1,0:T(8,128)(2,1)S(1)} %dynamic-slice_bitcast_fusion.4.top_ref, bf16[32,8192]{1,0:T(8,128)(2,1)S(1)} %copy.34.x_ref.up_ref, bf16[640,8192]{1,0:T(8,128)(2,1)} %get-tuple-element.726.w_ref), custom_call_target="tpu_custom_call" | custom-call | flops 335544320 | bytes 11616256 | tf_op jit(solution)/shard_map/while/body/eval_jaxpr/pallas_call | solution.py:37
  89.0 0.2 copy-done
  89.2 4.5 %fusion.26 = (f32[32]{0:T(128)S(1)}, bf16[32,8192]{1,0:T(8,128)(2,1)S(1)}) fusion(f32[2,64,8192]{2,1,0:T(8,128)} %get-tuple-element.730, s32[]{:T(128)S(6)} %select_n.236, s32[]{:T(128)S(6)} %select_n.237, f32[8192]{0:T(1024)S(1)} %bitcast.85, bf16[8192,640]{1,0:T(8,128)(2,1)S(1)} %copy-done, f32[32,640]{1,0:T(8,128)S(1)} %get-tuple-element.653, ...), kind=kOutput, calls=%fused_computation.2.clone.1 | convolution fusion | flops 337080288 | bytes 12191368 | tf_op jit(solution)/shard_map/while/body/eval_jaxpr/dot_general | solution.py:273
  93.8 21.3 %eval_jaxpr.17 = (bf16[32,512]{1,0:T(8,128)(2,1)S(1)}, bf16[32,8192]{1,0:T(8,128)(2,1)S(1)}, f32[1,512]{1,0:T(1,128)S(1)}) custom-call(bf16[32,8192]{1,0:T(8,128)(2,1)S(1)} %get-tuple-element.655.x_ref, f32[8,128]{1,0:T(8,128)S(1)} %scatter.19.s_ref, f32[32,640]{1,0:T(8,128)S(1)} %dynamic-slice_bitcast_fusion.5.aux_ref, f32[1,512]{1,0:T(1,128)S(1)} %bitcast.91, ...), custom_call_target="tpu_custom_call" | custom-call | tf_op jit(solution)/shard_map/while/body/eval_jaxpr/pallas_call | solution.py:164
  115.4 6.7 %eval_jaxpr.16 = f32[32,640]{1,0:T(8,128)S(1)} custom-call(bf16[32,8192]{1,0:T(8,128)(2,1)S(1)} %dynamic-slice_bitcast_fusion.4.top_ref, bf16[32,8192]{1,0:T(8,128)(2,1)S(1)} %copy.34.x_ref.up_ref, bf16[640,8192]{1,0:T(8,128)(2,1)} %get-tuple-element.726.w_ref), custom_call_target="tpu_custom_call" | custom-call | flops 335544320 | bytes 11616256 | tf_op jit(solution)/shard_map/while/body/eval_jaxpr/pallas_call | solution.py:37
  122.5 4.5 %fusion.26 = (f32[32]{0:T(128)S(1)}, bf16[32,8192]{1,0:T(8,128)(2,1)S(1)}) fusion(f32[2,64,8192]{2,1,0:T(8,128)} %get-tuple-element.730, s32[]{:T(128)S(6)} %select_n.236, s32[]{:T(128)S(6)} %select_n.237, f32[8192]{0:T(1024)S(1)} %bitcast.85, bf16[8192,640]{1,0:T(8,128)(2,1)S(1)} %copy-done, f32[32,640]{1,0:T(8,128)S(1)} %get-tuple-element.653, ...), kind=kOutput, calls=%fused_computation.2.clone.1 | convolution fusion | flops 337080288 | bytes 12191368 | tf_op jit(solution)/shard_map/while/body/eval_jaxpr/dot_general | solution.py:273
  127.1 22.9 %eval_jaxpr.17 = (bf16[32,512]{1,0:T(8,128)(2,1)S(1)}, bf16[32,8192]{1,0:T(8,128)(2,1)S(1)}, f32[1,512]{1,0:T(1,128)S(1)}) custom-call(bf16[32,8192]{1,0:T(8,128)(2,1)S(1)} %get-tuple-element.655.x_ref, f32[8,128]{1,0:T(8,128)S(1)} %scatter.19.s_ref, f32[32,640]{1,0:T(8,128)S(1)} %dynamic-slice_bitcast_fusion.5.aux_ref, f32[1,512]{1,0:T(1,128)S(1)} %bitcast.91, ...), custom_call_target="tpu_custom_call" | custom-call | tf_op jit(solution)/shard_map/while/body/eval_jaxpr/pallas_call | solution.py:164
  150.2 6.7 %eval_jaxpr.16 = f32[32,640]{1,0:T(8,128)S(1)} custom-call(bf16[32,8192]{1,0:T(8,128)(2,1)S(1)} %dynamic-slice_bitcast_fusion.4.top_ref, bf16[32,8192]{1,0:T(8,128)(2,1)S(1)} %copy.34.x_ref.up_ref, bf16[640,8192]{1,0:T(8,128)(2,1)} %get-tuple-element.726.w_ref), custom_call_target="tpu_custom_call" | custom-call | flops 335544320 | bytes 11616256 | tf_op jit(solution)/shard_map/while/body/eval_jaxpr/pallas_call | solution.py:37
  157.1 0.2 copy-done
  157.4 4.5 %fusion.26 = (f32[32]{0:T(128)S(1)}, bf16[32,8192]{1,0:T(8,128)(2,1)S(1)}) fusion(f32[2,64,8192]{2,1,0:T(8,128)} %get-tuple-element.730, s32[]{:T(128)S(6)} %select_n.236, s32[]{:T(128)S(6)} %select_n.237, f32[8192]{0:T(1024)S(1)} %bitcast.85, bf16[8192,640]{1,0:T(8,128)(2,1)S(1)} %copy-done, f32[32,640]{1,0:T(8,128)S(1)} %get-tuple-element.653, ...), kind=kOutput, calls=%fused_computation.2.clone.1 | convolution fusion | flops 337080288 | bytes 12191368 | tf_op jit(solution)/shard_map/while/body/eval_jaxpr/dot_general | solution.py:273
  161.9 21.2 %eval_jaxpr.17 = (bf16[32,512]{1,0:T(8,128)(2,1)S(1)}, bf16[32,8192]{1,0:T(8,128)(2,1)S(1)}, f32[1,512]{1,0:T(1,128)S(1)}) custom-call(bf16[32,8192]{1,0:T(8,128)(2,1)S(1)} %get-tuple-element.655.x_ref, f32[8,128]{1,0:T(8,128)S(1)} %scatter.19.s_ref, f32[32,640]{1,0:T(8,128)S(1)} %dynamic-slice_bitcast_fusion.5.aux_ref, f32[1,512]{1,0:T(1,128)S(1)} %bitcast.91, ...), custom_call_target="tpu_custom_call" | custom-call | tf_op jit(solution)/shard_map/while/body/eval_jaxpr/pallas_call | solution.py:164
  183.4 6.7 %eval_jaxpr.16 = f32[32,640]{1,0:T(8,128)S(1)} custom-call(bf16[32,8192]{1,0:T(8,128)(2,1)S(1)} %dynamic-slice_bitcast_fusion.4.top_ref, bf16[32,8192]{1,0:T(8,128)(2,1)S(1)} %copy.34.x_ref.up_ref, bf16[640,8192]{1,0:T(8,128)(2,1)} %get-tuple-element.726.w_ref), custom_call_target="tpu_custom_call" | custom-call | flops 335544320 | bytes 11616256 | tf_op jit(solution)/shard_map/while/body/eval_jaxpr/pallas_call | solution.py:37
  190.5 4.5 %fusion.26 = (f32[32]{0:T(128)S(1)}, bf16[32,8192]{1,0:T(8,128)(2,1)S(1)}) fusion(f32[2,64,8192]{2,1,0:T(8,128)} %get-tuple-element.730, s32[]{:T(128)S(6)} %select_n.236, s32[]{:T(128)S(6)} %select_n.237, f32[8192]{0:T(1024)S(1)} %bitcast.85, bf16[8192,640]{1,0:T(8,128)(2,1)S(1)} %copy-done, f32[32,640]{1,0:T(8,128)S(1)} %get-tuple-element.653, ...), kind=kOutput, calls=%fused_computation.2.clone.1 | convolution fusion | flops 337080288 | bytes 12191368 | tf_op jit(solution)/shard_map/while/body/eval_jaxpr/dot_general | solution.py:273
  195.1 20.5 %eval_jaxpr.17 = (bf16[32,512]{1,0:T(8,128)(2,1)S(1)}, bf16[32,8192]{1,0:T(8,128)(2,1)S(1)}, f32[1,512]{1,0:T(1,128)S(1)}) custom-call(bf16[32,8192]{1,0:T(8,128)(2,1)S(1)} %get-tuple-element.655.x_ref, f32[8,128]{1,0:T(8,128)S(1)} %scatter.19.s_ref, f32[32,640]{1,0:T(8,128)S(1)} %dynamic-slice_bitcast_fusion.5.aux_ref, f32[1,512]{1,0:T(1,128)S(1)} %bitcast.91, ...), custom_call_target="tpu_custom_call" | custom-call | tf_op jit(solution)/shard_map/while/body/eval_jaxpr/pallas_call | solution.py:164
  215.9 6.7 %eval_jaxpr.16 = f32[32,640]{1,0:T(8,128)S(1)} custom-call(bf16[32,8192]{1,0:T(8,128)(2,1)S(1)} %dynamic-slice_bitcast_fusion.4.top_ref, bf16[32,8192]{1,0:T(8,128)(2,1)S(1)} %copy.34.x_ref.up_ref, bf16[640,8192]{1,0:T(8,128)(2,1)} %get-tuple-element.726.w_ref), custom_call_target="tpu_custom_call" | custom-call | flops 335544320 | bytes 11616256 | tf_op jit(solution)/shard_map/while/body/eval_jaxpr/pallas_call | solution.py:37
  222.8 0.2 copy-done
  223.1 4.5 %fusion.26 = (f32[32]{0:T(128)S(1)}, bf16[32,8192]{1,0:T(8,128)(2,1)S(1)}) fusion(f32[2,64,8192]{2,1,0:T(8,128)} %get-tuple-element.730, s32[]{:T(128)S(6)} %select_n.236, s32[]{:T(128)S(6)} %select_n.237, f32[8192]{0:T(1024)S(1)} %bitcast.85, bf16[8192,640]{1,0:T(8,128)(2,1)S(1)} %copy-done, f32[32,640]{1,0:T(8,128)S(1)} %get-tuple-element.653, ...), kind=kOutput, calls=%fused_computation.2.clone.1 | convolution fusion | flops 337080288 | bytes 12191368 | tf_op jit(solution)/shard_map/while/body/eval_jaxpr/dot_general | solution.py:273
  227.6 21.5 %eval_jaxpr.17 = (bf16[32,512]{1,0:T(8,128)(2,1)S(1)}, bf16[32,8192]{1,0:T(8,128)(2,1)S(1)}, f32[1,512]{1,0:T(1,128)S(1)}) custom-call(bf16[32,8192]{1,0:T(8,128)(2,1)S(1)} %get-tuple-element.655.x_ref, f32[8,128]{1,0:T(8,128)S(1)} %scatter.19.s_ref, f32[32,640]{1,0:T(8,128)S(1)} %dynamic-slice_bitcast_fusion.5.aux_ref, f32[1,512]{1,0:T(1,128)S(1)} %bitcast.91, ...), custom_call_target="tpu_custom_call" | custom-call | tf_op jit(solution)/shard_map/while/body/eval_jaxpr/pallas_call | solution.py:164
  249.4 6.7 %eval_jaxpr.16 = f32[32,640]{1,0:T(8,128)S(1)} custom-call(bf16[32,8192]{1,0:T(8,128)(2,1)S(1)} %dynamic-slice_bitcast_fusion.4.top_ref, bf16[32,8192]{1,0:T(8,128)(2,1)S(1)} %copy.34.x_ref.up_ref, bf16[640,8192]{1,0:T(8,128)(2,1)} %get-tuple-element.726.w_ref), custom_call_target="tpu_custom_call" | custom-call | flops 335544320 | bytes 11616256 | tf_op jit(solution)/shard_map/while/body/eval_jaxpr/pallas_call | solution.py:37
  256.3 0.2 copy-done
  256.5 4.5 %fusion.26 = (f32[32]{0:T(128)S(1)}, bf16[32,8192]{1,0:T(8,128)(2,1)S(1)}) fusion(f32[2,64,8192]{2,1,0:T(8,128)} %get-tuple-element.730, s32[]{:T(128)S(6)} %select_n.236, s32[]{:T(128)S(6)} %select_n.237, f32[8192]{0:T(1024)S(1)} %bitcast.85, bf16[8192,640]{1,0:T(8,128)(2,1)S(1)} %copy-done, f32[32,640]{1,0:T(8,128)S(1)} %get-tuple-element.653, ...), kind=kOutput, calls=%fused_computation.2.clone.1 | convolution fusion | flops 337080288 | bytes 12191368 | tf_op jit(solution)/shard_map/while/body/eval_jaxpr/dot_general | solution.py:273
  261.1 21.2 %eval_jaxpr.17 = (bf16[32,512]{1,0:T(8,128)(2,1)S(1)}, bf16[32,8192]{1,0:T(8,128)(2,1)S(1)}, f32[1,512]{1,0:T(1,128)S(1)}) custom-call(bf16[32,8192]{1,0:T(8,128)(2,1)S(1)} %get-tuple-element.655.x_ref, f32[8,128]{1,0:T(8,128)S(1)} %scatter.19.s_ref, f32[32,640]{1,0:T(8,128)S(1)} %dynamic-slice_bitcast_fusion.5.aux_ref, f32[1,512]{1,0:T(1,128)S(1)} %bitcast.91, ...), custom_call_target="tpu_custom_call" | custom-call | tf_op jit(solution)/shard_map/while/body/eval_jaxpr/pallas_call | solution.py:164
  282.6 6.7 %eval_jaxpr.16 = f32[32,640]{1,0:T(8,128)S(1)} custom-call(bf16[32,8192]{1,0:T(8,128)(2,1)S(1)} %dynamic-slice_bitcast_fusion.4.top_ref, bf16[32,8192]{1,0:T(8,128)(2,1)S(1)} %copy.34.x_ref.up_ref, bf16[640,8192]{1,0:T(8,128)(2,1)} %get-tuple-element.726.w_ref), custom_call_target="tpu_custom_call" | custom-call | flops 335544320 | bytes 11616256 | tf_op jit(solution)/shard_map/while/body/eval_jaxpr/pallas_call | solution.py:37
  289.7 4.5 %fusion.26 = (f32[32]{0:T(128)S(1)}, bf16[32,8192]{1,0:T(8,128)(2,1)S(1)}) fusion(f32[2,64,8192]{2,1,0:T(8,128)} %get-tuple-element.730, s32[]{:T(128)S(6)} %select_n.236, s32[]{:T(128)S(6)} %select_n.237, f32[8192]{0:T(1024)S(1)} %bitcast.85, bf16[8192,640]{1,0:T(8,128)(2,1)S(1)} %copy-done, f32[32,640]{1,0:T(8,128)S(1)} %get-tuple-element.653, ...), kind=kOutput, calls=%fused_computation.2.clone.1 | convolution fusion | flops 337080288 | bytes 12191368 | tf_op jit(solution)/shard_map/while/body/eval_jaxpr/dot_general | solution.py:273
  294.2 24.1 %eval_jaxpr.17 = (bf16[32,512]{1,0:T(8,128)(2,1)S(1)}, bf16[32,8192]{1,0:T(8,128)(2,1)S(1)}, f32[1,512]{1,0:T(1,128)S(1)}) custom-call(bf16[32,8192]{1,0:T(8,128)(2,1)S(1)} %get-tuple-element.655.x_ref, f32[8,128]{1,0:T(8,128)S(1)} %scatter.19.s_ref, f32[32,640]{1,0:T(8,128)S(1)} %dynamic-slice_bitcast_fusion.5.aux_ref, f32[1,512]{1,0:T(1,128)S(1)} %bitcast.91, ...), custom_call_target="tpu_custom_call" | custom-call | tf_op jit(solution)/shard_map/while/body/eval_jaxpr/pallas_call | solution.py:164
  318.6 6.7 %eval_jaxpr.16 = f32[32,640]{1,0:T(8,128)S(1)} custom-call(bf16[32,8192]{1,0:T(8,128)(2,1)S(1)} %dynamic-slice_bitcast_fusion.4.top_ref, bf16[32,8192]{1,0:T(8,128)(2,1)S(1)} %copy.34.x_ref.up_ref, bf16[640,8192]{1,0:T(8,128)(2,1)} %get-tuple-element.726.w_ref), custom_call_target="tpu_custom_call" | custom-call | flops 335544320 | bytes 11616256 | tf_op jit(solution)/shard_map/while/body/eval_jaxpr/pallas_call | solution.py:37
  325.5 0.2 copy-done
  325.8 4.5 %fusion.26 = (f32[32]{0:T(128)S(1)}, bf16[32,8192]{1,0:T(8,128)(2,1)S(1)}) fusion(f32[2,64,8192]{2,1,0:T(8,128)} %get-tuple-element.730, s32[]{:T(128)S(6)} %select_n.236, s32[]{:T(128)S(6)} %select_n.237, f32[8192]{0:T(1024)S(1)} %bitcast.85, bf16[8192,640]{1,0:T(8,128)(2,1)S(1)} %copy-done, f32[32,640]{1,0:T(8,128)S(1)} %get-tuple-element.653, ...), kind=kOutput, calls=%fused_computation.2.clone.1 | convolution fusion | flops 337080288 | bytes 12191368 | tf_op jit(solution)/shard_map/while/body/eval_jaxpr/dot_general | solution.py:273
  330.3 20.2 %eval_jaxpr.17 = (bf16[32,512]{1,0:T(8,128)(2,1)S(1)}, bf16[32,8192]{1,0:T(8,128)(2,1)S(1)}, f32[1,512]{1,0:T(1,128)S(1)}) custom-call(bf16[32,8192]{1,0:T(8,128)(2,1)S(1)} %get-tuple-element.655.x_ref, f32[8,128]{1,0:T(8,128)S(1)} %scatter.19.s_ref, f32[32,640]{1,0:T(8,128)S(1)} %dynamic-slice_bitcast_fusion.5.aux_ref, f32[1,512]{1,0:T(1,128)S(1)} %bitcast.91, ...), custom_call_target="tpu_custom_call" | custom-call | tf_op jit(solution)/shard_map/while/body/eval_jaxpr/pallas_call | solution.py:164
  350.8 6.7 %eval_jaxpr.16 = f32[32,640]{1,0:T(8,128)S(1)} custom-call(bf16[32,8192]{1,0:T(8,128)(2,1)S(1)} %dynamic-slice_bitcast_fusion.4.top_ref, bf16[32,8192]{1,0:T(8,128)(2,1)S(1)} %copy.34.x_ref.up_ref, bf16[640,8192]{1,0:T(8,128)(2,1)} %get-tuple-element.726.w_ref), custom_call_target="tpu_custom_call" | custom-call | flops 335544320 | bytes 11616256 | tf_op jit(solution)/shard_map/while/body/eval_jaxpr/pallas_call | solution.py:37
  358.0 4.5 %fusion.26 = (f32[32]{0:T(128)S(1)}, bf16[32,8192]{1,0:T(8,128)(2,1)S(1)}) fusion(f32[2,64,8192]{2,1,0:T(8,128)} %get-tuple-element.730, s32[]{:T(128)S(6)} %select_n.236, s32[]{:T(128)S(6)} %select_n.237, f32[8192]{0:T(1024)S(1)} %bitcast.85, bf16[8192,640]{1,0:T(8,128)(2,1)S(1)} %copy-done, f32[32,640]{1,0:T(8,128)S(1)} %get-tuple-element.653, ...), kind=kOutput, calls=%fused_computation.2.clone.1 | convolution fusion | flops 337080288 | bytes 12191368 | tf_op jit(solution)/shard_map/while/body/eval_jaxpr/dot_general | solution.py:273
  362.5 21.4 %eval_jaxpr.17 = (bf16[32,512]{1,0:T(8,128)(2,1)S(1)}, bf16[32,8192]{1,0:T(8,128)(2,1)S(1)}, f32[1,512]{1,0:T(1,128)S(1)}) custom-call(bf16[32,8192]{1,0:T(8,128)(2,1)S(1)} %get-tuple-element.655.x_ref, f32[8,128]{1,0:T(8,128)S(1)} %scatter.19.s_ref, f32[32,640]{1,0:T(8,128)S(1)} %dynamic-slice_bitcast_fusion.5.aux_ref, f32[1,512]{1,0:T(1,128)S(1)} %bitcast.91, ...), custom_call_target="tpu_custom_call" | custom-call | tf_op jit(solution)/shard_map/while/body/eval_jaxpr/pallas_call | solution.py:164
  384.4 38.8 %all_to_all.15 = bf16[16,144,512]{2,1,0:T(8,128)(2,1)S(1)} all-to-all(bf16[16,144,512]{2,1,0:T(8,128)(2,1)S(1)} %broadcast_in_dim.97), channel_id=1, replica_groups=mesh['section'=8,'tensor'=16] {'tensor'}, dimensions={0} | all-to-all | bytes 4718592 | tf_op jit(solution)/shard_map/all_to_all | solution.py:305
  423.2 0.7 fusion.19
  424.0 1.2 copy.12
  425.2 2.3 broadcast_in_dim_reshape.3
  (225 shorter events, 6.1 us)
Async XLA Ops:
  0.6 2.3 copy-start.1
  2.9 2.5 copy-start.2
  2.9 3.4 copy-start.6
  3.0 3.4 copy-start.7
  3.0 3.5 copy-start.5
  6.5 2.0 copy-start.3
  8.8 7.1 %copy-start = (bf16[8192,640]{1,0:T(8,128)(2,1)S(1)}, bf16[8192,640]{1,0:T(8,128)(2,1)}, u32[]{:S(2)}) copy-start(bf16[8192,640]{1,0:T(8,128)(2,1)} %get-tuple-element.728) | copy-start | bytes 31457284 | tf_op jit(solution)/shard_map/while
  45.0 7.1 %copy-start = (bf16[8192,640]{1,0:T(8,128)(2,1)S(1)}, bf16[8192,640]{1,0:T(8,128)(2,1)}, u32[]{:S(2)}) copy-start(bf16[8192,640]{1,0:T(8,128)(2,1)} %get-tuple-element.728) | copy-start | bytes 31457284 | tf_op jit(solution)/shard_map/while
  82.1 7.1 %copy-start = (bf16[8192,640]{1,0:T(8,128)(2,1)S(1)}, bf16[8192,640]{1,0:T(8,128)(2,1)}, u32[]{:S(2)}) copy-start(bf16[8192,640]{1,0:T(8,128)(2,1)} %get-tuple-element.728) | copy-start | bytes 31457284 | tf_op jit(solution)/shard_map/while
  115.4 7.1 %copy-start = (bf16[8192,640]{1,0:T(8,128)(2,1)S(1)}, bf16[8192,640]{1,0:T(8,128)(2,1)}, u32[]{:S(2)}) copy-start(bf16[8192,640]{1,0:T(8,128)(2,1)} %get-tuple-element.728) | copy-start | bytes 31457284 | tf_op jit(solution)/shard_map/while
  150.2 7.1 %copy-start = (bf16[8192,640]{1,0:T(8,128)(2,1)S(1)}, bf16[8192,640]{1,0:T(8,128)(2,1)}, u32[]{:S(2)}) copy-start(bf16[8192,640]{1,0:T(8,128)(2,1)} %get-tuple-element.728) | copy-start | bytes 31457284 | tf_op jit(solution)/shard_map/while
  183.4 7.1 %copy-start = (bf16[8192,640]{1,0:T(8,128)(2,1)S(1)}, bf16[8192,640]{1,0:T(8,128)(2,1)}, u32[]{:S(2)}) copy-start(bf16[8192,640]{1,0:T(8,128)(2,1)} %get-tuple-element.728) | copy-start | bytes 31457284 | tf_op jit(solution)/shard_map/while
  215.9 7.1 %copy-start = (bf16[8192,640]{1,0:T(8,128)(2,1)S(1)}, bf16[8192,640]{1,0:T(8,128)(2,1)}, u32[]{:S(2)}) copy-start(bf16[8192,640]{1,0:T(8,128)(2,1)} %get-tuple-element.728) | copy-start | bytes 31457284 | tf_op jit(solution)/shard_map/while
  249.4 7.1 %copy-start = (bf16[8192,640]{1,0:T(8,128)(2,1)S(1)}, bf16[8192,640]{1,0:T(8,128)(2,1)}, u32[]{:S(2)}) copy-start(bf16[8192,640]{1,0:T(8,128)(2,1)} %get-tuple-element.728) | copy-start | bytes 31457284 | tf_op jit(solution)/shard_map/while
  282.6 7.1 %copy-start = (bf16[8192,640]{1,0:T(8,128)(2,1)S(1)}, bf16[8192,640]{1,0:T(8,128)(2,1)}, u32[]{:S(2)}) copy-start(bf16[8192,640]{1,0:T(8,128)(2,1)} %get-tuple-element.728) | copy-start | bytes 31457284 | tf_op jit(solution)/shard_map/while
  318.6 7.1 %copy-start = (bf16[8192,640]{1,0:T(8,128)(2,1)S(1)}, bf16[8192,640]{1,0:T(8,128)(2,1)}, u32[]{:S(2)}) copy-start(bf16[8192,640]{1,0:T(8,128)(2,1)} %get-tuple-element.728) | copy-start | bytes 31457284 | tf_op jit(solution)/shard_map/while
  350.8 7.1 %copy-start = (bf16[8192,640]{1,0:T(8,128)(2,1)S(1)}, bf16[8192,640]{1,0:T(8,128)(2,1)}, u32[]{:S(2)}) copy-start(bf16[8192,640]{1,0:T(8,128)(2,1)} %get-tuple-element.728) | copy-start | bytes 31457284 | tf_op jit(solution)/shard_map/while
  384.0 39.1 %copy-start.4 = (f32[4,640]{1,0:T(4,128)}, f32[4,640]{1,0:T(4,128)S(1)}, u32[]{:S(2)}) copy-start(f32[4,640]{1,0:T(4,128)S(1)} %get-tuple-element.434) | copy-start | bytes 30724

commit v13 on v12

--- a/solution.py
+++ b/solution.py
@@ -299,7 +299,7 @@
     own = last_state[1].reshape(batches * seq_len, width)
     gain_hi = last_state[2].astype(jnp.bfloat16)
     gain_lo = (last_state[2] - gain_hi.astype(jnp.float32)).astype(jnp.bfloat16)
-    extra = jnp.zeros((16, width), jnp.bfloat16).at[0].set(gain_hi).at[1].set(gain_lo)
+    extra = jnp.stack([gain_hi, gain_lo])
     own = jnp.concatenate([own, extra], axis=0)
     copies = jnp.broadcast_to(own, (tensors, *own.shape))
     gathered = lax.all_to_all(copies, "tensor", split_axis=0, concat_axis=2, tiled=True)[0]

time: 428 us -> 427 us (level)
  no operation moved by 1% of the time
where the time goes in v13:
time: 427 us; the launch traced here: 426 us
  Pallas kernels  317 us (74%)
  matrix products  50 us (12%)
  blocking collectives  37.4 us (9%)
  other arithmetic  9.68 us (2%)
  local copies, waits for them, and re-layouts  9.3 us (2%)
    pallas_call x11, Pallas kernels, layer_exchange(): pl.pallas_call(functools.partial(layer_exchange_kernel, n, n_sec, width),...  243 us
    pallas_call x11, Pallas kernels, matmul_nt(): pl.pallas_call(functools.partial(matmul_nt_kernel, n_sec), out_shape=jax....  73.4 us
    dot_general x11, matrix products, step_rows(): lax.dot_general(d_vals, w_in, contract, preferred_element_type=jnp.float32)  50 us
    all_to_all x1, blocking collectives, local(): lax.all_to_all(copies, 'tensor', split_axis=0, concat_axis=2, tiled=True)[0]  37.4 us

profile of v13, /device:TPU:32, one launch (start us, length us, event | category | flops | bytes accessed | tf_op | source)
XLA Modules:
  0.0 426.1 jit_solution(15204815053545955200)
XLA Ops:
  0.7 2.3 fusion.18
  3.0 2.4 convert_multiply_fusion
  5.4 1.0 constant_dynamic-slice_fusion.1
  6.5 1.8 broadcast_select_fusion.1
  8.5 375.5 %while.25 = (s32[]{:T(128)}, bf16[32,8192]{1,0:T(8,128)(2,1)S(1)}, bf16[2,2,32,512]{3,2,1,0:T(8,128)(2,1)S(1)}, f32[512]{0:T(512)S(1)}, f32[4,640]{1,0:T(4,128)S...) while((s32[]{:T(128)}, bf16[32,8192]{1,0:T(8,128)(2,1)S(1)}, ...), condition=%wide.region_7.8_spmd.clone, body=%wide.region_1.7_spmd.clone.sunk | while | flops 673154560 | bytes 68873840 | solution.py:298
  8.8 6.7 %eval_jaxpr.16 = f32[32,640]{1,0:T(8,128)S(1)} custom-call(bf16[32,8192]{1,0:T(8,128)(2,1)S(1)} %dynamic-slice_bitcast_fusion.4.top_ref, bf16[32,8192]{1,0:T(8,128)(2,1)S(1)} %copy.33.x_ref.up_ref, bf16[640,8192]{1,0:T(8,128)(2,1)} %get-tuple-element.702.w_ref), custom_call_target="tpu_custom_call" | custom-call | flops 335544320 | bytes 11616256 | tf_op jit(solution)/shard_map/while/body/eval_jaxpr/pallas_call | solution.py:37
  15.7 0.2 copy-done
  15.9 4.5 %fusion.26 = (f32[32]{0:T(128)S(1)}, bf16[32,8192]{1,0:T(8,128)(2,1)S(1)}) fusion(f32[2,64,8192]{2,1,0:T(8,128)} %get-tuple-element.706, s32[]{:T(128)S(6)} %select_n.236, s32[]{:T(128)S(6)} %select_n.237, f32[8192]{0:T(1024)S(1)} %bitcast.85, bf16[8192,640]{1,0:T(8,128)(2,1)S(1)} %copy-done, f32[32,640]{1,0:T(8,128)S(1)} %get-tuple-element.629, ...), kind=kOutput, calls=%fused_computation.2.clone.1 | convolution fusion | flops 337080288 | bytes 12191368 | tf_op jit(solution)/shard_map/while/body/eval_jaxpr/dot_general | solution.py:273
  20.5 24.2 %eval_jaxpr.17 = (bf16[32,512]{1,0:T(8,128)(2,1)S(1)}, bf16[32,8192]{1,0:T(8,128)(2,1)S(1)}, f32[1,512]{1,0:T(1,128)S(1)}) custom-call(bf16[32,8192]{1,0:T(8,128)(2,1)S(1)} %get-tuple-element.631.x_ref, f32[8,128]{1,0:T(8,128)S(1)} %scatter.7.s_ref, f32[32,640]{1,0:T(8,128)S(1)} %dynamic-slice_bitcast_fusion.5.aux_ref, f32[1,512]{1,0:T(1,128)S(1)} %bitcast.91, ...), custom_call_target="tpu_custom_call" | custom-call | tf_op jit(solution)/shard_map/while/body/eval_jaxpr/pallas_call | solution.py:164
  45.0 6.7 %eval_jaxpr.16 = f32[32,640]{1,0:T(8,128)S(1)} custom-call(bf16[32,8192]{1,0:T(8,128)(2,1)S(1)} %dynamic-slice_bitcast_fusion.4.top_ref, bf16[32,8192]{1,0:T(8,128)(2,1)S(1)} %copy.33.x_ref.up_ref, bf16[640,8192]{1,0:T(8,128)(2,1)} %get-tuple-element.702.w_ref), custom_call_target="tpu_custom_call" | custom-call | flops 335544320 | bytes 11616256 | tf_op jit(solution)/shard_map/while/body/eval_jaxpr/pallas_call | solution.py:37
  52.1 4.5 %fusion.26 = (f32[32]{0:T(128)S(1)}, bf16[32,8192]{1,0:T(8,128)(2,1)S(1)}) fusion(f32[2,64,8192]{2,1,0:T(8,128)} %get-tuple-element.706, s32[]{:T(128)S(6)} %select_n.236, s32[]{:T(128)S(6)} %select_n.237, f32[8192]{0:T(1024)S(1)} %bitcast.85, bf16[8192,640]{1,0:T(8,128)(2,1)S(1)} %copy-done, f32[32,640]{1,0:T(8,128)S(1)} %get-tuple-element.629, ...), kind=kOutput, calls=%fused_computation.2.clone.1 | convolution fusion | flops 337080288 | bytes 12191368 | tf_op jit(solution)/shard_map/while/body/eval_jaxpr/dot_general | solution.py:273
  56.7 25.1 %eval_jaxpr.17 = (bf16[32,512]{1,0:T(8,128)(2,1)S(1)}, bf16[32,8192]{1,0:T(8,128)(2,1)S(1)}, f32[1,512]{1,0:T(1,128)S(1)}) custom-call(bf16[32,8192]{1,0:T(8,128)(2,1)S(1)} %get-tuple-element.631.x_ref, f32[8,128]{1,0:T(8,128)S(1)} %scatter.7.s_ref, f32[32,640]{1,0:T(8,128)S(1)} %dynamic-slice_bitcast_fusion.5.aux_ref, f32[1,512]{1,0:T(1,128)S(1)} %bitcast.91, ...), custom_call_target="tpu_custom_call" | custom-call | tf_op jit(solution)/shard_map/while/body/eval_jaxpr/pallas_call | solution.py:164
  82.1 6.7 %eval_jaxpr.16 = f32[32,640]{1,0:T(8,128)S(1)} custom-call(bf16[32,8192]{1,0:T(8,128)(2,1)S(1)} %dynamic-slice_bitcast_fusion.4.top_ref, bf16[32,8192]{1,0:T(8,128)(2,1)S(1)} %copy.33.x_ref.up_ref, bf16[640,8192]{1,0:T(8,128)(2,1)} %get-tuple-element.702.w_ref), custom_call_target="tpu_custom_call" | custom-call | flops 335544320 | bytes 11616256 | tf_op jit(solution)/shard_map/while/body/eval_jaxpr/pallas_call | solution.py:37
  89.0 0.2 copy-done
  89.2 4.5 %fusion.26 = (f32[32]{0:T(128)S(1)}, bf16[32,8192]{1,0:T(8,128)(2,1)S(1)}) fusion(f32[2,64,8192]{2,1,0:T(8,128)} %get-tuple-element.706, s32[]{:T(128)S(6)} %select_n.236, s32[]{:T(128)S(6)} %select_n.237, f32[8192]{0:T(1024)S(1)} %bitcast.85, bf16[8192,640]{1,0:T(8,128)(2,1)S(1)} %copy-done, f32[32,640]{1,0:T(8,128)S(1)} %get-tuple-element.629, ...), kind=kOutput, calls=%fused_computation.2.clone.1 | convolution fusion | flops 337080288 | bytes 12191368 | tf_op jit(solution)/shard_map/while/body/eval_jaxpr/dot_general | solution.py:273
  93.8 21.3 %eval_jaxpr.17 = (bf16[32,512]{1,0:T(8,128)(2,1)S(1)}, bf16[32,8192]{1,0:T(8,128)(2,1)S(1)}, f32[1,512]{1,0:T(1,128)S(1)}) custom-call(bf16[32,8192]{1,0:T(8,128)(2,1)S(1)} %get-tuple-element.631.x_ref, f32[8,128]{1,0:T(8,128)S(1)} %scatter.7.s_ref, f32[32,640]{1,0:T(8,128)S(1)} %dynamic-slice_bitcast_fusion.5.aux_ref, f32[1,512]{1,0:T(1,128)S(1)} %bitcast.91, ...), custom_call_target="tpu_custom_call" | custom-call | tf_op jit(solution)/shard_map/while/body/eval_jaxpr/pallas_call | solution.py:164
  115.4 6.7 %eval_jaxpr.16 = f32[32,640]{1,0:T(8,128)S(1)} custom-call(bf16[32,8192]{1,0:T(8,128)(2,1)S(1)} %dynamic-slice_bitcast_fusion.4.top_ref, bf16[32,8192]{1,0:T(8,128)(2,1)S(1)} %copy.33.x_ref.up_ref, bf16[640,8192]{1,0:T(8,128)(2,1)} %get-tuple-element.702.w_ref), custom_call_target="tpu_custom_call" | custom-call | flops 335544320 | bytes 11616256 | tf_op jit(solution)/shard_map/while/body/eval_jaxpr/pallas_call | solution.py:37
  122.5 4.5 %fusion.26 = (f32[32]{0:T(128)S(1)}, bf16[32,8192]{1,0:T(8,128)(2,1)S(1)}) fusion(f32[2,64,8192]{2,1,0:T(8,128)} %get-tuple-element.706, s32[]{:T(128)S(6)} %select_n.236, s32[]{:T(128)S(6)} %select_n.237, f32[8192]{0:T(1024)S(1)} %bitcast.85, bf16[8192,640]{1,0:T(8,128)(2,1)S(1)} %copy-done, f32[32,640]{1,0:T(8,128)S(1)} %get-tuple-element.629, ...), kind=kOutput, calls=%fused_computation.2.clone.1 | convolution fusion | flops 337080288 | bytes 12191368 | tf_op jit(solution)/shard_map/while/body/eval_jaxpr/dot_general | solution.py:273
  127.1 22.9 %eval_jaxpr.17 = (bf16[32,512]{1,0:T(8,128)(2,1)S(1)}, bf16[32,8192]{1,0:T(8,128)(2,1)S(1)}, f32[1,512]{1,0:T(1,128)S(1)}) custom-call(bf16[32,8192]{1,0:T(8,128)(2,1)S(1)} %get-tuple-element.631.x_ref, f32[8,128]{1,0:T(8,128)S(1)} %scatter.7.s_ref, f32[32,640]{1,0:T(8,128)S(1)} %dynamic-slice_bitcast_fusion.5.aux_ref, f32[1,512]{1,0:T(1,128)S(1)} %bitcast.91, ...), custom_call_target="tpu_custom_call" | custom-call | tf_op jit(solution)/shard_map/while/body/eval_jaxpr/pallas_call | solution.py:164
  150.2 6.7 %eval_jaxpr.16 = f32[32,640]{1,0:T(8,128)S(1)} custom-call(bf16[32,8192]{1,0:T(8,128)(2,1)S(1)} %dynamic-slice_bitcast_fusion.4.top_ref, bf16[32,8192]{1,0:T(8,128)(2,1)S(1)} %copy.33.x_ref.up_ref, bf16[640,8192]{1,0:T(8,128)(2,1)} %get-tuple-element.702.w_ref), custom_call_target="tpu_custom_call" | custom-call | flops 335544320 | bytes 11616256 | tf_op jit(solution)/shard_map/while/body/eval_jaxpr/pallas_call | solution.py:37
  157.1 0.2 copy-done
  157.4 4.5 %fusion.26 = (f32[32]{0:T(128)S(1)}, bf16[32,8192]{1,0:T(8,128)(2,1)S(1)}) fusion(f32[2,64,8192]{2,1,0:T(8,128)} %get-tuple-element.706, s32[]{:T(128)S(6)} %select_n.236, s32[]{:T(128)S(6)} %select_n.237, f32[8192]{0:T(1024)S(1)} %bitcast.85, bf16[8192,640]{1,0:T(8,128)(2,1)S(1)} %copy-done, f32[32,640]{1,0:T(8,128)S(1)} %get-tuple-element.629, ...), kind=kOutput, calls=%fused_computation.2.clone.1 | convolution fusion | flops 337080288 | bytes 12191368 | tf_op jit(solution)/shard_map/while/body/eval_jaxpr/dot_general | solution.py:273
  161.9 21.2 %eval_jaxpr.17 = (bf16[32,512]{1,0:T(8,128)(2,1)S(1)}, bf16[32,8192]{1,0:T(8,128)(2,1)S(1)}, f32[1,512]{1,0:T(1,128)S(1)}) custom-call(bf16[32,8192]{1,0:T(8,128)(2,1)S(1)} %get-tuple-element.631.x_ref, f32[8,128]{1,0:T(8,128)S(1)} %scatter.7.s_ref, f32[32,640]{1,0:T(8,128)S(1)} %dynamic-slice_bitcast_fusion.5.aux_ref, f32[1,512]{1,0:T(1,128)S(1)} %bitcast.91, ...), custom_call_target="tpu_custom_call" | custom-call | tf_op jit(solution)/shard_map/while/body/eval_jaxpr/pallas_call | solution.py:164
  183.4 6.7 %eval_jaxpr.16 = f32[32,640]{1,0:T(8,128)S(1)} custom-call(bf16[32,8192]{1,0:T(8,128)(2,1)S(1)} %dynamic-slice_bitcast_fusion.4.top_ref, bf16[32,8192]{1,0:T(8,128)(2,1)S(1)} %copy.33.x_ref.up_ref, bf16[640,8192]{1,0:T(8,128)(2,1)} %get-tuple-element.702.w_ref), custom_call_target="tpu_custom_call" | custom-call | flops 335544320 | bytes 11616256 | tf_op jit(solution)/shard_map/while/body/eval_jaxpr/pallas_call | solution.py:37
  190.5 4.5 %fusion.26 = (f32[32]{0:T(128)S(1)}, bf16[32,8192]{1,0:T(8,128)(2,1)S(1)}) fusion(f32[2,64,8192]{2,1,0:T(8,128)} %get-tuple-element.706, s32[]{:T(128)S(6)} %select_n.236, s32[]{:T(128)S(6)} %select_n.237, f32[8192]{0:T(1024)S(1)} %bitcast.85, bf16[8192,640]{1,0:T(8,128)(2,1)S(1)} %copy-done, f32[32,640]{1,0:T(8,128)S(1)} %get-tuple-element.629, ...), kind=kOutput, calls=%fused_computation.2.clone.1 | convolution fusion | flops 337080288 | bytes 12191368 | tf_op jit(solution)/shard_map/while/body/eval_jaxpr/dot_general | solution.py:273
  195.1 20.5 %eval_jaxpr.17 = (bf16[32,512]{1,0:T(8,128)(2,1)S(1)}, bf16[32,8192]{1,0:T(8,128)(2,1)S(1)}, f32[1,512]{1,0:T(1,128)S(1)}) custom-call(bf16[32,8192]{1,0:T(8,128)(2,1)S(1)} %get-tuple-element.631.x_ref, f32[8,128]{1,0:T(8,128)S(1)} %scatter.7.s_ref, f32[32,640]{1,0:T(8,128)S(1)} %dynamic-slice_bitcast_fusion.5.aux_ref, f32[1,512]{1,0:T(1,128)S(1)} %bitcast.91, ...), custom_call_target="tpu_custom_call" | custom-call | tf_op jit(solution)/shard_map/while/body/eval_jaxpr/pallas_call | solution.py:164
  215.9 6.7 %eval_jaxpr.16 = f32[32,640]{1,0:T(8,128)S(1)} custom-call(bf16[32,8192]{1,0:T(8,128)(2,1)S(1)} %dynamic-slice_bitcast_fusion.4.top_ref, bf16[32,8192]{1,0:T(8,128)(2,1)S(1)} %copy.33.x_ref.up_ref, bf16[640,8192]{1,0:T(8,128)(2,1)} %get-tuple-element.702.w_ref), custom_call_target="tpu_custom_call" | custom-call | flops 335544320 | bytes 11616256 | tf_op jit(solution)/shard_map/while/body/eval_jaxpr/pallas_call | solution.py:37
  222.8 0.2 copy-done
  223.1 4.5 %fusion.26 = (f32[32]{0:T(128)S(1)}, bf16[32,8192]{1,0:T(8,128)(2,1)S(1)}) fusion(f32[2,64,8192]{2,1,0:T(8,128)} %get-tuple-element.706, s32[]{:T(128)S(6)} %select_n.236, s32[]{:T(128)S(6)} %select_n.237, f32[8192]{0:T(1024)S(1)} %bitcast.85, bf16[8192,640]{1,0:T(8,128)(2,1)S(1)} %copy-done, f32[32,640]{1,0:T(8,128)S(1)} %get-tuple-element.629, ...), kind=kOutput, calls=%fused_computation.2.clone.1 | convolution fusion | flops 337080288 | bytes 12191368 | tf_op jit(solution)/shard_map/while/body/eval_jaxpr/dot_general | solution.py:273
  227.6 21.5 %eval_jaxpr.17 = (bf16[32,512]{1,0:T(8,128)(2,1)S(1)}, bf16[32,8192]{1,0:T(8,128)(2,1)S(1)}, f32[1,512]{1,0:T(1,128)S(1)}) custom-call(bf16[32,8192]{1,0:T(8,128)(2,1)S(1)} %get-tuple-element.631.x_ref, f32[8,128]{1,0:T(8,128)S(1)} %scatter.7.s_ref, f32[32,640]{1,0:T(8,128)S(1)} %dynamic-slice_bitcast_fusion.5.aux_ref, f32[1,512]{1,0:T(1,128)S(1)} %bitcast.91, ...), custom_call_target="tpu_custom_call" | custom-call | tf_op jit(solution)/shard_map/while/body/eval_jaxpr/pallas_call | solution.py:164
  249.4 6.7 %eval_jaxpr.16 = f32[32,640]{1,0:T(8,128)S(1)} custom-call(bf16[32,8192]{1,0:T(8,128)(2,1)S(1)} %dynamic-slice_bitcast_fusion.4.top_ref, bf16[32,8192]{1,0:T(8,128)(2,1)S(1)} %copy.33.x_ref.up_ref, bf16[640,8192]{1,0:T(8,128)(2,1)} %get-tuple-element.702.w_ref), custom_call_target="tpu_custom_call" | custom-call | flops 335544320 | bytes 11616256 | tf_op jit(solution)/shard_map/while/body/eval_jaxpr/pallas_call | solution.py:37
  256.3 0.2 copy-done
  256.5 4.5 %fusion.26 = (f32[32]{0:T(128)S(1)}, bf16[32,8192]{1,0:T(8,128)(2,1)S(1)}) fusion(f32[2,64,8192]{2,1,0:T(8,128)} %get-tuple-element.706, s32[]{:T(128)S(6)} %select_n.236, s32[]{:T(128)S(6)} %select_n.237, f32[8192]{0:T(1024)S(1)} %bitcast.85, bf16[8192,640]{1,0:T(8,128)(2,1)S(1)} %copy-done, f32[32,640]{1,0:T(8,128)S(1)} %get-tuple-element.629, ...), kind=kOutput, calls=%fused_computation.2.clone.1 | convolution fusion | flops 337080288 | bytes 12191368 | tf_op jit(solution)/shard_map/while/body/eval_jaxpr/dot_general | solution.py:273
  261.1 21.2 %eval_jaxpr.17 = (bf16[32,512]{1,0:T(8,128)(2,1)S(1)}, bf16[32,8192]{1,0:T(8,128)(2,1)S(1)}, f32[1,512]{1,0:T(1,128)S(1)}) custom-call(bf16[32,8192]{1,0:T(8,128)(2,1)S(1)} %get-tuple-element.631.x_ref, f32[8,128]{1,0:T(8,128)S(1)} %scatter.7.s_ref, f32[32,640]{1,0:T(8,128)S(1)} %dynamic-slice_bitcast_fusion.5.aux_ref, f32[1,512]{1,0:T(1,128)S(1)} %bitcast.91, ...), custom_call_target="tpu_custom_call" | custom-call | tf_op jit(solution)/shard_map/while/body/eval_jaxpr/pallas_call | solution.py:164
  282.6 6.7 %eval_jaxpr.16 = f32[32,640]{1,0:T(8,128)S(1)} custom-call(bf16[32,8192]{1,0:T(8,128)(2,1)S(1)} %dynamic-slice_bitcast_fusion.4.top_ref, bf16[32,8192]{1,0:T(8,128)(2,1)S(1)} %copy.33.x_ref.up_ref, bf16[640,8192]{1,0:T(8,128)(2,1)} %get-tuple-element.702.w_ref), custom_call_target="tpu_custom_call" | custom-call | flops 335544320 | bytes 11616256 | tf_op jit(solution)/shard_map/while/body/eval_jaxpr/pallas_call | solution.py:37
  289.7 4.5 %fusion.26 = (f32[32]{0:T(128)S(1)}, bf16[32,8192]{1,0:T(8,128)(2,1)S(1)}) fusion(f32[2,64,8192]{2,1,0:T(8,128)} %get-tuple-element.706, s32[]{:T(128)S(6)} %select_n.236, s32[]{:T(128)S(6)} %select_n.237, f32[8192]{0:T(1024)S(1)} %bitcast.85, bf16[8192,640]{1,0:T(8,128)(2,1)S(1)} %copy-done, f32[32,640]{1,0:T(8,128)S(1)} %get-tuple-element.629, ...), kind=kOutput, calls=%fused_computation.2.clone.1 | convolution fusion | flops 337080288 | bytes 12191368 | tf_op jit(solution)/shard_map/while/body/eval_jaxpr/dot_general | solution.py:273
  294.2 24.1 %eval_jaxpr.17 = (bf16[32,512]{1,0:T(8,128)(2,1)S(1)}, bf16[32,8192]{1,0:T(8,128)(2,1)S(1)}, f32[1,512]{1,0:T(1,128)S(1)}) custom-call(bf16[32,8192]{1,0:T(8,128)(2,1)S(1)} %get-tuple-element.631.x_ref, f32[8,128]{1,0:T(8,128)S(1)} %scatter.7.s_ref, f32[32,640]{1,0:T(8,128)S(1)} %dynamic-slice_bitcast_fusion.5.aux_ref, f32[1,512]{1,0:T(1,128)S(1)} %bitcast.91, ...), custom_call_target="tpu_custom_call" | custom-call | tf_op jit(solution)/shard_map/while/body/eval_jaxpr/pallas_call | solution.py:164
  318.6 6.7 %eval_jaxpr.16 = f32[32,640]{1,0:T(8,128)S(1)} custom-call(bf16[32,8192]{1,0:T(8,128)(2,1)S(1)} %dynamic-slice_bitcast_fusion.4.top_ref, bf16[32,8192]{1,0:T(8,128)(2,1)S(1)} %copy.33.x_ref.up_ref, bf16[640,8192]{1,0:T(8,128)(2,1)} %get-tuple-element.702.w_ref), custom_call_target="tpu_custom_call" | custom-call | flops 335544320 | bytes 11616256 | tf_op jit(solution)/shard_map/while/body/eval_jaxpr/pallas_call | solution.py:37
  325.5 0.2 copy-done
  325.8 4.5 %fusion.26 = (f32[32]{0:T(128)S(1)}, bf16[32,8192]{1,0:T(8,128)(2,1)S(1)}) fusion(f32[2,64,8192]{2,1,0:T(8,128)} %get-tuple-element.706, s32[]{:T(128)S(6)} %select_n.236, s32[]{:T(128)S(6)} %select_n.237, f32[8192]{0:T(1024)S(1)} %bitcast.85, bf16[8192,640]{1,0:T(8,128)(2,1)S(1)} %copy-done, f32[32,640]{1,0:T(8,128)S(1)} %get-tuple-element.629, ...), kind=kOutput, calls=%fused_computation.2.clone.1 | convolution fusion | flops 337080288 | bytes 12191368 | tf_op jit(solution)/shard_map/while/body/eval_jaxpr/dot_general | solution.py:273
  330.3 20.2 %eval_jaxpr.17 = (bf16[32,512]{1,0:T(8,128)(2,1)S(1)}, bf16[32,8192]{1,0:T(8,128)(2,1)S(1)}, f32[1,512]{1,0:T(1,128)S(1)}) custom-call(bf16[32,8192]{1,0:T(8,128)(2,1)S(1)} %get-tuple-element.631.x_ref, f32[8,128]{1,0:T(8,128)S(1)} %scatter.7.s_ref, f32[32,640]{1,0:T(8,128)S(1)} %dynamic-slice_bitcast_fusion.5.aux_ref, f32[1,512]{1,0:T(1,128)S(1)} %bitcast.91, ...), custom_call_target="tpu_custom_call" | custom-call | tf_op jit(solution)/shard_map/while/body/eval_jaxpr/pallas_call | solution.py:164
  350.8 6.7 %eval_jaxpr.16 = f32[32,640]{1,0:T(8,128)S(1)} custom-call(bf16[32,8192]{1,0:T(8,128)(2,1)S(1)} %dynamic-slice_bitcast_fusion.4.top_ref, bf16[32,8192]{1,0:T(8,128)(2,1)S(1)} %copy.33.x_ref.up_ref, bf16[640,8192]{1,0:T(8,128)(2,1)} %get-tuple-element.702.w_ref), custom_call_target="tpu_custom_call" | custom-call | flops 335544320 | bytes 11616256 | tf_op jit(solution)/shard_map/while/body/eval_jaxpr/pallas_call | solution.py:37
  358.0 4.5 %fusion.26 = (f32[32]{0:T(128)S(1)}, bf16[32,8192]{1,0:T(8,128)(2,1)S(1)}) fusion(f32[2,64,8192]{2,1,0:T(8,128)} %get-tuple-element.706, s32[]{:T(128)S(6)} %select_n.236, s32[]{:T(128)S(6)} %select_n.237, f32[8192]{0:T(1024)S(1)} %bitcast.85, bf16[8192,640]{1,0:T(8,128)(2,1)S(1)} %copy-done, f32[32,640]{1,0:T(8,128)S(1)} %get-tuple-element.629, ...), kind=kOutput, calls=%fused_computation.2.clone.1 | convolution fusion | flops 337080288 | bytes 12191368 | tf_op jit(solution)/shard_map/while/body/eval_jaxpr/dot_general | solution.py:273
  362.5 21.4 %eval_jaxpr.17 = (bf16[32,512]{1,0:T(8,128)(2,1)S(1)}, bf16[32,8192]{1,0:T(8,128)(2,1)S(1)}, f32[1,512]{1,0:T(1,128)S(1)}) custom-call(bf16[32,8192]{1,0:T(8,128)(2,1)S(1)} %get-tuple-element.631.x_ref, f32[8,128]{1,0:T(8,128)S(1)} %scatter.7.s_ref, f32[32,640]{1,0:T(8,128)S(1)} %dynamic-slice_bitcast_fusion.5.aux_ref, f32[1,512]{1,0:T(1,128)S(1)} %bitcast.91, ...), custom_call_target="tpu_custom_call" | custom-call | tf_op jit(solution)/shard_map/while/body/eval_jaxpr/pallas_call | solution.py:164
  384.2 37.4 %all_to_all.15 = bf16[16,130,512]{2,1,0:T(8,128)(2,1)S(1)} all-to-all(bf16[16,130,512]{2,1,0:T(8,128)(2,1)S(1)} %broadcast_in_dim.96), channel_id=1, replica_groups=mesh['section'=8,'tensor'=16] {'tensor'}, dimensions={0} | all-to-all | bytes 4259840 | tf_op jit(solution)/shard_map/all_to_all | solution.py:305
  421.7 0.7 fusion.19
  422.6 1.2 copy.12
  423.7 2.3 broadcast_in_dim_reshape.3
  (223 shorter events, 6.0 us)
Async XLA Ops:
  0.6 2.3 copy-start.1
  2.9 2.5 copy-start.2
  2.9 3.4 copy-start.6
  3.0 3.4 copy-start.7
  3.0 3.5 copy-start.5
  6.5 2.0 copy-start.3
  8.8 7.1 %copy-start = (bf16[8192,640]{1,0:T(8,128)(2,1)S(1)}, bf16[8192,640]{1,0:T(8,128)(2,1)}, u32[]{:S(2)}) copy-start(bf16[8192,640]{1,0:T(8,128)(2,1)} %get-tuple-element.704) | copy-start | bytes 31457284 | tf_op jit(solution)/shard_map/while
  45.0 7.1 %copy-start = (bf16[8192,640]{1,0:T(8,128)(2,1)S(1)}, bf16[8192,640]{1,0:T(8,128)(2,1)}, u32[]{:S(2)}) copy-start(bf16[8192,640]{1,0:T(8,128)(2,1)} %get-tuple-element.704) | copy-start | bytes 31457284 | tf_op jit(solution)/shard_map/while
  82.1 7.1 %copy-start = (bf16[8192,640]{1,0:T(8,128)(2,1)S(1)}, bf16[8192,640]{1,0:T(8,128)(2,1)}, u32[]{:S(2)}) copy-start(bf16[8192,640]{1,0:T(8,128)(2,1)} %get-tuple-element.704) | copy-start | bytes 31457284 | tf_op jit(solution)/shard_map/while
  115.4 7.1 %copy-start = (bf16[8192,640]{1,0:T(8,128)(2,1)S(1)}, bf16[8192,640]{1,0:T(8,128)(2,1)}, u32[]{:S(2)}) copy-start(bf16[8192,640]{1,0:T(8,128)(2,1)} %get-tuple-element.704) | copy-start | bytes 31457284 | tf_op jit(solution)/shard_map/while
  150.2 7.1 %copy-start = (bf16[8192,640]{1,0:T(8,128)(2,1)S(1)}, bf16[8192,640]{1,0:T(8,128)(2,1)}, u32[]{:S(2)}) copy-start(bf16[8192,640]{1,0:T(8,128)(2,1)} %get-tuple-element.704) | copy-start | bytes 31457284 | tf_op jit(solution)/shard_map/while
  183.4 7.1 %copy-start = (bf16[8192,640]{1,0:T(8,128)(2,1)S(1)}, bf16[8192,640]{1,0:T(8,128)(2,1)}, u32[]{:S(2)}) copy-start(bf16[8192,640]{1,0:T(8,128)(2,1)} %get-tuple-element.704) | copy-start | bytes 31457284 | tf_op jit(solution)/shard_map/while
  215.9 7.1 %copy-start = (bf16[8192,640]{1,0:T(8,128)(2,1)S(1)}, bf16[8192,640]{1,0:T(8,128)(2,1)}, u32[]{:S(2)}) copy-start(bf16[8192,640]{1,0:T(8,128)(2,1)} %get-tuple-element.704) | copy-start | bytes 31457284 | tf_op jit(solution)/shard_map/while
  249.4 7.1 %copy-start = (bf16[8192,640]{1,0:T(8,128)(2,1)S(1)}, bf16[8192,640]{1,0:T(8,128)(2,1)}, u32[]{:S(2)}) copy-start(bf16[8192,640]{1,0:T(8,128)(2,1)} %get-tuple-element.704) | copy-start | bytes 31457284 | tf_op jit(solution)/shard_map/while
  282.6 7.1 %copy-start = (bf16[8192,640]{1,0:T(8,128)(2,1)S(1)}, bf16[8192,640]{1,0:T(8,128)(2,1)}, u32[]{:S(2)}) copy-start(bf16[8192,640]{1,0:T(8,128)(2,1)} %get-tuple-element.704) | copy-start | bytes 31457284 | tf_op jit(solution)/shard_map/while
  318.6 7.1 %copy-start = (bf16[8192,640]{1,0:T(8,128)(2,1)S(1)}, bf16[8192,640]{1,0:T(8,128)(2,1)}, u32[]{:S(2)}) copy-start(bf16[8192,640]{1,0:T(8,128)(2,1)} %get-tuple-element.704) | copy-start | bytes 31457284 | tf_op jit(solution)/shard_map/while
  350.8 7.1 %copy-start = (bf16[8192,640]{1,0:T(8,128)(2,1)S(1)}, bf16[8192,640]{1,0:T(8,128)(2,1)}, u32[]{:S(2)}) copy-start(bf16[8192,640]{1,0:T(8,128)(2,1)} %get-tuple-element.704) | copy-start | bytes 31457284 | tf_op jit(solution)/shard_map/while
  384.0 37.7 %copy-start.4 = (f32[4,640]{1,0:T(4,128)}, f32[4,640]{1,0:T(4,128)S(1)}, u32[]{:S(2)}) copy-start(f32[4,640]{1,0:T(4,128)S(1)} %get-tuple-element.410) | copy-start | bytes 30724

commit v14 on v13

--- a/solution.py
+++ b/solution.py
@@ -264,7 +264,7 @@
         batch_slot, half_now, join_now, active = pick_block(step_idx)
         row_start = half_now * chunk_len
         top_chunk = rows_of(top_grads, batch_slot, row_start, chunk_len)
-        d_act = matmul_nt(top_chunk, incoming, w_out, w_out.shape[0], 2048, jnp.float32, sections)
+        d_act = matmul_nt(top_chunk, incoming, w_out, w_out.shape[0], 4096, jnp.float32, sections)
         ext_vals = lax.dynamic_slice(
             conv_padded, (batch_slot, row_start, 0), (1, chunk_len + kernel_width - 1, local_channels)
         )[0].astype(jnp.float32)

time: 427 us -> 426 us (level)
  Pallas kernels: 317 us -> 310 us
  local copies, waits for them, and re-layouts: 9.3 us -> 15.4 us
    pallas_call x11, Pallas kernels: 73.4 us -> 66.1 us  [matmul_nt(): pl.pallas_call(functools.partial(matmul_nt_kernel, n_sec), out_shape=jax....]
    while x33, local copies, waits for them, and re-layouts: 2.93 us -> 9.04 us
where the time goes in v14:
time: 426 us; the launch traced here: 425 us
  Pallas kernels  310 us (73%)
  matrix products  50 us (12%)
  blocking collectives  36.7 us (9%)
  local copies, waits for them, and re-layouts  15.4 us (4%)
  other arithmetic  9.68 us (2%)
    pallas_call x11, Pallas kernels, layer_exchange(): pl.pallas_call(functools.partial(layer_exchange_kernel, n, n_sec, width),...  244 us
    pallas_call x11, Pallas kernels, matmul_nt(): pl.pallas_call(functools.partial(matmul_nt_kernel, n_sec), out_shape=jax....  66.1 us
    dot_general x11, matrix products, step_rows(): lax.dot_general(d_vals, w_in, contract, preferred_element_type=jnp.float32)  50 us
    all_to_all x1, blocking collectives, local(): lax.all_to_all(copies, 'tensor', split_axis=0, concat_axis=2, tiled=True)[0]  36.7 us
    while x33, local copies, waits for them, and re-layouts  9.04 us

profile of v14, /device:TPU:32, one launch (start us, length us, event | category | flops | bytes accessed | tf_op | source)
XLA Modules:
  0.0 424.6 jit_solution(1006804164705660789)
XLA Ops:
  0.7 2.3 fusion.18
  3.0 2.4 convert_multiply_fusion
  5.4 1.0 constant_dynamic-slice_fusion.1
  6.5 1.8 broadcast_select_fusion.1
  8.5 374.7 %while.25 = (s32[]{:T(128)}, bf16[32,8192]{1,0:T(8,128)(2,1)S(1)}, bf16[2,2,32,512]{3,2,1,0:T(8,128)(2,1)S(1)}, f32[512]{0:T(512)S(1)}, f32[4,640]{1,0:T(4,128)S...) while((s32[]{:T(128)}, bf16[32,8192]{1,0:T(8,128)(2,1)S(1)}, ...), condition=%wide.region_7.8_spmd.clone, body=%wide.region_1.7_spmd.clone.sunk | while | flops 673154560 | bytes 68873840 | solution.py:298
  8.8 6.0 %eval_jaxpr.16 = f32[32,640]{1,0:T(8,128)S(1)} custom-call(bf16[32,8192]{1,0:T(8,128)(2,1)S(1)} %dynamic-slice_bitcast_fusion.4.top_ref, bf16[32,8192]{1,0:T(8,128)(2,1)S(1)} %copy.33.x_ref.up_ref, bf16[640,8192]{1,0:T(8,128)(2,1)} %get-tuple-element.702.w_ref), custom_call_target="tpu_custom_call" | custom-call | flops 335544320 | bytes 11616256 | tf_op jit(solution)/shard_map/while/body/eval_jaxpr/pallas_call | solution.py:37
  15.8 4.5 %fusion.26 = (f32[32]{0:T(128)S(1)}, bf16[32,8192]{1,0:T(8,128)(2,1)S(1)}) fusion(f32[2,64,8192]{2,1,0:T(8,128)} %get-tuple-element.706, s32[]{:T(128)S(6)} %select_n.236, s32[]{:T(128)S(6)} %select_n.237, f32[8192]{0:T(1024)S(1)} %bitcast.85, bf16[8192,640]{1,0:T(8,128)(2,1)S(1)} %copy-done, f32[32,640]{1,0:T(8,128)S(1)} %get-tuple-element.629, ...), kind=kOutput, calls=%fused_computation.2.clone.1 | convolution fusion | flops 337080288 | bytes 12191368 | tf_op jit(solution)/shard_map/while/body/eval_jaxpr/dot_general | solution.py:273
  20.4 24.2 %eval_jaxpr.17 = (bf16[32,512]{1,0:T(8,128)(2,1)S(1)}, bf16[32,8192]{1,0:T(8,128)(2,1)S(1)}, f32[1,512]{1,0:T(1,128)S(1)}) custom-call(bf16[32,8192]{1,0:T(8,128)(2,1)S(1)} %get-tuple-element.631.x_ref, f32[8,128]{1,0:T(8,128)S(1)} %scatter.7.s_ref, f32[32,640]{1,0:T(8,128)S(1)} %dynamic-slice_bitcast_fusion.5.aux_ref, f32[1,512]{1,0:T(1,128)S(1)} %bitcast.91, ...), custom_call_target="tpu_custom_call" | custom-call | tf_op jit(solution)/shard_map/while/body/eval_jaxpr/pallas_call | solution.py:164
  44.9 6.0 %eval_jaxpr.16 = f32[32,640]{1,0:T(8,128)S(1)} custom-call(bf16[32,8192]{1,0:T(8,128)(2,1)S(1)} %dynamic-slice_bitcast_fusion.4.top_ref, bf16[32,8192]{1,0:T(8,128)(2,1)S(1)} %copy.33.x_ref.up_ref, bf16[640,8192]{1,0:T(8,128)(2,1)} %get-tuple-element.702.w_ref), custom_call_target="tpu_custom_call" | custom-call | flops 335544320 | bytes 11616256 | tf_op jit(solution)/shard_map/while/body/eval_jaxpr/pallas_call | solution.py:37
  51.1 0.8 copy-done
  51.9 4.5 %fusion.26 = (f32[32]{0:T(128)S(1)}, bf16[32,8192]{1,0:T(8,128)(2,1)S(1)}) fusion(f32[2,64,8192]{2,1,0:T(8,128)} %get-tuple-element.706, s32[]{:T(128)S(6)} %select_n.236, s32[]{:T(128)S(6)} %select_n.237, f32[8192]{0:T(1024)S(1)} %bitcast.85, bf16[8192,640]{1,0:T(8,128)(2,1)S(1)} %copy-done, f32[32,640]{1,0:T(8,128)S(1)} %get-tuple-element.629, ...), kind=kOutput, calls=%fused_computation.2.clone.1 | convolution fusion | flops 337080288 | bytes 12191368 | tf_op jit(solution)/shard_map/while/body/eval_jaxpr/dot_general | solution.py:273
  56.5 25.1 %eval_jaxpr.17 = (bf16[32,512]{1,0:T(8,128)(2,1)S(1)}, bf16[32,8192]{1,0:T(8,128)(2,1)S(1)}, f32[1,512]{1,0:T(1,128)S(1)}) custom-call(bf16[32,8192]{1,0:T(8,128)(2,1)S(1)} %get-tuple-element.631.x_ref, f32[8,128]{1,0:T(8,128)S(1)} %scatter.7.s_ref, f32[32,640]{1,0:T(8,128)S(1)} %dynamic-slice_bitcast_fusion.5.aux_ref, f32[1,512]{1,0:T(1,128)S(1)} %bitcast.91, ...), custom_call_target="tpu_custom_call" | custom-call | tf_op jit(solution)/shard_map/while/body/eval_jaxpr/pallas_call | solution.py:164
  81.9 6.0 %eval_jaxpr.16 = f32[32,640]{1,0:T(8,128)S(1)} custom-call(bf16[32,8192]{1,0:T(8,128)(2,1)S(1)} %dynamic-slice_bitcast_fusion.4.top_ref, bf16[32,8192]{1,0:T(8,128)(2,1)S(1)} %copy.33.x_ref.up_ref, bf16[640,8192]{1,0:T(8,128)(2,1)} %get-tuple-element.702.w_ref), custom_call_target="tpu_custom_call" | custom-call | flops 335544320 | bytes 11616256 | tf_op jit(solution)/shard_map/while/body/eval_jaxpr/pallas_call | solution.py:37
  88.9 4.5 %fusion.26 = (f32[32]{0:T(128)S(1)}, bf16[32,8192]{1,0:T(8,128)(2,1)S(1)}) fusion(f32[2,64,8192]{2,1,0:T(8,128)} %get-tuple-element.706, s32[]{:T(128)S(6)} %select_n.236, s32[]{:T(128)S(6)} %select_n.237, f32[8192]{0:T(1024)S(1)} %bitcast.85, bf16[8192,640]{1,0:T(8,128)(2,1)S(1)} %copy-done, f32[32,640]{1,0:T(8,128)S(1)} %get-tuple-element.629, ...), kind=kOutput, calls=%fused_computation.2.clone.1 | convolution fusion | flops 337080288 | bytes 12191368 | tf_op jit(solution)/shard_map/while/body/eval_jaxpr/dot_general | solution.py:273
  93.4 22.4 %eval_jaxpr.17 = (bf16[32,512]{1,0:T(8,128)(2,1)S(1)}, bf16[32,8192]{1,0:T(8,128)(2,1)S(1)}, f32[1,512]{1,0:T(1,128)S(1)}) custom-call(bf16[32,8192]{1,0:T(8,128)(2,1)S(1)} %get-tuple-element.631.x_ref, f32[8,128]{1,0:T(8,128)S(1)} %scatter.7.s_ref, f32[32,640]{1,0:T(8,128)S(1)} %dynamic-slice_bitcast_fusion.5.aux_ref, f32[1,512]{1,0:T(1,128)S(1)} %bitcast.91, ...), custom_call_target="tpu_custom_call" | custom-call | tf_op jit(solution)/shard_map/while/body/eval_jaxpr/pallas_call | solution.py:164
  116.1 6.0 %eval_jaxpr.16 = f32[32,640]{1,0:T(8,128)S(1)} custom-call(bf16[32,8192]{1,0:T(8,128)(2,1)S(1)} %dynamic-slice_bitcast_fusion.4.top_ref, bf16[32,8192]{1,0:T(8,128)(2,1)S(1)} %copy.33.x_ref.up_ref, bf16[640,8192]{1,0:T(8,128)(2,1)} %get-tuple-element.702.w_ref), custom_call_target="tpu_custom_call" | custom-call | flops 335544320 | bytes 11616256 | tf_op jit(solution)/shard_map/while/body/eval_jaxpr/pallas_call | solution.py:37
  123.1 4.5 %fusion.26 = (f32[32]{0:T(128)S(1)}, bf16[32,8192]{1,0:T(8,128)(2,1)S(1)}) fusion(f32[2,64,8192]{2,1,0:T(8,128)} %get-tuple-element.706, s32[]{:T(128)S(6)} %select_n.236, s32[]{:T(128)S(6)} %select_n.237, f32[8192]{0:T(1024)S(1)} %bitcast.85, bf16[8192,640]{1,0:T(8,128)(2,1)S(1)} %copy-done, f32[32,640]{1,0:T(8,128)S(1)} %get-tuple-element.629, ...), kind=kOutput, calls=%fused_computation.2.clone.1 | convolution fusion | flops 337080288 | bytes 12191368 | tf_op jit(solution)/shard_map/while/body/eval_jaxpr/dot_general | solution.py:273
  127.7 19.8 %eval_jaxpr.17 = (bf16[32,512]{1,0:T(8,128)(2,1)S(1)}, bf16[32,8192]{1,0:T(8,128)(2,1)S(1)}, f32[1,512]{1,0:T(1,128)S(1)}) custom-call(bf16[32,8192]{1,0:T(8,128)(2,1)S(1)} %get-tuple-element.631.x_ref, f32[8,128]{1,0:T(8,128)S(1)} %scatter.7.s_ref, f32[32,640]{1,0:T(8,128)S(1)} %dynamic-slice_bitcast_fusion.5.aux_ref, f32[1,512]{1,0:T(1,128)S(1)} %bitcast.91, ...), custom_call_target="tpu_custom_call" | custom-call | tf_op jit(solution)/shard_map/while/body/eval_jaxpr/pallas_call | solution.py:164
  147.8 6.0 %eval_jaxpr.16 = f32[32,640]{1,0:T(8,128)S(1)} custom-call(bf16[32,8192]{1,0:T(8,128)(2,1)S(1)} %dynamic-slice_bitcast_fusion.4.top_ref, bf16[32,8192]{1,0:T(8,128)(2,1)S(1)} %copy.33.x_ref.up_ref, bf16[640,8192]{1,0:T(8,128)(2,1)} %get-tuple-element.702.w_ref), custom_call_target="tpu_custom_call" | custom-call | flops 335544320 | bytes 11616256 | tf_op jit(solution)/shard_map/while/body/eval_jaxpr/pallas_call | solution.py:37
  154.0 0.8 copy-done
  154.8 4.5 %fusion.26 = (f32[32]{0:T(128)S(1)}, bf16[32,8192]{1,0:T(8,128)(2,1)S(1)}) fusion(f32[2,64,8192]{2,1,0:T(8,128)} %get-tuple-element.706, s32[]{:T(128)S(6)} %select_n.236, s32[]{:T(128)S(6)} %select_n.237, f32[8192]{0:T(1024)S(1)} %bitcast.85, bf16[8192,640]{1,0:T(8,128)(2,1)S(1)} %copy-done, f32[32,640]{1,0:T(8,128)S(1)} %get-tuple-element.629, ...), kind=kOutput, calls=%fused_computation.2.clone.1 | convolution fusion | flops 337080288 | bytes 12191368 | tf_op jit(solution)/shard_map/while/body/eval_jaxpr/dot_general | solution.py:273
  159.4 20.3 %eval_jaxpr.17 = (bf16[32,512]{1,0:T(8,128)(2,1)S(1)}, bf16[32,8192]{1,0:T(8,128)(2,1)S(1)}, f32[1,512]{1,0:T(1,128)S(1)}) custom-call(bf16[32,8192]{1,0:T(8,128)(2,1)S(1)} %get-tuple-element.631.x_ref, f32[8,128]{1,0:T(8,128)S(1)} %scatter.7.s_ref, f32[32,640]{1,0:T(8,128)S(1)} %dynamic-slice_bitcast_fusion.5.aux_ref, f32[1,512]{1,0:T(1,128)S(1)} %bitcast.91, ...), custom_call_target="tpu_custom_call" | custom-call | tf_op jit(solution)/shard_map/while/body/eval_jaxpr/pallas_call | solution.py:164
  180.0 6.0 %eval_jaxpr.16 = f32[32,640]{1,0:T(8,128)S(1)} custom-call(bf16[32,8192]{1,0:T(8,128)(2,1)S(1)} %dynamic-slice_bitcast_fusion.4.top_ref, bf16[32,8192]{1,0:T(8,128)(2,1)S(1)} %copy.33.x_ref.up_ref, bf16[640,8192]{1,0:T(8,128)(2,1)} %get-tuple-element.702.w_ref), custom_call_target="tpu_custom_call" | custom-call | flops 335544320 | bytes 11616256 | tf_op jit(solution)/shard_map/while/body/eval_jaxpr/pallas_call | solution.py:37
  187.0 4.5 %fusion.26 = (f32[32]{0:T(128)S(1)}, bf16[32,8192]{1,0:T(8,128)(2,1)S(1)}) fusion(f32[2,64,8192]{2,1,0:T(8,128)} %get-tuple-element.706, s32[]{:T(128)S(6)} %select_n.236, s32[]{:T(128)S(6)} %select_n.237, f32[8192]{0:T(1024)S(1)} %bitcast.85, bf16[8192,640]{1,0:T(8,128)(2,1)S(1)} %copy-done, f32[32,640]{1,0:T(8,128)S(1)} %get-tuple-element.629, ...), kind=kOutput, calls=%fused_computation.2.clone.1 | convolution fusion | flops 337080288 | bytes 12191368 | tf_op jit(solution)/shard_map/while/body/eval_jaxpr/dot_general | solution.py:273
  191.6 24.3 %eval_jaxpr.17 = (bf16[32,512]{1,0:T(8,128)(2,1)S(1)}, bf16[32,8192]{1,0:T(8,128)(2,1)S(1)}, f32[1,512]{1,0:T(1,128)S(1)}) custom-call(bf16[32,8192]{1,0:T(8,128)(2,1)S(1)} %get-tuple-element.631.x_ref, f32[8,128]{1,0:T(8,128)S(1)} %scatter.7.s_ref, f32[32,640]{1,0:T(8,128)S(1)} %dynamic-slice_bitcast_fusion.5.aux_ref, f32[1,512]{1,0:T(1,128)S(1)} %bitcast.91, ...), custom_call_target="tpu_custom_call" | custom-call | tf_op jit(solution)/shard_map/while/body/eval_jaxpr/pallas_call | solution.py:164
  216.2 6.0 %eval_jaxpr.16 = f32[32,640]{1,0:T(8,128)S(1)} custom-call(bf16[32,8192]{1,0:T(8,128)(2,1)S(1)} %dynamic-slice_bitcast_fusion.4.top_ref, bf16[32,8192]{1,0:T(8,128)(2,1)S(1)} %copy.33.x_ref.up_ref, bf16[640,8192]{1,0:T(8,128)(2,1)} %get-tuple-element.702.w_ref), custom_call_target="tpu_custom_call" | custom-call | flops 335544320 | bytes 11616256 | tf_op jit(solution)/shard_map/while/body/eval_jaxpr/pallas_call | solution.py:37
  222.4 0.8 copy-done
  223.2 4.5 %fusion.26 = (f32[32]{0:T(128)S(1)}, bf16[32,8192]{1,0:T(8,128)(2,1)S(1)}) fusion(f32[2,64,8192]{2,1,0:T(8,128)} %get-tuple-element.706, s32[]{:T(128)S(6)} %select_n.236, s32[]{:T(128)S(6)} %select_n.237, f32[8192]{0:T(1024)S(1)} %bitcast.85, bf16[8192,640]{1,0:T(8,128)(2,1)S(1)} %copy-done, f32[32,640]{1,0:T(8,128)S(1)} %get-tuple-element.629, ...), kind=kOutput, calls=%fused_computation.2.clone.1 | convolution fusion | flops 337080288 | bytes 12191368 | tf_op jit(solution)/shard_map/while/body/eval_jaxpr/dot_general | solution.py:273
  227.8 21.9 %eval_jaxpr.17 = (bf16[32,512]{1,0:T(8,128)(2,1)S(1)}, bf16[32,8192]{1,0:T(8,128)(2,1)S(1)}, f32[1,512]{1,0:T(1,128)S(1)}) custom-call(bf16[32,8192]{1,0:T(8,128)(2,1)S(1)} %get-tuple-element.631.x_ref, f32[8,128]{1,0:T(8,128)S(1)} %scatter.7.s_ref, f32[32,640]{1,0:T(8,128)S(1)} %dynamic-slice_bitcast_fusion.5.aux_ref, f32[1,512]{1,0:T(1,128)S(1)} %bitcast.91, ...), custom_call_target="tpu_custom_call" | custom-call | tf_op jit(solution)/shard_map/while/body/eval_jaxpr/pallas_call | solution.py:164
  250.0 6.0 %eval_jaxpr.16 = f32[32,640]{1,0:T(8,128)S(1)} custom-call(bf16[32,8192]{1,0:T(8,128)(2,1)S(1)} %dynamic-slice_bitcast_fusion.4.top_ref, bf16[32,8192]{1,0:T(8,128)(2,1)S(1)} %copy.33.x_ref.up_ref, bf16[640,8192]{1,0:T(8,128)(2,1)} %get-tuple-element.702.w_ref), custom_call_target="tpu_custom_call" | custom-call | flops 335544320 | bytes 11616256 | tf_op jit(solution)/shard_map/while/body/eval_jaxpr/pallas_call | solution.py:37
  256.3 0.8 copy-done
  257.0 4.5 %fusion.26 = (f32[32]{0:T(128)S(1)}, bf16[32,8192]{1,0:T(8,128)(2,1)S(1)}) fusion(f32[2,64,8192]{2,1,0:T(8,128)} %get-tuple-element.706, s32[]{:T(128)S(6)} %select_n.236, s32[]{:T(128)S(6)} %select_n.237, f32[8192]{0:T(1024)S(1)} %bitcast.85, bf16[8192,640]{1,0:T(8,128)(2,1)S(1)} %copy-done, f32[32,640]{1,0:T(8,128)S(1)} %get-tuple-element.629, ...), kind=kOutput, calls=%fused_computation.2.clone.1 | convolution fusion | flops 337080288 | bytes 12191368 | tf_op jit(solution)/shard_map/while/body/eval_jaxpr/dot_general | solution.py:273
  261.6 20.0 %eval_jaxpr.17 = (bf16[32,512]{1,0:T(8,128)(2,1)S(1)}, bf16[32,8192]{1,0:T(8,128)(2,1)S(1)}, f32[1,512]{1,0:T(1,128)S(1)}) custom-call(bf16[32,8192]{1,0:T(8,128)(2,1)S(1)} %get-tuple-element.631.x_ref, f32[8,128]{1,0:T(8,128)S(1)} %scatter.7.s_ref, f32[32,640]{1,0:T(8,128)S(1)} %dynamic-slice_bitcast_fusion.5.aux_ref, f32[1,512]{1,0:T(1,128)S(1)} %bitcast.91, ...), custom_call_target="tpu_custom_call" | custom-call | tf_op jit(solution)/shard_map/while/body/eval_jaxpr/pallas_call | solution.py:164
  281.9 6.0 %eval_jaxpr.16 = f32[32,640]{1,0:T(8,128)S(1)} custom-call(bf16[32,8192]{1,0:T(8,128)(2,1)S(1)} %dynamic-slice_bitcast_fusion.4.top_ref, bf16[32,8192]{1,0:T(8,128)(2,1)S(1)} %copy.33.x_ref.up_ref, bf16[640,8192]{1,0:T(8,128)(2,1)} %get-tuple-element.702.w_ref), custom_call_target="tpu_custom_call" | custom-call | flops 335544320 | bytes 11616256 | tf_op jit(solution)/shard_map/while/body/eval_jaxpr/pallas_call | solution.py:37
  288.2 0.8 copy-done
  288.9 4.5 %fusion.26 = (f32[32]{0:T(128)S(1)}, bf16[32,8192]{1,0:T(8,128)(2,1)S(1)}) fusion(f32[2,64,8192]{2,1,0:T(8,128)} %get-tuple-element.706, s32[]{:T(128)S(6)} %select_n.236, s32[]{:T(128)S(6)} %select_n.237, f32[8192]{0:T(1024)S(1)} %bitcast.85, bf16[8192,640]{1,0:T(8,128)(2,1)S(1)} %copy-done, f32[32,640]{1,0:T(8,128)S(1)} %get-tuple-element.629, ...), kind=kOutput, calls=%fused_computation.2.clone.1 | convolution fusion | flops 337080288 | bytes 12191368 | tf_op jit(solution)/shard_map/while/body/eval_jaxpr/dot_general | solution.py:273
  293.5 22.8 %eval_jaxpr.17 = (bf16[32,512]{1,0:T(8,128)(2,1)S(1)}, bf16[32,8192]{1,0:T(8,128)(2,1)S(1)}, f32[1,512]{1,0:T(1,128)S(1)}) custom-call(bf16[32,8192]{1,0:T(8,128)(2,1)S(1)} %get-tuple-element.631.x_ref, f32[8,128]{1,0:T(8,128)S(1)} %scatter.7.s_ref, f32[32,640]{1,0:T(8,128)S(1)} %dynamic-slice_bitcast_fusion.5.aux_ref, f32[1,512]{1,0:T(1,128)S(1)} %bitcast.91, ...), custom_call_target="tpu_custom_call" | custom-call | tf_op jit(solution)/shard_map/while/body/eval_jaxpr/pallas_call | solution.py:164
  316.6 6.0 %eval_jaxpr.16 = f32[32,640]{1,0:T(8,128)S(1)} custom-call(bf16[32,8192]{1,0:T(8,128)(2,1)S(1)} %dynamic-slice_bitcast_fusion.4.top_ref, bf16[32,8192]{1,0:T(8,128)(2,1)S(1)} %copy.33.x_ref.up_ref, bf16[640,8192]{1,0:T(8,128)(2,1)} %get-tuple-element.702.w_ref), custom_call_target="tpu_custom_call" | custom-call | flops 335544320 | bytes 11616256 | tf_op jit(solution)/shard_map/while/body/eval_jaxpr/pallas_call | solution.py:37
  322.8 0.8 copy-done
  323.6 4.5 %fusion.26 = (f32[32]{0:T(128)S(1)}, bf16[32,8192]{1,0:T(8,128)(2,1)S(1)}) fusion(f32[2,64,8192]{2,1,0:T(8,128)} %get-tuple-element.706, s32[]{:T(128)S(6)} %select_n.236, s32[]{:T(128)S(6)} %select_n.237, f32[8192]{0:T(1024)S(1)} %bitcast.85, bf16[8192,640]{1,0:T(8,128)(2,1)S(1)} %copy-done, f32[32,640]{1,0:T(8,128)S(1)} %get-tuple-element.629, ...), kind=kOutput, calls=%fused_computation.2.clone.1 | convolution fusion | flops 337080288 | bytes 12191368 | tf_op jit(solution)/shard_map/while/body/eval_jaxpr/dot_general | solution.py:273
  328.2 21.9 %eval_jaxpr.17 = (bf16[32,512]{1,0:T(8,128)(2,1)S(1)}, bf16[32,8192]{1,0:T(8,128)(2,1)S(1)}, f32[1,512]{1,0:T(1,128)S(1)}) custom-call(bf16[32,8192]{1,0:T(8,128)(2,1)S(1)} %get-tuple-element.631.x_ref, f32[8,128]{1,0:T(8,128)S(1)} %scatter.7.s_ref, f32[32,640]{1,0:T(8,128)S(1)} %dynamic-slice_bitcast_fusion.5.aux_ref, f32[1,512]{1,0:T(1,128)S(1)} %bitcast.91, ...), custom_call_target="tpu_custom_call" | custom-call | tf_op jit(solution)/shard_map/while/body/eval_jaxpr/pallas_call | solution.py:164
  350.3 6.0 %eval_jaxpr.16 = f32[32,640]{1,0:T(8,128)S(1)} custom-call(bf16[32,8192]{1,0:T(8,128)(2,1)S(1)} %dynamic-slice_bitcast_fusion.4.top_ref, bf16[32,8192]{1,0:T(8,128)(2,1)S(1)} %copy.33.x_ref.up_ref, bf16[640,8192]{1,0:T(8,128)(2,1)} %get-tuple-element.702.w_ref), custom_call_target="tpu_custom_call" | custom-call | flops 335544320 | bytes 11616256 | tf_op jit(solution)/shard_map/while/body/eval_jaxpr/pallas_call | solution.py:37
  356.6 0.8 copy-done
  357.4 4.5 %fusion.26 = (f32[32]{0:T(128)S(1)}, bf16[32,8192]{1,0:T(8,128)(2,1)S(1)}) fusion(f32[2,64,8192]{2,1,0:T(8,128)} %get-tuple-element.706, s32[]{:T(128)S(6)} %select_n.236, s32[]{:T(128)S(6)} %select_n.237, f32[8192]{0:T(1024)S(1)} %bitcast.85, bf16[8192,640]{1,0:T(8,128)(2,1)S(1)} %copy-done, f32[32,640]{1,0:T(8,128)S(1)} %get-tuple-element.629, ...), kind=kOutput, calls=%fused_computation.2.clone.1 | convolution fusion | flops 337080288 | bytes 12191368 | tf_op jit(solution)/shard_map/while/body/eval_jaxpr/dot_general | solution.py:273
  361.9 21.2 %eval_jaxpr.17 = (bf16[32,512]{1,0:T(8,128)(2,1)S(1)}, bf16[32,8192]{1,0:T(8,128)(2,1)S(1)}, f32[1,512]{1,0:T(1,128)S(1)}) custom-call(bf16[32,8192]{1,0:T(8,128)(2,1)S(1)} %get-tuple-element.631.x_ref, f32[8,128]{1,0:T(8,128)S(1)} %scatter.7.s_ref, f32[32,640]{1,0:T(8,128)S(1)} %dynamic-slice_bitcast_fusion.5.aux_ref, f32[1,512]{1,0:T(1,128)S(1)} %bitcast.91, ...), custom_call_target="tpu_custom_call" | custom-call | tf_op jit(solution)/shard_map/while/body/eval_jaxpr/pallas_call | solution.py:164
  383.4 36.7 %all_to_all.15 = bf16[16,130,512]{2,1,0:T(8,128)(2,1)S(1)} all-to-all(bf16[16,130,512]{2,1,0:T(8,128)(2,1)S(1)} %broadcast_in_dim.96), channel_id=1, replica_groups=mesh['section'=8,'tensor'=16] {'tensor'}, dimensions={0} | all-to-all | bytes 4259840 | tf_op jit(solution)/shard_map/all_to_all | solution.py:305
  421.1 1.2 copy.12
  422.2 2.3 broadcast_in_dim_reshape.3
  (223 shorter events, 8.7 us)
Async XLA Ops:
  0.6 2.3 copy-start.1
  2.9 2.5 copy-start.2
  2.9 3.4 copy-start.6
  3.0 3.4 copy-start.7
  3.0 3.5 copy-start.5
  6.5 2.0 copy-start.3
  8.8 7.0 %copy-start = (bf16[8192,640]{1,0:T(8,128)(2,1)S(1)}, bf16[8192,640]{1,0:T(8,128)(2,1)}, u32[]{:S(2)}) copy-start(bf16[8192,640]{1,0:T(8,128)(2,1)} %get-tuple-element.704) | copy-start | bytes 31457284 | tf_op jit(solution)/shard_map/while
  44.9 7.0 %copy-start = (bf16[8192,640]{1,0:T(8,128)(2,1)S(1)}, bf16[8192,640]{1,0:T(8,128)(2,1)}, u32[]{:S(2)}) copy-start(bf16[8192,640]{1,0:T(8,128)(2,1)} %get-tuple-element.704) | copy-start | bytes 31457284 | tf_op jit(solution)/shard_map/while
  81.8 7.0 %copy-start = (bf16[8192,640]{1,0:T(8,128)(2,1)S(1)}, bf16[8192,640]{1,0:T(8,128)(2,1)}, u32[]{:S(2)}) copy-start(bf16[8192,640]{1,0:T(8,128)(2,1)} %get-tuple-element.704) | copy-start | bytes 31457284 | tf_op jit(solution)/shard_map/while
  116.1 7.0 %copy-start = (bf16[8192,640]{1,0:T(8,128)(2,1)S(1)}, bf16[8192,640]{1,0:T(8,128)(2,1)}, u32[]{:S(2)}) copy-start(bf16[8192,640]{1,0:T(8,128)(2,1)} %get-tuple-element.704) | copy-start | bytes 31457284 | tf_op jit(solution)/shard_map/while
  147.8 7.0 %copy-start = (bf16[8192,640]{1,0:T(8,128)(2,1)S(1)}, bf16[8192,640]{1,0:T(8,128)(2,1)}, u32[]{:S(2)}) copy-start(bf16[8192,640]{1,0:T(8,128)(2,1)} %get-tuple-element.704) | copy-start | bytes 31457284 | tf_op jit(solution)/shard_map/while
  180.0 7.0 %copy-start = (bf16[8192,640]{1,0:T(8,128)(2,1)S(1)}, bf16[8192,640]{1,0:T(8,128)(2,1)}, u32[]{:S(2)}) copy-start(bf16[8192,640]{1,0:T(8,128)(2,1)} %get-tuple-element.704) | copy-start | bytes 31457284 | tf_op jit(solution)/shard_map/while
  216.2 7.0 %copy-start = (bf16[8192,640]{1,0:T(8,128)(2,1)S(1)}, bf16[8192,640]{1,0:T(8,128)(2,1)}, u32[]{:S(2)}) copy-start(bf16[8192,640]{1,0:T(8,128)(2,1)} %get-tuple-element.704) | copy-start | bytes 31457284 | tf_op jit(solution)/shard_map/while
  250.0 7.0 %copy-start = (bf16[8192,640]{1,0:T(8,128)(2,1)S(1)}, bf16[8192,640]{1,0:T(8,128)(2,1)}, u32[]{:S(2)}) copy-start(bf16[8192,640]{1,0:T(8,128)(2,1)} %get-tuple-element.704) | copy-start | bytes 31457284 | tf_op jit(solution)/shard_map/while
  281.9 7.0 %copy-start = (bf16[8192,640]{1,0:T(8,128)(2,1)S(1)}, bf16[8192,640]{1,0:T(8,128)(2,1)}, u32[]{:S(2)}) copy-start(bf16[8192,640]{1,0:T(8,128)(2,1)} %get-tuple-element.704) | copy-start | bytes 31457284 | tf_op jit(solution)/shard_map/while
  316.6 7.0 %copy-start = (bf16[8192,640]{1,0:T(8,128)(2,1)S(1)}, bf16[8192,640]{1,0:T(8,128)(2,1)}, u32[]{:S(2)}) copy-start(bf16[8192,640]{1,0:T(8,128)(2,1)} %get-tuple-element.704) | copy-start | bytes 31457284 | tf_op jit(solution)/shard_map/while
  350.3 7.0 %copy-start = (bf16[8192,640]{1,0:T(8,128)(2,1)S(1)}, bf16[8192,640]{1,0:T(8,128)(2,1)}, u32[]{:S(2)}) copy-start(bf16[8192,640]{1,0:T(8,128)(2,1)} %get-tuple-element.704) | copy-start | bytes 31457284 | tf_op jit(solution)/shard_map/while
  383.2 37.0 %copy-start.4 = (f32[4,640]{1,0:T(4,128)}, f32[4,640]{1,0:T(4,128)S(1)}, u32[]{:S(2)}) copy-start(f32[4,640]{1,0:T(4,128)S(1)} %get-tuple-element.410) | copy-start | bytes 30724

commit v15 on v14

--- a/solution.py
+++ b/solution.py
@@ -63,13 +63,13 @@
     me = lax.axis_index("tensor")
     sec = lax.axis_index("section")
     barrier = pltpu.get_barrier_semaphore()
+    @pl.when(sec < n_sec - 1)
+    def _():
+        for t in range(n):
+            pl.semaphore_signal(barrier, inc=1, device_id=(sec + 1, t), device_id_type=MESH)
+
     for k in range(1, n):
         pl.semaphore_signal(barrier, inc=1, device_id=(sec, lax.rem(me + k, n)), device_id_type=MESH)
-
-    @pl.when(sec < n_sec - 1)
-    def _():
-        for t in range(n):
-            pl.semaphore_signal(barrier, inc=1, device_id=(sec + 1, t), device_id_type=MESH)
 
     @pl.when(sec > 0)
     def _():

time: 426 us -> 425 us (level)
  no operation moved by 1% of the time
where the time goes in v15:
time: 425 us; the launch traced here: 424 us
  Pallas kernels  311 us (73%)
  matrix products  50 us (12%)
  blocking collectives  35.2 us (8%)
  local copies, waits for them, and re-layouts  15.4 us (4%)
  other arithmetic  9.68 us (2%)
    pallas_call x11, Pallas kernels, layer_exchange(): pl.pallas_call(functools.partial(layer_exchange_kernel, n, n_sec, width),...  245 us
    pallas_call x11, Pallas kernels, matmul_nt(): pl.pallas_call(functools.partial(matmul_nt_kernel, n_sec), out_shape=jax....  66.1 us
    dot_general x11, matrix products, step_rows(): lax.dot_general(d_vals, w_in, contract, preferred_element_type=jnp.float32)  50 us
    all_to_all x1, blocking collectives, local(): lax.all_to_all(copies, 'tensor', split_axis=0, concat_axis=2, tiled=True)[0]  35.2 us
    while x33, local copies, waits for them, and re-layouts  9.03 us

profile of v15, /device:TPU:32, one launch (start us, length us, event | category | flops | bytes accessed | tf_op | source)
XLA Modules:
  0.0 424.0 jit_solution(2018344098142514838)
XLA Ops:
  0.7 2.3 fusion.18
  3.0 2.4 convert_multiply_fusion
  5.4 1.0 constant_dynamic-slice_fusion.1
  6.5 1.8 broadcast_select_fusion.1
  8.5 375.6 %while.25 = (s32[]{:T(128)}, bf16[32,8192]{1,0:T(8,128)(2,1)S(1)}, bf16[2,2,32,512]{3,2,1,0:T(8,128)(2,1)S(1)}, f32[512]{0:T(512)S(1)}, f32[4,640]{1,0:T(4,128)S...) while((s32[]{:T(128)}, bf16[32,8192]{1,0:T(8,128)(2,1)S(1)}, ...), condition=%wide.region_7.8_spmd.clone, body=%wide.region_1.7_spmd.clone.sunk | while | flops 673154560 | bytes 68873840 | solution.py:298
  8.8 6.0 %eval_jaxpr.16 = f32[32,640]{1,0:T(8,128)S(1)} custom-call(bf16[32,8192]{1,0:T(8,128)(2,1)S(1)} %dynamic-slice_bitcast_fusion.4.top_ref, bf16[32,8192]{1,0:T(8,128)(2,1)S(1)} %copy.33.x_ref.up_ref, bf16[640,8192]{1,0:T(8,128)(2,1)} %get-tuple-element.702.w_ref), custom_call_target="tpu_custom_call" | custom-call | flops 335544320 | bytes 11616256 | tf_op jit(solution)/shard_map/while/body/eval_jaxpr/pallas_call | solution.py:37
  15.8 4.5 %fusion.26 = (f32[32]{0:T(128)S(1)}, bf16[32,8192]{1,0:T(8,128)(2,1)S(1)}) fusion(f32[2,64,8192]{2,1,0:T(8,128)} %get-tuple-element.706, s32[]{:T(128)S(6)} %select_n.236, s32[]{:T(128)S(6)} %select_n.237, f32[8192]{0:T(1024)S(1)} %bitcast.85, bf16[8192,640]{1,0:T(8,128)(2,1)S(1)} %copy-done, f32[32,640]{1,0:T(8,128)S(1)} %get-tuple-element.629, ...), kind=kOutput, calls=%fused_computation.2.clone.1 | convolution fusion | flops 337080288 | bytes 12191368 | tf_op jit(solution)/shard_map/while/body/eval_jaxpr/dot_general | solution.py:273
  20.4 23.1 %eval_jaxpr.17 = (bf16[32,512]{1,0:T(8,128)(2,1)S(1)}, bf16[32,8192]{1,0:T(8,128)(2,1)S(1)}, f32[1,512]{1,0:T(1,128)S(1)}) custom-call(bf16[32,8192]{1,0:T(8,128)(2,1)S(1)} %get-tuple-element.631.x_ref, f32[8,128]{1,0:T(8,128)S(1)} %scatter.7.s_ref, f32[32,640]{1,0:T(8,128)S(1)} %dynamic-slice_bitcast_fusion.5.aux_ref, f32[1,512]{1,0:T(1,128)S(1)} %bitcast.91, ...), custom_call_target="tpu_custom_call" | custom-call | tf_op jit(solution)/shard_map/while/body/eval_jaxpr/pallas_call | solution.py:164
  43.8 6.0 %eval_jaxpr.16 = f32[32,640]{1,0:T(8,128)S(1)} custom-call(bf16[32,8192]{1,0:T(8,128)(2,1)S(1)} %dynamic-slice_bitcast_fusion.4.top_ref, bf16[32,8192]{1,0:T(8,128)(2,1)S(1)} %copy.33.x_ref.up_ref, bf16[640,8192]{1,0:T(8,128)(2,1)} %get-tuple-element.702.w_ref), custom_call_target="tpu_custom_call" | custom-call | flops 335544320 | bytes 11616256 | tf_op jit(solution)/shard_map/while/body/eval_jaxpr/pallas_call | solution.py:37
  50.0 0.8 copy-done
  50.8 4.5 %fusion.26 = (f32[32]{0:T(128)S(1)}, bf16[32,8192]{1,0:T(8,128)(2,1)S(1)}) fusion(f32[2,64,8192]{2,1,0:T(8,128)} %get-tuple-element.706, s32[]{:T(128)S(6)} %select_n.236, s32[]{:T(128)S(6)} %select_n.237, f32[8192]{0:T(1024)S(1)} %bitcast.85, bf16[8192,640]{1,0:T(8,128)(2,1)S(1)} %copy-done, f32[32,640]{1,0:T(8,128)S(1)} %get-tuple-element.629, ...), kind=kOutput, calls=%fused_computation.2.clone.1 | convolution fusion | flops 337080288 | bytes 12191368 | tf_op jit(solution)/shard_map/while/body/eval_jaxpr/dot_general | solution.py:273
  55.4 25.5 %eval_jaxpr.17 = (bf16[32,512]{1,0:T(8,128)(2,1)S(1)}, bf16[32,8192]{1,0:T(8,128)(2,1)S(1)}, f32[1,512]{1,0:T(1,128)S(1)}) custom-call(bf16[32,8192]{1,0:T(8,128)(2,1)S(1)} %get-tuple-element.631.x_ref, f32[8,128]{1,0:T(8,128)S(1)} %scatter.7.s_ref, f32[32,640]{1,0:T(8,128)S(1)} %dynamic-slice_bitcast_fusion.5.aux_ref, f32[1,512]{1,0:T(1,128)S(1)} %bitcast.91, ...), custom_call_target="tpu_custom_call" | custom-call | tf_op jit(solution)/shard_map/while/body/eval_jaxpr/pallas_call | solution.py:164
  81.2 6.0 %eval_jaxpr.16 = f32[32,640]{1,0:T(8,128)S(1)} custom-call(bf16[32,8192]{1,0:T(8,128)(2,1)S(1)} %dynamic-slice_bitcast_fusion.4.top_ref, bf16[32,8192]{1,0:T(8,128)(2,1)S(1)} %copy.33.x_ref.up_ref, bf16[640,8192]{1,0:T(8,128)(2,1)} %get-tuple-element.702.w_ref), custom_call_target="tpu_custom_call" | custom-call | flops 335544320 | bytes 11616256 | tf_op jit(solution)/shard_map/while/body/eval_jaxpr/pallas_call | solution.py:37
  87.4 0.8 copy-done
  88.2 4.5 %fusion.26 = (f32[32]{0:T(128)S(1)}, bf16[32,8192]{1,0:T(8,128)(2,1)S(1)}) fusion(f32[2,64,8192]{2,1,0:T(8,128)} %get-tuple-element.706, s32[]{:T(128)S(6)} %select_n.236, s32[]{:T(128)S(6)} %select_n.237, f32[8192]{0:T(1024)S(1)} %bitcast.85, bf16[8192,640]{1,0:T(8,128)(2,1)S(1)} %copy-done, f32[32,640]{1,0:T(8,128)S(1)} %get-tuple-element.629, ...), kind=kOutput, calls=%fused_computation.2.clone.1 | convolution fusion | flops 337080288 | bytes 12191368 | tf_op jit(solution)/shard_map/while/body/eval_jaxpr/dot_general | solution.py:273
  92.8 24.6 %eval_jaxpr.17 = (bf16[32,512]{1,0:T(8,128)(2,1)S(1)}, bf16[32,8192]{1,0:T(8,128)(2,1)S(1)}, f32[1,512]{1,0:T(1,128)S(1)}) custom-call(bf16[32,8192]{1,0:T(8,128)(2,1)S(1)} %get-tuple-element.631.x_ref, f32[8,128]{1,0:T(8,128)S(1)} %scatter.7.s_ref, f32[32,640]{1,0:T(8,128)S(1)} %dynamic-slice_bitcast_fusion.5.aux_ref, f32[1,512]{1,0:T(1,128)S(1)} %bitcast.91, ...), custom_call_target="tpu_custom_call" | custom-call | tf_op jit(solution)/shard_map/while/body/eval_jaxpr/pallas_call | solution.py:164
  117.6 6.0 %eval_jaxpr.16 = f32[32,640]{1,0:T(8,128)S(1)} custom-call(bf16[32,8192]{1,0:T(8,128)(2,1)S(1)} %dynamic-slice_bitcast_fusion.4.top_ref, bf16[32,8192]{1,0:T(8,128)(2,1)S(1)} %copy.33.x_ref.up_ref, bf16[640,8192]{1,0:T(8,128)(2,1)} %get-tuple-element.702.w_ref), custom_call_target="tpu_custom_call" | custom-call | flops 335544320 | bytes 11616256 | tf_op jit(solution)/shard_map/while/body/eval_jaxpr/pallas_call | solution.py:37
  123.9 0.8 copy-done
  124.6 4.5 %fusion.26 = (f32[32]{0:T(128)S(1)}, bf16[32,8192]{1,0:T(8,128)(2,1)S(1)}) fusion(f32[2,64,8192]{2,1,0:T(8,128)} %get-tuple-element.706, s32[]{:T(128)S(6)} %select_n.236, s32[]{:T(128)S(6)} %select_n.237, f32[8192]{0:T(1024)S(1)} %bitcast.85, bf16[8192,640]{1,0:T(8,128)(2,1)S(1)} %copy-done, f32[32,640]{1,0:T(8,128)S(1)} %get-tuple-element.629, ...), kind=kOutput, calls=%fused_computation.2.clone.1 | convolution fusion | flops 337080288 | bytes 12191368 | tf_op jit(solution)/shard_map/while/body/eval_jaxpr/dot_general | solution.py:273
  129.2 18.0 %eval_jaxpr.17 = (bf16[32,512]{1,0:T(8,128)(2,1)S(1)}, bf16[32,8192]{1,0:T(8,128)(2,1)S(1)}, f32[1,512]{1,0:T(1,128)S(1)}) custom-call(bf16[32,8192]{1,0:T(8,128)(2,1)S(1)} %get-tuple-element.631.x_ref, f32[8,128]{1,0:T(8,128)S(1)} %scatter.7.s_ref, f32[32,640]{1,0:T(8,128)S(1)} %dynamic-slice_bitcast_fusion.5.aux_ref, f32[1,512]{1,0:T(1,128)S(1)} %bitcast.91, ...), custom_call_target="tpu_custom_call" | custom-call | tf_op jit(solution)/shard_map/while/body/eval_jaxpr/pallas_call | solution.py:164
  147.6 6.0 %eval_jaxpr.16 = f32[32,640]{1,0:T(8,128)S(1)} custom-call(bf16[32,8192]{1,0:T(8,128)(2,1)S(1)} %dynamic-slice_bitcast_fusion.4.top_ref, bf16[32,8192]{1,0:T(8,128)(2,1)S(1)} %copy.33.x_ref.up_ref, bf16[640,8192]{1,0:T(8,128)(2,1)} %get-tuple-element.702.w_ref), custom_call_target="tpu_custom_call" | custom-call | flops 335544320 | bytes 11616256 | tf_op jit(solution)/shard_map/while/body/eval_jaxpr/pallas_call | solution.py:37
  153.8 0.8 copy-done
  154.6 4.5 %fusion.26 = (f32[32]{0:T(128)S(1)}, bf16[32,8192]{1,0:T(8,128)(2,1)S(1)}) fusion(f32[2,64,8192]{2,1,0:T(8,128)} %get-tuple-element.706, s32[]{:T(128)S(6)} %select_n.236, s32[]{:T(128)S(6)} %select_n.237, f32[8192]{0:T(1024)S(1)} %bitcast.85, bf16[8192,640]{1,0:T(8,128)(2,1)S(1)} %copy-done, f32[32,640]{1,0:T(8,128)S(1)} %get-tuple-element.629, ...), kind=kOutput, calls=%fused_computation.2.clone.1 | convolution fusion | flops 337080288 | bytes 12191368 | tf_op jit(solution)/shard_map/while/body/eval_jaxpr/dot_general | solution.py:273
  159.1 23.6 %eval_jaxpr.17 = (bf16[32,512]{1,0:T(8,128)(2,1)S(1)}, bf16[32,8192]{1,0:T(8,128)(2,1)S(1)}, f32[1,512]{1,0:T(1,128)S(1)}) custom-call(bf16[32,8192]{1,0:T(8,128)(2,1)S(1)} %get-tuple-element.631.x_ref, f32[8,128]{1,0:T(8,128)S(1)} %scatter.7.s_ref, f32[32,640]{1,0:T(8,128)S(1)} %dynamic-slice_bitcast_fusion.5.aux_ref, f32[1,512]{1,0:T(1,128)S(1)} %bitcast.91, ...), custom_call_target="tpu_custom_call" | custom-call | tf_op jit(solution)/shard_map/while/body/eval_jaxpr/pallas_call | solution.py:164
  183.1 6.0 %eval_jaxpr.16 = f32[32,640]{1,0:T(8,128)S(1)} custom-call(bf16[32,8192]{1,0:T(8,128)(2,1)S(1)} %dynamic-slice_bitcast_fusion.4.top_ref, bf16[32,8192]{1,0:T(8,128)(2,1)S(1)} %copy.33.x_ref.up_ref, bf16[640,8192]{1,0:T(8,128)(2,1)} %get-tuple-element.702.w_ref), custom_call_target="tpu_custom_call" | custom-call | flops 335544320 | bytes 11616256 | tf_op jit(solution)/shard_map/while/body/eval_jaxpr/pallas_call | solution.py:37
  190.1 4.5 %fusion.26 = (f32[32]{0:T(128)S(1)}, bf16[32,8192]{1,0:T(8,128)(2,1)S(1)}) fusion(f32[2,64,8192]{2,1,0:T(8,128)} %get-tuple-element.706, s32[]{:T(128)S(6)} %select_n.236, s32[]{:T(128)S(6)} %select_n.237, f32[8192]{0:T(1024)S(1)} %bitcast.85, bf16[8192,640]{1,0:T(8,128)(2,1)S(1)} %copy-done, f32[32,640]{1,0:T(8,128)S(1)} %get-tuple-element.629, ...), kind=kOutput, calls=%fused_computation.2.clone.1 | convolution fusion | flops 337080288 | bytes 12191368 | tf_op jit(solution)/shard_map/while/body/eval_jaxpr/dot_general | solution.py:273
  194.6 20.0 %eval_jaxpr.17 = (bf16[32,512]{1,0:T(8,128)(2,1)S(1)}, bf16[32,8192]{1,0:T(8,128)(2,1)S(1)}, f32[1,512]{1,0:T(1,128)S(1)}) custom-call(bf16[32,8192]{1,0:T(8,128)(2,1)S(1)} %get-tuple-element.631.x_ref, f32[8,128]{1,0:T(8,128)S(1)} %scatter.7.s_ref, f32[32,640]{1,0:T(8,128)S(1)} %dynamic-slice_bitcast_fusion.5.aux_ref, f32[1,512]{1,0:T(1,128)S(1)} %bitcast.91, ...), custom_call_target="tpu_custom_call" | custom-call | tf_op jit(solution)/shard_map/while/body/eval_jaxpr/pallas_call | solution.py:164
  215.0 6.0 %eval_jaxpr.16 = f32[32,640]{1,0:T(8,128)S(1)} custom-call(bf16[32,8192]{1,0:T(8,128)(2,1)S(1)} %dynamic-slice_bitcast_fusion.4.top_ref, bf16[32,8192]{1,0:T(8,128)(2,1)S(1)} %copy.33.x_ref.up_ref, bf16[640,8192]{1,0:T(8,128)(2,1)} %get-tuple-element.702.w_ref), custom_call_target="tpu_custom_call" | custom-call | flops 335544320 | bytes 11616256 | tf_op jit(solution)/shard_map/while/body/eval_jaxpr/pallas_call | solution.py:37
  221.2 0.8 copy-done
  222.0 4.5 %fusion.26 = (f32[32]{0:T(128)S(1)}, bf16[32,8192]{1,0:T(8,128)(2,1)S(1)}) fusion(f32[2,64,8192]{2,1,0:T(8,128)} %get-tuple-element.706, s32[]{:T(128)S(6)} %select_n.236, s32[]{:T(128)S(6)} %select_n.237, f32[8192]{0:T(1024)S(1)} %bitcast.85, bf16[8192,640]{1,0:T(8,128)(2,1)S(1)} %copy-done, f32[32,640]{1,0:T(8,128)S(1)} %get-tuple-element.629, ...), kind=kOutput, calls=%fused_computation.2.clone.1 | convolution fusion | flops 337080288 | bytes 12191368 | tf_op jit(solution)/shard_map/while/body/eval_jaxpr/dot_general | solution.py:273
  226.5 21.6 %eval_jaxpr.17 = (bf16[32,512]{1,0:T(8,128)(2,1)S(1)}, bf16[32,8192]{1,0:T(8,128)(2,1)S(1)}, f32[1,512]{1,0:T(1,128)S(1)}) custom-call(bf16[32,8192]{1,0:T(8,128)(2,1)S(1)} %get-tuple-element.631.x_ref, f32[8,128]{1,0:T(8,128)S(1)} %scatter.7.s_ref, f32[32,640]{1,0:T(8,128)S(1)} %dynamic-slice_bitcast_fusion.5.aux_ref, f32[1,512]{1,0:T(1,128)S(1)} %bitcast.91, ...), custom_call_target="tpu_custom_call" | custom-call | tf_op jit(solution)/shard_map/while/body/eval_jaxpr/pallas_call | solution.py:164
  248.4 6.0 %eval_jaxpr.16 = f32[32,640]{1,0:T(8,128)S(1)} custom-call(bf16[32,8192]{1,0:T(8,128)(2,1)S(1)} %dynamic-slice_bitcast_fusion.4.top_ref, bf16[32,8192]{1,0:T(8,128)(2,1)S(1)} %copy.33.x_ref.up_ref, bf16[640,8192]{1,0:T(8,128)(2,1)} %get-tuple-element.702.w_ref), custom_call_target="tpu_custom_call" | custom-call | flops 335544320 | bytes 11616256 | tf_op jit(solution)/shard_map/while/body/eval_jaxpr/pallas_call | solution.py:37
  255.4 4.5 %fusion.26 = (f32[32]{0:T(128)S(1)}, bf16[32,8192]{1,0:T(8,128)(2,1)S(1)}) fusion(f32[2,64,8192]{2,1,0:T(8,128)} %get-tuple-element.706, s32[]{:T(128)S(6)} %select_n.236, s32[]{:T(128)S(6)} %select_n.237, f32[8192]{0:T(1024)S(1)} %bitcast.85, bf16[8192,640]{1,0:T(8,128)(2,1)S(1)} %copy-done, f32[32,640]{1,0:T(8,128)S(1)} %get-tuple-element.629, ...), kind=kOutput, calls=%fused_computation.2.clone.1 | convolution fusion | flops 337080288 | bytes 12191368 | tf_op jit(solution)/shard_map/while/body/eval_jaxpr/dot_general | solution.py:273
  260.0 21.9 %eval_jaxpr.17 = (bf16[32,512]{1,0:T(8,128)(2,1)S(1)}, bf16[32,8192]{1,0:T(8,128)(2,1)S(1)}, f32[1,512]{1,0:T(1,128)S(1)}) custom-call(bf16[32,8192]{1,0:T(8,128)(2,1)S(1)} %get-tuple-element.631.x_ref, f32[8,128]{1,0:T(8,128)S(1)} %scatter.7.s_ref, f32[32,640]{1,0:T(8,128)S(1)} %dynamic-slice_bitcast_fusion.5.aux_ref, f32[1,512]{1,0:T(1,128)S(1)} %bitcast.91, ...), custom_call_target="tpu_custom_call" | custom-call | tf_op jit(solution)/shard_map/while/body/eval_jaxpr/pallas_call | solution.py:164
  282.2 6.0 %eval_jaxpr.16 = f32[32,640]{1,0:T(8,128)S(1)} custom-call(bf16[32,8192]{1,0:T(8,128)(2,1)S(1)} %dynamic-slice_bitcast_fusion.4.top_ref, bf16[32,8192]{1,0:T(8,128)(2,1)S(1)} %copy.33.x_ref.up_ref, bf16[640,8192]{1,0:T(8,128)(2,1)} %get-tuple-element.702.w_ref), custom_call_target="tpu_custom_call" | custom-call | flops 335544320 | bytes 11616256 | tf_op jit(solution)/shard_map/while/body/eval_jaxpr/pallas_call | solution.py:37
  289.2 4.5 %fusion.26 = (f32[32]{0:T(128)S(1)}, bf16[32,8192]{1,0:T(8,128)(2,1)S(1)}) fusion(f32[2,64,8192]{2,1,0:T(8,128)} %get-tuple-element.706, s32[]{:T(128)S(6)} %select_n.236, s32[]{:T(128)S(6)} %select_n.237, f32[8192]{0:T(1024)S(1)} %bitcast.85, bf16[8192,640]{1,0:T(8,128)(2,1)S(1)} %copy-done, f32[32,640]{1,0:T(8,128)S(1)} %get-tuple-element.629, ...), kind=kOutput, calls=%fused_computation.2.clone.1 | convolution fusion | flops 337080288 | bytes 12191368 | tf_op jit(solution)/shard_map/while/body/eval_jaxpr/dot_general | solution.py:273
  293.8 22.2 %eval_jaxpr.17 = (bf16[32,512]{1,0:T(8,128)(2,1)S(1)}, bf16[32,8192]{1,0:T(8,128)(2,1)S(1)}, f32[1,512]{1,0:T(1,128)S(1)}) custom-call(bf16[32,8192]{1,0:T(8,128)(2,1)S(1)} %get-tuple-element.631.x_ref, f32[8,128]{1,0:T(8,128)S(1)} %scatter.7.s_ref, f32[32,640]{1,0:T(8,128)S(1)} %dynamic-slice_bitcast_fusion.5.aux_ref, f32[1,512]{1,0:T(1,128)S(1)} %bitcast.91, ...), custom_call_target="tpu_custom_call" | custom-call | tf_op jit(solution)/shard_map/while/body/eval_jaxpr/pallas_call | solution.py:164
  316.3 6.0 %eval_jaxpr.16 = f32[32,640]{1,0:T(8,128)S(1)} custom-call(bf16[32,8192]{1,0:T(8,128)(2,1)S(1)} %dynamic-slice_bitcast_fusion.4.top_ref, bf16[32,8192]{1,0:T(8,128)(2,1)S(1)} %copy.33.x_ref.up_ref, bf16[640,8192]{1,0:T(8,128)(2,1)} %get-tuple-element.702.w_ref), custom_call_target="tpu_custom_call" | custom-call | flops 335544320 | bytes 11616256 | tf_op jit(solution)/shard_map/while/body/eval_jaxpr/pallas_call | solution.py:37
  322.5 0.8 copy-done
  323.3 4.5 %fusion.26 = (f32[32]{0:T(128)S(1)}, bf16[32,8192]{1,0:T(8,128)(2,1)S(1)}) fusion(f32[2,64,8192]{2,1,0:T(8,128)} %get-tuple-element.706, s32[]{:T(128)S(6)} %select_n.236, s32[]{:T(128)S(6)} %select_n.237, f32[8192]{0:T(1024)S(1)} %bitcast.85, bf16[8192,640]{1,0:T(8,128)(2,1)S(1)} %copy-done, f32[32,640]{1,0:T(8,128)S(1)} %get-tuple-element.629, ...), kind=kOutput, calls=%fused_computation.2.clone.1 | convolution fusion | flops 337080288 | bytes 12191368 | tf_op jit(solution)/shard_map/while/body/eval_jaxpr/dot_general | solution.py:273
  327.9 22.6 %eval_jaxpr.17 = (bf16[32,512]{1,0:T(8,128)(2,1)S(1)}, bf16[32,8192]{1,0:T(8,128)(2,1)S(1)}, f32[1,512]{1,0:T(1,128)S(1)}) custom-call(bf16[32,8192]{1,0:T(8,128)(2,1)S(1)} %get-tuple-element.631.x_ref, f32[8,128]{1,0:T(8,128)S(1)} %scatter.7.s_ref, f32[32,640]{1,0:T(8,128)S(1)} %dynamic-slice_bitcast_fusion.5.aux_ref, f32[1,512]{1,0:T(1,128)S(1)} %bitcast.91, ...), custom_call_target="tpu_custom_call" | custom-call | tf_op jit(solution)/shard_map/while/body/eval_jaxpr/pallas_call | solution.py:164
  350.8 6.0 %eval_jaxpr.16 = f32[32,640]{1,0:T(8,128)S(1)} custom-call(bf16[32,8192]{1,0:T(8,128)(2,1)S(1)} %dynamic-slice_bitcast_fusion.4.top_ref, bf16[32,8192]{1,0:T(8,128)(2,1)S(1)} %copy.33.x_ref.up_ref, bf16[640,8192]{1,0:T(8,128)(2,1)} %get-tuple-element.702.w_ref), custom_call_target="tpu_custom_call" | custom-call | flops 335544320 | bytes 11616256 | tf_op jit(solution)/shard_map/while/body/eval_jaxpr/pallas_call | solution.py:37
  357.0 0.8 copy-done
  357.8 4.5 %fusion.26 = (f32[32]{0:T(128)S(1)}, bf16[32,8192]{1,0:T(8,128)(2,1)S(1)}) fusion(f32[2,64,8192]{2,1,0:T(8,128)} %get-tuple-element.706, s32[]{:T(128)S(6)} %select_n.236, s32[]{:T(128)S(6)} %select_n.237, f32[8192]{0:T(1024)S(1)} %bitcast.85, bf16[8192,640]{1,0:T(8,128)(2,1)S(1)} %copy-done, f32[32,640]{1,0:T(8,128)S(1)} %get-tuple-element.629, ...), kind=kOutput, calls=%fused_computation.2.clone.1 | convolution fusion | flops 337080288 | bytes 12191368 | tf_op jit(solution)/shard_map/while/body/eval_jaxpr/dot_general | solution.py:273
  362.3 21.7 %eval_jaxpr.17 = (bf16[32,512]{1,0:T(8,128)(2,1)S(1)}, bf16[32,8192]{1,0:T(8,128)(2,1)S(1)}, f32[1,512]{1,0:T(1,128)S(1)}) custom-call(bf16[32,8192]{1,0:T(8,128)(2,1)S(1)} %get-tuple-element.631.x_ref, f32[8,128]{1,0:T(8,128)S(1)} %scatter.7.s_ref, f32[32,640]{1,0:T(8,128)S(1)} %dynamic-slice_bitcast_fusion.5.aux_ref, f32[1,512]{1,0:T(1,128)S(1)} %bitcast.91, ...), custom_call_target="tpu_custom_call" | custom-call | tf_op jit(solution)/shard_map/while/body/eval_jaxpr/pallas_call | solution.py:164
  384.3 35.2 %all_to_all.15 = bf16[16,130,512]{2,1,0:T(8,128)(2,1)S(1)} all-to-all(bf16[16,130,512]{2,1,0:T(8,128)(2,1)S(1)} %broadcast_in_dim.96), channel_id=1, replica_groups=mesh['section'=8,'tensor'=16] {'tensor'}, dimensions={0} | all-to-all | bytes 4259840 | tf_op jit(solution)/shard_map/all_to_all | solution.py:305
  420.4 1.2 copy.12
  421.6 2.3 broadcast_in_dim_reshape.3
  (223 shorter events, 8.7 us)
Async XLA Ops:
  0.6 2.3 copy-start.1
  2.9 2.5 copy-start.2
  2.9 3.4 copy-start.6
  3.0 3.4 copy-start.7
  3.0 3.5 copy-start.5
  6.5 2.0 copy-start.3
  8.8 7.0 %copy-start = (bf16[8192,640]{1,0:T(8,128)(2,1)S(1)}, bf16[8192,640]{1,0:T(8,128)(2,1)}, u32[]{:S(2)}) copy-start(bf16[8192,640]{1,0:T(8,128)(2,1)} %get-tuple-element.704) | copy-start | bytes 31457284 | tf_op jit(solution)/shard_map/while
  43.8 7.0 %copy-start = (bf16[8192,640]{1,0:T(8,128)(2,1)S(1)}, bf16[8192,640]{1,0:T(8,128)(2,1)}, u32[]{:S(2)}) copy-start(bf16[8192,640]{1,0:T(8,128)(2,1)} %get-tuple-element.704) | copy-start | bytes 31457284 | tf_op jit(solution)/shard_map/while
  81.2 7.0 %copy-start = (bf16[8192,640]{1,0:T(8,128)(2,1)S(1)}, bf16[8192,640]{1,0:T(8,128)(2,1)}, u32[]{:S(2)}) copy-start(bf16[8192,640]{1,0:T(8,128)(2,1)} %get-tuple-element.704) | copy-start | bytes 31457284 | tf_op jit(solution)/shard_map/while
  117.6 7.0 %copy-start = (bf16[8192,640]{1,0:T(8,128)(2,1)S(1)}, bf16[8192,640]{1,0:T(8,128)(2,1)}, u32[]{:S(2)}) copy-start(bf16[8192,640]{1,0:T(8,128)(2,1)} %get-tuple-element.704) | copy-start | bytes 31457284 | tf_op jit(solution)/shard_map/while
  147.5 7.0 %copy-start = (bf16[8192,640]{1,0:T(8,128)(2,1)S(1)}, bf16[8192,640]{1,0:T(8,128)(2,1)}, u32[]{:S(2)}) copy-start(bf16[8192,640]{1,0:T(8,128)(2,1)} %get-tuple-element.704) | copy-start | bytes 31457284 | tf_op jit(solution)/shard_map/while
  183.0 7.0 %copy-start = (bf16[8192,640]{1,0:T(8,128)(2,1)S(1)}, bf16[8192,640]{1,0:T(8,128)(2,1)}, u32[]{:S(2)}) copy-start(bf16[8192,640]{1,0:T(8,128)(2,1)} %get-tuple-element.704) | copy-start | bytes 31457284 | tf_op jit(solution)/shard_map/while
  214.9 7.0 %copy-start = (bf16[8192,640]{1,0:T(8,128)(2,1)S(1)}, bf16[8192,640]{1,0:T(8,128)(2,1)}, u32[]{:S(2)}) copy-start(bf16[8192,640]{1,0:T(8,128)(2,1)} %get-tuple-element.704) | copy-start | bytes 31457284 | tf_op jit(solution)/shard_map/while
  248.4 7.0 %copy-start = (bf16[8192,640]{1,0:T(8,128)(2,1)S(1)}, bf16[8192,640]{1,0:T(8,128)(2,1)}, u32[]{:S(2)}) copy-start(bf16[8192,640]{1,0:T(8,128)(2,1)} %get-tuple-element.704) | copy-start | bytes 31457284 | tf_op jit(solution)/shard_map/while
  282.2 7.0 %copy-start = (bf16[8192,640]{1,0:T(8,128)(2,1)S(1)}, bf16[8192,640]{1,0:T(8,128)(2,1)}, u32[]{:S(2)}) copy-start(bf16[8192,640]{1,0:T(8,128)(2,1)} %get-tuple-element.704) | copy-start | bytes 31457284 | tf_op jit(solution)/shard_map/while
  316.3 7.0 %copy-start = (bf16[8192,640]{1,0:T(8,128)(2,1)S(1)}, bf16[8192,640]{1,0:T(8,128)(2,1)}, u32[]{:S(2)}) copy-start(bf16[8192,640]{1,0:T(8,128)(2,1)} %get-tuple-element.704) | copy-start | bytes 31457284 | tf_op jit(solution)/shard_map/while
  350.7 7.0 %copy-start = (bf16[8192,640]{1,0:T(8,128)(2,1)S(1)}, bf16[8192,640]{1,0:T(8,128)(2,1)}, u32[]{:S(2)}) copy-start(bf16[8192,640]{1,0:T(8,128)(2,1)} %get-tuple-element.704) | copy-start | bytes 31457284 | tf_op jit(solution)/shard_map/while
  384.1 35.4 %copy-start.4 = (f32[4,640]{1,0:T(4,128)}, f32[4,640]{1,0:T(4,128)S(1)}, u32[]{:S(2)}) copy-start(f32[4,640]{1,0:T(4,128)S(1)} %get-tuple-element.410) | copy-start | bytes 30724

commit v16 on v15

--- a/solution.py
+++ b/solution.py
@@ -9,7 +9,7 @@
 
 EPSILON = 1e-05
 MESH = pl.DeviceIdType.MESH
-CHUNKS_PER_BATCH = 2
+CHUNKS_PER_BATCH = 4
 
 
 def sent_to_all(x, axis):

time: 425 us -> 476 us (1.12)
  Pallas kernels: 311 us -> 341 us
  matrix products: 50 us -> 59.7 us
  local copies, waits for them, and re-layouts: 15.4 us -> 24.2 us
    pallas_call x11 -> x15, Pallas kernels: 66.1 us -> 85.1 us  [matmul_nt(): pl.pallas_call(functools.partial(matmul_nt_kernel, n_sec), out_shape=jax....]
    pallas_call x11 -> x15, Pallas kernels: 245 us -> 256 us  [layer_exchange(): pl.pallas_call(functools.partial(layer_exchange_kernel, n, n_sec, width),...]
    dot_general x11 -> x15, matrix products: 50 us -> 59.7 us  [step_rows(): lax.dot_general(d_vals, w_in, contract, preferred_element_type=jnp.float32)]
    while x33 -> x45, local copies, waits for them, and re-layouts: 9.03 us -> 17.6 us
where the time goes in v16:
time: 476 us; the launch traced here: 474 us
  Pallas kernels  341 us (72%)
  matrix products  59.7 us (13%)
  blocking collectives  35.4 us (7%)
  local copies, waits for them, and re-layouts  24.2 us (5%)
  other arithmetic  10 us (2%)
    pallas_call x15, Pallas kernels, layer_exchange(): pl.pallas_call(functools.partial(layer_exchange_kernel, n, n_sec, width),...  256 us
    pallas_call x15, Pallas kernels, matmul_nt(): pl.pallas_call(functools.partial(matmul_nt_kernel, n_sec), out_shape=jax....  85.1 us
    dot_general x15, matrix products, step_rows(): lax.dot_general(d_vals, w_in, contract, preferred_element_type=jnp.float32)  59.7 us
    all_to_all x1, blocking collectives, local(): lax.all_to_all(copies, 'tensor', split_axis=0, concat_axis=2, tiled=True)[0]  35.4 us
    while x45, local copies, waits for them, and re-layouts  17.6 us

profile of v16, /device:TPU:32, one launch (start us, length us, event | category | flops | bytes accessed | tf_op | source)
XLA Modules:
  0.0 474.3 jit_solution(18297988570555060245)
XLA Ops:
  3.0 2.4 convert_multiply_fusion
  8.5 425.7 %while.25 = (s32[]{:T(128)}, bf16[16,8192]{1,0:T(8,128)(2,1)S(1)}, bf16[2,4,16,512]{3,2,1,0:T(8,128)(2,1)S(1)}, f32[512]{0:T(512)S(1)}, f32[4,640]{1,0:T(4,128)S...) while((s32[]{:T(128)}, bf16[16,8192]{1,0:T(8,128)(2,1)S(1)}, ...), condition=%wide.region_7.8_spmd.clone, body=%wide.region_1.7_spmd.clone.sunk | while | flops 336588288 | bytes 65994224 | solution.py:298
  8.7 5.7 %eval_jaxpr.16 = f32[16,640]{1,0:T(8,128)S(1)} custom-call(bf16[16,8192]{1,0:T(8,128)(2,1)S(1)} %dynamic-slice_bitcast_fusion.4.top_ref, bf16[16,8192]{1,0:T(8,128)(2,1)S(1)} %copy.33.x_ref.up_ref, bf16[640,8192]{1,0:T(8,128)(2,1)} %get-tuple-element.704.w_ref), custom_call_target="tpu_custom_call" | custom-call | flops 167772160 | bytes 11051008 | tf_op jit(solution)/shard_map/while/body/eval_jaxpr/pallas_call | solution.py:37
  15.7 4.0 fusion.26
  19.7 18.4 %eval_jaxpr.17 = (bf16[16,512]{1,0:T(8,128)(2,1)S(1)}, bf16[16,8192]{1,0:T(8,128)(2,1)S(1)}, f32[1,512]{1,0:T(1,128)S(1)}) custom-call(bf16[16,8192]{1,0:T(8,128)(2,1)S(1)} %get-tuple-element.631.x_ref, f32[8,128]{1,0:T(8,128)S(1)} %scatter.7.s_ref, f32[16,640]{1,0:T(8,128)S(1)} %dynamic-slice_bitcast_fusion.5.aux_ref, f32[1,512]{1,0:T(1,128)S(1)} %bitcast.91, ...), custom_call_target="tpu_custom_call" | custom-call | tf_op jit(solution)/shard_map/while/body/eval_jaxpr/pallas_call | solution.py:164
  38.4 5.7 %eval_jaxpr.16 = f32[16,640]{1,0:T(8,128)S(1)} custom-call(bf16[16,8192]{1,0:T(8,128)(2,1)S(1)} %dynamic-slice_bitcast_fusion.4.top_ref, bf16[16,8192]{1,0:T(8,128)(2,1)S(1)} %copy.33.x_ref.up_ref, bf16[640,8192]{1,0:T(8,128)(2,1)} %get-tuple-element.704.w_ref), custom_call_target="tpu_custom_call" | custom-call | flops 167772160 | bytes 11051008 | tf_op jit(solution)/shard_map/while/body/eval_jaxpr/pallas_call | solution.py:37
  45.4 4.0 fusion.26
  49.4 18.2 %eval_jaxpr.17 = (bf16[16,512]{1,0:T(8,128)(2,1)S(1)}, bf16[16,8192]{1,0:T(8,128)(2,1)S(1)}, f32[1,512]{1,0:T(1,128)S(1)}) custom-call(bf16[16,8192]{1,0:T(8,128)(2,1)S(1)} %get-tuple-element.631.x_ref, f32[8,128]{1,0:T(8,128)S(1)} %scatter.7.s_ref, f32[16,640]{1,0:T(8,128)S(1)} %dynamic-slice_bitcast_fusion.5.aux_ref, f32[1,512]{1,0:T(1,128)S(1)} %bitcast.91, ...), custom_call_target="tpu_custom_call" | custom-call | tf_op jit(solution)/shard_map/while/body/eval_jaxpr/pallas_call | solution.py:164
  67.8 5.7 %eval_jaxpr.16 = f32[16,640]{1,0:T(8,128)S(1)} custom-call(bf16[16,8192]{1,0:T(8,128)(2,1)S(1)} %dynamic-slice_bitcast_fusion.4.top_ref, bf16[16,8192]{1,0:T(8,128)(2,1)S(1)} %copy.33.x_ref.up_ref, bf16[640,8192]{1,0:T(8,128)(2,1)} %get-tuple-element.704.w_ref), custom_call_target="tpu_custom_call" | custom-call | flops 167772160 | bytes 11051008 | tf_op jit(solution)/shard_map/while/body/eval_jaxpr/pallas_call | solution.py:37
  74.9 4.0 fusion.26
  78.9 17.6 %eval_jaxpr.17 = (bf16[16,512]{1,0:T(8,128)(2,1)S(1)}, bf16[16,8192]{1,0:T(8,128)(2,1)S(1)}, f32[1,512]{1,0:T(1,128)S(1)}) custom-call(bf16[16,8192]{1,0:T(8,128)(2,1)S(1)} %get-tuple-element.631.x_ref, f32[8,128]{1,0:T(8,128)S(1)} %scatter.7.s_ref, f32[16,640]{1,0:T(8,128)S(1)} %dynamic-slice_bitcast_fusion.5.aux_ref, f32[1,512]{1,0:T(1,128)S(1)} %bitcast.91, ...), custom_call_target="tpu_custom_call" | custom-call | tf_op jit(solution)/shard_map/while/body/eval_jaxpr/pallas_call | solution.py:164
  96.7 5.7 %eval_jaxpr.16 = f32[16,640]{1,0:T(8,128)S(1)} custom-call(bf16[16,8192]{1,0:T(8,128)(2,1)S(1)} %dynamic-slice_bitcast_fusion.4.top_ref, bf16[16,8192]{1,0:T(8,128)(2,1)S(1)} %copy.33.x_ref.up_ref, bf16[640,8192]{1,0:T(8,128)(2,1)} %get-tuple-element.704.w_ref), custom_call_target="tpu_custom_call" | custom-call | flops 167772160 | bytes 11051008 | tf_op jit(solution)/shard_map/while/body/eval_jaxpr/pallas_call | solution.py:37
  103.8 4.0 fusion.26
  107.8 16.6 %eval_jaxpr.17 = (bf16[16,512]{1,0:T(8,128)(2,1)S(1)}, bf16[16,8192]{1,0:T(8,128)(2,1)S(1)}, f32[1,512]{1,0:T(1,128)S(1)}) custom-call(bf16[16,8192]{1,0:T(8,128)(2,1)S(1)} %get-tuple-element.631.x_ref, f32[8,128]{1,0:T(8,128)S(1)} %scatter.7.s_ref, f32[16,640]{1,0:T(8,128)S(1)} %dynamic-slice_bitcast_fusion.5.aux_ref, f32[1,512]{1,0:T(1,128)S(1)} %bitcast.91, ...), custom_call_target="tpu_custom_call" | custom-call | tf_op jit(solution)/shard_map/while/body/eval_jaxpr/pallas_call | solution.py:164
  124.6 5.7 %eval_jaxpr.16 = f32[16,640]{1,0:T(8,128)S(1)} custom-call(bf16[16,8192]{1,0:T(8,128)(2,1)S(1)} %dynamic-slice_bitcast_fusion.4.top_ref, bf16[16,8192]{1,0:T(8,128)(2,1)S(1)} %copy.33.x_ref.up_ref, bf16[640,8192]{1,0:T(8,128)(2,1)} %get-tuple-element.704.w_ref), custom_call_target="tpu_custom_call" | custom-call | flops 167772160 | bytes 11051008 | tf_op jit(solution)/shard_map/while/body/eval_jaxpr/pallas_call | solution.py:37
  131.6 4.0 fusion.26
  135.6 15.5 %eval_jaxpr.17 = (bf16[16,512]{1,0:T(8,128)(2,1)S(1)}, bf16[16,8192]{1,0:T(8,128)(2,1)S(1)}, f32[1,512]{1,0:T(1,128)S(1)}) custom-call(bf16[16,8192]{1,0:T(8,128)(2,1)S(1)} %get-tuple-element.631.x_ref, f32[8,128]{1,0:T(8,128)S(1)} %scatter.7.s_ref, f32[16,640]{1,0:T(8,128)S(1)} %dynamic-slice_bitcast_fusion.5.aux_ref, f32[1,512]{1,0:T(1,128)S(1)} %bitcast.91, ...), custom_call_target="tpu_custom_call" | custom-call | tf_op jit(solution)/shard_map/while/body/eval_jaxpr/pallas_call | solution.py:164
  151.4 5.7 %eval_jaxpr.16 = f32[16,640]{1,0:T(8,128)S(1)} custom-call(bf16[16,8192]{1,0:T(8,128)(2,1)S(1)} %dynamic-slice_bitcast_fusion.4.top_ref, bf16[16,8192]{1,0:T(8,128)(2,1)S(1)} %copy.33.x_ref.up_ref, bf16[640,8192]{1,0:T(8,128)(2,1)} %get-tuple-element.704.w_ref), custom_call_target="tpu_custom_call" | custom-call | flops 167772160 | bytes 11051008 | tf_op jit(solution)/shard_map/while/body/eval_jaxpr/pallas_call | solution.py:37
  158.4 4.0 fusion.26
  162.4 17.6 %eval_jaxpr.17 = (bf16[16,512]{1,0:T(8,128)(2,1)S(1)}, bf16[16,8192]{1,0:T(8,128)(2,1)S(1)}, f32[1,512]{1,0:T(1,128)S(1)}) custom-call(bf16[16,8192]{1,0:T(8,128)(2,1)S(1)} %get-tuple-element.631.x_ref, f32[8,128]{1,0:T(8,128)S(1)} %scatter.7.s_ref, f32[16,640]{1,0:T(8,128)S(1)} %dynamic-slice_bitcast_fusion.5.aux_ref, f32[1,512]{1,0:T(1,128)S(1)} %bitcast.91, ...), custom_call_target="tpu_custom_call" | custom-call | tf_op jit(solution)/shard_map/while/body/eval_jaxpr/pallas_call | solution.py:164
  180.3 5.7 %eval_jaxpr.16 = f32[16,640]{1,0:T(8,128)S(1)} custom-call(bf16[16,8192]{1,0:T(8,128)(2,1)S(1)} %dynamic-slice_bitcast_fusion.4.top_ref, bf16[16,8192]{1,0:T(8,128)(2,1)S(1)} %copy.33.x_ref.up_ref, bf16[640,8192]{1,0:T(8,128)(2,1)} %get-tuple-element.704.w_ref), custom_call_target="tpu_custom_call" | custom-call | flops 167772160 | bytes 11051008 | tf_op jit(solution)/shard_map/while/body/eval_jaxpr/pallas_call | solution.py:37
  187.3 4.0 fusion.26
  191.3 16.5 %eval_jaxpr.17 = (bf16[16,512]{1,0:T(8,128)(2,1)S(1)}, bf16[16,8192]{1,0:T(8,128)(2,1)S(1)}, f32[1,512]{1,0:T(1,128)S(1)}) custom-call(bf16[16,8192]{1,0:T(8,128)(2,1)S(1)} %get-tuple-element.631.x_ref, f32[8,128]{1,0:T(8,128)S(1)} %scatter.7.s_ref, f32[16,640]{1,0:T(8,128)S(1)} %dynamic-slice_bitcast_fusion.5.aux_ref, f32[1,512]{1,0:T(1,128)S(1)} %bitcast.91, ...), custom_call_target="tpu_custom_call" | custom-call | tf_op jit(solution)/shard_map/while/body/eval_jaxpr/pallas_call | solution.py:164
  208.1 5.7 %eval_jaxpr.16 = f32[16,640]{1,0:T(8,128)S(1)} custom-call(bf16[16,8192]{1,0:T(8,128)(2,1)S(1)} %dynamic-slice_bitcast_fusion.4.top_ref, bf16[16,8192]{1,0:T(8,128)(2,1)S(1)} %copy.33.x_ref.up_ref, bf16[640,8192]{1,0:T(8,128)(2,1)} %get-tuple-element.704.w_ref), custom_call_target="tpu_custom_call" | custom-call | flops 167772160 | bytes 11051008 | tf_op jit(solution)/shard_map/while/body/eval_jaxpr/pallas_call | solution.py:37
  215.1 4.0 fusion.26
  219.1 16.8 %eval_jaxpr.17 = (bf16[16,512]{1,0:T(8,128)(2,1)S(1)}, bf16[16,8192]{1,0:T(8,128)(2,1)S(1)}, f32[1,512]{1,0:T(1,128)S(1)}) custom-call(bf16[16,8192]{1,0:T(8,128)(2,1)S(1)} %get-tuple-element.631.x_ref, f32[8,128]{1,0:T(8,128)S(1)} %scatter.7.s_ref, f32[16,640]{1,0:T(8,128)S(1)} %dynamic-slice_bitcast_fusion.5.aux_ref, f32[1,512]{1,0:T(1,128)S(1)} %bitcast.91, ...), custom_call_target="tpu_custom_call" | custom-call | tf_op jit(solution)/shard_map/while/body/eval_jaxpr/pallas_call | solution.py:164
  236.2 5.7 %eval_jaxpr.16 = f32[16,640]{1,0:T(8,128)S(1)} custom-call(bf16[16,8192]{1,0:T(8,128)(2,1)S(1)} %dynamic-slice_bitcast_fusion.4.top_ref, bf16[16,8192]{1,0:T(8,128)(2,1)S(1)} %copy.33.x_ref.up_ref, bf16[640,8192]{1,0:T(8,128)(2,1)} %get-tuple-element.704.w_ref), custom_call_target="tpu_custom_call" | custom-call | flops 167772160 | bytes 11051008 | tf_op jit(solution)/shard_map/while/body/eval_jaxpr/pallas_call | solution.py:37
  243.2 4.0 fusion.26
  247.2 17.9 %eval_jaxpr.17 = (bf16[16,512]{1,0:T(8,128)(2,1)S(1)}, bf16[16,8192]{1,0:T(8,128)(2,1)S(1)}, f32[1,512]{1,0:T(1,128)S(1)}) custom-call(bf16[16,8192]{1,0:T(8,128)(2,1)S(1)} %get-tuple-element.631.x_ref, f32[8,128]{1,0:T(8,128)S(1)} %scatter.7.s_ref, f32[16,640]{1,0:T(8,128)S(1)} %dynamic-slice_bitcast_fusion.5.aux_ref, f32[1,512]{1,0:T(1,128)S(1)} %bitcast.91, ...), custom_call_target="tpu_custom_call" | custom-call | tf_op jit(solution)/shard_map/while/body/eval_jaxpr/pallas_call | solution.py:164
  265.4 5.7 %eval_jaxpr.16 = f32[16,640]{1,0:T(8,128)S(1)} custom-call(bf16[16,8192]{1,0:T(8,128)(2,1)S(1)} %dynamic-slice_bitcast_fusion.4.top_ref, bf16[16,8192]{1,0:T(8,128)(2,1)S(1)} %copy.33.x_ref.up_ref, bf16[640,8192]{1,0:T(8,128)(2,1)} %get-tuple-element.704.w_ref), custom_call_target="tpu_custom_call" | custom-call | flops 167772160 | bytes 11051008 | tf_op jit(solution)/shard_map/while/body/eval_jaxpr/pallas_call | solution.py:37
  272.4 4.0 fusion.26
  276.4 16.6 %eval_jaxpr.17 = (bf16[16,512]{1,0:T(8,128)(2,1)S(1)}, bf16[16,8192]{1,0:T(8,128)(2,1)S(1)}, f32[1,512]{1,0:T(1,128)S(1)}) custom-call(bf16[16,8192]{1,0:T(8,128)(2,1)S(1)} %get-tuple-element.631.x_ref, f32[8,128]{1,0:T(8,128)S(1)} %scatter.7.s_ref, f32[16,640]{1,0:T(8,128)S(1)} %dynamic-slice_bitcast_fusion.5.aux_ref, f32[1,512]{1,0:T(1,128)S(1)} %bitcast.91, ...), custom_call_target="tpu_custom_call" | custom-call | tf_op jit(solution)/shard_map/while/body/eval_jaxpr/pallas_call | solution.py:164
  293.3 5.7 %eval_jaxpr.16 = f32[16,640]{1,0:T(8,128)S(1)} custom-call(bf16[16,8192]{1,0:T(8,128)(2,1)S(1)} %dynamic-slice_bitcast_fusion.4.top_ref, bf16[16,8192]{1,0:T(8,128)(2,1)S(1)} %copy.33.x_ref.up_ref, bf16[640,8192]{1,0:T(8,128)(2,1)} %get-tuple-element.704.w_ref), custom_call_target="tpu_custom_call" | custom-call | flops 167772160 | bytes 11051008 | tf_op jit(solution)/shard_map/while/body/eval_jaxpr/pallas_call | solution.py:37
  300.4 4.0 fusion.26
  304.4 16.6 %eval_jaxpr.17 = (bf16[16,512]{1,0:T(8,128)(2,1)S(1)}, bf16[16,8192]{1,0:T(8,128)(2,1)S(1)}, f32[1,512]{1,0:T(1,128)S(1)}) custom-call(bf16[16,8192]{1,0:T(8,128)(2,1)S(1)} %get-tuple-element.631.x_ref, f32[8,128]{1,0:T(8,128)S(1)} %scatter.7.s_ref, f32[16,640]{1,0:T(8,128)S(1)} %dynamic-slice_bitcast_fusion.5.aux_ref, f32[1,512]{1,0:T(1,128)S(1)} %bitcast.91, ...), custom_call_target="tpu_custom_call" | custom-call | tf_op jit(solution)/shard_map/while/body/eval_jaxpr/pallas_call | solution.py:164
  321.3 5.7 %eval_jaxpr.16 = f32[16,640]{1,0:T(8,128)S(1)} custom-call(bf16[16,8192]{1,0:T(8,128)(2,1)S(1)} %dynamic-slice_bitcast_fusion.4.top_ref, bf16[16,8192]{1,0:T(8,128)(2,1)S(1)} %copy.33.x_ref.up_ref, bf16[640,8192]{1,0:T(8,128)(2,1)} %get-tuple-element.704.w_ref), custom_call_target="tpu_custom_call" | custom-call | flops 167772160 | bytes 11051008 | tf_op jit(solution)/shard_map/while/body/eval_jaxpr/pallas_call | solution.py:37
  328.3 4.0 fusion.26
  332.3 17.4 %eval_jaxpr.17 = (bf16[16,512]{1,0:T(8,128)(2,1)S(1)}, bf16[16,8192]{1,0:T(8,128)(2,1)S(1)}, f32[1,512]{1,0:T(1,128)S(1)}) custom-call(bf16[16,8192]{1,0:T(8,128)(2,1)S(1)} %get-tuple-element.631.x_ref, f32[8,128]{1,0:T(8,128)S(1)} %scatter.7.s_ref, f32[16,640]{1,0:T(8,128)S(1)} %dynamic-slice_bitcast_fusion.5.aux_ref, f32[1,512]{1,0:T(1,128)S(1)} %bitcast.91, ...), custom_call_target="tpu_custom_call" | custom-call | tf_op jit(solution)/shard_map/while/body/eval_jaxpr/pallas_call | solution.py:164
  349.9 5.7 %eval_jaxpr.16 = f32[16,640]{1,0:T(8,128)S(1)} custom-call(bf16[16,8192]{1,0:T(8,128)(2,1)S(1)} %dynamic-slice_bitcast_fusion.4.top_ref, bf16[16,8192]{1,0:T(8,128)(2,1)S(1)} %copy.33.x_ref.up_ref, bf16[640,8192]{1,0:T(8,128)(2,1)} %get-tuple-element.704.w_ref), custom_call_target="tpu_custom_call" | custom-call | flops 167772160 | bytes 11051008 | tf_op jit(solution)/shard_map/while/body/eval_jaxpr/pallas_call | solution.py:37
  357.0 4.0 fusion.26
  361.0 15.9 %eval_jaxpr.17 = (bf16[16,512]{1,0:T(8,128)(2,1)S(1)}, bf16[16,8192]{1,0:T(8,128)(2,1)S(1)}, f32[1,512]{1,0:T(1,128)S(1)}) custom-call(bf16[16,8192]{1,0:T(8,128)(2,1)S(1)} %get-tuple-element.631.x_ref, f32[8,128]{1,0:T(8,128)S(1)} %scatter.7.s_ref, f32[16,640]{1,0:T(8,128)S(1)} %dynamic-slice_bitcast_fusion.5.aux_ref, f32[1,512]{1,0:T(1,128)S(1)} %bitcast.91, ...), custom_call_target="tpu_custom_call" | custom-call | tf_op jit(solution)/shard_map/while/body/eval_jaxpr/pallas_call | solution.py:164
  377.1 5.7 %eval_jaxpr.16 = f32[16,640]{1,0:T(8,128)S(1)} custom-call(bf16[16,8192]{1,0:T(8,128)(2,1)S(1)} %dynamic-slice_bitcast_fusion.4.top_ref, bf16[16,8192]{1,0:T(8,128)(2,1)S(1)} %copy.33.x_ref.up_ref, bf16[640,8192]{1,0:T(8,128)(2,1)} %get-tuple-element.704.w_ref), custom_call_target="tpu_custom_call" | custom-call | flops 167772160 | bytes 11051008 | tf_op jit(solution)/shard_map/while/body/eval_jaxpr/pallas_call | solution.py:37
  384.2 4.0 fusion.26
  388.2 18.3 %eval_jaxpr.17 = (bf16[16,512]{1,0:T(8,128)(2,1)S(1)}, bf16[16,8192]{1,0:T(8,128)(2,1)S(1)}, f32[1,512]{1,0:T(1,128)S(1)}) custom-call(bf16[16,8192]{1,0:T(8,128)(2,1)S(1)} %get-tuple-element.631.x_ref, f32[8,128]{1,0:T(8,128)S(1)} %scatter.7.s_ref, f32[16,640]{1,0:T(8,128)S(1)} %dynamic-slice_bitcast_fusion.5.aux_ref, f32[1,512]{1,0:T(1,128)S(1)} %bitcast.91, ...), custom_call_target="tpu_custom_call" | custom-call | tf_op jit(solution)/shard_map/while/body/eval_jaxpr/pallas_call | solution.py:164
  406.7 5.7 %eval_jaxpr.16 = f32[16,640]{1,0:T(8,128)S(1)} custom-call(bf16[16,8192]{1,0:T(8,128)(2,1)S(1)} %dynamic-slice_bitcast_fusion.4.top_ref, bf16[16,8192]{1,0:T(8,128)(2,1)S(1)} %copy.33.x_ref.up_ref, bf16[640,8192]{1,0:T(8,128)(2,1)} %get-tuple-element.704.w_ref), custom_call_target="tpu_custom_call" | custom-call | flops 167772160 | bytes 11051008 | tf_op jit(solution)/shard_map/while/body/eval_jaxpr/pallas_call | solution.py:37
  413.7 4.0 fusion.26
  417.7 16.4 %eval_jaxpr.17 = (bf16[16,512]{1,0:T(8,128)(2,1)S(1)}, bf16[16,8192]{1,0:T(8,128)(2,1)S(1)}, f32[1,512]{1,0:T(1,128)S(1)}) custom-call(bf16[16,8192]{1,0:T(8,128)(2,1)S(1)} %get-tuple-element.631.x_ref, f32[8,128]{1,0:T(8,128)S(1)} %scatter.7.s_ref, f32[16,640]{1,0:T(8,128)S(1)} %dynamic-slice_bitcast_fusion.5.aux_ref, f32[1,512]{1,0:T(1,128)S(1)} %bitcast.91, ...), custom_call_target="tpu_custom_call" | custom-call | tf_op jit(solution)/shard_map/while/body/eval_jaxpr/pallas_call | solution.py:164
  434.4 35.4 %all_to_all.15 = bf16[16,130,512]{2,1,0:T(8,128)(2,1)S(1)} all-to-all(bf16[16,130,512]{2,1,0:T(8,128)(2,1)S(1)} %broadcast_in_dim.96), channel_id=1, replica_groups=mesh['section'=8,'tensor'=16] {'tensor'}, dimensions={0} | all-to-all | bytes 4259840 | tf_op jit(solution)/shard_map/all_to_all | solution.py:305
  (307 shorter events, 31.8 us)
Async XLA Ops:
  0.6 2.3 copy-start.1
  2.9 2.5 copy-start.2
  2.9 3.4 copy-start.6
  3.0 3.4 copy-start.7
  3.0 3.5 copy-start.5
  6.5 2.0 copy-start.3
  8.7 7.0 %copy-start = (bf16[8192,640]{1,0:T(8,128)(2,1)S(1)}, bf16[8192,640]{1,0:T(8,128)(2,1)}, u32[]{:S(2)}) copy-start(bf16[8192,640]{1,0:T(8,128)(2,1)} %get-tuple-element.706) | copy-start | bytes 31457284 | tf_op jit(solution)/shard_map/while
  38.4 7.0 %copy-start = (bf16[8192,640]{1,0:T(8,128)(2,1)S(1)}, bf16[8192,640]{1,0:T(8,128)(2,1)}, u32[]{:S(2)}) copy-start(bf16[8192,640]{1,0:T(8,128)(2,1)} %get-tuple-element.706) | copy-start | bytes 31457284 | tf_op jit(solution)/shard_map/while
  67.8 7.0 %copy-start = (bf16[8192,640]{1,0:T(8,128)(2,1)S(1)}, bf16[8192,640]{1,0:T(8,128)(2,1)}, u32[]{:S(2)}) copy-start(bf16[8192,640]{1,0:T(8,128)(2,1)} %get-tuple-element.706) | copy-start | bytes 31457284 | tf_op jit(solution)/shard_map/while
  96.7 7.0 %copy-start = (bf16[8192,640]{1,0:T(8,128)(2,1)S(1)}, bf16[8192,640]{1,0:T(8,128)(2,1)}, u32[]{:S(2)}) copy-start(bf16[8192,640]{1,0:T(8,128)(2,1)} %get-tuple-element.706) | copy-start | bytes 31457284 | tf_op jit(solution)/shard_map/while
  124.6 7.0 %copy-start = (bf16[8192,640]{1,0:T(8,128)(2,1)S(1)}, bf16[8192,640]{1,0:T(8,128)(2,1)}, u32[]{:S(2)}) copy-start(bf16[8192,640]{1,0:T(8,128)(2,1)} %get-tuple-element.706) | copy-start | bytes 31457284 | tf_op jit(solution)/shard_map/while
  151.4 7.0 %copy-start = (bf16[8192,640]{1,0:T(8,128)(2,1)S(1)}, bf16[8192,640]{1,0:T(8,128)(2,1)}, u32[]{:S(2)}) copy-start(bf16[8192,640]{1,0:T(8,128)(2,1)} %get-tuple-element.706) | copy-start | bytes 31457284 | tf_op jit(solution)/shard_map/while
  180.3 7.0 %copy-start = (bf16[8192,640]{1,0:T(8,128)(2,1)S(1)}, bf16[8192,640]{1,0:T(8,128)(2,1)}, u32[]{:S(2)}) copy-start(bf16[8192,640]{1,0:T(8,128)(2,1)} %get-tuple-element.706) | copy-start | bytes 31457284 | tf_op jit(solution)/shard_map/while
  208.1 7.0 %copy-start = (bf16[8192,640]{1,0:T(8,128)(2,1)S(1)}, bf16[8192,640]{1,0:T(8,128)(2,1)}, u32[]{:S(2)}) copy-start(bf16[8192,640]{1,0:T(8,128)(2,1)} %get-tuple-element.706) | copy-start | bytes 31457284 | tf_op jit(solution)/shard_map/while
  236.2 7.0 %copy-start = (bf16[8192,640]{1,0:T(8,128)(2,1)S(1)}, bf16[8192,640]{1,0:T(8,128)(2,1)}, u32[]{:S(2)}) copy-start(bf16[8192,640]{1,0:T(8,128)(2,1)} %get-tuple-element.706) | copy-start | bytes 31457284 | tf_op jit(solution)/shard_map/while
  265.4 7.0 %copy-start = (bf16[8192,640]{1,0:T(8,128)(2,1)S(1)}, bf16[8192,640]{1,0:T(8,128)(2,1)}, u32[]{:S(2)}) copy-start(bf16[8192,640]{1,0:T(8,128)(2,1)} %get-tuple-element.706) | copy-start | bytes 31457284 | tf_op jit(solution)/shard_map/while
  293.3 7.0 %copy-start = (bf16[8192,640]{1,0:T(8,128)(2,1)S(1)}, bf16[8192,640]{1,0:T(8,128)(2,1)}, u32[]{:S(2)}) copy-start(bf16[8192,640]{1,0:T(8,128)(2,1)} %get-tuple-element.706) | copy-start | bytes 31457284 | tf_op jit(solution)/shard_map/while
  321.2 7.0 %copy-start = (bf16[8192,640]{1,0:T(8,128)(2,1)S(1)}, bf16[8192,640]{1,0:T(8,128)(2,1)}, u32[]{:S(2)}) copy-start(bf16[8192,640]{1,0:T(8,128)(2,1)} %get-tuple-element.706) | copy-start | bytes 31457284 | tf_op jit(solution)/shard_map/while
  349.9 7.0 %copy-start = (bf16[8192,640]{1,0:T(8,128)(2,1)S(1)}, bf16[8192,640]{1,0:T(8,128)(2,1)}, u32[]{:S(2)}) copy-start(bf16[8192,640]{1,0:T(8,128)(2,1)} %get-tuple-element.706) | copy-start | bytes 31457284 | tf_op jit(solution)/shard_map/while
  377.1 7.0 %copy-start = (bf16[8192,640]{1,0:T(8,128)(2,1)S(1)}, bf16[8192,640]{1,0:T(8,128)(2,1)}, u32[]{:S(2)}) copy-start(bf16[8192,640]{1,0:T(8,128)(2,1)} %get-tuple-element.706) | copy-start | bytes 31457284 | tf_op jit(solution)/shard_map/while
  406.7 7.0 %copy-start = (bf16[8192,640]{1,0:T(8,128)(2,1)S(1)}, bf16[8192,640]{1,0:T(8,128)(2,1)}, u32[]{:S(2)}) copy-start(bf16[8192,640]{1,0:T(8,128)(2,1)} %get-tuple-element.706) | copy-start | bytes 31457284 | tf_op jit(solution)/shard_map/while
  434.2 35.7 %copy-start.4 = (f32[4,640]{1,0:T(4,128)}, f32[4,640]{1,0:T(4,128)S(1)}, u32[]{:S(2)}) copy-start(f32[4,640]{1,0:T(4,128)S(1)} %get-tuple-element.410) | copy-start | bytes 30724

commit v17 on v15

--- a/solution.py
+++ b/solution.py
@@ -58,7 +58,7 @@
 def layer_exchange_kernel(
     n, n_sec, width, x_ref, s_ref, aux_ref, gain_ref, top_ref, up_ref,
     g_ref, next_ref, gain_out_ref,
-    recv, srecv, gbuf, down, send_sem, recv_sem, ssend_sem, srecv_sem, dsend_sem, drecv_sem,
+    recv, srecv, down, send_sem, recv_sem, ssend_sem, srecv_sem, dsend_sem, drecv_sem,
 ):
     me = lax.axis_index("tensor")
     sec = lax.axis_index("section")
@@ -119,7 +119,6 @@
     d_in = inv_rms * (total * gain_ref[...] - normed * row_mean)
     upstream = jnp.where(sec == n_sec - 1, top_ref[:, mine], up_ref[:, mine])
     result = (upstream.astype(jnp.float32) + d_in).astype(g_ref.dtype)
-    gbuf[...] = result
     g_ref[...] = result
     gain_out_ref[...] = jnp.sum(total * normed, axis=0, keepdims=True)
 
@@ -128,7 +127,7 @@
         sends = []
         for t in range(n):
             copy = pltpu.make_async_remote_copy(
-                src_ref=gbuf,
+                src_ref=g_ref,
                 dst_ref=down.at[:, mine],
                 send_sem=dsend_sem.at[t],
                 recv_sem=drecv_sem.at[me],
@@ -144,7 +143,7 @@
     def _():
         for src in range(n):
             pltpu.make_async_remote_copy(
-                src_ref=gbuf,
+                src_ref=g_ref,
                 dst_ref=down.at[:, pl.ds(src * width, width)],
                 send_sem=dsend_sem.at[src],
                 recv_sem=drecv_sem.at[src],
@@ -173,7 +172,6 @@
         scratch_shapes=[
             pltpu.VMEM((n, rows, width), partial.dtype),
             pltpu.VMEM((n, *stats.shape), jnp.float32),
-            pltpu.VMEM((rows, width), jnp.bfloat16),
             pltpu.VMEM((rows, n * width), jnp.bfloat16),
             pltpu.SemaphoreType.DMA((n,)),
             pltpu.SemaphoreType.DMA((n,)),

time: 425 us -> 425 us (level)
  no operation moved by 1% of the time
where the time goes in v17:
time: 425 us; the launch traced here: 424 us
  Pallas kernels  311 us (73%)
  matrix products  50 us (12%)
  blocking collectives  35.2 us (8%)
  local copies, waits for them, and re-layouts  15.4 us (4%)
  other arithmetic  9.68 us (2%)
    pallas_call x11, Pallas kernels, layer_exchange(): pl.pallas_call(functools.partial(layer_exchange_kernel, n, n_sec, width),...  245 us
    pallas_call x11, Pallas kernels, matmul_nt(): pl.pallas_call(functools.partial(matmul_nt_kernel, n_sec), out_shape=jax....  66.1 us
    dot_general x11, matrix products, step_rows(): lax.dot_general(d_vals, w_in, contract, preferred_element_type=jnp.float32)  50 us
    all_to_all x1, blocking collectives, local(): lax.all_to_all(copies, 'tensor', split_axis=0, concat_axis=2, tiled=True)[0]  35.2 us
    while x33, local copies, waits for them, and re-layouts  9.03 us

profile of v17, /device:TPU:32, one launch (start us, length us, event | category | flops | bytes accessed | tf_op | source)
XLA Modules:
  0.0 424.0 jit_solution(15912327702881893006)
XLA Ops:
  0.7 2.3 fusion.18
  3.0 2.4 convert_multiply_fusion
  5.4 1.0 constant_dynamic-slice_fusion.1
  6.5 1.8 broadcast_select_fusion.1
  8.5 375.6 %while.25 = (s32[]{:T(128)}, bf16[32,8192]{1,0:T(8,128)(2,1)S(1)}, bf16[2,2,32,512]{3,2,1,0:T(8,128)(2,1)S(1)}, f32[512]{0:T(512)S(1)}, f32[4,640]{1,0:T(4,128)S...) while((s32[]{:T(128)}, bf16[32,8192]{1,0:T(8,128)(2,1)S(1)}, ...), condition=%wide.region_7.8_spmd.clone, body=%wide.region_1.7_spmd.clone.sunk | while | flops 673154560 | bytes 68873840 | solution.py:296
  8.8 6.0 %eval_jaxpr.16 = f32[32,640]{1,0:T(8,128)S(1)} custom-call(bf16[32,8192]{1,0:T(8,128)(2,1)S(1)} %dynamic-slice_bitcast_fusion.4.top_ref, bf16[32,8192]{1,0:T(8,128)(2,1)S(1)} %copy.33.x_ref.up_ref, bf16[640,8192]{1,0:T(8,128)(2,1)} %get-tuple-element.702.w_ref), custom_call_target="tpu_custom_call" | custom-call | flops 335544320 | bytes 11616256 | tf_op jit(solution)/shard_map/while/body/eval_jaxpr/pallas_call | solution.py:37
  15.8 4.5 %fusion.26 = (f32[32]{0:T(128)S(1)}, bf16[32,8192]{1,0:T(8,128)(2,1)S(1)}) fusion(f32[2,64,8192]{2,1,0:T(8,128)} %get-tuple-element.706, s32[]{:T(128)S(6)} %select_n.236, s32[]{:T(128)S(6)} %select_n.237, f32[8192]{0:T(1024)S(1)} %bitcast.85, bf16[8192,640]{1,0:T(8,128)(2,1)S(1)} %copy-done, f32[32,640]{1,0:T(8,128)S(1)} %get-tuple-element.629, ...), kind=kOutput, calls=%fused_computation.2.clone.1 | convolution fusion | flops 337080288 | bytes 12191368 | tf_op jit(solution)/shard_map/while/body/eval_jaxpr/dot_general | solution.py:271
  20.4 23.1 %eval_jaxpr.17 = (bf16[32,512]{1,0:T(8,128)(2,1)S(1)}, bf16[32,8192]{1,0:T(8,128)(2,1)S(1)}, f32[1,512]{1,0:T(1,128)S(1)}) custom-call(bf16[32,8192]{1,0:T(8,128)(2,1)S(1)} %get-tuple-element.631.x_ref, f32[8,128]{1,0:T(8,128)S(1)} %scatter.7.s_ref, f32[32,640]{1,0:T(8,128)S(1)} %dynamic-slice_bitcast_fusion.5.aux_ref, f32[1,512]{1,0:T(1,128)S(1)} %bitcast.91, ...), custom_call_target="tpu_custom_call" | custom-call | tf_op jit(solution)/shard_map/while/body/eval_jaxpr/pallas_call | solution.py:163
  43.8 6.0 %eval_jaxpr.16 = f32[32,640]{1,0:T(8,128)S(1)} custom-call(bf16[32,8192]{1,0:T(8,128)(2,1)S(1)} %dynamic-slice_bitcast_fusion.4.top_ref, bf16[32,8192]{1,0:T(8,128)(2,1)S(1)} %copy.33.x_ref.up_ref, bf16[640,8192]{1,0:T(8,128)(2,1)} %get-tuple-element.702.w_ref), custom_call_target="tpu_custom_call" | custom-call | flops 335544320 | bytes 11616256 | tf_op jit(solution)/shard_map/while/body/eval_jaxpr/pallas_call | solution.py:37
  50.0 0.8 copy-done
  50.8 4.5 %fusion.26 = (f32[32]{0:T(128)S(1)}, bf16[32,8192]{1,0:T(8,128)(2,1)S(1)}) fusion(f32[2,64,8192]{2,1,0:T(8,128)} %get-tuple-element.706, s32[]{:T(128)S(6)} %select_n.236, s32[]{:T(128)S(6)} %select_n.237, f32[8192]{0:T(1024)S(1)} %bitcast.85, bf16[8192,640]{1,0:T(8,128)(2,1)S(1)} %copy-done, f32[32,640]{1,0:T(8,128)S(1)} %get-tuple-element.629, ...), kind=kOutput, calls=%fused_computation.2.clone.1 | convolution fusion | flops 337080288 | bytes 12191368 | tf_op jit(solution)/shard_map/while/body/eval_jaxpr/dot_general | solution.py:271
  55.4 25.5 %eval_jaxpr.17 = (bf16[32,512]{1,0:T(8,128)(2,1)S(1)}, bf16[32,8192]{1,0:T(8,128)(2,1)S(1)}, f32[1,512]{1,0:T(1,128)S(1)}) custom-call(bf16[32,8192]{1,0:T(8,128)(2,1)S(1)} %get-tuple-element.631.x_ref, f32[8,128]{1,0:T(8,128)S(1)} %scatter.7.s_ref, f32[32,640]{1,0:T(8,128)S(1)} %dynamic-slice_bitcast_fusion.5.aux_ref, f32[1,512]{1,0:T(1,128)S(1)} %bitcast.91, ...), custom_call_target="tpu_custom_call" | custom-call | tf_op jit(solution)/shard_map/while/body/eval_jaxpr/pallas_call | solution.py:163
  81.2 6.0 %eval_jaxpr.16 = f32[32,640]{1,0:T(8,128)S(1)} custom-call(bf16[32,8192]{1,0:T(8,128)(2,1)S(1)} %dynamic-slice_bitcast_fusion.4.top_ref, bf16[32,8192]{1,0:T(8,128)(2,1)S(1)} %copy.33.x_ref.up_ref, bf16[640,8192]{1,0:T(8,128)(2,1)} %get-tuple-element.702.w_ref), custom_call_target="tpu_custom_call" | custom-call | flops 335544320 | bytes 11616256 | tf_op jit(solution)/shard_map/while/body/eval_jaxpr/pallas_call | solution.py:37
  87.4 0.8 copy-done
  88.2 4.5 %fusion.26 = (f32[32]{0:T(128)S(1)}, bf16[32,8192]{1,0:T(8,128)(2,1)S(1)}) fusion(f32[2,64,8192]{2,1,0:T(8,128)} %get-tuple-element.706, s32[]{:T(128)S(6)} %select_n.236, s32[]{:T(128)S(6)} %select_n.237, f32[8192]{0:T(1024)S(1)} %bitcast.85, bf16[8192,640]{1,0:T(8,128)(2,1)S(1)} %copy-done, f32[32,640]{1,0:T(8,128)S(1)} %get-tuple-element.629, ...), kind=kOutput, calls=%fused_computation.2.clone.1 | convolution fusion | flops 337080288 | bytes 12191368 | tf_op jit(solution)/shard_map/while/body/eval_jaxpr/dot_general | solution.py:271
  92.8 24.6 %eval_jaxpr.17 = (bf16[32,512]{1,0:T(8,128)(2,1)S(1)}, bf16[32,8192]{1,0:T(8,128)(2,1)S(1)}, f32[1,512]{1,0:T(1,128)S(1)}) custom-call(bf16[32,8192]{1,0:T(8,128)(2,1)S(1)} %get-tuple-element.631.x_ref, f32[8,128]{1,0:T(8,128)S(1)} %scatter.7.s_ref, f32[32,640]{1,0:T(8,128)S(1)} %dynamic-slice_bitcast_fusion.5.aux_ref, f32[1,512]{1,0:T(1,128)S(1)} %bitcast.91, ...), custom_call_target="tpu_custom_call" | custom-call | tf_op jit(solution)/shard_map/while/body/eval_jaxpr/pallas_call | solution.py:163
  117.6 6.0 %eval_jaxpr.16 = f32[32,640]{1,0:T(8,128)S(1)} custom-call(bf16[32,8192]{1,0:T(8,128)(2,1)S(1)} %dynamic-slice_bitcast_fusion.4.top_ref, bf16[32,8192]{1,0:T(8,128)(2,1)S(1)} %copy.33.x_ref.up_ref, bf16[640,8192]{1,0:T(8,128)(2,1)} %get-tuple-element.702.w_ref), custom_call_target="tpu_custom_call" | custom-call | flops 335544320 | bytes 11616256 | tf_op jit(solution)/shard_map/while/body/eval_jaxpr/pallas_call | solution.py:37
  123.9 0.8 copy-done
  124.6 4.5 %fusion.26 = (f32[32]{0:T(128)S(1)}, bf16[32,8192]{1,0:T(8,128)(2,1)S(1)}) fusion(f32[2,64,8192]{2,1,0:T(8,128)} %get-tuple-element.706, s32[]{:T(128)S(6)} %select_n.236, s32[]{:T(128)S(6)} %select_n.237, f32[8192]{0:T(1024)S(1)} %bitcast.85, bf16[8192,640]{1,0:T(8,128)(2,1)S(1)} %copy-done, f32[32,640]{1,0:T(8,128)S(1)} %get-tuple-element.629, ...), kind=kOutput, calls=%fused_computation.2.clone.1 | convolution fusion | flops 337080288 | bytes 12191368 | tf_op jit(solution)/shard_map/while/body/eval_jaxpr/dot_general | solution.py:271
  129.2 18.0 %eval_jaxpr.17 = (bf16[32,512]{1,0:T(8,128)(2,1)S(1)}, bf16[32,8192]{1,0:T(8,128)(2,1)S(1)}, f32[1,512]{1,0:T(1,128)S(1)}) custom-call(bf16[32,8192]{1,0:T(8,128)(2,1)S(1)} %get-tuple-element.631.x_ref, f32[8,128]{1,0:T(8,128)S(1)} %scatter.7.s_ref, f32[32,640]{1,0:T(8,128)S(1)} %dynamic-slice_bitcast_fusion.5.aux_ref, f32[1,512]{1,0:T(1,128)S(1)} %bitcast.91, ...), custom_call_target="tpu_custom_call" | custom-call | tf_op jit(solution)/shard_map/while/body/eval_jaxpr/pallas_call | solution.py:163
  147.6 6.0 %eval_jaxpr.16 = f32[32,640]{1,0:T(8,128)S(1)} custom-call(bf16[32,8192]{1,0:T(8,128)(2,1)S(1)} %dynamic-slice_bitcast_fusion.4.top_ref, bf16[32,8192]{1,0:T(8,128)(2,1)S(1)} %copy.33.x_ref.up_ref, bf16[640,8192]{1,0:T(8,128)(2,1)} %get-tuple-element.702.w_ref), custom_call_target="tpu_custom_call" | custom-call | flops 335544320 | bytes 11616256 | tf_op jit(solution)/shard_map/while/body/eval_jaxpr/pallas_call | solution.py:37
  153.8 0.8 copy-done
  154.6 4.5 %fusion.26 = (f32[32]{0:T(128)S(1)}, bf16[32,8192]{1,0:T(8,128)(2,1)S(1)}) fusion(f32[2,64,8192]{2,1,0:T(8,128)} %get-tuple-element.706, s32[]{:T(128)S(6)} %select_n.236, s32[]{:T(128)S(6)} %select_n.237, f32[8192]{0:T(1024)S(1)} %bitcast.85, bf16[8192,640]{1,0:T(8,128)(2,1)S(1)} %copy-done, f32[32,640]{1,0:T(8,128)S(1)} %get-tuple-element.629, ...), kind=kOutput, calls=%fused_computation.2.clone.1 | convolution fusion | flops 337080288 | bytes 12191368 | tf_op jit(solution)/shard_map/while/body/eval_jaxpr/dot_general | solution.py:271
  159.1 23.6 %eval_jaxpr.17 = (bf16[32,512]{1,0:T(8,128)(2,1)S(1)}, bf16[32,8192]{1,0:T(8,128)(2,1)S(1)}, f32[1,512]{1,0:T(1,128)S(1)}) custom-call(bf16[32,8192]{1,0:T(8,128)(2,1)S(1)} %get-tuple-element.631.x_ref, f32[8,128]{1,0:T(8,128)S(1)} %scatter.7.s_ref, f32[32,640]{1,0:T(8,128)S(1)} %dynamic-slice_bitcast_fusion.5.aux_ref, f32[1,512]{1,0:T(1,128)S(1)} %bitcast.91, ...), custom_call_target="tpu_custom_call" | custom-call | tf_op jit(solution)/shard_map/while/body/eval_jaxpr/pallas_call | solution.py:163
  183.1 6.0 %eval_jaxpr.16 = f32[32,640]{1,0:T(8,128)S(1)} custom-call(bf16[32,8192]{1,0:T(8,128)(2,1)S(1)} %dynamic-slice_bitcast_fusion.4.top_ref, bf16[32,8192]{1,0:T(8,128)(2,1)S(1)} %copy.33.x_ref.up_ref, bf16[640,8192]{1,0:T(8,128)(2,1)} %get-tuple-element.702.w_ref), custom_call_target="tpu_custom_call" | custom-call | flops 335544320 | bytes 11616256 | tf_op jit(solution)/shard_map/while/body/eval_jaxpr/pallas_call | solution.py:37
  190.1 4.5 %fusion.26 = (f32[32]{0:T(128)S(1)}, bf16[32,8192]{1,0:T(8,128)(2,1)S(1)}) fusion(f32[2,64,8192]{2,1,0:T(8,128)} %get-tuple-element.706, s32[]{:T(128)S(6)} %select_n.236, s32[]{:T(128)S(6)} %select_n.237, f32[8192]{0:T(1024)S(1)} %bitcast.85, bf16[8192,640]{1,0:T(8,128)(2,1)S(1)} %copy-done, f32[32,640]{1,0:T(8,128)S(1)} %get-tuple-element.629, ...), kind=kOutput, calls=%fused_computation.2.clone.1 | convolution fusion | flops 337080288 | bytes 12191368 | tf_op jit(solution)/shard_map/while/body/eval_jaxpr/dot_general | solution.py:271
  194.6 20.0 %eval_jaxpr.17 = (bf16[32,512]{1,0:T(8,128)(2,1)S(1)}, bf16[32,8192]{1,0:T(8,128)(2,1)S(1)}, f32[1,512]{1,0:T(1,128)S(1)}) custom-call(bf16[32,8192]{1,0:T(8,128)(2,1)S(1)} %get-tuple-element.631.x_ref, f32[8,128]{1,0:T(8,128)S(1)} %scatter.7.s_ref, f32[32,640]{1,0:T(8,128)S(1)} %dynamic-slice_bitcast_fusion.5.aux_ref, f32[1,512]{1,0:T(1,128)S(1)} %bitcast.91, ...), custom_call_target="tpu_custom_call" | custom-call | tf_op jit(solution)/shard_map/while/body/eval_jaxpr/pallas_call | solution.py:163
  215.0 6.0 %eval_jaxpr.16 = f32[32,640]{1,0:T(8,128)S(1)} custom-call(bf16[32,8192]{1,0:T(8,128)(2,1)S(1)} %dynamic-slice_bitcast_fusion.4.top_ref, bf16[32,8192]{1,0:T(8,128)(2,1)S(1)} %copy.33.x_ref.up_ref, bf16[640,8192]{1,0:T(8,128)(2,1)} %get-tuple-element.702.w_ref), custom_call_target="tpu_custom_call" | custom-call | flops 335544320 | bytes 11616256 | tf_op jit(solution)/shard_map/while/body/eval_jaxpr/pallas_call | solution.py:37
  221.2 0.8 copy-done
  222.0 4.5 %fusion.26 = (f32[32]{0:T(128)S(1)}, bf16[32,8192]{1,0:T(8,128)(2,1)S(1)}) fusion(f32[2,64,8192]{2,1,0:T(8,128)} %get-tuple-element.706, s32[]{:T(128)S(6)} %select_n.236, s32[]{:T(128)S(6)} %select_n.237, f32[8192]{0:T(1024)S(1)} %bitcast.85, bf16[8192,640]{1,0:T(8,128)(2,1)S(1)} %copy-done, f32[32,640]{1,0:T(8,128)S(1)} %get-tuple-element.629, ...), kind=kOutput, calls=%fused_computation.2.clone.1 | convolution fusion | flops 337080288 | bytes 12191368 | tf_op jit(solution)/shard_map/while/body/eval_jaxpr/dot_general | solution.py:271
  226.5 21.6 %eval_jaxpr.17 = (bf16[32,512]{1,0:T(8,128)(2,1)S(1)}, bf16[32,8192]{1,0:T(8,128)(2,1)S(1)}, f32[1,512]{1,0:T(1,128)S(1)}) custom-call(bf16[32,8192]{1,0:T(8,128)(2,1)S(1)} %get-tuple-element.631.x_ref, f32[8,128]{1,0:T(8,128)S(1)} %scatter.7.s_ref, f32[32,640]{1,0:T(8,128)S(1)} %dynamic-slice_bitcast_fusion.5.aux_ref, f32[1,512]{1,0:T(1,128)S(1)} %bitcast.91, ...), custom_call_target="tpu_custom_call" | custom-call | tf_op jit(solution)/shard_map/while/body/eval_jaxpr/pallas_call | solution.py:163
  248.4 6.0 %eval_jaxpr.16 = f32[32,640]{1,0:T(8,128)S(1)} custom-call(bf16[32,8192]{1,0:T(8,128)(2,1)S(1)} %dynamic-slice_bitcast_fusion.4.top_ref, bf16[32,8192]{1,0:T(8,128)(2,1)S(1)} %copy.33.x_ref.up_ref, bf16[640,8192]{1,0:T(8,128)(2,1)} %get-tuple-element.702.w_ref), custom_call_target="tpu_custom_call" | custom-call | flops 335544320 | bytes 11616256 | tf_op jit(solution)/shard_map/while/body/eval_jaxpr/pallas_call | solution.py:37
  255.4 4.5 %fusion.26 = (f32[32]{0:T(128)S(1)}, bf16[32,8192]{1,0:T(8,128)(2,1)S(1)}) fusion(f32[2,64,8192]{2,1,0:T(8,128)} %get-tuple-element.706, s32[]{:T(128)S(6)} %select_n.236, s32[]{:T(128)S(6)} %select_n.237, f32[8192]{0:T(1024)S(1)} %bitcast.85, bf16[8192,640]{1,0:T(8,128)(2,1)S(1)} %copy-done, f32[32,640]{1,0:T(8,128)S(1)} %get-tuple-element.629, ...), kind=kOutput, calls=%fused_computation.2.clone.1 | convolution fusion | flops 337080288 | bytes 12191368 | tf_op jit(solution)/shard_map/while/body/eval_jaxpr/dot_general | solution.py:271
  260.0 21.9 %eval_jaxpr.17 = (bf16[32,512]{1,0:T(8,128)(2,1)S(1)}, bf16[32,8192]{1,0:T(8,128)(2,1)S(1)}, f32[1,512]{1,0:T(1,128)S(1)}) custom-call(bf16[32,8192]{1,0:T(8,128)(2,1)S(1)} %get-tuple-element.631.x_ref, f32[8,128]{1,0:T(8,128)S(1)} %scatter.7.s_ref, f32[32,640]{1,0:T(8,128)S(1)} %dynamic-slice_bitcast_fusion.5.aux_ref, f32[1,512]{1,0:T(1,128)S(1)} %bitcast.91, ...), custom_call_target="tpu_custom_call" | custom-call | tf_op jit(solution)/shard_map/while/body/eval_jaxpr/pallas_call | solution.py:163
  282.2 6.0 %eval_jaxpr.16 = f32[32,640]{1,0:T(8,128)S(1)} custom-call(bf16[32,8192]{1,0:T(8,128)(2,1)S(1)} %dynamic-slice_bitcast_fusion.4.top_ref, bf16[32,8192]{1,0:T(8,128)(2,1)S(1)} %copy.33.x_ref.up_ref, bf16[640,8192]{1,0:T(8,128)(2,1)} %get-tuple-element.702.w_ref), custom_call_target="tpu_custom_call" | custom-call | flops 335544320 | bytes 11616256 | tf_op jit(solution)/shard_map/while/body/eval_jaxpr/pallas_call | solution.py:37
  289.2 4.5 %fusion.26 = (f32[32]{0:T(128)S(1)}, bf16[32,8192]{1,0:T(8,128)(2,1)S(1)}) fusion(f32[2,64,8192]{2,1,0:T(8,128)} %get-tuple-element.706, s32[]{:T(128)S(6)} %select_n.236, s32[]{:T(128)S(6)} %select_n.237, f32[8192]{0:T(1024)S(1)} %bitcast.85, bf16[8192,640]{1,0:T(8,128)(2,1)S(1)} %copy-done, f32[32,640]{1,0:T(8,128)S(1)} %get-tuple-element.629, ...), kind=kOutput, calls=%fused_computation.2.clone.1 | convolution fusion | flops 337080288 | bytes 12191368 | tf_op jit(solution)/shard_map/while/body/eval_jaxpr/dot_general | solution.py:271
  293.8 22.2 %eval_jaxpr.17 = (bf16[32,512]{1,0:T(8,128)(2,1)S(1)}, bf16[32,8192]{1,0:T(8,128)(2,1)S(1)}, f32[1,512]{1,0:T(1,128)S(1)}) custom-call(bf16[32,8192]{1,0:T(8,128)(2,1)S(1)} %get-tuple-element.631.x_ref, f32[8,128]{1,0:T(8,128)S(1)} %scatter.7.s_ref, f32[32,640]{1,0:T(8,128)S(1)} %dynamic-slice_bitcast_fusion.5.aux_ref, f32[1,512]{1,0:T(1,128)S(1)} %bitcast.91, ...), custom_call_target="tpu_custom_call" | custom-call | tf_op jit(solution)/shard_map/while/body/eval_jaxpr/pallas_call | solution.py:163
  316.3 6.0 %eval_jaxpr.16 = f32[32,640]{1,0:T(8,128)S(1)} custom-call(bf16[32,8192]{1,0:T(8,128)(2,1)S(1)} %dynamic-slice_bitcast_fusion.4.top_ref, bf16[32,8192]{1,0:T(8,128)(2,1)S(1)} %copy.33.x_ref.up_ref, bf16[640,8192]{1,0:T(8,128)(2,1)} %get-tuple-element.702.w_ref), custom_call_target="tpu_custom_call" | custom-call | flops 335544320 | bytes 11616256 | tf_op jit(solution)/shard_map/while/body/eval_jaxpr/pallas_call | solution.py:37
  322.5 0.8 copy-done
  323.3 4.5 %fusion.26 = (f32[32]{0:T(128)S(1)}, bf16[32,8192]{1,0:T(8,128)(2,1)S(1)}) fusion(f32[2,64,8192]{2,1,0:T(8,128)} %get-tuple-element.706, s32[]{:T(128)S(6)} %select_n.236, s32[]{:T(128)S(6)} %select_n.237, f32[8192]{0:T(1024)S(1)} %bitcast.85, bf16[8192,640]{1,0:T(8,128)(2,1)S(1)} %copy-done, f32[32,640]{1,0:T(8,128)S(1)} %get-tuple-element.629, ...), kind=kOutput, calls=%fused_computation.2.clone.1 | convolution fusion | flops 337080288 | bytes 12191368 | tf_op jit(solution)/shard_map/while/body/eval_jaxpr/dot_general | solution.py:271
  327.9 22.6 %eval_jaxpr.17 = (bf16[32,512]{1,0:T(8,128)(2,1)S(1)}, bf16[32,8192]{1,0:T(8,128)(2,1)S(1)}, f32[1,512]{1,0:T(1,128)S(1)}) custom-call(bf16[32,8192]{1,0:T(8,128)(2,1)S(1)} %get-tuple-element.631.x_ref, f32[8,128]{1,0:T(8,128)S(1)} %scatter.7.s_ref, f32[32,640]{1,0:T(8,128)S(1)} %dynamic-slice_bitcast_fusion.5.aux_ref, f32[1,512]{1,0:T(1,128)S(1)} %bitcast.91, ...), custom_call_target="tpu_custom_call" | custom-call | tf_op jit(solution)/shard_map/while/body/eval_jaxpr/pallas_call | solution.py:163
  350.8 6.0 %eval_jaxpr.16 = f32[32,640]{1,0:T(8,128)S(1)} custom-call(bf16[32,8192]{1,0:T(8,128)(2,1)S(1)} %dynamic-slice_bitcast_fusion.4.top_ref, bf16[32,8192]{1,0:T(8,128)(2,1)S(1)} %copy.33.x_ref.up_ref, bf16[640,8192]{1,0:T(8,128)(2,1)} %get-tuple-element.702.w_ref), custom_call_target="tpu_custom_call" | custom-call | flops 335544320 | bytes 11616256 | tf_op jit(solution)/shard_map/while/body/eval_jaxpr/pallas_call | solution.py:37
  357.0 0.8 copy-done
  357.8 4.5 %fusion.26 = (f32[32]{0:T(128)S(1)}, bf16[32,8192]{1,0:T(8,128)(2,1)S(1)}) fusion(f32[2,64,8192]{2,1,0:T(8,128)} %get-tuple-element.706, s32[]{:T(128)S(6)} %select_n.236, s32[]{:T(128)S(6)} %select_n.237, f32[8192]{0:T(1024)S(1)} %bitcast.85, bf16[8192,640]{1,0:T(8,128)(2,1)S(1)} %copy-done, f32[32,640]{1,0:T(8,128)S(1)} %get-tuple-element.629, ...), kind=kOutput, calls=%fused_computation.2.clone.1 | convolution fusion | flops 337080288 | bytes 12191368 | tf_op jit(solution)/shard_map/while/body/eval_jaxpr/dot_general | solution.py:271
  362.3 21.7 %eval_jaxpr.17 = (bf16[32,512]{1,0:T(8,128)(2,1)S(1)}, bf16[32,8192]{1,0:T(8,128)(2,1)S(1)}, f32[1,512]{1,0:T(1,128)S(1)}) custom-call(bf16[32,8192]{1,0:T(8,128)(2,1)S(1)} %get-tuple-element.631.x_ref, f32[8,128]{1,0:T(8,128)S(1)} %scatter.7.s_ref, f32[32,640]{1,0:T(8,128)S(1)} %dynamic-slice_bitcast_fusion.5.aux_ref, f32[1,512]{1,0:T(1,128)S(1)} %bitcast.91, ...), custom_call_target="tpu_custom_call" | custom-call | tf_op jit(solution)/shard_map/while/body/eval_jaxpr/pallas_call | solution.py:163
  384.3 35.2 %all_to_all.15 = bf16[16,130,512]{2,1,0:T(8,128)(2,1)S(1)} all-to-all(bf16[16,130,512]{2,1,0:T(8,128)(2,1)S(1)} %broadcast_in_dim.96), channel_id=1, replica_groups=mesh['section'=8,'tensor'=16] {'tensor'}, dimensions={0} | all-to-all | bytes 4259840 | tf_op jit(solution)/shard_map/all_to_all | solution.py:303
  420.4 1.2 copy.12
  421.6 2.3 broadcast_in_dim_reshape.3
  (223 shorter events, 8.7 us)
Async XLA Ops:
  0.6 2.3 copy-start.1
  2.9 2.5 copy-start.2
  2.9 3.4 copy-start.6
  3.0 3.4 copy-start.7
  3.0 3.5 copy-start.5
  6.5 2.0 copy-start.3
  8.8 7.0 %copy-start = (bf16[8192,640]{1,0:T(8,128)(2,1)S(1)}, bf16[8192,640]{1,0:T(8,128)(2,1)}, u32[]{:S(2)}) copy-start(bf16[8192,640]{1,0:T(8,128)(2,1)} %get-tuple-element.704) | copy-start | bytes 31457284 | tf_op jit(solution)/shard_map/while
  43.8 7.0 %copy-start = (bf16[8192,640]{1,0:T(8,128)(2,1)S(1)}, bf16[8192,640]{1,0:T(8,128)(2,1)}, u32[]{:S(2)}) copy-start(bf16[8192,640]{1,0:T(8,128)(2,1)} %get-tuple-element.704) | copy-start | bytes 31457284 | tf_op jit(solution)/shard_map/while
  81.2 7.0 %copy-start = (bf16[8192,640]{1,0:T(8,128)(2,1)S(1)}, bf16[8192,640]{1,0:T(8,128)(2,1)}, u32[]{:S(2)}) copy-start(bf16[8192,640]{1,0:T(8,128)(2,1)} %get-tuple-element.704) | copy-start | bytes 31457284 | tf_op jit(solution)/shard_map/while
  117.6 7.0 %copy-start = (bf16[8192,640]{1,0:T(8,128)(2,1)S(1)}, bf16[8192,640]{1,0:T(8,128)(2,1)}, u32[]{:S(2)}) copy-start(bf16[8192,640]{1,0:T(8,128)(2,1)} %get-tuple-element.704) | copy-start | bytes 31457284 | tf_op jit(solution)/shard_map/while
  147.5 7.0 %copy-start = (bf16[8192,640]{1,0:T(8,128)(2,1)S(1)}, bf16[8192,640]{1,0:T(8,128)(2,1)}, u32[]{:S(2)}) copy-start(bf16[8192,640]{1,0:T(8,128)(2,1)} %get-tuple-element.704) | copy-start | bytes 31457284 | tf_op jit(solution)/shard_map/while
  183.0 7.0 %copy-start = (bf16[8192,640]{1,0:T(8,128)(2,1)S(1)}, bf16[8192,640]{1,0:T(8,128)(2,1)}, u32[]{:S(2)}) copy-start(bf16[8192,640]{1,0:T(8,128)(2,1)} %get-tuple-element.704) | copy-start | bytes 31457284 | tf_op jit(solution)/shard_map/while
  214.9 7.0 %copy-start = (bf16[8192,640]{1,0:T(8,128)(2,1)S(1)}, bf16[8192,640]{1,0:T(8,128)(2,1)}, u32[]{:S(2)}) copy-start(bf16[8192,640]{1,0:T(8,128)(2,1)} %get-tuple-element.704) | copy-start | bytes 31457284 | tf_op jit(solution)/shard_map/while
  248.4 7.0 %copy-start = (bf16[8192,640]{1,0:T(8,128)(2,1)S(1)}, bf16[8192,640]{1,0:T(8,128)(2,1)}, u32[]{:S(2)}) copy-start(bf16[8192,640]{1,0:T(8,128)(2,1)} %get-tuple-element.704) | copy-start | bytes 31457284 | tf_op jit(solution)/shard_map/while
  282.2 7.0 %copy-start = (bf16[8192,640]{1,0:T(8,128)(2,1)S(1)}, bf16[8192,640]{1,0:T(8,128)(2,1)}, u32[]{:S(2)}) copy-start(bf16[8192,640]{1,0:T(8,128)(2,1)} %get-tuple-element.704) | copy-start | bytes 31457284 | tf_op jit(solution)/shard_map/while
  316.3 7.0 %copy-start = (bf16[8192,640]{1,0:T(8,128)(2,1)S(1)}, bf16[8192,640]{1,0:T(8,128)(2,1)}, u32[]{:S(2)}) copy-start(bf16[8192,640]{1,0:T(8,128)(2,1)} %get-tuple-element.704) | copy-start | bytes 31457284 | tf_op jit(solution)/shard_map/while
  350.7 7.0 %copy-start = (bf16[8192,640]{1,0:T(8,128)(2,1)S(1)}, bf16[8192,640]{1,0:T(8,128)(2,1)}, u32[]{:S(2)}) copy-start(bf16[8192,640]{1,0:T(8,128)(2,1)} %get-tuple-element.704) | copy-start | bytes 31457284 | tf_op jit(solution)/shard_map/while
  384.1 35.4 %copy-start.4 = (f32[4,640]{1,0:T(4,128)}, f32[4,640]{1,0:T(4,128)S(1)}, u32[]{:S(2)}) copy-start(f32[4,640]{1,0:T(4,128)S(1)} %get-tuple-element.410) | copy-start | bytes 30724
